TPU v7x, 128 devices: a whole 4x4x4 slice. The times are simulated.
128 devices in a mesh: dp: 16 (over y, x), seq: 8 (over z, core).
Axes of the slice: x: 4, y: 4, z: 4, core: 2. Of those that a mesh axis runs over, the one named last changes fastest.
Arguments:
- feats: bfloat16 [65536, 1024], P(('dp', 'seq')), may hold values from -6 to 6
- gain: float32 [1024], replicated, may hold values from 0.1 to 1.9
- w_qkv: bfloat16 [1024, 3072], replicated, as said below
- w_out: bfloat16 [1024, 1024], replicated, may hold values from -3 to 3
- block_cols: int32 [16, 32, 8], P('dp'), may hold values from 0 to 31, as said below
- block_counts: int32 [16, 32], P('dp'), may hold values from 1 to 8, 128 in all within a row
- cotan: bfloat16 [65536, 1024], P(('dp', 'seq')), may hold values from -0.3984375 to 0.3984375
Outputs:
- result: bfloat16 [65536, 1024], P(('dp', 'seq'))
- grad_feats: bfloat16 [65536, 1024], P(('dp', 'seq'))
- grad_qkv: bfloat16 [1024, 3072], P('seq')
- grad_out: bfloat16 [1024, 1024], P('seq')
Inputs may be any that keep to these rules, and one draw needn't show every extreme that they name: `block_cols`: for every batch and row block r, the 8 listed column blocks are distinct and the first is r itself. `block_counts`: each batch's counts sum to 128. `w_qkv`: entries lie within 70 / sqrt(1024) in magnitude.
All inputs are finite; a program needn't handle non-finite values.
Results may differ from a plain program's by a relative error of at most 0.014.
Values may be sent and summed in bfloat16 or wider, within the bound.
A program may use at most 128 MiB of HBM per device.

v0:
```python
import jax
import jax.numpy as jnp
from jax import lax
from jax.sharding import PartitionSpec as P

HD = 64
BLK = 128
MAXB = 8


EPSILON = 1e-05


def layer_norm(feats, gain):
    values_f = feats.astype(jnp.float32)
    centred = values_f - jnp.mean(values_f, axis=1, keepdims=True)
    inverse = lax.rsqrt(jnp.mean(centred * centred, axis=1, keepdims=True) + EPSILON)
    scaled = centred * inverse
    return (scaled, inverse, (scaled * gain[None, :]).astype(jnp.bfloat16))


def live_slots(counts):
    return jnp.arange(MAXB, dtype=jnp.int32)[None, :] < counts[:, None]


def contract_rows(left_cols, right_cols):
    return lax.dot_general(
        left_cols, right_cols, (((0,), (0,)), ((), ())), preferred_element_type=jnp.float32
    )


def stacked_table(key_heads, value_heads, block_total, head_count):
    key_b = key_heads.reshape(block_total, BLK, head_count, HD)
    value_b = value_heads.reshape(block_total, BLK, head_count, HD)
    return jnp.concatenate([key_b, value_b], axis=3).reshape(block_total, BLK * head_count * 2 * HD)


def select_blocks(onehot, table, head_count):
    picked = jnp.einsum("gsc,cf->gsf", onehot, table, preferred_element_type=jnp.float32).astype(
        jnp.bfloat16
    )
    picked = picked.reshape(onehot.shape[0], onehot.shape[1], BLK, head_count, 2 * HD)
    return (picked[..., :HD], picked[..., HD:])


def forward_blocks(query_heads, key_heads, value_heads, col_blocks, counts, head_count):
    per_step = 4
    block_total = query_heads.shape[0] // BLK
    steps_count = block_total // per_step
    query_b = query_heads.reshape(steps_count, per_step, BLK, head_count, HD)
    table = stacked_table(key_heads, value_heads, block_total, head_count)
    col_steps = col_blocks.reshape(steps_count, per_step, MAXB)
    count_steps = counts.reshape(steps_count, per_step)
    block_range = jnp.arange(block_total, dtype=jnp.int32)
    score_scale = HD ** (-0.5)

    def forward_block_step(inputs):
        query_g, col_g, count_g = inputs
        onehot = (col_g[:, :, None] == block_range[None, None, :]).astype(jnp.bfloat16)
        key_g, value_g = select_blocks(onehot, table, head_count)
        scores = (
            jnp.einsum("gqhd,gskhd->ghqsk", query_g, key_g, preferred_element_type=jnp.float32)
            * score_scale
        )
        live_mask = live_slots(count_g)[:, None, None, :, None]
        row_max = jnp.max(jnp.where(live_mask, scores, -jnp.inf), axis=(3, 4), keepdims=True)
        row_total = jnp.sum(
            jnp.where(live_mask, jnp.exp(scores - row_max), 0.0), axis=(3, 4), keepdims=True
        )
        log_total = row_max + jnp.log(row_total)
        probabilities = jnp.where(live_mask, jnp.exp(scores - log_total), 0.0).astype(jnp.bfloat16)
        attended = jnp.einsum(
            "ghqsk,gskhd->gqhd", probabilities, value_g, preferred_element_type=jnp.float32
        )
        return (attended.astype(jnp.bfloat16), log_total[:, :, :, 0, 0])

    attended, log_total = lax.map(forward_block_step, (query_b, col_steps, count_steps))
    return (attended.reshape(query_heads.shape), log_total)


def backward_blocks(
    query_heads,
    key_heads,
    value_heads,
    attended_heads,
    grad_heads,
    log_total,
    col_blocks,
    counts,
    head_count,
):
    per_step = 4
    block_total = query_heads.shape[0] // BLK
    steps_count = block_total // per_step
    query_b = query_heads.reshape(steps_count, per_step, BLK, head_count, HD)
    grad_b = grad_heads.reshape(steps_count, per_step, BLK, head_count, HD)
    attended_b = attended_heads.reshape(steps_count, per_step, BLK, head_count, HD)
    table = stacked_table(key_heads, value_heads, block_total, head_count)
    col_steps = col_blocks.reshape(steps_count, per_step, MAXB)
    count_steps = counts.reshape(steps_count, per_step)
    delta_all = jnp.sum(attended_b.astype(jnp.float32) * grad_b.astype(jnp.float32), axis=4)
    block_range = jnp.arange(block_total, dtype=jnp.int32)
    score_scale = HD ** (-0.5)

    def backward_block_step(carry, inputs):
        key_sum, value_sum = carry
        query_g, grad_g, delta_g, log_g, col_g, count_g = inputs
        matches = col_g[:, :, None] == block_range[None, None, :]
        key_g, value_g = select_blocks(matches.astype(jnp.bfloat16), table, head_count)
        scores = (
            jnp.einsum("gqhd,gskhd->ghqsk", query_g, key_g, preferred_element_type=jnp.float32)
            * score_scale
        )
        live_mask = live_slots(count_g)[:, None, None, :, None]
        probabilities = jnp.where(
            live_mask, jnp.exp(scores - log_g[:, :, :, None, None]), 0.0
        ).astype(jnp.bfloat16)
        prob_grad = jnp.einsum(
            "gqhd,gskhd->ghqsk", grad_g, value_g, preferred_element_type=jnp.float32
        )
        delta_t = jnp.transpose(delta_g, (0, 2, 1))[:, :, :, None, None]
        score_grad = (
            probabilities.astype(jnp.float32) * (prob_grad - delta_t) * score_scale
        ).astype(jnp.bfloat16)
        query_grad = jnp.einsum(
            "ghqsk,gskhd->gqhd", score_grad, key_g, preferred_element_type=jnp.float32
        ).astype(jnp.bfloat16)
        key_pairs = jnp.einsum(
            "ghqsk,gqhd->gskhd", score_grad, query_g, preferred_element_type=jnp.float32
        )
        value_pairs = jnp.einsum(
            "ghqsk,gqhd->gskhd", probabilities, grad_g, preferred_element_type=jnp.float32
        )
        selector = matches.astype(jnp.float32)
        key_sum = key_sum + jnp.einsum(
            "gsc,gskhd->ckhd", selector, key_pairs, precision=lax.Precision.HIGHEST
        )
        value_sum = value_sum + jnp.einsum(
            "gsc,gskhd->ckhd", selector, value_pairs, precision=lax.Precision.HIGHEST
        )
        return ((key_sum, value_sum), query_grad)

    zeros_f = jnp.zeros((block_total, BLK, head_count, HD), jnp.float32)
    (key_sum, value_sum), query_grad = lax.scan(
        backward_block_step,
        (zeros_f, zeros_f),
        (query_b, grad_b, delta_all, log_total, col_steps, count_steps),
    )
    shape = query_heads.shape
    return (
        query_grad.reshape(shape),
        key_sum.reshape(shape).astype(jnp.bfloat16),
        value_sum.reshape(shape).astype(jnp.bfloat16),
    )


def body(feats, gain, w_qkv, w_out, block_cols, block_counts, cotan):
    seq_count = lax.axis_size("seq")
    model_width = feats.shape[1]
    qkv_width = 3 * model_width
    scaled, inverse, normed = layer_norm(feats, gain)
    mixed_proj = jnp.dot(normed, w_qkv, preferred_element_type=jnp.float32).astype(jnp.bfloat16)
    query_rows = mixed_proj[:, :model_width]
    key_rows = mixed_proj[:, model_width : 2 * model_width]
    value_rows = mixed_proj[:, 2 * model_width :]
    query_heads, key_heads, value_heads = (
        lax.all_to_all(query_rows, "seq", split_axis=1, concat_axis=0, tiled=True),
        lax.all_to_all(key_rows, "seq", split_axis=1, concat_axis=0, tiled=True),
        lax.all_to_all(value_rows, "seq", split_axis=1, concat_axis=0, tiled=True),
    )
    head_count = query_heads.shape[1] // HD
    col_blocks = block_cols[0]
    counts = block_counts[0]
    attended_heads, log_total = forward_blocks(
        query_heads, key_heads, value_heads, col_blocks, counts, head_count
    )
    attended = lax.all_to_all(attended_heads, "seq", split_axis=0, concat_axis=1, tiled=True)
    result = (
        feats.astype(jnp.float32) + jnp.dot(attended, w_out, preferred_element_type=jnp.float32)
    ).astype(jnp.bfloat16)
    grad_att = lax.dot_general(
        cotan, w_out, (((1,), (1,)), ((), ())), preferred_element_type=jnp.float32
    ).astype(jnp.bfloat16)
    grad_heads = lax.all_to_all(grad_att, "seq", split_axis=1, concat_axis=0, tiled=True)
    query_grad, key_grad, value_grad = backward_blocks(
        query_heads,
        key_heads,
        value_heads,
        attended_heads,
        grad_heads,
        log_total,
        col_blocks,
        counts,
        head_count,
    )
    query_back, key_back, value_back = (
        lax.all_to_all(query_grad, "seq", split_axis=0, concat_axis=1, tiled=True),
        lax.all_to_all(key_grad, "seq", split_axis=0, concat_axis=1, tiled=True),
        lax.all_to_all(value_grad, "seq", split_axis=0, concat_axis=1, tiled=True),
    )
    grad_mixed = jnp.concatenate([query_back, key_back, value_back], axis=1)
    grad_normed = lax.dot_general(
        grad_mixed, w_qkv, (((1,), (1,)), ((), ())), preferred_element_type=jnp.float32
    )
    gained = grad_normed * gain[None, :]
    mean_one = jnp.mean(gained, axis=1, keepdims=True)
    mean_two = jnp.mean(gained * scaled, axis=1, keepdims=True)
    grad_feats = (
        cotan.astype(jnp.float32) + inverse * (gained - mean_one - scaled * mean_two)
    ).astype(jnp.bfloat16)
    summed = lax.psum(
        jnp.concatenate(
            [contract_rows(normed, grad_mixed), contract_rows(attended, cotan)], axis=1
        ),
        ("dp", "seq"),
    )
    shard_rows = model_width // seq_count
    own_rows = lax.dynamic_slice_in_dim(summed, lax.axis_index("seq") * shard_rows, shard_rows, 0)
    grad_qkv = own_rows[:, :qkv_width].astype(jnp.bfloat16)
    grad_out = own_rows[:, qkv_width:].astype(jnp.bfloat16)
    return (result, grad_feats, grad_qkv, grad_out)


def solution(mesh):
    in_specs = (
        P(("dp", "seq"), None),
        P(),
        P(),
        P(),
        P("dp", None, None),
        P("dp", None),
        P(("dp", "seq"), None),
    )
    out_specs = (P(("dp", "seq"), None), P(("dp", "seq"), None), P("seq", None), P("seq", None))
    return jax.shard_map(body, mesh=mesh, in_specs=in_specs, out_specs=out_specs, check_vma=False)
```

profile of v0, /device:TPU:0, one launch (start us, length us, event | category | flops | bytes accessed | tf_op | source)
XLA Modules:
  0.0 628.2 jit_solution(8621975070728321357)
XLA Ops:
  4.0 6.7 %convolution_convert_fusion.2 = bf16[512,3072]{1,0:T(8,128)(2,1)S(1)} fusion(bf16[1024,3072]{1,0:T(8,128)(2,1)} %param.13, bf16[512,1024]{1,0:T(8,128)(2,1)S(1)} %copy-done.8, f32[1024]{0:T(1024)S(1)} %copy-done.19, f32[512]{0:T(512)S(1)} %add_rsqrt_fusion, f32[512]{0:T(512)S(1)} %broadcast_multiply_fusion.2), kind=kOutput, calls=%fused_computation.70 | convolution fusion | flops 3225419776 | bytes 10493952 | tf_op jit(solution)/shard_map/dot_general | solution.py:162
  13.7 5.4 all-to-all-start.1
  21.4 13.7 %all-to-all-done.1 = bf16[512,8,128]{0,2,1:T(8,128)(2,1)S(1)} async-done(((bf16[512,8,128]{0,2,1:T(8,128)(2,1)}), bf16[512,8,128]{0,2,1:T(8,128)(2,1)S(1)}, u32[]{:S(2)}, u32[]{:S(2)}) %all-to-all-start.1) | async-done | bytes 1048608 | tf_op jit(solution)/shard_map/all_to_all | solution.py:169
  35.0 4.2 all-to-all-start
  41.6 13.7 %all-to-all-done = bf16[512,8,128]{0,2,1:T(8,128)(2,1)} async-done(((bf16[512,8,128]{0,2,1:T(8,128)(2,1)}), bf16[512,8,128]{0,2,1:T(8,128)(2,1)}, u32[]{:S(2)}, u32[]{:S(2)}) %all-to-all-start) | async-done | bytes 1048608 | tf_op jit(solution)/shard_map/all_to_all | solution.py:168
  55.2 4.2 all-to-all-start.2
  77.0 4.7 copy.69
  81.7 4.5 reshape.177
  86.2 5.2 all-to-all-start.4
  94.5 59.6 %while.28 = (s32[]{:T(128)}, bf16[8,4,128,2,64]{2,1,4,3,0:T(4,128)(2,1)S(1)}, f32[8,4,2,128]{3,2,1,0:T(2,128)S(1)}, s32[8,4,8]{2,1,0:T(4,128)S(1)}, bf16[32,3276...) while((s32[]{:T(128)}, ...), condition=%wide.region_5.6_spmd.clone, body=%wide.region_2.5_spmd.clone.sunk | while | flops 348192800 | bytes 23626400 | solution.py:77
  155.3 4.8 all-to-all-start.3
  165.6 239.2 %while.29 = (s32[]{:T(128)}, f32[32,128,2,64]{1,0,3,2:T(8,128)}, f32[32,128,2,64]{1,0,3,2:T(8,128)}, bf16[8,4,128,2,64]{2,1,4,3,0:T(4,128)(2,1)}, s32[8,4,8]{2,1...) while((s32[]{:T(128)}, f32[32,128,2,64]{1,0,3,2:T(8,128)}, ...), condition=%wide.region_8.9_spmd.clone, body=%wide.region_7.8_spmd.clone.sunk | while | flops 1153502208 | bytes 98731120 | solution.py:144
  182.9 5.5 bitcast_add_fusion.4
  189.9 3.5 bitcast_add_fusion.5
  212.2 6.1 bitcast_add_fusion.4
  242.1 6.1 bitcast_add_fusion.4
  272.0 6.1 bitcast_add_fusion.4
  302.0 6.1 bitcast_add_fusion.4
  331.9 6.1 bitcast_add_fusion.4
  361.8 6.1 bitcast_add_fusion.4
  391.8 6.1 bitcast_add_fusion.4
  410.6 4.8 all-to-all-start.7
  421.3 10.2 %all-to-all-done.7 = bf16[8,512,128]{1,2,0:T(8,128)(2,1)} async-done(((bf16[8,512,128]{1,2,0:T(8,128)(2,1)}), bf16[8,512,128]{1,2,0:T(8,128)(2,1)}, u32[]{:S(2)}, u32[]{:S(2)}) %all-to-all-start.7) | async-done | bytes 1048608 | tf_op jit(solution)/shard_map/all_to_all | solution.py:199
  431.5 4.2 all-to-all-start.6
  437.0 14.7 %all-to-all-done.6 = bf16[8,512,128]{1,2,0:T(8,128)(2,1)} async-done(((bf16[8,512,128]{1,2,0:T(8,128)(2,1)}), bf16[8,512,128]{1,2,0:T(8,128)(2,1)}, u32[]{:S(2)}, u32[]{:S(2)}) %all-to-all-start.6) | async-done | bytes 1048608 | tf_op jit(solution)/shard_map/all_to_all | solution.py:198
  451.7 4.2 all-to-all-start.5
  456.0 4.8 fusion.76
  464.3 7.6 %all-to-all-done.5 = bf16[8,512,128]{1,2,0:T(8,128)(2,1)} async-done(((bf16[8,512,128]{1,2,0:T(8,128)(2,1)}), bf16[8,512,128]{1,2,0:T(8,128)(2,1)}, u32[]{:S(2)}, u32[]{:S(2)}) %all-to-all-start.5) | async-done | bytes 1048608 | tf_op jit(solution)/shard_map/all_to_all | solution.py:197
  471.9 8.9 %multiply_reduce_fusion.1 = (f32[512]{0:T(512)S(1)}, f32[512]{0:T(512)S(1)}, f32[512,1024]{1,0:T(8,128)}) fusion(f32[1024]{0:T(1024)S(1)} %copy-done.20, f32[512]{0:T(512)S(1)} %copy-done.17, f32[512]{0:T(512)S(1)} %copy-done.15, bf16[512,1024]{1,0:T(8,128)(2,1)S(1)} %copy-done.9, bf16[1024,3072]{1,0:T(8,128)(2,1)} %param.13, ...), kind=kOutput, calls=%fused_computation.91 | convolution fusion | flops 3234331648 | bytes 12595200 | tf_op jit(solution)/shard_map/dot_general | solution.py:202
  480.8 5.8 fusion.67
  486.6 6.0 pad_maximum_fusion
  492.7 130.1 %all-reduce.1 = bf16[1024,4096]{1,0:T(8,128)(2,1)} all-reduce(f32[1024,4096]{1,0:T(8,128)} %pad_maximum_fusion), channel_id=1, replica_groups=mesh['dp'=16,'seq'=8] {'dp','seq'}, use_global_device_ids=true, to_apply=%region_11.12 | all-reduce | flops 4194304 | bytes 25165824 | tf_op jit(solution)/shard_map/psum | solution.py:211
  (402 shorter events, 304.6 us)
Async XLA Ops:
  0.6 60.2 %copy-start = (bf16[1024,1024]{1,0:T(8,128)(2,1)S(1)}, bf16[1024,1024]{1,0:T(8,128)(2,1)}, u32[]{:S(2)}) copy-start(bf16[1024,1024]{1,0:T(8,128)(2,1)} %param.14) | copy-start | bytes 6291460
  2.3 8.4 %copy-start.14 = (f32[512]{0:T(512)}, f32[512]{0:T(512)S(1)}, u32[]{:S(2)}) copy-start(f32[512]{0:T(512)S(1)} %broadcast_multiply_fusion.2) | copy-start | bytes 6148
  3.9 6.7 %copy-start.16 = (f32[512]{0:T(512)}, f32[512]{0:T(512)S(1)}, u32[]{:S(2)}) copy-start(f32[512]{0:T(512)S(1)} %add_rsqrt_fusion) | copy-start | bytes 6148
  13.7 21.4 %all-to-all-start.1 = ((bf16[512,8,128]{0,2,1:T(8,128)(2,1)}), bf16[512,8,128]{0,2,1:T(8,128)(2,1)S(1)}, u32[]{:S(2)}, u32[]{:S(2)}) async-start(bf16[512,8,128]{0,2,1:T(8,128)(2,1)} %bitcast.208), calls=%async_computation.1 | async-start | bytes 2097152 | tf_op jit(solution)/shard_map/all_to_all | solution.py:169
  35.0 20.2 %all-to-all-start = ((bf16[512,8,128]{0,2,1:T(8,128)(2,1)}), bf16[512,8,128]{0,2,1:T(8,128)(2,1)}, u32[]{:S(2)}, u32[]{:S(2)}) async-start(bf16[512,8,128]{0,2,1:T(8,128)(2,1)} %bitcast.207), calls=%async_computation | async-start | bytes 2097152 | tf_op jit(solution)/shard_map/all_to_all | solution.py:168
  39.3 20.2 %copy-start.18 = (s32[1,32,8]{1,2,0:T(8,128)S(1)}, s32[1,32,8]{1,2,0:T(8,128)}, u32[]{:S(2)}) copy-start(s32[1,32,8]{1,2,0:T(8,128)} %param.15) | copy-start | bytes 3076
  39.3 20.8 %copy-start.21 = (s32[1,32]{1,0:T(1,128)S(1)}, s32[1,32]{1,0:T(1,128)}, u32[]{:S(2)}) copy-start(s32[1,32]{1,0:T(1,128)} %param.16) | copy-start | bytes 388
  55.2 31.0 %all-to-all-start.2 = ((bf16[512,8,128]{0,2,1:T(8,128)(2,1)}), bf16[512,8,128]{0,2,1:T(8,128)(2,1)}, u32[]{:S(2)}, u32[]{:S(2)}) async-start(bf16[512,8,128]{0,2,1:T(8,128)(2,1)} %bitcast.206), calls=%async_computation.2 | async-start | bytes 2097152 | tf_op jit(solution)/shard_map/all_to_all | solution.py:167
  86.2 69.1 %all-to-all-start.4 = ((bf16[512,8,128]{0,2,1:T(8,128)(2,1)}), bf16[512,8,128]{0,2,1:T(8,128)(2,1)}, u32[]{:S(2)}, u32[]{:S(2)}) async-start(bf16[512,8,128]{0,2,1:T(8,128)(2,1)} %bitcast.9), calls=%async_computation.4 | async-start | bytes 2097152 | tf_op jit(solution)/shard_map/all_to_all | solution.py:184
  155.3 255.3 %all-to-all-start.3 = ((bf16[8,512,128]{1,2,0:T(8,128)(2,1)}), bf16[8,512,128]{1,2,0:T(8,128)(2,1)}, u32[]{:S(2)}, u32[]{:S(2)}) async-start(bf16[8,512,128]{1,2,0:T(8,128)(2,1)} %all_to_all.109), calls=%async_computation.3 | async-start | bytes 2097152 | tf_op jit(solution)/shard_map/all_to_all | solution.py:177
  182.9 5.5 copy-start.4
  189.9 3.5 copy-start.2
  212.2 6.1 copy-start.4
  219.9 3.5 copy-start.2
  242.1 6.1 copy-start.4
  249.8 3.5 copy-start.2
  272.0 6.1 copy-start.4
  279.7 3.5 copy-start.2
  302.0 6.1 copy-start.4
  309.7 3.5 copy-start.2
  331.9 6.1 copy-start.4
  361.8 6.1 copy-start.4
  391.8 6.1 copy-start.4
  410.6 20.9 %all-to-all-start.7 = ((bf16[8,512,128]{1,2,0:T(8,128)(2,1)}), bf16[8,512,128]{1,2,0:T(8,128)(2,1)}, u32[]{:S(2)}, u32[]{:S(2)}) async-start(bf16[8,512,128]{1,2,0:T(8,128)(2,1)} %copy.80), calls=%async_computation.7 | async-start | bytes 2097152 | tf_op jit(solution)/shard_map/all_to_all | solution.py:199
  418.7 17.1 %copy-start.10 = (bf16[8,4,128,2,64]{2,1,4,3,0:T(4,128)(2,1)S(1)}, bf16[8,4,128,2,64]{2,1,4,3,0:T(4,128)(2,1)}, u32[]{:S(2)}) copy-start(bf16[8,4,128,2,64]{2,1,4,3,0:T(4,128)(2,1)} %get-tuple-element.113) | copy-start | bytes 3145732
  431.5 20.2 %all-to-all-start.6 = ((bf16[8,512,128]{1,2,0:T(8,128)(2,1)}), bf16[8,512,128]{1,2,0:T(8,128)(2,1)}, u32[]{:S(2)}, u32[]{:S(2)}) async-start(bf16[8,512,128]{1,2,0:T(8,128)(2,1)} %copy.79), calls=%async_computation.6 | async-start | bytes 2097152 | tf_op jit(solution)/shard_map/all_to_all | solution.py:198
  451.7 20.2 %all-to-all-start.5 = ((bf16[8,512,128]{1,2,0:T(8,128)(2,1)}), bf16[8,512,128]{1,2,0:T(8,128)(2,1)}, u32[]{:S(2)}, u32[]{:S(2)}) async-start(bf16[8,512,128]{1,2,0:T(8,128)(2,1)} %all_to_all.116), calls=%async_computation.5 | async-start | bytes 2097152 | tf_op jit(solution)/shard_map/all_to_all | solution.py:197
  456.0 4.8 copy-start.9
  460.8 11.1 %copy-start.15 = (f32[512]{0:T(512)S(1)}, f32[512]{0:T(512)}, u32[]{:S(2)}) copy-start(f32[512]{0:T(512)} %copy-done.14) | copy-start | bytes 6148
  460.8 11.1 %copy-start.17 = (f32[512]{0:T(512)S(1)}, f32[512]{0:T(512)}, u32[]{:S(2)}) copy-start(f32[512]{0:T(512)} %copy-done.16) | copy-start | bytes 6148
  460.8 11.1 %copy-start.20 = (f32[1024]{0:T(1024)S(1)}, f32[1024]{0:T(1024)}, u32[]{:S(2)}) copy-start(f32[1024]{0:T(1024)} %param.12) | copy-start | bytes 12292
  480.8 5.8 copy-start.11
  (47 other events, 107.5 us)
where the time goes:
time: 637 us; the launch traced here: 628 us
  matrix products  231 us (36%)
  local copies, waits for them, and re-layouts  138 us (22%)
  blocking collectives  130 us (20%)
  waiting for transfers between devices  59.9 us (9%)
  starting transfers between devices  37.2 us (6%)
  other arithmetic  28.9 us (5%)
    psum x1, blocking collectives, body(): lax.psum(jnp.concatenate([contract_rows(normed, grad_mixed), contract_row...  130 us
    dot_general x8, matrix products, backward_block_step(): jnp.einsum('gsc,gskhd->ckhd', selector, key_pairs, precision=lax.Precisio...  48.1 us
    while x120, local copies, waits for them, and re-layouts  42.8 us
    dot_general x16, matrix products, select_blocks(): jnp.einsum('gsc,cf->gsf', onehot, table, preferred_element_type=jnp.float32)  37.4 us
    slice x16, local copies, waits for them, and re-layouts, select_blocks(): return (picked[..., :HD], picked[..., HD:])  31.4 us
    dot_general x8, matrix products, backward_block_step(): jnp.einsum('gsc,gskhd->ckhd', selector, value_pairs, precision=lax.Precis...  28.1 us
    dot_general x8, matrix products, backward_block_step(): jnp.einsum('ghqsk,gqhd->gskhd', score_grad, query_g, preferred_element_ty...  21.4 us
    dot_general x8, matrix products, backward_block_step(): jnp.einsum('gqhd,gskhd->ghqsk', query_g, key_g, preferred_element_type=jn...  18.3 us
  transfers between devices with their start and end apart: 8, of which 5 were waited for; matrix products, arithmetic and copies ran while one was open for 54% of the time, Pallas kernels for 0%

commit v1 on v0

v1 whole, which is shorter than its diff:
```python
import functools

import jax
import jax.numpy as jnp
from jax import lax
from jax.experimental import pallas as pl
from jax.experimental.pallas import tpu as pltpu
from jax.sharding import PartitionSpec as P

HD = 64
BLK = 128
MAXB = 8
SCALE = HD ** (-0.5)
NEG = -1e30

EPSILON = 1e-05


def layer_norm(feats, gain):
    values_f = feats.astype(jnp.float32)
    centred = values_f - jnp.mean(values_f, axis=1, keepdims=True)
    inverse = lax.rsqrt(jnp.mean(centred * centred, axis=1, keepdims=True) + EPSILON)
    scaled = centred * inverse
    return (scaled, inverse, (scaled * gain[None, :]).astype(jnp.bfloat16))


def contract_rows(left_cols, right_cols):
    return lax.dot_general(
        left_cols, right_cols, (((0,), (0,)), ((), ())), preferred_element_type=jnp.float32
    )


def head_masks(width):
    lane = lax.broadcasted_iota(jnp.int32, (1, width), 1)
    return [(lane >= h * HD) & (lane < (h + 1) * HD) for h in range(width // HD)]


def stack_heads(x, masks):
    return jnp.concatenate([jnp.where(m, x, jnp.zeros_like(x)) for m in masks], axis=0)


def unstack_heads(y, masks):
    out = y[0:BLK]
    for h in range(1, len(masks)):
        out = jnp.where(masks[h], y[h * BLK : (h + 1) * BLK], out)
    return out


def nt_dot(a, b):
    return lax.dot_general(a, b, (((1,), (1,)), ((), ())), preferred_element_type=jnp.float32)


def tn_dot(a, b):
    return lax.dot_general(a, b, (((0,), (0,)), ((), ())), preferred_element_type=jnp.float32)


def attn_fwd_kernel(cols_ref, counts_ref, q_ref, k_ref, v_ref, o_ref, lse_ref):
    width = q_ref.shape[1]
    nblk = q_ref.shape[0] // BLK
    masks = head_masks(width)
    rows = len(masks) * BLK

    def row_body(r, carry):
        row0 = pl.multiple_of(r * BLK, BLK)
        cnt = counts_ref[r]
        q2 = stack_heads(q_ref[pl.ds(row0, BLK), :], masks)

        def scores(s):
            col0 = pl.multiple_of(cols_ref[r * MAXB + s] * BLK, BLK)
            return nt_dot(q2, k_ref[pl.ds(col0, BLK), :]) * SCALE, col0

        def first(s, mc):
            m, l = mc
            sc, _ = scores(s)
            m_new = jnp.maximum(m, jnp.max(sc, axis=1, keepdims=True))
            l = l * jnp.exp(m - m_new) + jnp.sum(jnp.exp(sc - m_new), axis=1, keepdims=True)
            return m_new, l

        m, l = lax.fori_loop(
            0,
            cnt,
            first,
            (jnp.full((rows, 1), NEG, jnp.float32), jnp.zeros((rows, 1), jnp.float32)),
        )
        lse = m + jnp.log(l)

        def second(s, acc):
            sc, col0 = scores(s)
            p = jnp.exp(sc - lse).astype(jnp.bfloat16)
            return acc + jnp.dot(p, v_ref[pl.ds(col0, BLK), :], preferred_element_type=jnp.float32)

        acc = lax.fori_loop(0, cnt, second, jnp.zeros((rows, width), jnp.float32))
        o_ref[pl.ds(row0, BLK), :] = unstack_heads(acc, masks).astype(o_ref.dtype)
        lse_ref[pl.ds(pl.multiple_of(r * rows, rows), rows), :] = jnp.broadcast_to(
            lse, (rows, lse_ref.shape[1])
        )
        return carry

    lax.fori_loop(0, nblk, row_body, 0)


def attn_bwd_kernel(
    cols_ref, counts_ref, q_ref, k_ref, v_ref, o_ref, do_ref, lse_ref, dq_ref, dk_ref, dv_ref, dk_acc, dv_acc
):
    width = q_ref.shape[1]
    nblk = q_ref.shape[0] // BLK
    masks = head_masks(width)
    rows = len(masks) * BLK
    dk_acc[...] = jnp.zeros_like(dk_acc)
    dv_acc[...] = jnp.zeros_like(dv_acc)

    def row_body(r, carry):
        row0 = pl.multiple_of(r * BLK, BLK)
        cnt = counts_ref[r]
        q2 = stack_heads(q_ref[pl.ds(row0, BLK), :], masks)
        do_blk = do_ref[pl.ds(row0, BLK), :]
        do2 = stack_heads(do_blk, masks)
        prod = o_ref[pl.ds(row0, BLK), :].astype(jnp.float32) * do_blk.astype(jnp.float32)
        delta = jnp.concatenate(
            [jnp.sum(jnp.where(m, prod, 0.0), axis=1, keepdims=True) for m in masks], axis=0
        )
        lse = lse_ref[pl.ds(pl.multiple_of(r * rows, rows), rows), :]

        def step(s, dq):
            col0 = pl.multiple_of(cols_ref[r * MAXB + s] * BLK, BLK)
            kb = k_ref[pl.ds(col0, BLK), :]
            vb = v_ref[pl.ds(col0, BLK), :]
            sc = nt_dot(q2, kb) * SCALE
            p = jnp.exp(sc - lse).astype(jnp.bfloat16)
            dp = nt_dot(do2, vb)
            ds = (p.astype(jnp.float32) * (dp - delta) * SCALE).astype(jnp.bfloat16)
            dk_acc[pl.ds(col0, BLK), :] += tn_dot(ds, q2)
            dv_acc[pl.ds(col0, BLK), :] += tn_dot(p, do2)
            return dq + jnp.dot(ds, kb, preferred_element_type=jnp.float32)

        dq = lax.fori_loop(0, cnt, step, jnp.zeros((rows, width), jnp.float32))
        dq_ref[pl.ds(row0, BLK), :] = unstack_heads(dq, masks).astype(dq_ref.dtype)
        return carry

    lax.fori_loop(0, nblk, row_body, 0)
    dk_ref[...] = dk_acc[...].astype(dk_ref.dtype)
    dv_ref[...] = dv_acc[...].astype(dv_ref.dtype)


def smem_spec():
    return pl.BlockSpec(memory_space=pltpu.SMEM)


def vmem_spec():
    return pl.BlockSpec(memory_space=pltpu.VMEM)


VMEM_LIMIT = 48 * 1024 * 1024


def attention_forward(q, k, v, cols, counts):
    n, width = q.shape
    rows = (width // HD) * BLK
    return pl.pallas_call(
        attn_fwd_kernel,
        out_shape=(
            jax.ShapeDtypeStruct((n, width), jnp.bfloat16),
            jax.ShapeDtypeStruct(((n // BLK) * rows, 128), jnp.float32),
        ),
        in_specs=[smem_spec(), smem_spec(), vmem_spec(), vmem_spec(), vmem_spec()],
        out_specs=(vmem_spec(), vmem_spec()),
        compiler_params=pltpu.CompilerParams(vmem_limit_bytes=VMEM_LIMIT),
    )(cols, counts, q, k, v)


def attention_backward(q, k, v, o, do, lse, cols, counts):
    n, width = q.shape
    return pl.pallas_call(
        attn_bwd_kernel,
        out_shape=tuple(jax.ShapeDtypeStruct((n, width), jnp.bfloat16) for _ in range(3)),
        in_specs=[smem_spec(), smem_spec()] + [vmem_spec()] * 6,
        out_specs=(vmem_spec(), vmem_spec(), vmem_spec()),
        scratch_shapes=[pltpu.VMEM((n, width), jnp.float32), pltpu.VMEM((n, width), jnp.float32)],
        compiler_params=pltpu.CompilerParams(vmem_limit_bytes=VMEM_LIMIT),
    )(cols, counts, q, k, v, o, do, lse)


def body(feats, gain, w_qkv, w_out, block_cols, block_counts, cotan):
    model_width = feats.shape[1]
    qkv_width = 3 * model_width
    scaled, inverse, normed = layer_norm(feats, gain)
    mixed_proj = jnp.dot(normed, w_qkv, preferred_element_type=jnp.float32).astype(jnp.bfloat16)
    query_rows = mixed_proj[:, :model_width]
    key_rows = mixed_proj[:, model_width : 2 * model_width]
    value_rows = mixed_proj[:, 2 * model_width :]
    query_heads, key_heads, value_heads = (
        lax.all_to_all(query_rows, "seq", split_axis=1, concat_axis=0, tiled=True),
        lax.all_to_all(key_rows, "seq", split_axis=1, concat_axis=0, tiled=True),
        lax.all_to_all(value_rows, "seq", split_axis=1, concat_axis=0, tiled=True),
    )
    cols = block_cols[0].reshape(-1)
    counts = block_counts[0]
    attended_heads, lse = attention_forward(query_heads, key_heads, value_heads, cols, counts)
    attended = lax.all_to_all(attended_heads, "seq", split_axis=0, concat_axis=1, tiled=True)
    result = (
        feats.astype(jnp.float32) + jnp.dot(attended, w_out, preferred_element_type=jnp.float32)
    ).astype(jnp.bfloat16)
    grad_att = lax.dot_general(
        cotan, w_out, (((1,), (1,)), ((), ())), preferred_element_type=jnp.float32
    ).astype(jnp.bfloat16)
    grad_heads = lax.all_to_all(grad_att, "seq", split_axis=1, concat_axis=0, tiled=True)
    query_grad, key_grad, value_grad = attention_backward(
        query_heads, key_heads, value_heads, attended_heads, grad_heads, lse, cols, counts
    )
    query_back, key_back, value_back = (
        lax.all_to_all(query_grad, "seq", split_axis=0, concat_axis=1, tiled=True),
        lax.all_to_all(key_grad, "seq", split_axis=0, concat_axis=1, tiled=True),
        lax.all_to_all(value_grad, "seq", split_axis=0, concat_axis=1, tiled=True),
    )
    grad_mixed = jnp.concatenate([query_back, key_back, value_back], axis=1)
    grad_normed = lax.dot_general(
        grad_mixed, w_qkv, (((1,), (1,)), ((), ())), preferred_element_type=jnp.float32
    )
    gained = grad_normed * gain[None, :]
    mean_one = jnp.mean(gained, axis=1, keepdims=True)
    mean_two = jnp.mean(gained * scaled, axis=1, keepdims=True)
    grad_feats = (
        cotan.astype(jnp.float32) + inverse * (gained - mean_one - scaled * mean_two)
    ).astype(jnp.bfloat16)
    terms = jnp.concatenate(
        [contract_rows(normed, grad_mixed), contract_rows(attended, cotan)], axis=1
    )
    own_rows = lax.psum(lax.psum_scatter(terms, "seq", scatter_dimension=0, tiled=True), "dp")
    grad_qkv = own_rows[:, :qkv_width].astype(jnp.bfloat16)
    grad_out = own_rows[:, qkv_width:].astype(jnp.bfloat16)
    return (result, grad_feats, grad_qkv, grad_out)


def solution(mesh):
    in_specs = (
        P(("dp", "seq"), None),
        P(),
        P(),
        P(),
        P("dp", None, None),
        P("dp", None),
        P(("dp", "seq"), None),
    )
    out_specs = (P(("dp", "seq"), None), P(("dp", "seq"), None), P("seq", None), P("seq", None))
    return jax.shard_map(body, mesh=mesh, in_specs=in_specs, out_specs=out_specs, check_vma=False)
```

time: 637 us -> 524 us (0.82); the launches traced: 628 us -> 523 us
  matrix products: 231 us -> 30.8 us
  Pallas kernels: 0 us -> 159 us
  local copies, waits for them, and re-layouts: 138 us -> 22.1 us
  waiting for transfers between devices: 59.9 us -> 157 us
  blocking collectives: 130 us -> 92.4 us
  other arithmetic: 28.9 us -> 11.1 us
  between operations: 1.36 us -> 14.3 us
    dot_general x88 -> x0, matrix products: 198 us -> none  [the longest x8 48.1 us: backward_block_step(): jnp.einsum('gsc,gskhd->ckhd', selector, key_pairs, precision=lax.Precisio...]
    pallas_call x0 -> x2, Pallas kernels: none -> 159 us  [the longest x1 92.3 us: attention_forward(): pl.pallas_call(attn_fwd_kernel, out_shape=(jax.ShapeDtypeStruct((n, width...]
    reduce_scatter x0 -> x1, waiting for transfers between devices: none -> 78.8 us  [body(): lax.psum_scatter(terms, 'seq', scatter_dimension=0, tiled=True)]
    while x120 -> x0, local copies, waits for them, and re-layouts: 42.8 us -> none
    psum x1, blocking collectives: 130 us -> 92.4 us  [body(): lax.psum(lax.psum_scatter(terms, 'seq', scatter_dimension=0, tiled=True),...]
    slice x17 -> x0, local copies, waits for them, and re-layouts: 33.1 us -> none  [the longest x16 31.4 us: select_blocks(): return (picked[..., :HD], picked[..., HD:])]
    all_to_all x1, waiting for transfers between devices: 0.01 us -> 12.2 us  [body(): lax.all_to_all(query_rows, 'seq', split_axis=1, concat_axis=0, tiled=True)]
    reshape x5 -> x0, local copies, waits for them, and re-layouts: 11.9 us -> none  [the longest x1 4.5 us: stacked_table(): jnp.concatenate([key_b, value_b], axis=3)]
  transfers between devices with their start and end apart: 8 -> 9, of which waited for: 5 -> 7; matrix products, arithmetic and copies ran while one was open for 54% -> 7% of each run, Pallas kernels for 0% -> 30%
where the time goes in v1:
time: 524 us; the launch traced here: 523 us
  Pallas kernels  159 us (30%)
  waiting for transfers between devices  157 us (30%)
  blocking collectives  92.4 us (18%)
  starting transfers between devices  36.4 us (7%)
  matrix products  30.8 us (6%)
  local copies, waits for them, and re-layouts  22.1 us (4%)
  between operations  14.3 us (3%)
  other arithmetic  11.1 us (2%)
    psum x1, blocking collectives, body(): lax.psum(lax.psum_scatter(terms, 'seq', scatter_dimension=0, tiled=True),...  92.4 us
    pallas_call x1, Pallas kernels, attention_forward(): pl.pallas_call(attn_fwd_kernel, out_shape=(jax.ShapeDtypeStruct((n, width...  92.3 us
    reduce_scatter x1, waiting for transfers between devices, body(): lax.psum_scatter(terms, 'seq', scatter_dimension=0, tiled=True)  78.8 us
    pallas_call x1, Pallas kernels, attention_backward(): pl.pallas_call(attn_bwd_kernel, out_shape=tuple((jax.ShapeDtypeStruct((n,...  66.2 us
    all_to_all x1, waiting for transfers between devices, body(): lax.all_to_all(query_grad, 'seq', split_axis=0, concat_axis=1, tiled=True)  14.6 us
    all_to_all x1, waiting for transfers between devices, body(): lax.all_to_all(key_grad, 'seq', split_axis=0, concat_axis=1, tiled=True)  13.8 us
    all_to_all x1, waiting for transfers between devices, body(): lax.all_to_all(key_rows, 'seq', split_axis=1, concat_axis=0, tiled=True)  13.6 us
    all_to_all x1, waiting for transfers between devices, body(): lax.all_to_all(value_rows, 'seq', split_axis=1, concat_axis=0, tiled=True)  13.6 us
  transfers between devices with their start and end apart: 9, of which 7 were waited for; matrix products, arithmetic and copies ran while one was open for 7% of the time, Pallas kernels for 30%

profile of v1, /device:TPU:0, one launch (start us, length us, event | category | flops | bytes accessed | tf_op | source)
XLA Modules:
  0.0 523.1 jit_solution(13356928197715794049)
XLA Ops:
  10.5 6.7 %convolution_convert_fusion = bf16[512,3072]{1,0:T(8,128)(2,1)S(1)} fusion(bf16[1024,3072]{1,0:T(8,128)(2,1)} %param.9, bf16[512,1024]{1,0:T(8,128)(2,1)S(1)} %copy-done.6, f32[1024]{0:T(1024)S(1)} %copy-done.11, f32[512]{0:T(512)S(1)} %add_rsqrt_fusion, f32[512]{0:T(512)S(1)} %broadcast_multiply_fusion.2), kind=kOutput, calls=%fused_computation.1 | convolution fusion | flops 3225419776 | bytes 10493952 | tf_op jit(solution)/shard_map/dot_general | solution.py:187
  17.1 2.0 slice_bitcast_fusion
  20.3 5.4 %all-to-all-start.2 = ((bf16[512,8,128]{2,0,1:T(8,128)(2,1)}), bf16[512,8,128]{2,0,1:T(8,128)(2,1)S(1)}, u32[]{:S(2)}, u32[]{:S(2)}) async-start(bf16[512,8,128]{2,0,1:T(8,128)(2,1)} %bitcast.68), calls=%async_computation.2 | async-start | bytes 2097152 | tf_op jit(solution)/shard_map/all_to_all | solution.py:194
  25.7 2.4 copy.37
  28.1 13.6 %all-to-all-done.2 = bf16[512,8,128]{2,0,1:T(8,128)(2,1)S(1)} async-done(((bf16[512,8,128]{2,0,1:T(8,128)(2,1)}), bf16[512,8,128]{2,0,1:T(8,128)(2,1)S(1)}, u32[]{:S(2)}, u32[]{:S(2)}) %all-to-all-start.2) | async-done | bytes 1048608 | tf_op jit(solution)/shard_map/all_to_all | solution.py:194
  41.7 4.3 all-to-all-start.1
  46.0 2.4 copy.38
  48.4 13.6 %all-to-all-done.1 = bf16[512,8,128]{2,0,1:T(8,128)(2,1)} async-done(((bf16[512,8,128]{2,0,1:T(8,128)(2,1)}), bf16[512,8,128]{2,0,1:T(8,128)(2,1)}, u32[]{:S(2)}, u32[]{:S(2)}) %all-to-all-start.1) | async-done | bytes 1048608 | tf_op jit(solution)/shard_map/all_to_all | solution.py:193
  61.9 4.2 all-to-all-start
  66.2 2.5 fusion.13
  70.0 12.2 %all-to-all-done = bf16[512,8,128]{2,0,1:T(8,128)(2,1)} async-done(((bf16[512,8,128]{2,0,1:T(8,128)(2,1)}), bf16[512,8,128]{2,0,1:T(8,128)(2,1)}, u32[]{:S(2)}, u32[]{:S(2)}) %all-to-all-start) | async-done | bytes 1048608 | tf_op jit(solution)/shard_map/all_to_all | solution.py:192
  82.2 4.2 all-to-all-start.4
  86.6 92.3 %shard_map.102 = (bf16[4096,128]{1,0:T(8,128)(2,1)S(1)}, f32[8192,128]{1,0:T(8,128)}) custom-call(s32[256]{0:T(256)S(1)} %reshape_squeeze.3.cols_ref, s32[32]{0:T(128)S(1)} %bitcast.63, bf16[4096,128]{1,0:T(8,128)(2,1)} %bitcast.2.q_ref, bf16[4096,128]{1,0:T(8,128)(2,1)} %bitcast.4.k_ref, bf16[4096,128]{1,0:T(8,128)(2,1)S(1)} %bitcast.57), custom_call_target="tpu_custom_call" | custom-call | tf_op jit(solution)/shard_map/pallas_call | solution.py:159
  179.9 2.3 copy.20
  182.2 4.7 all-to-all-start.3
  186.9 66.2 %shard_map.103 = (bf16[4096,128]{1,0:T(8,128)(2,1)S(1)}, bf16[4096,128]{1,0:T(8,128)(2,1)S(1)}, bf16[4096,128]{1,0:T(8,128)(2,1)S(1)}) custom-call(s32[256]{0:T(256)S(1)} %reshape_squeeze.3.cols_ref, s32[32]{0:T(128)S(1)} %bitcast.64, bf16[4096,128]{1,0:T(8,128)(2,1)} %bitcast.2.q_ref, bf16[4096,128]{1,0:T(8,128)(2,1)} %bitcast.4.k_ref, ...), custom_call_target="tpu_custom_call" | custom-call | tf_op jit(solution)/shard_map/pallas_call | solution.py:173
  255.0 2.3 copy.23
  257.3 4.8 all-to-all-start.6
  262.1 2.3 copy.22
  264.4 13.8 %all-to-all-done.6 = bf16[8,512,128]{1,2,0:T(8,128)(2,1)} async-done(((bf16[8,512,128]{1,2,0:T(8,128)(2,1)}), bf16[8,512,128]{1,2,0:T(8,128)(2,1)}, u32[]{:S(2)}, u32[]{:S(2)}) %all-to-all-start.6) | async-done | bytes 1048608 | tf_op jit(solution)/shard_map/all_to_all | solution.py:212
  278.2 4.3 all-to-all-start.5
  283.8 14.6 %all-to-all-done.5 = bf16[8,512,128]{1,2,0:T(8,128)(2,1)} async-done(((bf16[8,512,128]{1,2,0:T(8,128)(2,1)}), bf16[8,512,128]{1,2,0:T(8,128)(2,1)}, u32[]{:S(2)}, u32[]{:S(2)}) %all-to-all-start.5) | async-done | bytes 1048608 | tf_op jit(solution)/shard_map/all_to_all | solution.py:211
  298.4 4.3 all-to-all-start.7
  302.9 4.8 fusion.20
  307.8 10.9 %all-to-all-done.7 = bf16[8,512,128]{1,2,0:T(8,128)(2,1)} async-done(((bf16[8,512,128]{1,2,0:T(8,128)(2,1)}), bf16[8,512,128]{1,2,0:T(8,128)(2,1)}, u32[]{:S(2)}, u32[]{:S(2)}) %all-to-all-start.7) | async-done | bytes 1048608 | tf_op jit(solution)/shard_map/all_to_all | solution.py:213
  318.7 5.8 %fusion.14 = f32[1024,3072]{1,0:T(8,128)S(1)} fusion(bf16[512,1024]{0,1:T(8,128)(2,1)} %bitcast.23, bf16[512,1024]{0,1:T(8,128)(2,1)} %bitcast.20, bf16[512,1024]{0,1:T(8,128)(2,1)} %bitcast.17, bf16[512,1024]{1,0:T(8,128)(2,1)S(1)} %copy-done.7, f32[1024]{0:T(1024)S(1)} %copy-done.11, f32[512]{0:T(512)S(1)} %add_rsqrt_fusion, ...), kind=kOutput, calls=%fused_computation.22 | convolution fusion | flops 3233284096 | bytes 16785408 | tf_op jit(solution)/shard_map/dot_general | solution.py:28
  324.4 6.1 %pad_maximum_fusion = f32[1024,4096]{1,0:T(8,128)} fusion(f32[1024,1024]{1,0:T(8,128)S(1)} %copy-done.8, f32[1024,3072]{1,0:T(8,128)S(1)} %fusion.14), kind=kLoop, calls=%fused_computation | loop fusion | flops 4194304 | bytes 33554432 | tf_op jit(solution)/shard_map/concatenate | solution.py:225
  330.5 7.5 %multiply_reduce_fusion = (f32[512]{0:T(512)S(1)}, f32[512]{0:T(512)S(1)}, f32[512,1024]{1,0:T(8,128)S(1)}) fusion(f32[1024]{0:T(1024)S(1)} %copy-done.11, f32[512]{0:T(512)S(1)} %add_rsqrt_fusion, f32[512]{0:T(512)S(1)} %broadcast_multiply_fusion.2, bf16[512,1024]{1,0:T(8,128)(2,1)S(1)} %copy-done.7, bf16[1024,3072]{1,0:T(8,128)(2,1)} %param.9, ...), kind=kOutput, calls=%fused_computation.19 | convolution fusion | flops 3234331648 | bytes 12595200 | tf_op jit(solution)/shard_map/dot_general | solution.py:216
  338.1 1.8 fusion.10
  339.9 3.5 fusion.12
  343.4 78.8 %reduce-scatter.2.cloned.1.call-done = f32[128,4096]{1,0:T(8,128)} async-done(((f32[1024,4096]{1,0:T(8,128)}), f32[128,4096]{1,0:T(8,128)}) %reduce-scatter.2.cloned.1.call-update) | async-done | bytes 2097168 | tf_op jit(solution)/shard_map/reduce_scatter | solution.py:228
  422.1 92.4 %all-reduce.1 = bf16[128,4096]{1,0:T(8,128)(2,1)S(1)} all-reduce(f32[128,4096]{1,0:T(8,128)} %reduce-scatter.2.cloned.1.call-done), channel_id=1, replica_groups=mesh['dp'=16,'seq'=8] {'dp'}, use_global_device_ids=true, to_apply=%region_5.0 | all-reduce | flops 524288 | bytes 3145728 | tf_op jit(solution)/shard_map/psum | solution.py:228
  (40 shorter events, 12.0 us)
Async XLA Ops:
  7.2 59.0 %copy-start = (bf16[1024,1024]{1,0:T(8,128)(2,1)S(1)}, bf16[1024,1024]{1,0:T(8,128)(2,1)}, u32[]{:S(2)}) copy-start(bf16[1024,1024]{1,0:T(8,128)(2,1)} %param.10) | copy-start | bytes 6291460
  7.2 3.3 copy-start.6
  7.2 3.3 copy-start.11
  20.3 21.4 %all-to-all-start.2 = ((bf16[512,8,128]{2,0,1:T(8,128)(2,1)}), bf16[512,8,128]{2,0,1:T(8,128)(2,1)S(1)}, u32[]{:S(2)}, u32[]{:S(2)}) async-start(bf16[512,8,128]{2,0,1:T(8,128)(2,1)} %bitcast.68), calls=%async_computation.2 | async-start | bytes 2097152 | tf_op jit(solution)/shard_map/all_to_all | solution.py:194
  41.7 44.9 %copy-start.1 = (bf16[512,8,128]{2,0,1:T(8,128)(2,1)}, bf16[512,8,128]{2,0,1:T(8,128)(2,1)S(1)}, u32[]{:S(2)}) copy-start(bf16[512,8,128]{2,0,1:T(8,128)(2,1)S(1)} %all-to-all-done.2) | copy-start | bytes 3145732
  41.7 20.2 %all-to-all-start.1 = ((bf16[512,8,128]{2,0,1:T(8,128)(2,1)}), bf16[512,8,128]{2,0,1:T(8,128)(2,1)}, u32[]{:S(2)}, u32[]{:S(2)}) async-start(bf16[512,8,128]{2,0,1:T(8,128)(2,1)} %bitcast.66), calls=%async_computation.1 | async-start | bytes 2097152 | tf_op jit(solution)/shard_map/all_to_all | solution.py:193
  61.9 20.2 %all-to-all-start = ((bf16[512,8,128]{2,0,1:T(8,128)(2,1)}), bf16[512,8,128]{2,0,1:T(8,128)(2,1)}, u32[]{:S(2)}, u32[]{:S(2)}) async-start(bf16[512,8,128]{2,0,1:T(8,128)(2,1)} %bitcast.67), calls=%async_computation | async-start | bytes 2097152 | tf_op jit(solution)/shard_map/all_to_all | solution.py:192
  68.7 17.7 %copy-start.10 = (s32[1,32,8]{1,2,0:T(8,128)S(1)}, s32[1,32,8]{1,2,0:T(8,128)}, u32[]{:S(2)}) copy-start(s32[1,32,8]{1,2,0:T(8,128)} %param.11) | copy-start | bytes 3076
  68.7 17.9 %copy-start.5 = (s32[1,32]{1,0:T(1,128)S(1)}, s32[1,32]{1,0:T(1,128)}, u32[]{:S(2)}) copy-start(s32[1,32]{1,0:T(1,128)} %param.12) | copy-start | bytes 388
  82.2 100.0 %all-to-all-start.4 = ((bf16[512,8,128]{2,0,1:T(8,128)(2,1)}), bf16[512,8,128]{2,0,1:T(8,128)(2,1)}, u32[]{:S(2)}, u32[]{:S(2)}) async-start(bf16[512,8,128]{2,0,1:T(8,128)(2,1)} %bitcast.65), calls=%async_computation.4 | async-start | bytes 2097152 | tf_op jit(solution)/shard_map/all_to_all | solution.py:206
  178.9 1.0 copy-start.2
  182.2 75.1 %all-to-all-start.3 = ((bf16[8,512,128]{1,2,0:T(8,128)(2,1)}), bf16[8,512,128]{1,2,0:T(8,128)(2,1)}, u32[]{:S(2)}, u32[]{:S(2)}) async-start(bf16[8,512,128]{1,2,0:T(8,128)(2,1)} %copy.20), calls=%async_computation.3 | async-start | bytes 2097152 | tf_op jit(solution)/shard_map/all_to_all | solution.py:199
  253.1 1.0 copy-start.3
  254.1 1.0 copy-start.4
  257.3 20.9 %all-to-all-start.6 = ((bf16[8,512,128]{1,2,0:T(8,128)(2,1)}), bf16[8,512,128]{1,2,0:T(8,128)(2,1)}, u32[]{:S(2)}, u32[]{:S(2)}) async-start(bf16[8,512,128]{1,2,0:T(8,128)(2,1)} %copy.23), calls=%async_computation.6 | async-start | bytes 2097152 | tf_op jit(solution)/shard_map/all_to_all | solution.py:212
  278.2 20.2 %all-to-all-start.5 = ((bf16[8,512,128]{1,2,0:T(8,128)(2,1)}), bf16[8,512,128]{1,2,0:T(8,128)(2,1)}, u32[]{:S(2)}, u32[]{:S(2)}) async-start(bf16[8,512,128]{1,2,0:T(8,128)(2,1)} %copy.22), calls=%async_computation.5 | async-start | bytes 2097152 | tf_op jit(solution)/shard_map/all_to_all | solution.py:211
  298.4 20.2 %all-to-all-start.7 = ((bf16[8,512,128]{1,2,0:T(8,128)(2,1)}), bf16[8,512,128]{1,2,0:T(8,128)(2,1)}, u32[]{:S(2)}, u32[]{:S(2)}) async-start(bf16[8,512,128]{1,2,0:T(8,128)(2,1)} %copy.24), calls=%async_computation.7 | async-start | bytes 2097152 | tf_op jit(solution)/shard_map/all_to_all | solution.py:213
  302.7 119.4 %reduce-scatter.2.cloned.1.call-start = ((), (), s32[]{:S(2)}) async-start(), calls=%async_computation.9 | async-start | bytes 18874368 | tf_op jit(solution)/shard_map/reduce_scatter | solution.py:228
  302.9 15.7 %copy-start.7 = (bf16[512,1024]{1,0:T(8,128)(2,1)S(1)}, bf16[512,1024]{1,0:T(8,128)(2,1)}, u32[]{:S(2)}) copy-start(bf16[512,1024]{1,0:T(8,128)(2,1)} %param.7) | copy-start | bytes 3145732
  318.7 5.8 %copy-start.8 = (f32[1024,1024]{1,0:T(8,128)S(1)}, f32[1024,1024]{1,0:T(8,128)}, u32[]{:S(2)}) copy-start(f32[1024,1024]{1,0:T(8,128)} %fusion.20) | copy-start | bytes 12582916
  330.5 7.6 %copy-start.9 = (bf16[512,1024]{1,0:T(8,128)(2,1)S(1)}, bf16[512,1024]{1,0:T(8,128)(2,1)}, u32[]{:S(2)}) copy-start(bf16[512,1024]{1,0:T(8,128)(2,1)} %param.13) | copy-start | bytes 3145732
Sparse Core Ops, SparseCore 0:
  330.6 91.4 reduce-scatter.1

commit v2 on v1

--- a/solution.py
+++ b/solution.py
@@ -54,6 +54,20 @@
     return lax.dot_general(a, b, (((0,), (0,)), ((), ())), preferred_element_type=jnp.float32)
 
 
+def gather_blocks(ref, cols_ref, r):
+    return jnp.concatenate(
+        [
+            ref[pl.ds(pl.multiple_of(cols_ref[r * MAXB + s] * BLK, BLK), BLK), :]
+            for s in range(MAXB)
+        ],
+        axis=0,
+    )
+
+
+def live_lanes(cnt):
+    return lax.broadcasted_iota(jnp.int32, (1, MAXB * BLK), 1) < cnt * BLK
+
+
 def attn_fwd_kernel(cols_ref, counts_ref, q_ref, k_ref, v_ref, o_ref, lse_ref):
     width = q_ref.shape[1]
     nblk = q_ref.shape[0] // BLK
@@ -62,37 +76,17 @@
 
     def row_body(r, carry):
         row0 = pl.multiple_of(r * BLK, BLK)
-        cnt = counts_ref[r]
+        live = live_lanes(counts_ref[r])
         q2 = stack_heads(q_ref[pl.ds(row0, BLK), :], masks)
-
-        def scores(s):
-            col0 = pl.multiple_of(cols_ref[r * MAXB + s] * BLK, BLK)
-            return nt_dot(q2, k_ref[pl.ds(col0, BLK), :]) * SCALE, col0
-
-        def first(s, mc):
-            m, l = mc
-            sc, _ = scores(s)
-            m_new = jnp.maximum(m, jnp.max(sc, axis=1, keepdims=True))
-            l = l * jnp.exp(m - m_new) + jnp.sum(jnp.exp(sc - m_new), axis=1, keepdims=True)
-            return m_new, l
-
-        m, l = lax.fori_loop(
-            0,
-            cnt,
-            first,
-            (jnp.full((rows, 1), NEG, jnp.float32), jnp.zeros((rows, 1), jnp.float32)),
-        )
-        lse = m + jnp.log(l)
-
-        def second(s, acc):
-            sc, col0 = scores(s)
-            p = jnp.exp(sc - lse).astype(jnp.bfloat16)
-            return acc + jnp.dot(p, v_ref[pl.ds(col0, BLK), :], preferred_element_type=jnp.float32)
-
-        acc = lax.fori_loop(0, cnt, second, jnp.zeros((rows, width), jnp.float32))
+        sc = jnp.where(live, nt_dot(q2, gather_blocks(k_ref, cols_ref, r)) * SCALE, NEG)
+        m = jnp.max(sc, axis=1, keepdims=True)
+        e = jnp.where(live, jnp.exp(sc - m), 0.0)
+        l = jnp.sum(e, axis=1, keepdims=True)
+        p = (e * (1.0 / l)).astype(jnp.bfloat16)
+        acc = jnp.dot(p, gather_blocks(v_ref, cols_ref, r), preferred_element_type=jnp.float32)
         o_ref[pl.ds(row0, BLK), :] = unstack_heads(acc, masks).astype(o_ref.dtype)
         lse_ref[pl.ds(pl.multiple_of(r * rows, rows), rows), :] = jnp.broadcast_to(
-            lse, (rows, lse_ref.shape[1])
+            m + jnp.log(l), (rows, lse_ref.shape[1])
         )
         return carry
 
@@ -112,6 +106,7 @@
     def row_body(r, carry):
         row0 = pl.multiple_of(r * BLK, BLK)
         cnt = counts_ref[r]
+        live = live_lanes(cnt)
         q2 = stack_heads(q_ref[pl.ds(row0, BLK), :], masks)
         do_blk = do_ref[pl.ds(row0, BLK), :]
         do2 = stack_heads(do_blk, masks)
@@ -119,22 +114,25 @@
         delta = jnp.concatenate(
             [jnp.sum(jnp.where(m, prod, 0.0), axis=1, keepdims=True) for m in masks], axis=0
         )
-        lse = lse_ref[pl.ds(pl.multiple_of(r * rows, rows), rows), :]
-
-        def step(s, dq):
-            col0 = pl.multiple_of(cols_ref[r * MAXB + s] * BLK, BLK)
-            kb = k_ref[pl.ds(col0, BLK), :]
-            vb = v_ref[pl.ds(col0, BLK), :]
-            sc = nt_dot(q2, kb) * SCALE
-            p = jnp.exp(sc - lse).astype(jnp.bfloat16)
-            dp = nt_dot(do2, vb)
-            ds = (p.astype(jnp.float32) * (dp - delta) * SCALE).astype(jnp.bfloat16)
-            dk_acc[pl.ds(col0, BLK), :] += tn_dot(ds, q2)
-            dv_acc[pl.ds(col0, BLK), :] += tn_dot(p, do2)
-            return dq + jnp.dot(ds, kb, preferred_element_type=jnp.float32)
-
-        dq = lax.fori_loop(0, cnt, step, jnp.zeros((rows, width), jnp.float32))
+        lse = lse_ref[pl.ds(pl.multiple_of(r * rows, rows), rows), :][:, 0:1]
+        kc = gather_blocks(k_ref, cols_ref, r)
+        vc = gather_blocks(v_ref, cols_ref, r)
+        sc = nt_dot(q2, kc) * SCALE
+        p = jnp.where(live, jnp.exp(sc - lse), 0.0).astype(jnp.bfloat16)
+        dp = nt_dot(do2, vc)
+        ds = (p.astype(jnp.float32) * (dp - delta) * SCALE).astype(jnp.bfloat16)
+        dq = jnp.dot(ds, kc, preferred_element_type=jnp.float32)
         dq_ref[pl.ds(row0, BLK), :] = unstack_heads(dq, masks).astype(dq_ref.dtype)
+        dkc = tn_dot(ds, q2)
+        dvc = tn_dot(p, do2)
+        for s in range(MAXB):
+
+            @pl.when(s < cnt)
+            def _():
+                col0 = pl.multiple_of(cols_ref[r * MAXB + s] * BLK, BLK)
+                dk_acc[pl.ds(col0, BLK), :] += dkc[s * BLK : (s + 1) * BLK]
+                dv_acc[pl.ds(col0, BLK), :] += dvc[s * BLK : (s + 1) * BLK]
+
         return carry
 
     lax.fori_loop(0, nblk, row_body, 0)
@@ -225,9 +223,10 @@
     terms = jnp.concatenate(
         [contract_rows(normed, grad_mixed), contract_rows(attended, cotan)], axis=1
     )
-    own_rows = lax.psum(lax.psum_scatter(terms, "seq", scatter_dimension=0, tiled=True), "dp")
-    grad_qkv = own_rows[:, :qkv_width].astype(jnp.bfloat16)
-    grad_out = own_rows[:, qkv_width:].astype(jnp.bfloat16)
+    piece = lax.psum_scatter(terms, ("seq", "dp"), scatter_dimension=0, tiled=True)
+    own_rows = lax.all_gather(piece.astype(jnp.bfloat16), "dp", axis=0, tiled=True)
+    grad_qkv = own_rows[:, :qkv_width]
+    grad_out = own_rows[:, qkv_width:]
     return (result, grad_feats, grad_qkv, grad_out)
 
 

time: 524 us -> 966 us (1.84)
  waiting for transfers between devices: 157 us -> 778 us
  blocking collectives: 92.4 us -> 0 us
  Pallas kernels: 159 us -> 68.4 us
    reduce_scatter x1, waiting for transfers between devices: 78.8 us -> 674 us  [body(): lax.psum_scatter(terms, ('seq', 'dp'), scatter_dimension=0, tiled=True)]
    psum x1 -> x0, blocking collectives: 92.4 us -> none  [body(): lax.psum(lax.psum_scatter(terms, 'seq', scatter_dimension=0, tiled=True),...]
    pallas_call x1, Pallas kernels: 92.3 us -> 29.7 us  [attention_forward(): pl.pallas_call(attn_fwd_kernel, out_shape=(jax.ShapeDtypeStruct((n, width...]
    pallas_call x1, Pallas kernels: 66.2 us -> 38.7 us  [attention_backward(): pl.pallas_call(attn_bwd_kernel, out_shape=tuple((jax.ShapeDtypeStruct((n,...]
    all_gather x0 -> x1, waiting for transfers between devices: none -> 25.1 us  [body(): lax.all_gather(piece.astype(jnp.bfloat16), 'dp', axis=0, tiled=True)]
  transfers between devices with their start and end apart: 9 -> 10, of which waited for: 7 -> 8; matrix products, arithmetic and copies ran while one was open for 7% -> 4% of each run, Pallas kernels for 30% -> 7%
where the time goes in v2:
time: 966 us; the launch traced here: 965 us
  waiting for transfers between devices  778 us (81%)
  Pallas kernels  68.4 us (7%)
  starting transfers between devices  36.4 us (4%)
  matrix products  30.8 us (3%)
  local copies, waits for them, and re-layouts  24.2 us (3%)
  between operations  14.3 us (1%)
  other arithmetic  12.6 us (1%)
    reduce_scatter x1, waiting for transfers between devices, body(): lax.psum_scatter(terms, ('seq', 'dp'), scatter_dimension=0, tiled=True)  674 us
    pallas_call x1, Pallas kernels, attention_backward(): pl.pallas_call(attn_bwd_kernel, out_shape=tuple((jax.ShapeDtypeStruct((n,...  38.7 us
    pallas_call x1, Pallas kernels, attention_forward(): pl.pallas_call(attn_fwd_kernel, out_shape=(jax.ShapeDtypeStruct((n, width...  29.7 us
    all_gather x1, waiting for transfers between devices, body(): lax.all_gather(piece.astype(jnp.bfloat16), 'dp', axis=0, tiled=True)  25.1 us
  transfers between devices with their start and end apart: 10, of which 8 were waited for; matrix products, arithmetic and copies ran while one was open for 4% of the time, Pallas kernels for 7%

profile of v2, /device:TPU:0, one launch (start us, length us, event | category | flops | bytes accessed | tf_op | source)
XLA Modules:
  0.0 964.8 jit_solution(9205849259055860648)
XLA Ops:
  10.5 6.7 convolution_convert_fusion
  17.1 2.0 slice_bitcast_fusion
  20.3 5.4 all-to-all-start.2
  25.7 2.4 copy.37
  28.1 13.6 %all-to-all-done.2 = bf16[512,8,128]{2,0,1:T(8,128)(2,1)S(1)} async-done(((bf16[512,8,128]{2,0,1:T(8,128)(2,1)}), bf16[512,8,128]{2,0,1:T(8,128)(2,1)S(1)}, u32[]{:S(2)}, u32[]{:S(2)}) %all-to-all-start.2) | async-done | bytes 1048608 | tf_op jit(solution)/shard_map/all_to_all | solution.py:192
  41.7 4.2 all-to-all-start.1
  45.9 2.4 copy.38
  48.3 13.6 %all-to-all-done.1 = bf16[512,8,128]{2,0,1:T(8,128)(2,1)} async-done(((bf16[512,8,128]{2,0,1:T(8,128)(2,1)}), bf16[512,8,128]{2,0,1:T(8,128)(2,1)}, u32[]{:S(2)}, u32[]{:S(2)}) %all-to-all-start.1) | async-done | bytes 1048608 | tf_op jit(solution)/shard_map/all_to_all | solution.py:191
  61.9 4.3 all-to-all-start
  66.2 2.5 fusion.13
  70.0 12.2 %all-to-all-done = bf16[512,8,128]{2,0,1:T(8,128)(2,1)} async-done(((bf16[512,8,128]{2,0,1:T(8,128)(2,1)}), bf16[512,8,128]{2,0,1:T(8,128)(2,1)}, u32[]{:S(2)}, u32[]{:S(2)}) %all-to-all-start) | async-done | bytes 1048608 | tf_op jit(solution)/shard_map/all_to_all | solution.py:190
  82.1 4.2 all-to-all-start.4
  86.6 29.7 %shard_map.102 = (bf16[4096,128]{1,0:T(8,128)(2,1)S(1)}, f32[8192,128]{1,0:T(8,128)}) custom-call(s32[256]{0:T(256)S(1)} %reshape_squeeze.3.cols_ref, s32[32]{0:T(128)S(1)} %bitcast.63, bf16[4096,128]{1,0:T(8,128)(2,1)} %bitcast.2.q_ref, bf16[4096,128]{1,0:T(8,128)(2,1)} %bitcast.4.k_ref, bf16[4096,128]{1,0:T(8,128)(2,1)S(1)} %bitcast.57), custom_call_target="tpu_custom_call" | custom-call | tf_op jit(solution)/shard_map/pallas_call | solution.py:157
  117.3 2.3 copy.20
  119.5 4.7 all-to-all-start.3
  124.2 38.7 %shard_map.103 = (bf16[4096,128]{1,0:T(8,128)(2,1)S(1)}, bf16[4096,128]{1,0:T(8,128)(2,1)S(1)}, bf16[4096,128]{1,0:T(8,128)(2,1)S(1)}) custom-call(s32[256]{0:T(256)S(1)} %reshape_squeeze.3.cols_ref, s32[32]{0:T(128)S(1)} %bitcast.64, bf16[4096,128]{1,0:T(8,128)(2,1)} %bitcast.2.q_ref, bf16[4096,128]{1,0:T(8,128)(2,1)} %bitcast.4.k_ref, ...), custom_call_target="tpu_custom_call" | custom-call | tf_op jit(solution)/shard_map/pallas_call | solution.py:171
  164.8 2.3 copy.23
  167.1 4.8 all-to-all-start.6
  171.9 2.3 copy.22
  174.2 13.8 %all-to-all-done.6 = bf16[8,512,128]{1,2,0:T(8,128)(2,1)} async-done(((bf16[8,512,128]{1,2,0:T(8,128)(2,1)}), bf16[8,512,128]{1,2,0:T(8,128)(2,1)}, u32[]{:S(2)}, u32[]{:S(2)}) %all-to-all-start.6) | async-done | bytes 1048608 | tf_op jit(solution)/shard_map/all_to_all | solution.py:210
  188.0 4.3 all-to-all-start.5
  193.6 14.6 %all-to-all-done.5 = bf16[8,512,128]{1,2,0:T(8,128)(2,1)} async-done(((bf16[8,512,128]{1,2,0:T(8,128)(2,1)}), bf16[8,512,128]{1,2,0:T(8,128)(2,1)}, u32[]{:S(2)}, u32[]{:S(2)}) %all-to-all-start.5) | async-done | bytes 1048608 | tf_op jit(solution)/shard_map/all_to_all | solution.py:209
  208.2 4.2 all-to-all-start.7
  212.7 4.8 fusion.20
  217.6 10.9 %all-to-all-done.7 = bf16[8,512,128]{1,2,0:T(8,128)(2,1)} async-done(((bf16[8,512,128]{1,2,0:T(8,128)(2,1)}), bf16[8,512,128]{1,2,0:T(8,128)(2,1)}, u32[]{:S(2)}, u32[]{:S(2)}) %all-to-all-start.7) | async-done | bytes 1048608 | tf_op jit(solution)/shard_map/all_to_all | solution.py:211
  228.5 5.8 fusion.14
  234.2 6.0 pad_maximum_fusion
  240.3 674.4 %reduce-scatter.2.cloned.1.call-done = f32[8,4096]{1,0:T(8,128)} async-done(((f32[1024,4096]{1,0:T(8,128)}), f32[8,4096]{1,0:T(8,128)}) %reduce-scatter.2.cloned.1.call-update) | async-done | bytes 131088 | tf_op jit(solution)/shard_map/reduce_scatter | solution.py:226
  916.3 7.5 multiply_reduce_fusion
  925.7 3.5 fusion.12
  929.1 25.1 %all-gather.2.cloned.1.call-done = bf16[128,4096]{1,0:T(8,128)(2,1)} async-done(((bf16[8,4096]{1,0:T(8,128)(2,1)}), bf16[128,4096]{1,0:T(8,128)(2,1)}) %all-gather.2.cloned.1.call-update) | async-done | bytes 1048592 | tf_op jit(solution)/shard_map/all_gather | solution.py:227
  955.9 2.1 slice.23
  (43 shorter events, 15.4 us)
Async XLA Ops:
  7.2 59.0 %copy-start = (bf16[1024,1024]{1,0:T(8,128)(2,1)S(1)}, bf16[1024,1024]{1,0:T(8,128)(2,1)}, u32[]{:S(2)}) copy-start(bf16[1024,1024]{1,0:T(8,128)(2,1)} %param.10) | copy-start | bytes 6291460
  7.2 3.3 copy-start.6
  7.2 3.3 copy-start.11
  20.3 21.4 %all-to-all-start.2 = ((bf16[512,8,128]{2,0,1:T(8,128)(2,1)}), bf16[512,8,128]{2,0,1:T(8,128)(2,1)S(1)}, u32[]{:S(2)}, u32[]{:S(2)}) async-start(bf16[512,8,128]{2,0,1:T(8,128)(2,1)} %bitcast.68), calls=%async_computation.2 | async-start | bytes 2097152 | tf_op jit(solution)/shard_map/all_to_all | solution.py:192
  41.7 44.9 %copy-start.1 = (bf16[512,8,128]{2,0,1:T(8,128)(2,1)}, bf16[512,8,128]{2,0,1:T(8,128)(2,1)S(1)}, u32[]{:S(2)}) copy-start(bf16[512,8,128]{2,0,1:T(8,128)(2,1)S(1)} %all-to-all-done.2) | copy-start | bytes 3145732
  41.7 20.2 %all-to-all-start.1 = ((bf16[512,8,128]{2,0,1:T(8,128)(2,1)}), bf16[512,8,128]{2,0,1:T(8,128)(2,1)}, u32[]{:S(2)}, u32[]{:S(2)}) async-start(bf16[512,8,128]{2,0,1:T(8,128)(2,1)} %bitcast.66), calls=%async_computation.1 | async-start | bytes 2097152 | tf_op jit(solution)/shard_map/all_to_all | solution.py:191
  61.9 20.2 %all-to-all-start = ((bf16[512,8,128]{2,0,1:T(8,128)(2,1)}), bf16[512,8,128]{2,0,1:T(8,128)(2,1)}, u32[]{:S(2)}, u32[]{:S(2)}) async-start(bf16[512,8,128]{2,0,1:T(8,128)(2,1)} %bitcast.67), calls=%async_computation | async-start | bytes 2097152 | tf_op jit(solution)/shard_map/all_to_all | solution.py:190
  68.7 17.7 %copy-start.10 = (s32[1,32,8]{1,2,0:T(8,128)S(1)}, s32[1,32,8]{1,2,0:T(8,128)}, u32[]{:S(2)}) copy-start(s32[1,32,8]{1,2,0:T(8,128)} %param.11) | copy-start | bytes 3076
  68.7 17.9 %copy-start.5 = (s32[1,32]{1,0:T(1,128)S(1)}, s32[1,32]{1,0:T(1,128)}, u32[]{:S(2)}) copy-start(s32[1,32]{1,0:T(1,128)} %param.12) | copy-start | bytes 388
  82.1 37.4 %all-to-all-start.4 = ((bf16[512,8,128]{2,0,1:T(8,128)(2,1)}), bf16[512,8,128]{2,0,1:T(8,128)(2,1)}, u32[]{:S(2)}, u32[]{:S(2)}) async-start(bf16[512,8,128]{2,0,1:T(8,128)(2,1)} %bitcast.65), calls=%async_computation.4 | async-start | bytes 2097152 | tf_op jit(solution)/shard_map/all_to_all | solution.py:204
  116.3 1.0 copy-start.2
  119.5 47.6 %all-to-all-start.3 = ((bf16[8,512,128]{1,2,0:T(8,128)(2,1)}), bf16[8,512,128]{1,2,0:T(8,128)(2,1)}, u32[]{:S(2)}, u32[]{:S(2)}) async-start(bf16[8,512,128]{1,2,0:T(8,128)(2,1)} %copy.20), calls=%async_computation.3 | async-start | bytes 2097152 | tf_op jit(solution)/shard_map/all_to_all | solution.py:197
  162.9 1.0 copy-start.3
  163.9 1.0 copy-start.4
  167.1 20.9 %all-to-all-start.6 = ((bf16[8,512,128]{1,2,0:T(8,128)(2,1)}), bf16[8,512,128]{1,2,0:T(8,128)(2,1)}, u32[]{:S(2)}, u32[]{:S(2)}) async-start(bf16[8,512,128]{1,2,0:T(8,128)(2,1)} %copy.23), calls=%async_computation.6 | async-start | bytes 2097152 | tf_op jit(solution)/shard_map/all_to_all | solution.py:210
  188.0 20.2 %all-to-all-start.5 = ((bf16[8,512,128]{1,2,0:T(8,128)(2,1)}), bf16[8,512,128]{1,2,0:T(8,128)(2,1)}, u32[]{:S(2)}, u32[]{:S(2)}) async-start(bf16[8,512,128]{1,2,0:T(8,128)(2,1)} %copy.22), calls=%async_computation.5 | async-start | bytes 2097152 | tf_op jit(solution)/shard_map/all_to_all | solution.py:209
  208.2 20.2 %all-to-all-start.7 = ((bf16[8,512,128]{1,2,0:T(8,128)(2,1)}), bf16[8,512,128]{1,2,0:T(8,128)(2,1)}, u32[]{:S(2)}, u32[]{:S(2)}) async-start(bf16[8,512,128]{1,2,0:T(8,128)(2,1)} %copy.24), calls=%async_computation.7 | async-start | bytes 2097152 | tf_op jit(solution)/shard_map/all_to_all | solution.py:211
  212.5 702.2 %reduce-scatter.2.cloned.1.call-start = ((), (), s32[]{:S(2)}) async-start(), calls=%async_computation.9 | async-start | bytes 16908288 | tf_op jit(solution)/shard_map/reduce_scatter | solution.py:226
  212.7 15.7 %copy-start.7 = (bf16[512,1024]{1,0:T(8,128)(2,1)S(1)}, bf16[512,1024]{1,0:T(8,128)(2,1)}, u32[]{:S(2)}) copy-start(bf16[512,1024]{1,0:T(8,128)(2,1)} %param.7) | copy-start | bytes 3145732
  228.5 5.8 copy-start.8
  240.3 713.9 %all-gather.2.cloned.1.call-start = ((), (), s32[]{:S(2)}) async-start(), calls=%async_computation.10 | async-start | bytes 1114112 | tf_op jit(solution)/shard_map/all_gather | solution.py:227
  916.3 7.6 copy-start.9
Sparse Core Ops, SparseCore 0:
  240.4 674.2 reduce-scatter.1
  917.4 36.7 all-gather.1

commit v3 on v2

--- a/solution.py
+++ b/solution.py
@@ -223,10 +223,11 @@
     terms = jnp.concatenate(
         [contract_rows(normed, grad_mixed), contract_rows(attended, cotan)], axis=1
     )
-    piece = lax.psum_scatter(terms, ("seq", "dp"), scatter_dimension=0, tiled=True)
-    own_rows = lax.all_gather(piece.astype(jnp.bfloat16), "dp", axis=0, tiled=True)
-    grad_qkv = own_rows[:, :qkv_width]
-    grad_out = own_rows[:, qkv_width:]
+    summed = lax.psum(terms, ("dp", "seq"))
+    shard_rows = model_width // lax.axis_size("seq")
+    own_rows = lax.dynamic_slice_in_dim(summed, lax.axis_index("seq") * shard_rows, shard_rows, 0)
+    grad_qkv = own_rows[:, :qkv_width].astype(jnp.bfloat16)
+    grad_out = own_rows[:, qkv_width:].astype(jnp.bfloat16)
     return (result, grad_feats, grad_qkv, grad_out)
 
 

time: 966 us -> 379 us (0.39)
  waiting for transfers between devices: 778 us -> 75.1 us
  blocking collectives: 0 us -> 130 us
  between operations: 14.3 us -> 0.86 us
    reduce_scatter x1 -> x0, waiting for transfers between devices: 674 us -> none  [body(): lax.psum_scatter(terms, ('seq', 'dp'), scatter_dimension=0, tiled=True)]
    psum x0 -> x1, blocking collectives: none -> 130 us  [body(): summed = lax.psum(terms, ('dp', 'seq'))]
    all_gather x1 -> x0, waiting for transfers between devices: 25.1 us -> none  [body(): lax.all_gather(piece.astype(jnp.bfloat16), 'dp', axis=0, tiled=True)]
  transfers between devices with their start and end apart: 10 -> 8, of which waited for: 8 -> 6; matrix products, arithmetic and copies ran while one was open for 4% -> 7% of each run, Pallas kernels for 7% -> 18%
where the time goes in v3:
time: 379 us; the launch traced here: 378 us
  blocking collectives  130 us (34%)
  waiting for transfers between devices  75.1 us (20%)
  Pallas kernels  67.4 us (18%)
  starting transfers between devices  36.2 us (10%)
  matrix products  32.2 us (8%)
  local copies, waits for them, and re-layouts  24.6 us (6%)
  other arithmetic  11.1 us (3%)
    psum x1, blocking collectives, body(): summed = lax.psum(terms, ('dp', 'seq'))  130 us
    pallas_call x1, Pallas kernels, attention_backward(): pl.pallas_call(attn_bwd_kernel, out_shape=tuple((jax.ShapeDtypeStruct((n,...  37.7 us
    pallas_call x1, Pallas kernels, attention_forward(): pl.pallas_call(attn_fwd_kernel, out_shape=(jax.ShapeDtypeStruct((n, width...  29.7 us
    all_to_all x1, waiting for transfers between devices, body(): lax.all_to_all(key_grad, 'seq', split_axis=0, concat_axis=1, tiled=True)  14.6 us
    all_to_all x1, waiting for transfers between devices, body(): lax.all_to_all(value_grad, 'seq', split_axis=0, concat_axis=1, tiled=True)  13.7 us
    all_to_all x1, waiting for transfers between devices, body(): lax.all_to_all(key_rows, 'seq', split_axis=1, concat_axis=0, tiled=True)  13.6 us
    all_to_all x1, waiting for transfers between devices, body(): lax.all_to_all(query_rows, 'seq', split_axis=1, concat_axis=0, tiled=True)  13.6 us
    all_to_all x1, waiting for transfers between devices, body(): lax.all_to_all(value_rows, 'seq', split_axis=1, concat_axis=0, tiled=True)  12.2 us
  transfers between devices with their start and end apart: 8, of which 6 were waited for; matrix products, arithmetic and copies ran while one was open for 7% of the time, Pallas kernels for 18%

profile of v3, /device:TPU:0, one launch (start us, length us, event | category | flops | bytes accessed | tf_op | source)
XLA Modules:
  0.0 377.8 jit_solution(13920582588867303463)
XLA Ops:
  2.3 1.6 fusion.11
  3.9 6.7 %convolution_convert_fusion = bf16[512,3072]{1,0:T(8,128)(2,1)S(1)} fusion(bf16[1024,3072]{1,0:T(8,128)(2,1)} %param.9, bf16[512,1024]{1,0:T(8,128)(2,1)S(1)} %copy-done.8, f32[1024]{0:T(1024)S(1)} %copy-done.14, f32[512]{0:T(512)S(1)} %add_rsqrt_fusion, f32[512]{0:T(512)S(1)} %broadcast_multiply_fusion.2), kind=kOutput, calls=%fused_computation.1 | convolution fusion | flops 3225419776 | bytes 10493952 | tf_op jit(solution)/shard_map/dot_general | solution.py:185
  10.6 2.0 slice_bitcast_fusion
  13.8 5.4 %all-to-all-start = ((bf16[512,8,128]{2,0,1:T(8,128)(2,1)}), bf16[512,8,128]{2,0,1:T(8,128)(2,1)S(1)}, u32[]{:S(2)}, u32[]{:S(2)}) async-start(bf16[512,8,128]{2,0,1:T(8,128)(2,1)} %bitcast.68), calls=%async_computation | async-start | bytes 2097152 | tf_op jit(solution)/shard_map/all_to_all | solution.py:190
  19.2 2.4 copy.37
  21.6 13.6 %all-to-all-done = bf16[512,8,128]{2,0,1:T(8,128)(2,1)S(1)} async-done(((bf16[512,8,128]{2,0,1:T(8,128)(2,1)}), bf16[512,8,128]{2,0,1:T(8,128)(2,1)S(1)}, u32[]{:S(2)}, u32[]{:S(2)}) %all-to-all-start) | async-done | bytes 1048608 | tf_op jit(solution)/shard_map/all_to_all | solution.py:190
  35.2 4.2 %all-to-all-start.1 = ((bf16[512,8,128]{2,0,1:T(8,128)(2,1)}), bf16[512,8,128]{2,0,1:T(8,128)(2,1)}, u32[]{:S(2)}, u32[]{:S(2)}) async-start(bf16[512,8,128]{2,0,1:T(8,128)(2,1)} %bitcast.66), calls=%async_computation.1 | async-start | bytes 2097152 | tf_op jit(solution)/shard_map/all_to_all | solution.py:191
  39.4 2.4 copy.36
  41.8 13.6 %all-to-all-done.1 = bf16[512,8,128]{2,0,1:T(8,128)(2,1)} async-done(((bf16[512,8,128]{2,0,1:T(8,128)(2,1)}), bf16[512,8,128]{2,0,1:T(8,128)(2,1)}, u32[]{:S(2)}, u32[]{:S(2)}) %all-to-all-start.1) | async-done | bytes 1048608 | tf_op jit(solution)/shard_map/all_to_all | solution.py:191
  55.4 4.2 %all-to-all-start.2 = ((bf16[512,8,128]{2,0,1:T(8,128)(2,1)}), bf16[512,8,128]{2,0,1:T(8,128)(2,1)}, u32[]{:S(2)}, u32[]{:S(2)}) async-start(bf16[512,8,128]{2,0,1:T(8,128)(2,1)} %bitcast.67), calls=%async_computation.2 | async-start | bytes 2097152 | tf_op jit(solution)/shard_map/all_to_all | solution.py:192
  59.6 2.5 fusion.13
  63.3 12.2 %all-to-all-done.2 = bf16[512,8,128]{2,0,1:T(8,128)(2,1)} async-done(((bf16[512,8,128]{2,0,1:T(8,128)(2,1)}), bf16[512,8,128]{2,0,1:T(8,128)(2,1)}, u32[]{:S(2)}, u32[]{:S(2)}) %all-to-all-start.2) | async-done | bytes 1048608 | tf_op jit(solution)/shard_map/all_to_all | solution.py:192
  75.6 4.2 %all-to-all-start.4 = ((bf16[512,8,128]{2,0,1:T(8,128)(2,1)}), bf16[512,8,128]{2,0,1:T(8,128)(2,1)}, u32[]{:S(2)}, u32[]{:S(2)}) async-start(bf16[512,8,128]{2,0,1:T(8,128)(2,1)} %bitcast.65), calls=%async_computation.4 | async-start | bytes 2097152 | tf_op jit(solution)/shard_map/all_to_all | solution.py:204
  80.0 29.7 %shard_map.102 = (bf16[4096,128]{1,0:T(8,128)(2,1)S(1)}, f32[8192,128]{1,0:T(8,128)}) custom-call(s32[256]{0:T(256)S(1)} %reshape_squeeze.3.cols_ref, s32[32]{0:T(128)S(1)} %bitcast.63, bf16[4096,128]{1,0:T(8,128)(2,1)S(1)} %bitcast.57, bf16[4096,128]{1,0:T(8,128)(2,1)} %bitcast.4.k_ref, bf16[4096,128]{1,0:T(8,128)(2,1)} %bitcast.6.v_ref), custom_call_target="tpu_custom_call" | custom-call | tf_op jit(solution)/shard_map/pallas_call | solution.py:157
  110.7 2.3 copy.20
  112.9 4.7 %all-to-all-start.3 = ((bf16[8,512,128]{1,2,0:T(8,128)(2,1)}), bf16[8,512,128]{1,2,0:T(8,128)(2,1)}, u32[]{:S(2)}, u32[]{:S(2)}) async-start(bf16[8,512,128]{1,2,0:T(8,128)(2,1)} %copy.20), calls=%async_computation.3 | async-start | bytes 2097152 | tf_op jit(solution)/shard_map/all_to_all | solution.py:197
  117.6 37.7 %shard_map.103 = (bf16[4096,128]{1,0:T(8,128)(2,1)S(1)}, bf16[4096,128]{1,0:T(8,128)(2,1)S(1)}, bf16[4096,128]{1,0:T(8,128)(2,1)S(1)}) custom-call(s32[256]{0:T(256)S(1)} %reshape_squeeze.3.cols_ref, s32[32]{0:T(128)S(1)} %bitcast.64, bf16[4096,128]{1,0:T(8,128)(2,1)S(1)} %bitcast.58, bf16[4096,128]{1,0:T(8,128)(2,1)} %bitcast.4.k_ref, ...), custom_call_target="tpu_custom_call" | custom-call | tf_op jit(solution)/shard_map/pallas_call | solution.py:171
  158.3 2.3 copy.24
  160.6 4.8 %all-to-all-start.7 = ((bf16[8,512,128]{1,2,0:T(8,128)(2,1)}), bf16[8,512,128]{1,2,0:T(8,128)(2,1)}, u32[]{:S(2)}, u32[]{:S(2)}) async-start(bf16[8,512,128]{1,2,0:T(8,128)(2,1)} %copy.24), calls=%async_computation.7 | async-start | bytes 2097152 | tf_op jit(solution)/shard_map/all_to_all | solution.py:211
  165.4 2.4 copy.23
  167.7 13.7 %all-to-all-done.7 = bf16[8,512,128]{1,2,0:T(8,128)(2,1)} async-done(((bf16[8,512,128]{1,2,0:T(8,128)(2,1)}), bf16[8,512,128]{1,2,0:T(8,128)(2,1)}, u32[]{:S(2)}, u32[]{:S(2)}) %all-to-all-start.7) | async-done | bytes 1048608 | tf_op jit(solution)/shard_map/all_to_all | solution.py:211
  181.4 4.2 %all-to-all-start.6 = ((bf16[8,512,128]{1,2,0:T(8,128)(2,1)}), bf16[8,512,128]{1,2,0:T(8,128)(2,1)}, u32[]{:S(2)}, u32[]{:S(2)}) async-start(bf16[8,512,128]{1,2,0:T(8,128)(2,1)} %copy.23), calls=%async_computation.6 | async-start | bytes 2097152 | tf_op jit(solution)/shard_map/all_to_all | solution.py:210
  187.1 14.6 %all-to-all-done.6 = bf16[8,512,128]{1,2,0:T(8,128)(2,1)} async-done(((bf16[8,512,128]{1,2,0:T(8,128)(2,1)}), bf16[8,512,128]{1,2,0:T(8,128)(2,1)}, u32[]{:S(2)}, u32[]{:S(2)}) %all-to-all-start.6) | async-done | bytes 1048608 | tf_op jit(solution)/shard_map/all_to_all | solution.py:210
  201.7 4.4 %all-to-all-start.5 = ((bf16[8,512,128]{1,2,0:T(8,128)(2,1)}), bf16[8,512,128]{1,2,0:T(8,128)(2,1)}, u32[]{:S(2)}, u32[]{:S(2)}) async-start(bf16[8,512,128]{1,2,0:T(8,128)(2,1)} %copy.22), calls=%async_computation.5 | async-start | bytes 2097152 | tf_op jit(solution)/shard_map/all_to_all | solution.py:209
  206.1 4.8 %fusion.20 = f32[1024,1024]{1,0:T(8,128)} fusion(bf16[512,1024]{0,1:T(8,128)(2,1)} %bitcast.9, bf16[512,1024]{1,0:T(8,128)(2,1)} %param.13), kind=kOutput, calls=%fused_computation.38 | convolution fusion | flops 1073741824 | bytes 6291456 | tf_op jit(solution)/shard_map/dot_general | solution.py:28
  210.9 3.5 fusion.12
  214.4 7.5 %all-to-all-done.5 = bf16[8,512,128]{1,2,0:T(8,128)(2,1)} async-done(((bf16[8,512,128]{1,2,0:T(8,128)(2,1)}), bf16[8,512,128]{1,2,0:T(8,128)(2,1)}, u32[]{:S(2)}, u32[]{:S(2)}) %all-to-all-start.5) | async-done | bytes 1048608 | tf_op jit(solution)/shard_map/all_to_all | solution.py:209
  221.9 8.9 %multiply_reduce_fusion = (f32[512]{0:T(512)S(1)}, f32[512]{0:T(512)S(1)}, f32[512,1024]{1,0:T(8,128)}) fusion(f32[1024]{0:T(1024)S(1)} %copy-done.14, f32[512]{0:T(512)S(1)} %add_rsqrt_fusion, f32[512]{0:T(512)S(1)} %broadcast_multiply_fusion.2, bf16[512,1024]{1,0:T(8,128)(2,1)S(1)} %copy-done.9, bf16[1024,3072]{1,0:T(8,128)(2,1)} %param.9, ...), kind=kOutput, calls=%fused_computation.20 | convolution fusion | flops 3234331648 | bytes 12595200 | tf_op jit(solution)/shard_map/dot_general | solution.py:214
  230.8 5.8 %fusion.14 = f32[1024,3072]{1,0:T(8,128)S(1)} fusion(bf16[512,1024]{0,1:T(8,128)(2,1)} %bitcast.23, bf16[512,1024]{0,1:T(8,128)(2,1)} %bitcast.20, bf16[512,1024]{0,1:T(8,128)(2,1)} %bitcast.17, bf16[512,1024]{1,0:T(8,128)(2,1)S(1)} %copy-done.9, f32[1024]{0:T(1024)S(1)} %copy-done.14, f32[512]{0:T(512)S(1)} %add_rsqrt_fusion, ...), kind=kOutput, calls=%fused_computation.23 | convolution fusion | flops 3233284096 | bytes 16785408 | tf_op jit(solution)/shard_map/dot_general | solution.py:28
  236.6 6.0 %pad_maximum_fusion = f32[1024,4096]{1,0:T(8,128)} fusion(f32[1024,1024]{1,0:T(8,128)S(1)} %copy-done.10, f32[1024,3072]{1,0:T(8,128)S(1)} %fusion.14), kind=kLoop, calls=%fused_computation | loop fusion | flops 4194304 | bytes 33554432 | tf_op jit(solution)/shard_map/concatenate | solution.py:223
  242.6 130.2 %all-reduce.1 = bf16[1024,4096]{1,0:T(8,128)(2,1)} all-reduce(f32[1024,4096]{1,0:T(8,128)} %pad_maximum_fusion), channel_id=1, replica_groups=mesh['dp'=16,'seq'=8] {'dp','seq'}, use_global_device_ids=true, to_apply=%region_4.0 | all-reduce | flops 4194304 | bytes 25165824 | tf_op jit(solution)/shard_map/psum | solution.py:226
  376.0 1.8 fusion.10
  (44 shorter events, 12.6 us)
Async XLA Ops:
  0.6 59.0 %copy-start = (bf16[1024,1024]{1,0:T(8,128)(2,1)S(1)}, bf16[1024,1024]{1,0:T(8,128)(2,1)}, u32[]{:S(2)}) copy-start(bf16[1024,1024]{1,0:T(8,128)(2,1)} %param.10) | copy-start | bytes 6291460
  0.6 3.3 copy-start.8
  0.7 3.3 copy-start.14
  13.8 21.4 %all-to-all-start = ((bf16[512,8,128]{2,0,1:T(8,128)(2,1)}), bf16[512,8,128]{2,0,1:T(8,128)(2,1)S(1)}, u32[]{:S(2)}, u32[]{:S(2)}) async-start(bf16[512,8,128]{2,0,1:T(8,128)(2,1)} %bitcast.68), calls=%async_computation | async-start | bytes 2097152 | tf_op jit(solution)/shard_map/all_to_all | solution.py:190
  35.2 20.2 %all-to-all-start.1 = ((bf16[512,8,128]{2,0,1:T(8,128)(2,1)}), bf16[512,8,128]{2,0,1:T(8,128)(2,1)}, u32[]{:S(2)}, u32[]{:S(2)}) async-start(bf16[512,8,128]{2,0,1:T(8,128)(2,1)} %bitcast.66), calls=%async_computation.1 | async-start | bytes 2097152 | tf_op jit(solution)/shard_map/all_to_all | solution.py:191
  55.4 20.2 %all-to-all-start.2 = ((bf16[512,8,128]{2,0,1:T(8,128)(2,1)}), bf16[512,8,128]{2,0,1:T(8,128)(2,1)}, u32[]{:S(2)}, u32[]{:S(2)}) async-start(bf16[512,8,128]{2,0,1:T(8,128)(2,1)} %bitcast.67), calls=%async_computation.2 | async-start | bytes 2097152 | tf_op jit(solution)/shard_map/all_to_all | solution.py:192
  62.1 17.7 %copy-start.13 = (s32[1,32,8]{1,2,0:T(8,128)S(1)}, s32[1,32,8]{1,2,0:T(8,128)}, u32[]{:S(2)}) copy-start(s32[1,32,8]{1,2,0:T(8,128)} %param.11) | copy-start | bytes 3076
  62.2 17.8 %copy-start.7 = (s32[1,32]{1,0:T(1,128)S(1)}, s32[1,32]{1,0:T(1,128)}, u32[]{:S(2)}) copy-start(s32[1,32]{1,0:T(1,128)} %param.12) | copy-start | bytes 388
  75.6 37.4 %all-to-all-start.4 = ((bf16[512,8,128]{2,0,1:T(8,128)(2,1)}), bf16[512,8,128]{2,0,1:T(8,128)(2,1)}, u32[]{:S(2)}, u32[]{:S(2)}) async-start(bf16[512,8,128]{2,0,1:T(8,128)(2,1)} %bitcast.65), calls=%async_computation.4 | async-start | bytes 2097152 | tf_op jit(solution)/shard_map/all_to_all | solution.py:204
  109.7 1.0 copy-start.2
  112.9 47.6 %all-to-all-start.3 = ((bf16[8,512,128]{1,2,0:T(8,128)(2,1)}), bf16[8,512,128]{1,2,0:T(8,128)(2,1)}, u32[]{:S(2)}, u32[]{:S(2)}) async-start(bf16[8,512,128]{1,2,0:T(8,128)(2,1)} %copy.20), calls=%async_computation.3 | async-start | bytes 2097152 | tf_op jit(solution)/shard_map/all_to_all | solution.py:197
  155.3 1.0 copy-start.3
  156.3 1.0 copy-start.5
  157.3 1.0 copy-start.6
  160.6 20.9 %all-to-all-start.7 = ((bf16[8,512,128]{1,2,0:T(8,128)(2,1)}), bf16[8,512,128]{1,2,0:T(8,128)(2,1)}, u32[]{:S(2)}, u32[]{:S(2)}) async-start(bf16[8,512,128]{1,2,0:T(8,128)(2,1)} %copy.24), calls=%async_computation.7 | async-start | bytes 2097152 | tf_op jit(solution)/shard_map/all_to_all | solution.py:211
  165.4 20.3 %copy-start.4 = (bf16[4096,128]{1,0:T(8,128)(2,1)S(1)}, bf16[4096,128]{1,0:T(8,128)(2,1)}, u32[]{:S(2)}) copy-start(bf16[4096,128]{1,0:T(8,128)(2,1)} %copy-done.3) | copy-start | bytes 3145732
  181.4 20.2 %all-to-all-start.6 = ((bf16[8,512,128]{1,2,0:T(8,128)(2,1)}), bf16[8,512,128]{1,2,0:T(8,128)(2,1)}, u32[]{:S(2)}, u32[]{:S(2)}) async-start(bf16[8,512,128]{1,2,0:T(8,128)(2,1)} %copy.23), calls=%async_computation.6 | async-start | bytes 2097152 | tf_op jit(solution)/shard_map/all_to_all | solution.py:210
  201.7 20.2 %all-to-all-start.5 = ((bf16[8,512,128]{1,2,0:T(8,128)(2,1)}), bf16[8,512,128]{1,2,0:T(8,128)(2,1)}, u32[]{:S(2)}, u32[]{:S(2)}) async-start(bf16[8,512,128]{1,2,0:T(8,128)(2,1)} %copy.22), calls=%async_computation.5 | async-start | bytes 2097152 | tf_op jit(solution)/shard_map/all_to_all | solution.py:209
  206.1 4.8 %copy-start.9 = (bf16[512,1024]{1,0:T(8,128)(2,1)S(1)}, bf16[512,1024]{1,0:T(8,128)(2,1)}, u32[]{:S(2)}) copy-start(bf16[512,1024]{1,0:T(8,128)(2,1)} %param.7) | copy-start | bytes 3145732
  230.8 5.8 %copy-start.10 = (f32[1024,1024]{1,0:T(8,128)S(1)}, f32[1024,1024]{1,0:T(8,128)}, u32[]{:S(2)}) copy-start(f32[1024,1024]{1,0:T(8,128)} %fusion.20) | copy-start | bytes 12582916
  372.8 3.1 copy-start.11
  372.8 3.2 copy-start.12
  376.0 1.9 copy-start.1

commit v4 on v2

--- a/solution.py
+++ b/solution.py
@@ -180,17 +180,25 @@
 
 def body(feats, gain, w_qkv, w_out, block_cols, block_counts, cotan):
     model_width = feats.shape[1]
-    qkv_width = 3 * model_width
+    seq_count = lax.axis_size("seq")
+    group_width = model_width // seq_count
+    seq_at = lax.axis_index("seq")
     scaled, inverse, normed = layer_norm(feats, gain)
-    mixed_proj = jnp.dot(normed, w_qkv, preferred_element_type=jnp.float32).astype(jnp.bfloat16)
-    query_rows = mixed_proj[:, :model_width]
-    key_rows = mixed_proj[:, model_width : 2 * model_width]
-    value_rows = mixed_proj[:, 2 * model_width :]
-    query_heads, key_heads, value_heads = (
-        lax.all_to_all(query_rows, "seq", split_axis=1, concat_axis=0, tiled=True),
-        lax.all_to_all(key_rows, "seq", split_axis=1, concat_axis=0, tiled=True),
-        lax.all_to_all(value_rows, "seq", split_axis=1, concat_axis=0, tiled=True),
-    )
+    normed_all = lax.all_gather(normed, "seq", axis=0, tiled=True)
+    cotan_all = lax.all_gather(cotan, "seq", axis=0, tiled=True)
+    w_heads = jnp.concatenate(
+        [
+            lax.dynamic_slice_in_dim(w_qkv, j * model_width + seq_at * group_width, group_width, 1)
+            for j in range(3)
+        ],
+        axis=1,
+    )
+    mixed_heads = jnp.dot(normed_all, w_heads, preferred_element_type=jnp.float32).astype(
+        jnp.bfloat16
+    )
+    query_heads = mixed_heads[:, :group_width]
+    key_heads = mixed_heads[:, group_width : 2 * group_width]
+    value_heads = mixed_heads[:, 2 * group_width :]
     cols = block_cols[0].reshape(-1)
     counts = block_counts[0]
     attended_heads, lse = attention_forward(query_heads, key_heads, value_heads, cols, counts)
@@ -198,10 +206,10 @@
     result = (
         feats.astype(jnp.float32) + jnp.dot(attended, w_out, preferred_element_type=jnp.float32)
     ).astype(jnp.bfloat16)
-    grad_att = lax.dot_general(
-        cotan, w_out, (((1,), (1,)), ((), ())), preferred_element_type=jnp.float32
+    w_out_rows = lax.dynamic_slice_in_dim(w_out, seq_at * group_width, group_width, 0)
+    grad_heads = lax.dot_general(
+        cotan_all, w_out_rows, (((1,), (1,)), ((), ())), preferred_element_type=jnp.float32
     ).astype(jnp.bfloat16)
-    grad_heads = lax.all_to_all(grad_att, "seq", split_axis=1, concat_axis=0, tiled=True)
     query_grad, key_grad, value_grad = attention_backward(
         query_heads, key_heads, value_heads, attended_heads, grad_heads, lse, cols, counts
     )
@@ -220,13 +228,19 @@
     grad_feats = (
         cotan.astype(jnp.float32) + inverse * (gained - mean_one - scaled * mean_two)
     ).astype(jnp.bfloat16)
-    terms = jnp.concatenate(
-        [contract_rows(normed, grad_mixed), contract_rows(attended, cotan)], axis=1
-    )
-    piece = lax.psum_scatter(terms, ("seq", "dp"), scatter_dimension=0, tiled=True)
-    own_rows = lax.all_gather(piece.astype(jnp.bfloat16), "dp", axis=0, tiled=True)
-    grad_qkv = own_rows[:, :qkv_width]
-    grad_out = own_rows[:, qkv_width:]
+    grad_heads_mixed = jnp.concatenate([query_grad, key_grad, value_grad], axis=1)
+    term_qkv = lax.psum(contract_rows(normed_all, grad_heads_mixed), "dp")
+    term_out = lax.psum(contract_rows(attended_heads, cotan_all), "dp")
+    moved = lax.all_to_all(
+        term_qkv.astype(jnp.bfloat16), "seq", split_axis=0, concat_axis=1, tiled=True
+    )
+    rows = moved.shape[0]
+    grad_qkv = (
+        moved.reshape(rows, seq_count, 3, group_width)
+        .transpose(0, 2, 1, 3)
+        .reshape(rows, 3 * model_width)
+    )
+    grad_out = term_out.astype(jnp.bfloat16)
     return (result, grad_feats, grad_qkv, grad_out)
 
 

time: 966 us -> 382 us (0.40)
  waiting for transfers between devices: 778 us -> 126 us
  blocking collectives: 0 us -> 93.6 us
  starting transfers between devices: 36.4 us -> 21.4 us
  local copies, waits for them, and re-layouts: 24.2 us -> 14 us
    reduce_scatter x1 -> x0, waiting for transfers between devices: 674 us -> none  [body(): lax.psum_scatter(terms, ('seq', 'dp'), scatter_dimension=0, tiled=True)]
    psum x0 -> x1, blocking collectives: none -> 93.6 us  [body(): term_qkv = lax.psum(contract_rows(normed_all, grad_heads_mixed), 'dp')]
    all_gather x1 -> x2, waiting for transfers between devices: 25.1 us -> 61.4 us  [the longest x1 50.4 us: body(): normed_all = lax.all_gather(normed, 'seq', axis=0, tiled=True)]
    all_to_all x4 -> x1, waiting for transfers between devices: 39.3 us -> 11.8 us  [body(): lax.all_to_all(term_qkv.astype(jnp.bfloat16), 'seq', split_axis=0, concat...]
    all_to_all x1, waiting for transfers between devices: 0.01 us -> 14.5 us  [body(): lax.all_to_all(attended_heads, 'seq', split_axis=0, concat_axis=1, tiled=...]
    all_to_all x4 -> x1, starting transfers between devices: 18.1 us -> 4.21 us  [body(): lax.all_to_all(term_qkv.astype(jnp.bfloat16), 'seq', split_axis=0, concat...]
  transfers between devices with their start and end apart: 10 -> 7, of which waited for: 8 -> 7; matrix products, arithmetic and copies ran while one was open for 4% -> 6% of each run, Pallas kernels for 7% -> 8%
where the time goes in v4:
time: 382 us; the launch traced here: 380 us
  waiting for transfers between devices  126 us (33%)
  blocking collectives  93.6 us (25%)
  Pallas kernels  66.8 us (17%)
  matrix products  37.5 us (10%)
  starting transfers between devices  21.4 us (6%)
  between operations  14.3 us (4%)
  local copies, waits for them, and re-layouts  14 us (4%)
  other arithmetic  6.41 us (2%)
    psum x1, blocking collectives, body(): term_qkv = lax.psum(contract_rows(normed_all, grad_heads_mixed), 'dp')  93.6 us
    all_gather x1, waiting for transfers between devices, body(): normed_all = lax.all_gather(normed, 'seq', axis=0, tiled=True)  50.4 us
    pallas_call x1, Pallas kernels, attention_backward(): pl.pallas_call(attn_bwd_kernel, out_shape=tuple((jax.ShapeDtypeStruct((n,...  37.9 us
    pallas_call x1, Pallas kernels, attention_forward(): pl.pallas_call(attn_fwd_kernel, out_shape=(jax.ShapeDtypeStruct((n, width...  28.9 us
    all_to_all x1, waiting for transfers between devices, body(): lax.all_to_all(key_grad, 'seq', split_axis=0, concat_axis=1, tiled=True)  14.6 us
    all_to_all x1, waiting for transfers between devices, body(): lax.all_to_all(attended_heads, 'seq', split_axis=0, concat_axis=1, tiled=...  14.5 us
    all_to_all x1, waiting for transfers between devices, body(): lax.all_to_all(value_grad, 'seq', split_axis=0, concat_axis=1, tiled=True)  13.6 us
    all_to_all x1, waiting for transfers between devices, body(): lax.all_to_all(term_qkv.astype(jnp.bfloat16), 'seq', split_axis=0, concat...  11.8 us
  transfers between devices with their start and end apart: 7, of which 7 were waited for; matrix products, arithmetic and copies ran while one was open for 6% of the time, Pallas kernels for 8%

profile of v4, /device:TPU:0, one launch (start us, length us, event | category | flops | bytes accessed | tf_op | source)
XLA Modules:
  0.0 380.5 jit_solution(1237020549044099283)
XLA Ops:
  7.2 1.6 convert_reduce_fusion
  8.8 1.6 fusion.24
  10.5 1.3 fusion.18
  12.8 1.2 constant_dynamic-slice_fusion.2
  14.0 50.4 %all-gather.3.cloned.1.call-done = bf16[4096,1024]{1,0:T(8,128)(2,1)} async-done(((bf16[512,1024]{1,0:T(8,128)(2,1)}), bf16[4096,1024]{1,0:T(8,128)(2,1)}) %all-gather.3.cloned.1.call-update) | async-done | bytes 8388624 | tf_op jit(solution)/shard_map/all_gather | solution.py:187
  64.5 8.3 %convolution_convert_fusion = bf16[4096,384]{1,0:T(8,128)(2,1)S(1)} fusion(bf16[4096,1024]{1,0:T(8,128)(2,1)} %all-gather.3.cloned.1.call-done, bf16[1024,128]{1,0:T(8,128)(2,1)S(1)} %get-tuple-element.20, bf16[1024,128]{1,0:T(8,128)(2,1)S(1)} %get-tuple-element.19, bf16[1024,128]{1,0:T(8,128)(2,1)S(1)} %get-tuple-element.18), kind=kOutput, calls=%fused_computation | convolution fusion | flops 3225157632 | bytes 12320768 | tf_op jit(solution)/shard_map/dot_general | solution.py:196
  73.4 28.9 %shard_map.102 = (bf16[4096,128]{1,0:T(8,128)(2,1)S(1)}, f32[8192,128]{1,0:T(8,128)}) custom-call(s32[256]{0:T(256)S(1)} %reshape_squeeze.3.cols_ref, s32[32]{0:T(128)S(1)} %bitcast.42, bf16[4096,128]{1,0:T(8,128)(2,1)S(1)} %get-tuple-element.23.q_ref, bf16[4096,128]{1,0:T(8,128)(2,1)S(1)} %get-tuple-element.22.k_ref, ...), custom_call_target="tpu_custom_call" | custom-call | tf_op jit(solution)/shard_map/pallas_call | solution.py:157
  105.1 11.0 %all-gather.5.cloned.1.call-done = bf16[4096,1024]{1,0:T(8,128)(2,1)} async-done(((bf16[512,1024]{1,0:T(8,128)(2,1)}), bf16[4096,1024]{1,0:T(8,128)(2,1)}) %all-gather.5.cloned.1.call-update) | async-done | bytes 8388624 | tf_op jit(solution)/shard_map/all_gather | solution.py:188
  116.2 6.9 %fusion.do_ref = bf16[4096,128]{1,0:T(8,128)(2,1)} fusion(bf16[4096,1024]{1,0:T(8,128)(2,1)} %all-gather.5.cloned.1.call-done, bf16[1024,1024]{1,0:T(8,128)(2,1)S(1)} %copy-done, s32[]{:T(128)S(6)} %select_n.15), kind=kOutput, calls=%fused_computation.2 | convolution fusion | flops 1074266112 | bytes 9699332 | tf_op jit(solution)/shard_map/dot_general | solution.py:210
  123.1 37.9 %shard_map.103 = (bf16[4096,128]{1,0:T(8,128)(2,1)S(1)}, bf16[4096,128]{1,0:T(8,128)(2,1)S(1)}, bf16[4096,128]{1,0:T(8,128)(2,1)S(1)}) custom-call(s32[256]{0:T(256)S(1)} %reshape_squeeze.3.cols_ref, s32[32]{0:T(128)S(1)} %bitcast.43, bf16[4096,128]{1,0:T(8,128)(2,1)S(1)} %copy-done.7, bf16[4096,128]{1,0:T(8,128)(2,1)S(1)} %copy-done.5, ...), custom_call_target="tpu_custom_call" | custom-call | tf_op jit(solution)/shard_map/pallas_call | solution.py:171
  161.1 9.3 %fusion.7 = f32[1024,384]{1,0:T(8,128)} fusion(bf16[4096,1024]{1,0:T(8,128)(2,1)} %all-gather.3.cloned.1.call-done, bf16[4096,128]{1,0:T(8,128)(2,1)S(1)} %get-tuple-element.13, bf16[4096,128]{1,0:T(8,128)(2,1)S(1)} %get-tuple-element.12, bf16[4096,128]{1,0:T(8,128)(2,1)S(1)} %get-tuple-element.11), kind=kOutput, calls=%fused_computation.9 | convolution fusion | flops 3230662656 | bytes 13107200 | tf_op jit(solution)/shard_map/dot_general | solution.py:28
  170.4 2.1 fusion.37
  172.5 93.6 %all-reduce.2 = (bf16[1024,384]{1,0:T(8,128)(2,1)}, bf16[128,1024]{1,0:T(8,128)(2,1)}) all-reduce(f32[1024,384]{1,0:T(8,128)} %fusion.7, f32[128,1024]{1,0:T(8,128)} %fusion.37), channel_id=1, replica_groups=mesh['dp'=16,'seq'=8] {'dp'}, use_global_device_ids=true, to_apply=%region_4.0 | all-reduce | flops 524288 | bytes 3145728 | tf_op jit(solution)/shard_map/psum | solution.py:232
  266.1 4.2 %all-to-all-start.4 = ((bf16[8,128,384]{2,1,0:T(8,128)(2,1)}), bf16[8,128,384]{2,1,0:T(8,128)(2,1)}, u32[]{:S(2)}, u32[]{:S(2)}) async-start(bf16[8,128,384]{2,1,0:T(8,128)(2,1)} %bitcast.48), calls=%async_computation.4 | async-start | bytes 1572864 | tf_op jit(solution)/shard_map/all_to_all | solution.py:234
  270.3 1.3 copy.21
  271.6 11.8 %all-to-all-done.4 = bf16[8,128,384]{2,1,0:T(8,128)(2,1)} async-done(((bf16[8,128,384]{2,1,0:T(8,128)(2,1)}), bf16[8,128,384]{2,1,0:T(8,128)(2,1)}, u32[]{:S(2)}, u32[]{:S(2)}) %all-to-all-start.4) | async-done | bytes 786464 | tf_op jit(solution)/shard_map/all_to_all | solution.py:234
  283.4 4.4 %all-to-all-start = ((bf16[8,512,128]{1,2,0:T(8,128)(2,1)}), bf16[8,512,128]{1,2,0:T(8,128)(2,1)}, u32[]{:S(2)}, u32[]{:S(2)}) async-start(bf16[8,512,128]{1,2,0:T(8,128)(2,1)} %copy.21), calls=%async_computation | async-start | bytes 2097152 | tf_op jit(solution)/shard_map/all_to_all | solution.py:205
  287.9 1.3 copy.25
  289.2 14.5 %all-to-all-done = bf16[8,512,128]{1,2,0:T(8,128)(2,1)} async-done(((bf16[8,512,128]{1,2,0:T(8,128)(2,1)}), bf16[8,512,128]{1,2,0:T(8,128)(2,1)}, u32[]{:S(2)}, u32[]{:S(2)}) %all-to-all-start) | async-done | bytes 1048608 | tf_op jit(solution)/shard_map/all_to_all | solution.py:205
  303.7 4.2 %all-to-all-start.3 = ((bf16[8,512,128]{1,2,0:T(8,128)(2,1)}), bf16[8,512,128]{1,2,0:T(8,128)(2,1)}, u32[]{:S(2)}, u32[]{:S(2)}) async-start(bf16[8,512,128]{1,2,0:T(8,128)(2,1)} %copy.25), calls=%async_computation.3 | async-start | bytes 2097152 | tf_op jit(solution)/shard_map/all_to_all | solution.py:219
  307.9 2.4 copy.24
  310.3 13.6 %all-to-all-done.3 = bf16[8,512,128]{1,2,0:T(8,128)(2,1)} async-done(((bf16[8,512,128]{1,2,0:T(8,128)(2,1)}), bf16[8,512,128]{1,2,0:T(8,128)(2,1)}, u32[]{:S(2)}, u32[]{:S(2)}) %all-to-all-start.3) | async-done | bytes 1048608 | tf_op jit(solution)/shard_map/all_to_all | solution.py:219
  323.9 4.2 %all-to-all-start.2 = ((bf16[8,512,128]{1,2,0:T(8,128)(2,1)}), bf16[8,512,128]{1,2,0:T(8,128)(2,1)}, u32[]{:S(2)}, u32[]{:S(2)}) async-start(bf16[8,512,128]{1,2,0:T(8,128)(2,1)} %copy.24), calls=%async_computation.2 | async-start | bytes 2097152 | tf_op jit(solution)/shard_map/all_to_all | solution.py:218
  328.1 1.3 copy.23
  329.5 14.6 %all-to-all-done.2 = bf16[8,512,128]{1,2,0:T(8,128)(2,1)} async-done(((bf16[8,512,128]{1,2,0:T(8,128)(2,1)}), bf16[8,512,128]{1,2,0:T(8,128)(2,1)}, u32[]{:S(2)}, u32[]{:S(2)}) %all-to-all-start.2) | async-done | bytes 1048608 | tf_op jit(solution)/shard_map/all_to_all | solution.py:218
  344.1 4.2 %all-to-all-start.1 = ((bf16[8,512,128]{1,2,0:T(8,128)(2,1)}), bf16[8,512,128]{1,2,0:T(8,128)(2,1)}, u32[]{:S(2)}, u32[]{:S(2)}) async-start(bf16[8,512,128]{1,2,0:T(8,128)(2,1)} %copy.23), calls=%async_computation.1 | async-start | bytes 2097152 | tf_op jit(solution)/shard_map/all_to_all | solution.py:217
  348.3 1.7 copy.26
  350.0 1.0 copy.30
  351.0 3.5 fusion.25
  354.5 9.8 %all-to-all-done.1 = bf16[8,512,128]{1,2,0:T(8,128)(2,1)} async-done(((bf16[8,512,128]{1,2,0:T(8,128)(2,1)}), bf16[8,512,128]{1,2,0:T(8,128)(2,1)}, u32[]{:S(2)}, u32[]{:S(2)}) %all-to-all-start.1) | async-done | bytes 1048608 | tf_op jit(solution)/shard_map/all_to_all | solution.py:217
  364.3 7.5 %multiply_reduce_fusion = (f32[512]{0:T(512)S(1)}, f32[512]{0:T(512)S(1)}, f32[512,1024]{1,0:T(8,128)S(1)}) fusion(f32[1024]{0:T(1024)S(1)} %copy-done.17, f32[512]{0:T(512)S(1)} %add_rsqrt_fusion, f32[512]{0:T(512)S(1)} %broadcast_multiply_fusion.2, bf16[512,1024]{1,0:T(8,128)(2,1)S(1)} %copy-done.15, bf16[1024,3072]{1,0:T(8,128)(2,1)} %param.9, ...), kind=kOutput, calls=%fused_computation.31 | convolution fusion | flops 3234331648 | bytes 12595200 | tf_op jit(solution)/shard_map/dot_general | solution.py:222
  371.8 1.8 fusion.23
  (53 shorter events, 4.6 us)
Async XLA Ops:
  7.2 109.0 %copy-start = (bf16[1024,1024]{1,0:T(8,128)(2,1)S(1)}, bf16[1024,1024]{1,0:T(8,128)(2,1)}, u32[]{:S(2)}) copy-start(bf16[1024,1024]{1,0:T(8,128)(2,1)} %param.10) | copy-start | bytes 6291460
  7.2 3.3 copy-start.14
  7.2 3.3 copy-start.17
  7.2 57.2 %all-gather.3.cloned.1.call-start = ((), (), s32[]{:S(2)}) async-start(), calls=%async_computation.5 | async-start | bytes 9437184 | tf_op jit(solution)/shard_map/all_gather | solution.py:187
  10.5 2.1 copy-start.18
  11.9 104.3 %all-gather.5.cloned.1.call-start = ((), (), s32[]{:S(2)}) async-start(), calls=%async_computation.6 | async-start | bytes 9437184 | tf_op jit(solution)/shard_map/all_gather | solution.py:188
  72.7 0.7 copy-start.13
  73.3 49.8 %copy-start.3 = (bf16[4096,128]{1,0:T(8,128)(2,1)}, bf16[4096,128]{1,0:T(8,128)(2,1)S(1)}, u32[]{:S(2)}) copy-start(bf16[4096,128]{1,0:T(8,128)(2,1)S(1)} %get-tuple-element.21.v_ref) | copy-start | bytes 3145732
  102.2 1.0 copy-start.1
  103.2 1.0 copy-start.4
  104.2 1.0 copy-start.6
  116.2 6.9 %copy-start.5 = (bf16[4096,128]{1,0:T(8,128)(2,1)S(1)}, bf16[4096,128]{1,0:T(8,128)(2,1)}, u32[]{:S(2)}) copy-start(bf16[4096,128]{1,0:T(8,128)(2,1)} %copy-done.4) | copy-start | bytes 3145732
  116.2 6.9 %copy-start.7 = (bf16[4096,128]{1,0:T(8,128)(2,1)S(1)}, bf16[4096,128]{1,0:T(8,128)(2,1)}, u32[]{:S(2)}) copy-start(bf16[4096,128]{1,0:T(8,128)(2,1)} %copy-done.6) | copy-start | bytes 3145732
  123.1 47.3 %slice-start = ((s8[8388608]{0:T(1024)(128)(4,1)}), s8[4194304]{0:T(1024)(128)(4,1)S(1)}, s32[]{:S(2)}) async-start(s8[8388608]{0:T(1024)(128)(4,1)} %bitcast.44), calls=%async_computation.7 | async-start | bytes 8388608
  161.0 9.3 %copy-start.8 = (bf16[4096,128]{1,0:T(8,128)(2,1)}, bf16[4096,128]{1,0:T(8,128)(2,1)S(1)}, u32[]{:S(2)}) copy-start(bf16[4096,128]{1,0:T(8,128)(2,1)S(1)} %get-tuple-element.11) | copy-start | bytes 3145732
  161.0 9.3 %copy-start.10 = (bf16[4096,128]{1,0:T(8,128)(2,1)}, bf16[4096,128]{1,0:T(8,128)(2,1)S(1)}, u32[]{:S(2)}) copy-start(bf16[4096,128]{1,0:T(8,128)(2,1)S(1)} %get-tuple-element.12) | copy-start | bytes 3145732
  161.0 9.3 %copy-start.11 = (bf16[4096,128]{1,0:T(8,128)(2,1)}, bf16[4096,128]{1,0:T(8,128)(2,1)S(1)}, u32[]{:S(2)}) copy-start(bf16[4096,128]{1,0:T(8,128)(2,1)S(1)} %get-tuple-element.13) | copy-start | bytes 3145732
  161.0 9.3 %copy-start.2 = (bf16[4096,128]{1,0:T(8,128)(2,1)S(1)}, bf16[4096,128]{1,0:T(8,128)(2,1)}, u32[]{:S(2)}) copy-start(bf16[4096,128]{1,0:T(8,128)(2,1)} %copy-done.1) | copy-start | bytes 3145732
  161.1 9.3 %slice-start.1 = ((s8[8388608]{0:T(1024)(128)(4,1)}), s8[4194304]{0:T(1024)(128)(4,1)S(1)}, s32[]{:S(2)}) async-start(s8[8388608]{0:T(1024)(128)(4,1)} %bitcast.44), calls=%async_computation.8 | async-start | bytes 8388608
  266.1 17.4 %all-to-all-start.4 = ((bf16[8,128,384]{2,1,0:T(8,128)(2,1)}), bf16[8,128,384]{2,1,0:T(8,128)(2,1)}, u32[]{:S(2)}, u32[]{:S(2)}) async-start(bf16[8,128,384]{2,1,0:T(8,128)(2,1)} %bitcast.48), calls=%async_computation.4 | async-start | bytes 1572864 | tf_op jit(solution)/shard_map/all_to_all | solution.py:234
  271.6 16.3 %copy-start.12 = (bf16[4096,128]{1,0:T(8,128)(2,1)S(1)}, bf16[4096,128]{1,0:T(8,128)(2,1)}, u32[]{:S(2)}) copy-start(bf16[4096,128]{1,0:T(8,128)(2,1)} %copy-done.11) | copy-start | bytes 3145732
  283.4 20.2 %all-to-all-start = ((bf16[8,512,128]{1,2,0:T(8,128)(2,1)}), bf16[8,512,128]{1,2,0:T(8,128)(2,1)}, u32[]{:S(2)}, u32[]{:S(2)}) async-start(bf16[8,512,128]{1,2,0:T(8,128)(2,1)} %copy.21), calls=%async_computation | async-start | bytes 2097152 | tf_op jit(solution)/shard_map/all_to_all | solution.py:205
  303.7 20.2 %all-to-all-start.3 = ((bf16[8,512,128]{1,2,0:T(8,128)(2,1)}), bf16[8,512,128]{1,2,0:T(8,128)(2,1)}, u32[]{:S(2)}, u32[]{:S(2)}) async-start(bf16[8,512,128]{1,2,0:T(8,128)(2,1)} %copy.25), calls=%async_computation.3 | async-start | bytes 2097152 | tf_op jit(solution)/shard_map/all_to_all | solution.py:219
  307.9 20.2 %copy-start.9 = (bf16[4096,128]{1,0:T(8,128)(2,1)S(1)}, bf16[4096,128]{1,0:T(8,128)(2,1)}, u32[]{:S(2)}) copy-start(bf16[4096,128]{1,0:T(8,128)(2,1)} %copy-done.8) | copy-start | bytes 3145732
  323.9 20.2 %all-to-all-start.2 = ((bf16[8,512,128]{1,2,0:T(8,128)(2,1)}), bf16[8,512,128]{1,2,0:T(8,128)(2,1)}, u32[]{:S(2)}, u32[]{:S(2)}) async-start(bf16[8,512,128]{1,2,0:T(8,128)(2,1)} %copy.24), calls=%async_computation.2 | async-start | bytes 2097152 | tf_op jit(solution)/shard_map/all_to_all | solution.py:218
  344.1 20.2 %all-to-all-start.1 = ((bf16[8,512,128]{1,2,0:T(8,128)(2,1)}), bf16[8,512,128]{1,2,0:T(8,128)(2,1)}, u32[]{:S(2)}, u32[]{:S(2)}) async-start(bf16[8,512,128]{1,2,0:T(8,128)(2,1)} %copy.23), calls=%async_computation.1 | async-start | bytes 2097152 | tf_op jit(solution)/shard_map/all_to_all | solution.py:217
  348.3 2.7 copy-start.15
  364.3 7.5 %copy-start.16 = (bf16[512,1024]{1,0:T(8,128)(2,1)S(1)}, bf16[512,1024]{1,0:T(8,128)(2,1)}, u32[]{:S(2)}) copy-start(bf16[512,1024]{1,0:T(8,128)(2,1)} %param.13) | copy-start | bytes 3145732
Sparse Core Ops, SparseCore 0:
  12.0 52.3 all-gather.2
  66.2 49.9 all-gather.4

commit v5 on v4

--- a/solution.py
+++ b/solution.py
@@ -178,6 +178,20 @@
     )(cols, counts, q, k, v, o, do, lse)
 
 
+def regroup_columns(moved, seq_count, group_width):
+    rows = moved.shape[0]
+    return (
+        moved.reshape(rows, seq_count, 3, group_width)
+        .transpose(0, 2, 1, 3)
+        .reshape(rows, 3 * seq_count * group_width)
+    )
+
+
+def sum_over_dp(term, axis):
+    piece = lax.psum_scatter(term, "dp", scatter_dimension=axis, tiled=True)
+    return lax.all_gather(piece.astype(jnp.bfloat16), "dp", axis=axis, tiled=True)
+
+
 def body(feats, gain, w_qkv, w_out, block_cols, block_counts, cotan):
     model_width = feats.shape[1]
     seq_count = lax.axis_size("seq")
@@ -213,12 +227,12 @@
     query_grad, key_grad, value_grad = attention_backward(
         query_heads, key_heads, value_heads, attended_heads, grad_heads, lse, cols, counts
     )
-    query_back, key_back, value_back = (
-        lax.all_to_all(query_grad, "seq", split_axis=0, concat_axis=1, tiled=True),
-        lax.all_to_all(key_grad, "seq", split_axis=0, concat_axis=1, tiled=True),
-        lax.all_to_all(value_grad, "seq", split_axis=0, concat_axis=1, tiled=True),
-    )
-    grad_mixed = jnp.concatenate([query_back, key_back, value_back], axis=1)
+    grad_heads_mixed = jnp.concatenate([query_grad, key_grad, value_grad], axis=1)
+    grad_mixed = regroup_columns(
+        lax.all_to_all(grad_heads_mixed, "seq", split_axis=0, concat_axis=1, tiled=True),
+        seq_count,
+        group_width,
+    )
     grad_normed = lax.dot_general(
         grad_mixed, w_qkv, (((1,), (1,)), ((), ())), preferred_element_type=jnp.float32
     )
@@ -228,19 +242,14 @@
     grad_feats = (
         cotan.astype(jnp.float32) + inverse * (gained - mean_one - scaled * mean_two)
     ).astype(jnp.bfloat16)
-    grad_heads_mixed = jnp.concatenate([query_grad, key_grad, value_grad], axis=1)
-    term_qkv = lax.psum(contract_rows(normed_all, grad_heads_mixed), "dp")
-    term_out = lax.psum(contract_rows(attended_heads, cotan_all), "dp")
-    moved = lax.all_to_all(
-        term_qkv.astype(jnp.bfloat16), "seq", split_axis=0, concat_axis=1, tiled=True
-    )
-    rows = moved.shape[0]
-    grad_qkv = (
-        moved.reshape(rows, seq_count, 3, group_width)
-        .transpose(0, 2, 1, 3)
-        .reshape(rows, 3 * model_width)
-    )
-    grad_out = term_out.astype(jnp.bfloat16)
+    term_qkv = sum_over_dp(contract_rows(normed_all, grad_heads_mixed), 0)
+    term_out = sum_over_dp(contract_rows(attended_heads, cotan_all), 1)
+    grad_qkv = regroup_columns(
+        lax.all_to_all(term_qkv, "seq", split_axis=0, concat_axis=1, tiled=True),
+        seq_count,
+        group_width,
+    )
+    grad_out = term_out
     return (result, grad_feats, grad_qkv, grad_out)
 
 

time: 382 us -> 328 us (0.86)
  blocking collectives: 93.6 us -> 49.2 us
  waiting for transfers between devices: 126 us -> 115 us
  starting transfers between devices: 21.4 us -> 13.6 us
  local copies, waits for them, and re-layouts: 14 us -> 20.7 us
    psum x1 -> x0, blocking collectives: 93.6 us -> none  [body(): term_qkv = lax.psum(contract_rows(normed_all, grad_heads_mixed), 'dp')]
    all_gather x0 -> x2, blocking collectives: none -> 49.2 us  [sum_over_dp(): lax.all_gather(piece.astype(jnp.bfloat16), 'dp', axis=axis, tiled=True)]
    reduce_scatter x0 -> x2, waiting for transfers between devices: none -> 43.8 us  [sum_over_dp(): piece = lax.psum_scatter(term, 'dp', scatter_dimension=axis, tiled=True)]
    all_to_all x4 -> x2, waiting for transfers between devices: 49.8 us -> 7.92 us  [the longest x1 4.21 us: body(): lax.all_to_all(term_qkv, 'seq', split_axis=0, concat_axis=1, tiled=True)]
    all_to_all x1, waiting for transfers between devices: 14.5 us -> 0.01 us  [body(): lax.all_to_all(attended_heads, 'seq', split_axis=0, concat_axis=1, tiled=...]
    all_to_all x4 -> x2, starting transfers between devices: 16.9 us -> 9.03 us  [the longest x1 4.6 us: body(): lax.all_to_all(grad_heads_mixed, 'seq', split_axis=0, concat_axis=1, tile...]
    transpose x0 -> x1, local copies, waits for them, and re-layouts: none -> 4.98 us  [regroup_columns(): return moved.reshape(rows, seq_count, 3, group_width).transpose(0, 2, 1,...]
  transfers between devices with their start and end apart: 7 -> 7, of which waited for: 7 -> 6; matrix products, arithmetic and copies ran while one was open for 6% -> 15% of each run, Pallas kernels for 8% -> 21%
where the time goes in v5:
time: 328 us; the launch traced here: 326 us
  waiting for transfers between devices  115 us (35%)
  Pallas kernels  66.9 us (20%)
  blocking collectives  49.2 us (15%)
  matrix products  39.1 us (12%)
  local copies, waits for them, and re-layouts  20.7 us (6%)
  between operations  14 us (4%)
  starting transfers between devices  13.6 us (4%)
  other arithmetic  8.08 us (2%)
    all_gather x1, waiting for transfers between devices, body(): normed_all = lax.all_gather(normed, 'seq', axis=0, tiled=True)  50.4 us
    all_gather x2, blocking collectives, sum_over_dp(): lax.all_gather(piece.astype(jnp.bfloat16), 'dp', axis=axis, tiled=True)  49.2 us
    reduce_scatter x2, waiting for transfers between devices, sum_over_dp(): piece = lax.psum_scatter(term, 'dp', scatter_dimension=axis, tiled=True)  43.8 us
    pallas_call x1, Pallas kernels, attention_backward(): pl.pallas_call(attn_bwd_kernel, out_shape=tuple((jax.ShapeDtypeStruct((n,...  38.2 us
    pallas_call x1, Pallas kernels, attention_forward(): pl.pallas_call(attn_fwd_kernel, out_shape=(jax.ShapeDtypeStruct((n, width...  28.7 us
    dot_general x2, matrix products, contract_rows(): lax.dot_general(left_cols, right_cols, (((0,), (0,)), ((), ())), preferre...  13.2 us
    all_gather x1, waiting for transfers between devices, body(): cotan_all = lax.all_gather(cotan, 'seq', axis=0, tiled=True)  11.7 us
    dot_general x1, matrix products, body(): jnp.dot(normed_all, w_heads, preferred_element_type=jnp.float32)  8.26 us
  transfers between devices with their start and end apart: 7, of which 6 were waited for; matrix products, arithmetic and copies ran while one was open for 15% of the time, Pallas kernels for 21%

profile of v5, /device:TPU:0, one launch (start us, length us, event | category | flops | bytes accessed | tf_op | source)
XLA Modules:
  0.0 326.2 jit_solution(14563194156473596723)
XLA Ops:
  7.2 1.6 convert_reduce_fusion
  8.8 1.6 fusion.12
  10.5 1.4 fusion.6
  12.9 1.2 constant_dynamic-slice_fusion.2
  14.1 50.4 %all-gather.3.cloned.1.call-done = bf16[4096,1024]{1,0:T(8,128)(2,1)} async-done(((bf16[512,1024]{1,0:T(8,128)(2,1)}), bf16[4096,1024]{1,0:T(8,128)(2,1)}) %all-gather.3.cloned.1.call-update) | async-done | bytes 8388624 | tf_op jit(solution)/shard_map/all_gather | solution.py:201
  64.5 8.3 %convolution_convert_fusion = bf16[4096,384]{1,0:T(8,128)(2,1)S(1)} fusion(bf16[4096,1024]{1,0:T(8,128)(2,1)} %all-gather.3.cloned.1.call-done, bf16[1024,128]{1,0:T(8,128)(2,1)S(1)} %get-tuple-element.30, bf16[1024,128]{1,0:T(8,128)(2,1)S(1)} %get-tuple-element.29, bf16[1024,128]{1,0:T(8,128)(2,1)S(1)} %get-tuple-element.28), kind=kOutput, calls=%fused_computation | convolution fusion | flops 3225157632 | bytes 12320768 | tf_op jit(solution)/shard_map/dot_general | solution.py:210
  73.4 28.7 %shard_map.102 = (bf16[4096,128]{1,0:T(8,128)(2,1)S(1)}, f32[8192,128]{1,0:T(8,128)}) custom-call(s32[256]{0:T(256)S(1)} %reshape_squeeze.3.cols_ref, s32[32]{0:T(128)S(1)} %bitcast.38, bf16[4096,128]{1,0:T(8,128)(2,1)S(1)} %get-tuple-element.33.q_ref, bf16[4096,128]{1,0:T(8,128)(2,1)S(1)} %get-tuple-element.32.k_ref, ...), custom_call_target="tpu_custom_call" | custom-call | tf_op jit(solution)/shard_map/pallas_call | solution.py:157
  102.1 1.0 copy-done.2
  103.1 1.4 copy.22
  104.5 11.7 %all-gather.5.cloned.1.call-done = bf16[4096,1024]{1,0:T(8,128)(2,1)} async-done(((bf16[512,1024]{1,0:T(8,128)(2,1)}), bf16[4096,1024]{1,0:T(8,128)(2,1)}) %all-gather.5.cloned.1.call-update) | async-done | bytes 8388624 | tf_op jit(solution)/shard_map/all_gather | solution.py:202
  116.2 7.5 %fusion.24 = f32[128,1024]{0,1:T(8,128)} fusion(bf16[4096,128]{1,0:T(8,128)(2,1)S(1)} %get-tuple-element.9.o_ref, bf16[4096,1024]{1,0:T(8,128)(2,1)} %all-gather.5.cloned.1.call-done), kind=kOutput, calls=%fused_computation.42 | convolution fusion | flops 1073741824 | bytes 9961472 | tf_op jit(solution)/shard_map/dot_general | solution.py:28
  123.8 4.3 %all-to-all-start = ((bf16[8,512,128]{1,2,0:T(8,128)(2,1)}), bf16[8,512,128]{1,2,0:T(8,128)(2,1)}, u32[]{:S(2)}, u32[]{:S(2)}) async-start(bf16[8,512,128]{1,2,0:T(8,128)(2,1)} %copy.22), calls=%async_computation | async-start | bytes 2097152 | tf_op jit(solution)/shard_map/all_to_all | solution.py:219
  128.3 7.0 %fusion.do_ref = bf16[4096,128]{1,0:T(8,128)(2,1)} fusion(bf16[4096,1024]{1,0:T(8,128)(2,1)} %all-gather.5.cloned.1.call-done, bf16[1024,1024]{1,0:T(8,128)(2,1)S(1)} %copy-done, s32[]{:T(128)S(6)} %select_n.15), kind=kOutput, calls=%fused_computation.2 | convolution fusion | flops 1074266112 | bytes 9699332 | tf_op jit(solution)/shard_map/dot_general | solution.py:224
  135.3 38.2 %shard_map.103 = (bf16[4096,128]{1,0:T(8,128)(2,1)S(1)}, bf16[4096,128]{1,0:T(8,128)(2,1)S(1)}, bf16[4096,128]{1,0:T(8,128)(2,1)S(1)}) custom-call(s32[256]{0:T(256)S(1)} %reshape_squeeze.3.cols_ref, s32[32]{0:T(128)S(1)} %bitcast.39, bf16[4096,128]{1,0:T(8,128)(2,1)S(1)} %copy-done.6, bf16[4096,128]{1,0:T(8,128)(2,1)S(1)} %copy-done.4, ...), custom_call_target="tpu_custom_call" | custom-call | tf_op jit(solution)/shard_map/pallas_call | solution.py:171
  174.2 1.7 copy-done.8
  175.9 5.7 %fusion.23 = f32[1024,384]{1,0:T(8,128)} fusion(bf16[4096,1024]{1,0:T(8,128)(2,1)S(1)} %bitcast.43, bf16[4096,384]{1,0:T(8,128)(2,1)S(1)} %constant_dynamic-update-slice_fusion), kind=kOutput, calls=%fused_computation.41 | convolution fusion | flops 3221225472 | bytes 13107200 | tf_op jit(solution)/shard_map/dot_general | solution.py:28
  181.6 4.6 %all-to-all-start.1 = ((bf16[8,512,384]{2,1,0:T(8,128)(2,1)}), bf16[8,512,384]{2,1,0:T(8,128)(2,1)}, u32[]{:S(2)}, u32[]{:S(2)}) async-start(bf16[8,512,384]{2,1,0:T(8,128)(2,1)} %bitcast.40), calls=%async_computation.1 | async-start | bytes 6291456 | tf_op jit(solution)/shard_map/all_to_all | solution.py:232
  186.2 3.5 %fusion.13 = bf16[512,1024]{1,0:T(8,128)(2,1)} fusion(bf16[512,1024]{1,0:T(8,128)(2,1)S(1)} %copy-done.10, bf16[512,1024]{0,1:T(8,128)(2,1)} %bitcast.3, bf16[1024,1024]{1,0:T(8,128)(2,1)S(1)} %copy-done), kind=kOutput, calls=%fused_computation.19 | convolution fusion | flops 1075314688 | bytes 5242880 | tf_op jit(solution)/shard_map/dot_general | solution.py:221
  189.7 6.4 %reduce-scatter.5.cloned.1.call-done = f32[128,64]{0,1:T(8,128)} async-done(((f32[128,1024]{0,1:T(8,128)}), f32[128,64]{0,1:T(8,128)}) %reduce-scatter.5.cloned.1.call-update) | async-done | bytes 32784 | tf_op jit(solution)/shard_map/reduce_scatter | solution.py:191
  196.9 23.3 %all_gather.15 = bf16[128,1024]{0,1:T(8,128)(2,1)S(1)} all-gather(bf16[128,64]{0,1:T(8,128)(2,1)S(1)} %convert_element_type.39), channel_id=1, replica_groups=mesh['dp'=16,'seq'=8] {'dp'}, dimensions={1}, use_global_device_ids=true | all-gather | bytes 278528 | tf_op jit(solution)/shard_map/all_gather | solution.py:192
  221.0 3.7 %all-to-all-done.1 = bf16[8,512,384]{2,1,0:T(8,128)(2,1)} async-done(((bf16[8,512,384]{2,1,0:T(8,128)(2,1)}), bf16[8,512,384]{2,1,0:T(8,128)(2,1)}, u32[]{:S(2)}, u32[]{:S(2)}) %all-to-all-start.1) | async-done | bytes 3145760 | tf_op jit(solution)/shard_map/all_to_all | solution.py:232
  224.7 5.5 %copy.32 = bf16[8,512,384]{2,0,1:T(8,128)(2,1)} copy(bf16[8,512,384]{2,1,0:T(8,128)(2,1)} %all-to-all-done.1) | data formatting | bytes 6291456 | tf_op jit(solution)/shard_map/all_to_all | solution.py:232
  230.2 5.0 %copy.25 = bf16[512,3,8,128]{0,3,2,1:T(8,128)(2,1)} copy(bf16[512,3,8,128]{3,2,1,0:T(8,128)(2,1)} %bitcast.41) | data formatting | bytes 6291456 | tf_op jit(solution)/shard_map/transpose | solution.py:185
  235.2 37.4 %reduce-scatter.3.cloned.1.call-done = f32[64,384]{1,0:T(8,128)} async-done(((f32[1024,384]{1,0:T(8,128)}), f32[64,384]{1,0:T(8,128)}) %reduce-scatter.3.cloned.1.call-update) | async-done | bytes 98320 | tf_op jit(solution)/shard_map/reduce_scatter | solution.py:191
  272.6 0.9 convert_element_type.38
  273.5 25.9 %all_gather.14 = bf16[1024,384]{1,0:T(8,128)(2,1)} all-gather(bf16[64,384]{1,0:T(8,128)(2,1)S(1)} %convert_element_type.38), channel_id=1, replica_groups=mesh['dp'=16,'seq'=8] {'dp'}, dimensions={0}, use_global_device_ids=true | all-gather | bytes 835584 | tf_op jit(solution)/shard_map/all_gather | solution.py:192
  299.4 4.4 %all-to-all-start.2 = ((bf16[8,128,384]{2,1,0:T(8,128)(2,1)}), bf16[8,128,384]{2,1,0:T(8,128)(2,1)}, u32[]{:S(2)}, u32[]{:S(2)}) async-start(bf16[8,128,384]{2,1,0:T(8,128)(2,1)} %bitcast.45), calls=%async_computation.3 | async-start | bytes 1572864 | tf_op jit(solution)/shard_map/all_to_all | solution.py:248
  303.8 7.2 %multiply_reduce_fusion = (f32[512]{0:T(512)S(1)}, f32[512]{0:T(512)S(1)}, f32[512,1024]{1,0:T(8,128)S(1)}) fusion(f32[1024]{0:T(1024)S(1)} %copy-done.12, f32[512]{0:T(512)S(1)} %add_rsqrt_fusion, f32[512]{0:T(512)S(1)} %broadcast_multiply_fusion.2, bf16[512,1024]{1,0:T(8,128)(2,1)S(1)} %copy-done.10, bf16[512,3072]{0,1:T(8,128)(2,1)} %bitcast.44, ...), kind=kOutput, calls=%fused_computation.20 | convolution fusion | flops 3224894464 | bytes 12595200 | tf_op jit(solution)/shard_map/dot_general | solution.py:236
  311.0 1.8 fusion.11
  312.8 4.2 %all-to-all-done.2 = bf16[8,128,384]{2,1,0:T(8,128)(2,1)} async-done(((bf16[8,128,384]{2,1,0:T(8,128)(2,1)}), bf16[8,128,384]{2,1,0:T(8,128)(2,1)}, u32[]{:S(2)}, u32[]{:S(2)}) %all-to-all-start.2) | async-done | bytes 786464 | tf_op jit(solution)/shard_map/all_to_all | solution.py:248
  317.1 1.6 copy.26
  318.7 1.0 copy.33
  (51 shorter events, 4.3 us)
Async XLA Ops:
  7.2 121.1 %copy-start = (bf16[1024,1024]{1,0:T(8,128)(2,1)S(1)}, bf16[1024,1024]{1,0:T(8,128)(2,1)}, u32[]{:S(2)}) copy-start(bf16[1024,1024]{1,0:T(8,128)(2,1)} %param.10) | copy-start | bytes 6291460
  7.2 3.3 %copy-start.9 = (bf16[512,1024]{1,0:T(8,128)(2,1)S(1)}, bf16[512,1024]{1,0:T(8,128)(2,1)}, u32[]{:S(2)}) copy-start(bf16[512,1024]{1,0:T(8,128)(2,1)} %param.7) | copy-start | bytes 3145732
  7.2 3.3 %copy-start.12 = (f32[1024]{0:T(1024)S(1)}, f32[1024]{0:T(1024)}, u32[]{:S(2)}) copy-start(f32[1024]{0:T(1024)} %param.8) | copy-start | bytes 12292
  7.2 57.3 %all-gather.3.cloned.1.call-start = ((), (), s32[]{:S(2)}) async-start(), calls=%async_computation.5 | async-start | bytes 9437184 | tf_op jit(solution)/shard_map/all_gather | solution.py:201
  10.5 2.2 copy-start.13
  11.9 104.3 %all-gather.5.cloned.1.call-start = ((), (), s32[]{:S(2)}) async-start(), calls=%async_computation.6 | async-start | bytes 9437184 | tf_op jit(solution)/shard_map/all_gather | solution.py:202
  12.6 183.5 %reduce-scatter.5.cloned.1.call-start = ((), (), s32[]{:S(2)}) async-start(), calls=%async_computation.8 | async-start | bytes 557056 | tf_op jit(solution)/shard_map/reduce_scatter | solution.py:191
  72.8 0.7 copy-start.7
  73.3 28.8 %copy-start.3 = (bf16[4096,128]{1,0:T(8,128)(2,1)}, bf16[4096,128]{1,0:T(8,128)(2,1)S(1)}, u32[]{:S(2)}) copy-start(bf16[4096,128]{1,0:T(8,128)(2,1)S(1)} %get-tuple-element.32.k_ref) | copy-start | bytes 3145732
  73.3 29.8 %copy-start.5 = (bf16[4096,128]{1,0:T(8,128)(2,1)}, bf16[4096,128]{1,0:T(8,128)(2,1)S(1)}, u32[]{:S(2)}) copy-start(bf16[4096,128]{1,0:T(8,128)(2,1)S(1)} %get-tuple-element.33.q_ref) | copy-start | bytes 3145732
  102.1 1.0 copy-start.2
  103.1 20.7 %copy-start.1 = (bf16[4096,128]{1,0:T(8,128)(2,1)}, bf16[4096,128]{1,0:T(8,128)(2,1)S(1)}, u32[]{:S(2)}) copy-start(bf16[4096,128]{1,0:T(8,128)(2,1)S(1)} %get-tuple-element.9.o_ref) | copy-start | bytes 3145732
  123.8 57.8 %all-to-all-start = ((bf16[8,512,128]{1,2,0:T(8,128)(2,1)}), bf16[8,512,128]{1,2,0:T(8,128)(2,1)}, u32[]{:S(2)}, u32[]{:S(2)}) async-start(bf16[8,512,128]{1,2,0:T(8,128)(2,1)} %copy.22), calls=%async_computation | async-start | bytes 2097152 | tf_op jit(solution)/shard_map/all_to_all | solution.py:219
  128.1 7.2 %copy-start.4 = (bf16[4096,128]{1,0:T(8,128)(2,1)S(1)}, bf16[4096,128]{1,0:T(8,128)(2,1)}, u32[]{:S(2)}) copy-start(bf16[4096,128]{1,0:T(8,128)(2,1)} %copy-done.3) | copy-start | bytes 3145732
  128.1 144.5 %reduce-scatter.3.cloned.1.call-start = ((), (), s32[]{:S(2)}) async-start(), calls=%async_computation.7 | async-start | bytes 1671168 | tf_op jit(solution)/shard_map/reduce_scatter | solution.py:191
  128.3 7.0 %copy-start.6 = (bf16[4096,128]{1,0:T(8,128)(2,1)S(1)}, bf16[4096,128]{1,0:T(8,128)(2,1)}, u32[]{:S(2)}) copy-start(bf16[4096,128]{1,0:T(8,128)(2,1)} %copy-done.5) | copy-start | bytes 3145732
  128.3 47.6 %slice-start = ((s8[8388608]{0:T(1024)(128)(4,1)}), s8[4194304]{0:T(1024)(128)(4,1)S(1)}, s32[]{:S(2)}) async-start(s8[8388608]{0:T(1024)(128)(4,1)} %bitcast.42), calls=%async_computation.9 | async-start | bytes 8388608
  135.3 40.6 %slice-start.1 = ((s8[8388608]{0:T(1024)(128)(4,1)}), s8[4194304]{0:T(1024)(128)(4,1)S(1)}, s32[]{:S(2)}) async-start(s8[8388608]{0:T(1024)(128)(4,1)} %bitcast.42), calls=%async_computation.10 | async-start | bytes 8388608
  174.2 1.7 copy-start.8
  181.6 4.6 %copy-start.10 = (bf16[512,1024]{1,0:T(8,128)(2,1)S(1)}, bf16[512,1024]{1,0:T(8,128)(2,1)}, u32[]{:S(2)}) copy-start(bf16[512,1024]{1,0:T(8,128)(2,1)} %param.7) | copy-start | bytes 3145732
  181.6 43.1 %all-to-all-start.1 = ((bf16[8,512,384]{2,1,0:T(8,128)(2,1)}), bf16[8,512,384]{2,1,0:T(8,128)(2,1)}, u32[]{:S(2)}, u32[]{:S(2)}) async-start(bf16[8,512,384]{2,1,0:T(8,128)(2,1)} %bitcast.40), calls=%async_computation.1 | async-start | bytes 6291456 | tf_op jit(solution)/shard_map/all_to_all | solution.py:232
  299.4 17.7 %all-to-all-start.2 = ((bf16[8,128,384]{2,1,0:T(8,128)(2,1)}), bf16[8,128,384]{2,1,0:T(8,128)(2,1)}, u32[]{:S(2)}, u32[]{:S(2)}) async-start(bf16[8,128,384]{2,1,0:T(8,128)(2,1)} %bitcast.45), calls=%async_computation.3 | async-start | bytes 1572864 | tf_op jit(solution)/shard_map/all_to_all | solution.py:248
  303.8 7.2 %copy-start.11 = (bf16[512,1024]{1,0:T(8,128)(2,1)S(1)}, bf16[512,1024]{1,0:T(8,128)(2,1)}, u32[]{:S(2)}) copy-start(bf16[512,1024]{1,0:T(8,128)(2,1)} %param.13) | copy-start | bytes 3145732
Sparse Core Ops, SparseCore 0:
  12.0 52.4 all-gather.2
  66.2 49.9 all-gather.4
  123.9 72.1 reduce-scatter.4
  199.5 72.9 reduce-scatter.2

commit v6 on v5

--- a/solution.py
+++ b/solution.py
@@ -187,9 +187,76 @@
     )
 
 
-def sum_over_dp(term, axis):
-    piece = lax.psum_scatter(term, "dp", scatter_dimension=axis, tiled=True)
-    return lax.all_gather(piece.astype(jnp.bfloat16), "dp", axis=axis, tiled=True)
+MESH = pl.DeviceIdType.MESH
+
+
+def dp_sum_kernel(n, x_ref, o_ref, recv, gath, send1, recv1, send2, recv2):
+    me = lax.axis_index("dp")
+    barrier = pltpu.get_barrier_semaphore()
+    for k in range(1, n):
+        pl.semaphore_signal(
+            barrier, inc=1, device_id={"dp": lax.rem(me + k, n)}, device_id_type=MESH
+        )
+    pl.semaphore_wait(barrier, n - 1)
+
+    def exchange(src_of, dst, send, arrive):
+        started = []
+        for k in range(1, n):
+            peer = lax.rem(me + k, n)
+            copy = pltpu.make_async_remote_copy(
+                src_ref=src_of(peer),
+                dst_ref=dst.at[me],
+                send_sem=send.at[peer],
+                recv_sem=arrive.at[me],
+                device_id={"dp": peer},
+                device_id_type=MESH,
+            )
+            copy.start()
+            started.append(copy)
+        for k in range(1, n):
+            source = lax.rem(me + n - k, n)
+            pltpu.make_async_remote_copy(
+                src_ref=src_of(source),
+                dst_ref=dst.at[source],
+                send_sem=send.at[source],
+                recv_sem=arrive.at[source],
+                device_id={"dp": source},
+                device_id_type=MESH,
+            ).wait_recv()
+        for copy in started:
+            copy.wait_send()
+
+    exchange(lambda peer: x_ref.at[peer], recv, send1, recv1)
+    total = x_ref[me]
+    for k in range(1, n):
+        total = total + recv[lax.rem(me + k, n)]
+    gath[me] = total.astype(gath.dtype)
+    exchange(lambda peer: gath.at[me], gath, send2, recv2)
+    o_ref[...] = gath[...]
+
+
+def sum_over_dp(term):
+    n = lax.axis_size("dp")
+    rows, cols = term.shape
+    chunked = term.reshape(n, rows // n, cols)
+    out = pl.pallas_call(
+        functools.partial(dp_sum_kernel, n),
+        out_shape=jax.ShapeDtypeStruct(chunked.shape, jnp.bfloat16),
+        in_specs=[vmem_spec()],
+        out_specs=vmem_spec(),
+        scratch_shapes=[
+            pltpu.VMEM(chunked.shape, jnp.float32),
+            pltpu.VMEM(chunked.shape, jnp.bfloat16),
+            pltpu.SemaphoreType.DMA((n,)),
+            pltpu.SemaphoreType.DMA((n,)),
+            pltpu.SemaphoreType.DMA((n,)),
+            pltpu.SemaphoreType.DMA((n,)),
+        ],
+        compiler_params=pltpu.CompilerParams(
+            collective_id=0, has_side_effects=True, vmem_limit_bytes=VMEM_LIMIT
+        ),
+    )(chunked)
+    return out.reshape(rows, cols)
 
 
 def body(feats, gain, w_qkv, w_out, block_cols, block_counts, cotan):
@@ -242,8 +309,14 @@
     grad_feats = (
         cotan.astype(jnp.float32) + inverse * (gained - mean_one - scaled * mean_two)
     ).astype(jnp.bfloat16)
-    term_qkv = sum_over_dp(contract_rows(normed_all, grad_heads_mixed), 0)
-    term_out = sum_over_dp(contract_rows(attended_heads, cotan_all), 1)
+    term_qkv = contract_rows(normed_all, grad_heads_mixed)
+    term_out = contract_rows(attended_heads, cotan_all)
+    qkv_cols = term_qkv.shape[1]
+    summed = sum_over_dp(
+        jnp.concatenate([term_qkv, term_out.reshape(term_qkv.shape[0], -1)], axis=1)
+    )
+    term_qkv = summed[:, :qkv_cols]
+    term_out = summed[:, qkv_cols:].reshape(term_out.shape)
     grad_qkv = regroup_columns(
         lax.all_to_all(term_qkv, "seq", split_axis=0, concat_axis=1, tiled=True),
         seq_count,

time: 328 us -> 338 us (1.030)
  Pallas kernels: 66.9 us -> 117 us
  blocking collectives: 49.2 us -> 20.3 us
  waiting for transfers between devices: 115 us -> 106 us
  local copies, waits for them, and re-layouts: 20.7 us -> 25.8 us
  starting transfers between devices: 13.6 us -> 8.76 us
    pallas_call x0 -> x1, Pallas kernels: none -> 50.5 us  [sum_over_dp(): pl.pallas_call(functools.partial(dp_sum_kernel, n), out_shape=jax.ShapeDt...]
    all_gather x2 -> x0, blocking collectives: 49.2 us -> none  [sum_over_dp(): lax.all_gather(piece.astype(jnp.bfloat16), 'dp', axis=axis, tiled=True)]
    reduce_scatter x2 -> x0, waiting for transfers between devices: 43.8 us -> none  [sum_over_dp(): piece = lax.psum_scatter(term, 'dp', scatter_dimension=axis, tiled=True)]
    all_to_all x1, waiting for transfers between devices: 3.71 us -> 31.6 us  [body(): lax.all_to_all(grad_heads_mixed, 'seq', split_axis=0, concat_axis=1, tile...]
    all_to_all x0 -> x1, blocking collectives: none -> 20.3 us  [body(): lax.all_to_all(attended_heads, 'seq', split_axis=0, concat_axis=1, tiled=...]
    all_to_all x1, waiting for transfers between devices: 4.21 us -> 11.8 us  [body(): lax.all_to_all(term_qkv, 'seq', split_axis=0, concat_axis=1, tiled=True)]
    all_to_all x1 -> x0, starting transfers between devices: 4.26 us -> none  [body(): lax.all_to_all(attended_heads, 'seq', split_axis=0, concat_axis=1, tiled=...]
  transfers between devices with their start and end apart: 7 -> 4, of which waited for: 6 -> 4; matrix products, arithmetic and copies ran while one was open for 15% -> 5% of each run, Pallas kernels for 21% -> 9%
where the time goes in v6:
time: 338 us; the launch traced here: 337 us
  Pallas kernels  117 us (35%)
  waiting for transfers between devices  106 us (31%)
  matrix products  38.4 us (11%)
  local copies, waits for them, and re-layouts  25.8 us (8%)
  blocking collectives  20.3 us (6%)
  between operations  14.3 us (4%)
  starting transfers between devices  8.76 us (3%)
  other arithmetic  6.63 us (2%)
    pallas_call x1, Pallas kernels, sum_over_dp(): pl.pallas_call(functools.partial(dp_sum_kernel, n), out_shape=jax.ShapeDt...  50.5 us
    all_gather x1, waiting for transfers between devices, body(): normed_all = lax.all_gather(normed, 'seq', axis=0, tiled=True)  50.4 us
    pallas_call x1, Pallas kernels, attention_backward(): pl.pallas_call(attn_bwd_kernel, out_shape=tuple((jax.ShapeDtypeStruct((n,...  37.8 us
    all_to_all x1, waiting for transfers between devices, body(): lax.all_to_all(grad_heads_mixed, 'seq', split_axis=0, concat_axis=1, tile...  31.6 us
    pallas_call x1, Pallas kernels, attention_forward(): pl.pallas_call(attn_fwd_kernel, out_shape=(jax.ShapeDtypeStruct((n, width...  28.7 us
    all_to_all x1, blocking collectives, body(): lax.all_to_all(attended_heads, 'seq', split_axis=0, concat_axis=1, tiled=...  20.3 us
    dot_general x2, matrix products, contract_rows(): lax.dot_general(left_cols, right_cols, (((0,), (0,)), ((), ())), preferre...  13.8 us
    all_to_all x1, waiting for transfers between devices, body(): lax.all_to_all(term_qkv, 'seq', split_axis=0, concat_axis=1, tiled=True)  11.8 us
  transfers between devices with their start and end apart: 4, of which 4 were waited for; matrix products, arithmetic and copies ran while one was open for 5% of the time, Pallas kernels for 9%

profile of v6, /device:TPU:0, one launch (start us, length us, event | category | flops | bytes accessed | tf_op | source)
XLA Modules:
  0.0 336.8 jit_solution(10718979821428683390)
XLA Ops:
  7.2 1.6 convert_reduce_fusion
  8.8 1.6 fusion.12
  10.5 1.4 fusion.6
  12.8 1.2 constant_dynamic-slice_fusion.2
  14.0 50.4 %all-gather.3.cloned.1.call-done = bf16[4096,1024]{1,0:T(8,128)(2,1)} async-done(((bf16[512,1024]{1,0:T(8,128)(2,1)}), bf16[4096,1024]{1,0:T(8,128)(2,1)}) %all-gather.3.cloned.1.call-update) | async-done | bytes 8388624 | tf_op jit(solution)/shard_map/all_gather | solution.py:268
  64.5 8.3 %convolution_convert_fusion = bf16[4096,384]{1,0:T(8,128)(2,1)S(1)} fusion(bf16[4096,1024]{1,0:T(8,128)(2,1)} %all-gather.3.cloned.1.call-done, bf16[1024,128]{1,0:T(8,128)(2,1)S(1)} %get-tuple-element.18, bf16[1024,128]{1,0:T(8,128)(2,1)S(1)} %get-tuple-element.17, bf16[1024,128]{1,0:T(8,128)(2,1)S(1)} %get-tuple-element.16), kind=kOutput, calls=%fused_computation | convolution fusion | flops 3225157632 | bytes 12320768 | tf_op jit(solution)/shard_map/dot_general | solution.py:277
  73.4 28.7 %shard_map.102 = (bf16[4096,128]{1,0:T(8,128)(2,1)S(1)}, f32[8192,128]{1,0:T(8,128)}) custom-call(s32[256]{0:T(256)S(1)} %reshape_squeeze.3.cols_ref, s32[32]{0:T(128)S(1)} %bitcast.41, bf16[4096,128]{1,0:T(8,128)(2,1)S(1)} %get-tuple-element.21.q_ref, bf16[4096,128]{1,0:T(8,128)(2,1)S(1)} %get-tuple-element.20.k_ref, ...), custom_call_target="tpu_custom_call" | custom-call | tf_op jit(solution)/shard_map/pallas_call | solution.py:157
  102.1 1.0 copy-done.3
  103.1 1.0 copy-done.4
  104.0 1.0 copy-done.6
  105.0 11.2 %all-gather.5.cloned.1.call-done = bf16[4096,1024]{1,0:T(8,128)(2,1)} async-done(((bf16[512,1024]{1,0:T(8,128)(2,1)}), bf16[4096,1024]{1,0:T(8,128)(2,1)}) %all-gather.5.cloned.1.call-update) | async-done | bytes 8388624 | tf_op jit(solution)/shard_map/all_gather | solution.py:269
  116.2 5.5 %fusion.24 = f32[128,1024]{1,0:T(8,128)} fusion(bf16[4096,128]{1,0:T(8,128)(2,1)S(1)} %get-tuple-element.9.o_ref, bf16[4096,1024]{1,0:T(8,128)(2,1)} %all-gather.5.cloned.1.call-done), kind=kOutput, calls=%fused_computation.43 | convolution fusion | flops 1073741824 | bytes 9961472 | tf_op jit(solution)/shard_map/dot_general | solution.py:28
  121.7 1.9 concatenate.17
  123.6 6.9 %fusion.do_ref = bf16[4096,128]{1,0:T(8,128)(2,1)} fusion(bf16[4096,1024]{1,0:T(8,128)(2,1)} %all-gather.5.cloned.1.call-done, bf16[1024,1024]{1,0:T(8,128)(2,1)S(1)} %copy-done, s32[]{:T(128)S(6)} %select_n.15), kind=kOutput, calls=%fused_computation.2 | convolution fusion | flops 1074266112 | bytes 9699332 | tf_op jit(solution)/shard_map/dot_general | solution.py:291
  130.5 37.8 %shard_map.103 = (bf16[4096,128]{1,0:T(8,128)(2,1)S(1)}, bf16[4096,128]{1,0:T(8,128)(2,1)S(1)}, bf16[4096,128]{1,0:T(8,128)(2,1)S(1)}) custom-call(s32[256]{0:T(256)S(1)} %reshape_squeeze.3.cols_ref, s32[32]{0:T(128)S(1)} %bitcast.42, bf16[4096,128]{1,0:T(8,128)(2,1)S(1)} %copy-done.7, bf16[4096,128]{1,0:T(8,128)(2,1)S(1)} %copy-done.5, ...), custom_call_target="tpu_custom_call" | custom-call | tf_op jit(solution)/shard_map/pallas_call | solution.py:171
  169.0 8.3 %fusion.23 = f32[1024,384]{1,0:T(8,128)S(1)} fusion(bf16[4096,1024]{1,0:T(8,128)(2,1)} %all-gather.3.cloned.1.call-done, bf16[4096,384]{1,0:T(8,128)(2,1)S(1)} %constant_dynamic-update-slice_fusion), kind=kOutput, calls=%fused_computation.42 | convolution fusion | flops 3221225472 | bytes 13107200 | tf_op jit(solution)/shard_map/dot_general | solution.py:28
  177.5 50.5 %shard_map.104 = bf16[16,64,512]{2,1,0:T(8,128)(2,1)S(1)} custom-call(f32[16,64,512]{2,1,0:T(8,128)S(1)} %pad_maximum_fusion.x_ref), custom_call_target="tpu_custom_call" | custom-call | tf_op jit(solution)/shard_map/pallas_call | solution.py:242
  229.0 1.0 slice.23
  229.9 4.2 %all-to-all-start.2 = ((bf16[8,128,384]{2,1,0:T(8,128)(2,1)}), bf16[8,128,384]{2,1,0:T(8,128)(2,1)}, u32[]{:S(2)}, u32[]{:S(2)}) async-start(bf16[8,128,384]{2,1,0:T(8,128)(2,1)} %bitcast.47), calls=%async_computation.2 | async-start | bytes 1572864 | tf_op jit(solution)/shard_map/all_to_all | solution.py:321
  234.2 1.3 copy.24
  235.5 11.8 %all-to-all-done.2 = bf16[8,128,384]{2,1,0:T(8,128)(2,1)} async-done(((bf16[8,128,384]{2,1,0:T(8,128)(2,1)}), bf16[8,128,384]{2,1,0:T(8,128)(2,1)}, u32[]{:S(2)}, u32[]{:S(2)}) %all-to-all-start.2) | async-done | bytes 786464 | tf_op jit(solution)/shard_map/all_to_all | solution.py:321
  247.3 20.3 %all_to_all.51 = bf16[8,512,128]{1,2,0:T(8,128)(2,1)} all-to-all(bf16[8,512,128]{1,2,0:T(8,128)(2,1)} %copy.24), channel_id=1, replica_groups=mesh['dp'=16,'seq'=8] {'seq'}, dimensions={0} | all-to-all | bytes 2097152 | tf_op jit(solution)/shard_map/all_to_all | solution.py:286
  267.6 4.5 %all-to-all-start.1 = ((bf16[8,512,384]{2,1,0:T(8,128)(2,1)}), bf16[8,512,384]{2,1,0:T(8,128)(2,1)}, u32[]{:S(2)}, u32[]{:S(2)}) async-start(bf16[8,512,384]{2,1,0:T(8,128)(2,1)} %bitcast.43), calls=%async_computation.1 | async-start | bytes 6291456 | tf_op jit(solution)/shard_map/all_to_all | solution.py:299
  272.1 1.1 slice.24
  274.0 1.7 copy.28
  275.7 1.0 copy.34
  276.7 2.3 fusion.13
  279.0 31.6 %all-to-all-done.1 = bf16[8,512,384]{2,1,0:T(8,128)(2,1)} async-done(((bf16[8,512,384]{2,1,0:T(8,128)(2,1)}), bf16[8,512,384]{2,1,0:T(8,128)(2,1)}, u32[]{:S(2)}, u32[]{:S(2)}) %all-to-all-start.1) | async-done | bytes 3145760 | tf_op jit(solution)/shard_map/all_to_all | solution.py:299
  310.5 5.4 %copy.33 = bf16[8,512,384]{2,0,1:T(8,128)(2,1)} copy(bf16[8,512,384]{2,1,0:T(8,128)(2,1)} %all-to-all-done.1) | data formatting | bytes 6291456 | tf_op jit(solution)/shard_map/all_to_all | solution.py:299
  315.9 5.0 %copy.27 = bf16[512,3,8,128]{0,3,2,1:T(8,128)(2,1)} copy(bf16[512,3,8,128]{3,2,1,0:T(8,128)(2,1)} %bitcast.44) | data formatting | bytes 6291456 | tf_op jit(solution)/shard_map/transpose | solution.py:185
  320.9 7.2 %multiply_reduce_fusion = (f32[512]{0:T(512)S(1)}, f32[512]{0:T(512)S(1)}, f32[512,1024]{1,0:T(8,128)S(1)}) fusion(f32[1024]{0:T(1024)S(1)} %copy-done.16, f32[512]{0:T(512)S(1)} %add_rsqrt_fusion, f32[512]{0:T(512)S(1)} %broadcast_multiply_fusion.2, bf16[512,1024]{1,0:T(8,128)(2,1)S(1)} %copy-done.12, bf16[512,3072]{0,1:T(8,128)(2,1)} %bitcast.46, ...), kind=kOutput, calls=%fused_computation.21 | convolution fusion | flops 3224894464 | bytes 12595200 | tf_op jit(solution)/shard_map/dot_general | solution.py:303
  328.1 1.8 fusion.11
  (48 shorter events, 4.4 us)
Async XLA Ops:
  7.2 116.4 %copy-start = (bf16[1024,1024]{1,0:T(8,128)(2,1)S(1)}, bf16[1024,1024]{1,0:T(8,128)(2,1)}, u32[]{:S(2)}) copy-start(bf16[1024,1024]{1,0:T(8,128)(2,1)} %param.10) | copy-start | bytes 6291460
  7.2 3.3 copy-start.11
  7.2 3.3 copy-start.16
  7.2 57.3 %all-gather.3.cloned.1.call-start = ((), (), s32[]{:S(2)}) async-start(), calls=%async_computation.3 | async-start | bytes 9437184 | tf_op jit(solution)/shard_map/all_gather | solution.py:268
  10.5 2.1 copy-start.17
  11.9 104.3 %all-gather.5.cloned.1.call-start = ((), (), s32[]{:S(2)}) async-start(), calls=%async_computation.4 | async-start | bytes 9437184 | tf_op jit(solution)/shard_map/all_gather | solution.py:269
  72.7 0.7 copy-start.9
  102.1 1.0 copy-start.3
  103.1 1.0 copy-start.4
  104.0 1.0 copy-start.6
  105.0 16.7 %copy-start.1 = (bf16[4096,128]{1,0:T(8,128)(2,1)}, bf16[4096,128]{1,0:T(8,128)(2,1)S(1)}, u32[]{:S(2)}) copy-start(bf16[4096,128]{1,0:T(8,128)(2,1)S(1)} %get-tuple-element.9.o_ref) | copy-start | bytes 3145732
  123.6 6.9 %copy-start.5 = (bf16[4096,128]{1,0:T(8,128)(2,1)S(1)}, bf16[4096,128]{1,0:T(8,128)(2,1)}, u32[]{:S(2)}) copy-start(bf16[4096,128]{1,0:T(8,128)(2,1)} %copy-done.4) | copy-start | bytes 3145732
  123.6 6.9 %copy-start.7 = (bf16[4096,128]{1,0:T(8,128)(2,1)S(1)}, bf16[4096,128]{1,0:T(8,128)(2,1)}, u32[]{:S(2)}) copy-start(bf16[4096,128]{1,0:T(8,128)(2,1)} %copy-done.6) | copy-start | bytes 3145732
  169.0 8.3 %copy-start.10 = (bf16[4096,384]{1,0:T(8,128)(2,1)}, bf16[4096,384]{1,0:T(8,128)(2,1)S(1)}, u32[]{:S(2)}) copy-start(bf16[4096,384]{1,0:T(8,128)(2,1)S(1)} %constant_dynamic-update-slice_fusion) | copy-start | bytes 9437188
  169.0 8.3 %copy-start.14 = (f32[16,64,128]{2,1,0:T(8,128)S(1)}, f32[16,64,128]{2,1,0:T(8,128)}, u32[]{:S(2)}) copy-start(f32[16,64,128]{2,1,0:T(8,128)} %concatenate.17) | copy-start | bytes 1572868
  228.0 1.0 copy-start.8
  228.0 6.2 %copy-start.2 = (bf16[4096,128]{1,0:T(8,128)(2,1)S(1)}, bf16[4096,128]{1,0:T(8,128)(2,1)}, u32[]{:S(2)}) copy-start(bf16[4096,128]{1,0:T(8,128)(2,1)} %copy-done.1) | copy-start | bytes 3145732
  229.9 17.4 %all-to-all-start.2 = ((bf16[8,128,384]{2,1,0:T(8,128)(2,1)}), bf16[8,128,384]{2,1,0:T(8,128)(2,1)}, u32[]{:S(2)}, u32[]{:S(2)}) async-start(bf16[8,128,384]{2,1,0:T(8,128)(2,1)} %bitcast.47), calls=%async_computation.2 | async-start | bytes 1572864 | tf_op jit(solution)/shard_map/all_to_all | solution.py:321
  267.6 42.9 %all-to-all-start.1 = ((bf16[8,512,384]{2,1,0:T(8,128)(2,1)}), bf16[8,512,384]{2,1,0:T(8,128)(2,1)}, u32[]{:S(2)}, u32[]{:S(2)}) async-start(bf16[8,512,384]{2,1,0:T(8,128)(2,1)} %bitcast.43), calls=%async_computation.1 | async-start | bytes 6291456 | tf_op jit(solution)/shard_map/all_to_all | solution.py:299
  272.1 4.6 %copy-start.12 = (bf16[512,1024]{1,0:T(8,128)(2,1)S(1)}, bf16[512,1024]{1,0:T(8,128)(2,1)}, u32[]{:S(2)}) copy-start(bf16[512,1024]{1,0:T(8,128)(2,1)} %param.7) | copy-start | bytes 3145732
  274.0 2.7 copy-start.15
  320.9 7.2 %copy-start.13 = (bf16[512,1024]{1,0:T(8,128)(2,1)S(1)}, bf16[512,1024]{1,0:T(8,128)(2,1)}, u32[]{:S(2)}) copy-start(bf16[512,1024]{1,0:T(8,128)(2,1)} %param.13) | copy-start | bytes 3145732
Sparse Core Ops, SparseCore 0:
  12.0 52.3 all-gather.2
  66.2 49.9 all-gather.4

commit v7 on v6

--- a/solution.py
+++ b/solution.py
@@ -190,73 +190,91 @@
 MESH = pl.DeviceIdType.MESH
 
 
-def dp_sum_kernel(n, x_ref, o_ref, recv, gath, send1, recv1, send2, recv2):
+def exchange_kernel(n, m, x_ref, g_ref, o_ref, moved_ref, recv, gath, landed, sems):
     me = lax.axis_index("dp")
+    here = lax.axis_index("seq")
     barrier = pltpu.get_barrier_semaphore()
     for k in range(1, n):
         pl.semaphore_signal(
             barrier, inc=1, device_id={"dp": lax.rem(me + k, n)}, device_id_type=MESH
         )
-    pl.semaphore_wait(barrier, n - 1)
-
-    def exchange(src_of, dst, send, arrive):
+    for k in range(1, m):
+        pl.semaphore_signal(
+            barrier, inc=1, device_id={"seq": lax.rem(here + k, m)}, device_id_type=MESH
+        )
+    pl.semaphore_wait(barrier, n - 1 + m - 1)
+
+    def start_all(src_of, dst, send, arrive, axis, at, size):
         started = []
-        for k in range(1, n):
-            peer = lax.rem(me + k, n)
+        for k in range(1, size):
+            peer = lax.rem(at + k, size)
             copy = pltpu.make_async_remote_copy(
                 src_ref=src_of(peer),
-                dst_ref=dst.at[me],
+                dst_ref=dst.at[at],
                 send_sem=send.at[peer],
-                recv_sem=arrive.at[me],
-                device_id={"dp": peer},
+                recv_sem=arrive.at[at],
+                device_id={axis: peer},
                 device_id_type=MESH,
             )
             copy.start()
             started.append(copy)
-        for k in range(1, n):
-            source = lax.rem(me + n - k, n)
+        return started
+
+    def finish_all(started, src_of, dst, send, arrive, axis, at, size):
+        for k in range(1, size):
+            source = lax.rem(at + size - k, size)
             pltpu.make_async_remote_copy(
                 src_ref=src_of(source),
                 dst_ref=dst.at[source],
                 send_sem=send.at[source],
                 recv_sem=arrive.at[source],
-                device_id={"dp": source},
+                device_id={axis: source},
                 device_id_type=MESH,
             ).wait_recv()
         for copy in started:
             copy.wait_send()
 
-    exchange(lambda peer: x_ref.at[peer], recv, send1, recv1)
+    a2a = (lambda peer: g_ref.at[peer], landed, sems.at[4], sems.at[5], "seq", here, m)
+    a2a_started = start_all(*a2a)
+    rs = (lambda peer: x_ref.at[peer], recv, sems.at[0], sems.at[1], "dp", me, n)
+    finish_all(start_all(*rs), *rs)
     total = x_ref[me]
     for k in range(1, n):
         total = total + recv[lax.rem(me + k, n)]
     gath[me] = total.astype(gath.dtype)
-    exchange(lambda peer: gath.at[me], gath, send2, recv2)
+    ag = (lambda peer: gath.at[me], gath, sems.at[2], sems.at[3], "dp", me, n)
+    finish_all(start_all(*ag), *ag)
     o_ref[...] = gath[...]
-
-
-def sum_over_dp(term):
+    landed[here] = g_ref[here]
+    finish_all(a2a_started, *a2a)
+    moved_ref[...] = landed[...]
+
+
+def sum_and_exchange(term, grads):
     n = lax.axis_size("dp")
+    m = lax.axis_size("seq")
     rows, cols = term.shape
     chunked = term.reshape(n, rows // n, cols)
-    out = pl.pallas_call(
-        functools.partial(dp_sum_kernel, n),
-        out_shape=jax.ShapeDtypeStruct(chunked.shape, jnp.bfloat16),
-        in_specs=[vmem_spec()],
-        out_specs=vmem_spec(),
+    pieces = grads.reshape(m, grads.shape[0] // m, grads.shape[1])
+    out, moved = pl.pallas_call(
+        functools.partial(exchange_kernel, n, m),
+        out_shape=(
+            jax.ShapeDtypeStruct(chunked.shape, jnp.bfloat16),
+            jax.ShapeDtypeStruct(pieces.shape, pieces.dtype),
+        ),
+        in_specs=[vmem_spec(), vmem_spec()],
+        out_specs=(vmem_spec(), vmem_spec()),
         scratch_shapes=[
             pltpu.VMEM(chunked.shape, jnp.float32),
             pltpu.VMEM(chunked.shape, jnp.bfloat16),
-            pltpu.SemaphoreType.DMA((n,)),
-            pltpu.SemaphoreType.DMA((n,)),
-            pltpu.SemaphoreType.DMA((n,)),
-            pltpu.SemaphoreType.DMA((n,)),
+            pltpu.VMEM(pieces.shape, pieces.dtype),
+            pltpu.SemaphoreType.DMA((6, max(n, m))),
         ],
         compiler_params=pltpu.CompilerParams(
             collective_id=0, has_side_effects=True, vmem_limit_bytes=VMEM_LIMIT
         ),
-    )(chunked)
-    return out.reshape(rows, cols)
+    )(chunked, pieces)
+    return out.reshape(rows, cols), jnp.concatenate(list(moved), axis=1)
 
 
 def body(feats, gain, w_qkv, w_out, block_cols, block_counts, cotan):
@@ -295,11 +313,14 @@
         query_heads, key_heads, value_heads, attended_heads, grad_heads, lse, cols, counts
     )
     grad_heads_mixed = jnp.concatenate([query_grad, key_grad, value_grad], axis=1)
-    grad_mixed = regroup_columns(
-        lax.all_to_all(grad_heads_mixed, "seq", split_axis=0, concat_axis=1, tiled=True),
-        seq_count,
-        group_width,
-    )
+    term_qkv = contract_rows(normed_all, grad_heads_mixed)
+    term_out = contract_rows(attended_heads, cotan_all)
+    qkv_cols = term_qkv.shape[1]
+    summed, moved_grads = sum_and_exchange(
+        jnp.concatenate([term_qkv, term_out.reshape(term_qkv.shape[0], -1)], axis=1),
+        grad_heads_mixed,
+    )
+    grad_mixed = regroup_columns(moved_grads, seq_count, group_width)
     grad_normed = lax.dot_general(
         grad_mixed, w_qkv, (((1,), (1,)), ((), ())), preferred_element_type=jnp.float32
     )
@@ -309,12 +330,6 @@
     grad_feats = (
         cotan.astype(jnp.float32) + inverse * (gained - mean_one - scaled * mean_two)
     ).astype(jnp.bfloat16)
-    term_qkv = contract_rows(normed_all, grad_heads_mixed)
-    term_out = contract_rows(attended_heads, cotan_all)
-    qkv_cols = term_qkv.shape[1]
-    summed = sum_over_dp(
-        jnp.concatenate([term_qkv, term_out.reshape(term_qkv.shape[0], -1)], axis=1)
-    )
     term_qkv = summed[:, :qkv_cols]
     term_out = summed[:, qkv_cols:].reshape(term_out.shape)
     grad_qkv = regroup_columns(

time: 338 us -> 298 us (0.88)
  waiting for transfers between devices: 106 us -> 62.2 us
  blocking collectives: 20.3 us -> 0 us
  local copies, waits for them, and re-layouts: 25.8 us -> 37.9 us
  Pallas kernels: 117 us -> 121 us
  other arithmetic: 6.63 us -> 10.1 us
    all_to_all x1, waiting for transfers between devices: 31.6 us -> 0.01 us  [body(): lax.all_to_all(attended_heads, 'seq', split_axis=0, concat_axis=1, tiled=...]
    all_to_all x1 -> x0, blocking collectives: 20.3 us -> none  [body(): lax.all_to_all(attended_heads, 'seq', split_axis=0, concat_axis=1, tiled=...]
    another operation x0 -> x9, local copies, waits for them, and re-layouts: none -> 18.2 us  [sum_and_exchange(): return (out.reshape(rows, cols), jnp.concatenate(list(moved), axis=1))]
    all_to_all x1, waiting for transfers between devices: 11.8 us -> 0.01 us  [body(): lax.all_to_all(term_qkv, 'seq', split_axis=0, concat_axis=1, tiled=True)]
    all_to_all x1 -> x0, local copies, waits for them, and re-layouts: 5.41 us -> none  [body(): lax.all_to_all(grad_heads_mixed, 'seq', split_axis=0, concat_axis=1, tile...]
    pallas_call x1, Pallas kernels: 50.5 us -> 54.5 us  [sum_and_exchange(): pl.pallas_call(functools.partial(exchange_kernel, n, m), out_shape=(jax.S...]
    unnamed x40 -> x43, local copies, waits for them, and re-layouts: 5.59 us -> 8.97 us
  transfers between devices with their start and end apart: 4 -> 4, of which waited for: 4 -> 2; matrix products, arithmetic and copies ran while one was open for 5% -> 16% of each run, Pallas kernels for 9% -> 10%
where the time goes in v7:
time: 298 us; the launch traced here: 296 us
  Pallas kernels  121 us (41%)
  waiting for transfers between devices  62.2 us (21%)
  matrix products  41.4 us (14%)
  local copies, waits for them, and re-layouts  37.9 us (13%)
  between operations  14.3 us (5%)
  other arithmetic  10.1 us (3%)
  starting transfers between devices  8.99 us (3%)
    pallas_call x1, Pallas kernels, sum_and_exchange(): pl.pallas_call(functools.partial(exchange_kernel, n, m), out_shape=(jax.S...  54.5 us
    all_gather x1, waiting for transfers between devices, body(): normed_all = lax.all_gather(normed, 'seq', axis=0, tiled=True)  50.4 us
    pallas_call x1, Pallas kernels, attention_backward(): pl.pallas_call(attn_bwd_kernel, out_shape=tuple((jax.ShapeDtypeStruct((n,...  37.8 us
    pallas_call x1, Pallas kernels, attention_forward(): pl.pallas_call(attn_fwd_kernel, out_shape=(jax.ShapeDtypeStruct((n, width...  28.7 us
    another operation x9, local copies, waits for them, and re-layouts, sum_and_exchange(): return (out.reshape(rows, cols), jnp.concatenate(list(moved), axis=1))  18.2 us
    dot_general x2, matrix products, contract_rows(): lax.dot_general(left_cols, right_cols, (((0,), (0,)), ((), ())), preferre...  13.8 us
    all_gather x1, waiting for transfers between devices, body(): cotan_all = lax.all_gather(cotan, 'seq', axis=0, tiled=True)  11.1 us
    dot_general x1, matrix products, body(): lax.dot_general(grad_mixed, w_qkv, (((1,), (1,)), ((), ())), preferred_el...  9.04 us
  transfers between devices with their start and end apart: 4, of which 2 were waited for; matrix products, arithmetic and copies ran while one was open for 16% of the time, Pallas kernels for 10%

profile of v7, /device:TPU:0, one launch (start us, length us, event | category | flops | bytes accessed | tf_op | source)
XLA Modules:
  0.0 295.9 jit_solution(4892782761635687976)
XLA Ops:
  7.2 1.6 convert_reduce_fusion
  8.8 1.6 fusion.12
  10.5 2.6 fusion.6
  14.0 1.2 constant_dynamic-slice_fusion.2
  15.2 50.4 %all-gather.3.cloned.1.call-done = bf16[4096,1024]{1,0:T(8,128)(2,1)} async-done(((bf16[512,1024]{1,0:T(8,128)(2,1)}), bf16[4096,1024]{1,0:T(8,128)(2,1)}) %all-gather.3.cloned.1.call-update) | async-done | bytes 8388624 | tf_op jit(solution)/shard_map/all_gather | solution.py:286
  65.6 8.3 %convolution_convert_fusion = bf16[4096,384]{1,0:T(8,128)(2,1)S(1)} fusion(bf16[4096,1024]{1,0:T(8,128)(2,1)} %all-gather.3.cloned.1.call-done, bf16[1024,128]{1,0:T(8,128)(2,1)S(1)} %get-tuple-element.22, bf16[1024,128]{1,0:T(8,128)(2,1)S(1)} %get-tuple-element.21, bf16[1024,128]{1,0:T(8,128)(2,1)S(1)} %get-tuple-element.20), kind=kOutput, calls=%fused_computation | convolution fusion | flops 3225157632 | bytes 12320768 | tf_op jit(solution)/shard_map/dot_general | solution.py:295
  74.6 28.7 %shard_map.102 = (bf16[4096,128]{1,0:T(8,128)(2,1)S(1)}, f32[8192,128]{1,0:T(8,128)}) custom-call(s32[256]{0:T(256)S(1)} %reshape_squeeze.3.cols_ref, s32[32]{0:T(128)S(1)} %bitcast.43, bf16[4096,128]{1,0:T(8,128)(2,1)S(1)} %get-tuple-element.33.q_ref, bf16[4096,128]{1,0:T(8,128)(2,1)S(1)} %get-tuple-element.32.k_ref, ...), custom_call_target="tpu_custom_call" | custom-call | tf_op jit(solution)/shard_map/pallas_call | solution.py:157
  106.3 11.1 %all-gather.5.cloned.1.call-done = bf16[4096,1024]{1,0:T(8,128)(2,1)} async-done(((bf16[512,1024]{1,0:T(8,128)(2,1)}), bf16[4096,1024]{1,0:T(8,128)(2,1)}) %all-gather.5.cloned.1.call-update) | async-done | bytes 8388624 | tf_op jit(solution)/shard_map/all_gather | solution.py:287
  117.3 5.5 %fusion.25 = f32[128,1024]{1,0:T(8,128)} fusion(bf16[4096,128]{1,0:T(8,128)(2,1)S(1)} %get-tuple-element.11.o_ref, bf16[4096,1024]{1,0:T(8,128)(2,1)} %all-gather.5.cloned.1.call-done), kind=kOutput, calls=%fused_computation.51 | convolution fusion | flops 1073741824 | bytes 9961472 | tf_op jit(solution)/shard_map/dot_general | solution.py:28
  122.8 2.0 concatenate.37
  124.8 1.3 copy.25
  126.1 6.9 %fusion.do_ref = bf16[4096,128]{1,0:T(8,128)(2,1)} fusion(bf16[4096,1024]{1,0:T(8,128)(2,1)} %all-gather.5.cloned.1.call-done, bf16[1024,1024]{1,0:T(8,128)(2,1)S(1)} %copy-done, s32[]{:T(128)S(6)} %select_n.15), kind=kOutput, calls=%fused_computation.2 | convolution fusion | flops 1074266112 | bytes 9699332 | tf_op jit(solution)/shard_map/dot_general | solution.py:309
  133.0 37.8 %shard_map.103 = (bf16[4096,128]{1,0:T(8,128)(2,1)S(1)}, bf16[4096,128]{1,0:T(8,128)(2,1)S(1)}, bf16[4096,128]{1,0:T(8,128)(2,1)S(1)}) custom-call(s32[256]{0:T(256)S(1)} %reshape_squeeze.3.cols_ref, s32[32]{0:T(128)S(1)} %bitcast.44, bf16[4096,128]{1,0:T(8,128)(2,1)S(1)} %copy-done.6, bf16[4096,128]{1,0:T(8,128)(2,1)S(1)} %copy-done.4, ...), custom_call_target="tpu_custom_call" | custom-call | tf_op jit(solution)/shard_map/pallas_call | solution.py:171
  171.5 8.3 %fusion.24 = f32[1024,384]{1,0:T(8,128)S(1)} fusion(bf16[4096,1024]{1,0:T(8,128)(2,1)} %all-gather.3.cloned.1.call-done, bf16[4096,384]{1,0:T(8,128)(2,1)S(1)} %constant_dynamic-update-slice_fusion), kind=kOutput, calls=%fused_computation.50 | convolution fusion | flops 3221225472 | bytes 13107200 | tf_op jit(solution)/shard_map/dot_general | solution.py:28
  180.0 54.5 %shard_map.104 = (bf16[16,64,512]{2,1,0:T(8,128)(2,1)S(1)}, bf16[8,512,384]{2,1,0:T(8,128)(2,1)}) custom-call(f32[16,64,512]{2,1,0:T(8,128)S(1)} %pad_maximum_fusion.x_ref, bf16[8,512,384]{2,1,0:T(8,128)(2,1)} %bitcast.45), custom_call_target="tpu_custom_call" | custom-call | tf_op jit(solution)/shard_map/pallas_call | solution.py:259
  234.6 3.5 %fusion.22 = (bf16[1,512,384]{2,1,0:T(8,128)(2,1)}, bf16[1,512,384]{2,1,0:T(8,128)(2,1)}, bf16[1,512,384]{2,1,0:T(8,128)(2,1)}, bf16[1,512,384]{2,1,0:T(8,128)(2...) fusion(bf16[8,512,384]{2,1,0:T(8,128)(2,1)} %get-tuple-element.16), kind=kLoop, calls=%fused_computation.48 | loop fusion | bytes 6291456 | tf_op jit(solution)/shard_map/unstack | solution.py:277
  238.1 1.2 copy.34
  240.2 4.2 %all-to-all-start.1 = ((bf16[8,128,384]{2,1,0:T(8,128)(2,1)}), bf16[8,128,384]{2,1,0:T(8,128)(2,1)}, u32[]{:S(2)}, u32[]{:S(2)}) async-start(bf16[8,128,384]{2,1,0:T(8,128)(2,1)} %bitcast.49), calls=%async_computation.1 | async-start | bytes 1572864 | tf_op jit(solution)/shard_map/all_to_all | solution.py:336
  244.4 1.9 copy.33
  246.4 1.9 copy.32
  248.3 1.9 copy.31
  250.2 1.9 copy.30
  252.1 1.9 copy.29
  254.1 1.9 copy.28
  256.0 1.9 copy.27
  257.9 1.1 constant_dynamic-update-slice_fusion.10
  262.3 1.9 copy.35
  264.3 4.7 %all-to-all-start = ((bf16[8,512,128]{1,2,0:T(8,128)(2,1)}), bf16[8,512,128]{1,2,0:T(8,128)(2,1)}, u32[]{:S(2)}, u32[]{:S(2)}) async-start(bf16[8,512,128]{1,2,0:T(8,128)(2,1)} %copy.25), calls=%async_computation | async-start | bytes 2097152 | tf_op jit(solution)/shard_map/all_to_all | solution.py:304
  269.0 9.0 %multiply_reduce_fusion = (f32[512]{0:T(512)S(1)}, f32[512]{0:T(512)S(1)}, f32[512,1024]{1,0:T(8,128)}) fusion(f32[1024]{0:T(1024)S(1)} %copy-done.14, f32[512]{0:T(512)S(1)} %add_rsqrt_fusion, f32[512]{0:T(512)S(1)} %broadcast_multiply_fusion.2, bf16[512,1024]{1,0:T(8,128)(2,1)} %param.7, bf16[512,3072]{0,1:T(8,128)(2,1)} %bitcast.48, ...), kind=kOutput, calls=%fused_computation.20 | convolution fusion | flops 3224894464 | bytes 12595200 | tf_op jit(solution)/shard_map/dot_general | solution.py:324
  278.9 4.1 %fusion.11 = bf16[512,1024]{1,0:T(8,128)(2,1)} fusion(bf16[512,1024]{1,0:T(8,128)(2,1)} %param.7, bf16[512,1024]{1,0:T(8,128)(2,1)} %param.13, f32[512,1024]{1,0:T(8,128)} %get-tuple-element.34, f32[512]{0:T(512)S(1)} %get-tuple-element.35, f32[512]{0:T(512)S(1)} %get-tuple-element.36, f32[1024]{0:T(1024)S(1)} %copy-done.14, f32[512]{0:T(512)S(1)} %add_rsqrt_fusion, ...), kind=kLoop, calls=%fused_computation.16 | loop fusion | flops 5767168 | bytes 5255168 | tf_op jit(solution)/shard_map/convert_element_type | solution.py:332
  283.0 1.6 copy.36
  285.6 3.5 %fusion.13 = bf16[512,1024]{1,0:T(8,128)(2,1)} fusion(bf16[512,1024]{1,0:T(8,128)(2,1)S(1)} %copy-done.9, bf16[512,1024]{0,1:T(8,128)(2,1)} %bitcast.3, bf16[1024,1024]{1,0:T(8,128)(2,1)S(1)} %copy-done), kind=kOutput, calls=%fused_computation.18 | convolution fusion | flops 1075314688 | bytes 5242880 | tf_op jit(solution)/shard_map/dot_general | solution.py:306
  (59 shorter events, 11.6 us)
Async XLA Ops:
  7.2 119.0 %copy-start = (bf16[1024,1024]{1,0:T(8,128)(2,1)S(1)}, bf16[1024,1024]{1,0:T(8,128)(2,1)}, u32[]{:S(2)}) copy-start(bf16[1024,1024]{1,0:T(8,128)(2,1)} %param.10) | copy-start | bytes 6291460
  7.2 6.7 %copy-start.15 = (s32[1,32,8]{1,2,0:T(8,128)S(1)}, s32[1,32,8]{1,2,0:T(8,128)}, u32[]{:S(2)}) copy-start(s32[1,32,8]{1,2,0:T(8,128)} %param.11) | copy-start | bytes 3076
  7.2 58.4 %all-gather.3.cloned.1.call-start = ((), (), s32[]{:S(2)}) async-start(), calls=%async_computation.2 | async-start | bytes 9437184 | tf_op jit(solution)/shard_map/all_gather | solution.py:286
  13.1 104.3 %all-gather.5.cloned.1.call-start = ((), (), s32[]{:S(2)}) async-start(), calls=%async_computation.3 | async-start | bytes 9437184 | tf_op jit(solution)/shard_map/all_gather | solution.py:287
  73.9 0.7 copy-start.7
  103.2 1.0 copy-start.2
  104.2 1.0 copy-start.3
  105.3 1.0 copy-start.5
  106.3 18.6 %copy-start.1 = (bf16[4096,128]{1,0:T(8,128)(2,1)}, bf16[4096,128]{1,0:T(8,128)(2,1)S(1)}, u32[]{:S(2)}) copy-start(bf16[4096,128]{1,0:T(8,128)(2,1)S(1)} %get-tuple-element.11.o_ref) | copy-start | bytes 3145732
  126.1 6.9 %copy-start.4 = (bf16[4096,128]{1,0:T(8,128)(2,1)S(1)}, bf16[4096,128]{1,0:T(8,128)(2,1)}, u32[]{:S(2)}) copy-start(bf16[4096,128]{1,0:T(8,128)(2,1)} %copy-done.3) | copy-start | bytes 3145732
  126.1 6.9 %copy-start.6 = (bf16[4096,128]{1,0:T(8,128)(2,1)S(1)}, bf16[4096,128]{1,0:T(8,128)(2,1)}, u32[]{:S(2)}) copy-start(bf16[4096,128]{1,0:T(8,128)(2,1)} %copy-done.5) | copy-start | bytes 3145732
  171.5 8.3 %copy-start.8 = (bf16[4096,384]{1,0:T(8,128)(2,1)}, bf16[4096,384]{1,0:T(8,128)(2,1)S(1)}, u32[]{:S(2)}) copy-start(bf16[4096,384]{1,0:T(8,128)(2,1)S(1)} %constant_dynamic-update-slice_fusion) | copy-start | bytes 9437188
  171.5 8.3 %copy-start.10 = (f32[16,64,128]{2,1,0:T(8,128)S(1)}, f32[16,64,128]{2,1,0:T(8,128)}, u32[]{:S(2)}) copy-start(f32[16,64,128]{2,1,0:T(8,128)} %concatenate.37) | copy-start | bytes 1572868
  240.2 24.0 %all-to-all-start.1 = ((bf16[8,128,384]{2,1,0:T(8,128)(2,1)}), bf16[8,128,384]{2,1,0:T(8,128)(2,1)}, u32[]{:S(2)}, u32[]{:S(2)}) async-start(bf16[8,128,384]{2,1,0:T(8,128)(2,1)} %bitcast.49), calls=%async_computation.1 | async-start | bytes 1572864 | tf_op jit(solution)/shard_map/all_to_all | solution.py:336
  257.9 4.2 %copy-start.13 = (bf16[1,512,384]{1,2,0:T(8,128)(2,1)S(1)}, bf16[1,512,384]{1,2,0:T(8,128)(2,1)}, u32[]{:S(2)}) copy-start(bf16[1,512,384]{1,2,0:T(8,128)(2,1)} %copy.31) | copy-start | bytes 1179652
  257.9 4.3 %copy-start.12 = (bf16[1,512,384]{1,2,0:T(8,128)(2,1)S(1)}, bf16[1,512,384]{1,2,0:T(8,128)(2,1)}, u32[]{:S(2)}) copy-start(bf16[1,512,384]{1,2,0:T(8,128)(2,1)} %copy.32) | copy-start | bytes 1179652
  257.9 4.3 %copy-start.11 = (bf16[1,512,384]{1,2,0:T(8,128)(2,1)S(1)}, bf16[1,512,384]{1,2,0:T(8,128)(2,1)}, u32[]{:S(2)}) copy-start(bf16[1,512,384]{1,2,0:T(8,128)(2,1)} %copy.33) | copy-start | bytes 1179652
  262.3 6.7 %copy-start.14 = (f32[1024]{0:T(1024)S(1)}, f32[1024]{0:T(1024)}, u32[]{:S(2)}) copy-start(f32[1024]{0:T(1024)} %param.8) | copy-start | bytes 12292
  264.3 21.3 %all-to-all-start = ((bf16[8,512,128]{1,2,0:T(8,128)(2,1)}), bf16[8,512,128]{1,2,0:T(8,128)(2,1)}, u32[]{:S(2)}, u32[]{:S(2)}) async-start(bf16[8,512,128]{1,2,0:T(8,128)(2,1)} %copy.25), calls=%async_computation | async-start | bytes 2097152 | tf_op jit(solution)/shard_map/all_to_all | solution.py:304
  278.9 6.7 %copy-start.9 = (bf16[512,1024]{1,0:T(8,128)(2,1)S(1)}, bf16[512,1024]{1,0:T(8,128)(2,1)}, u32[]{:S(2)}) copy-start(bf16[512,1024]{1,0:T(8,128)(2,1)} %param.7) | copy-start | bytes 3145732
Sparse Core Ops, SparseCore 0:
  13.2 52.3 all-gather.2
  67.3 49.9 all-gather.4

commit v8 on v7

--- a/solution.py
+++ b/solution.py
@@ -190,7 +190,9 @@
 MESH = pl.DeviceIdType.MESH
 
 
-def exchange_kernel(n, m, x_ref, g_ref, o_ref, moved_ref, recv, gath, landed, sems):
+def exchange_kernel(
+    n, m, x_ref, g_ref, a_ref, o_ref, moved_ref, att_ref, recv, gath, landed, att_landed, sems, a2a_sems
+):
     me = lax.axis_index("dp")
     here = lax.axis_index("seq")
     barrier = pltpu.get_barrier_semaphore()
@@ -234,8 +236,43 @@
         for copy in started:
             copy.wait_send()
 
-    a2a = (lambda peer: g_ref.at[peer], landed, sems.at[4], sems.at[5], "seq", here, m)
-    a2a_started = start_all(*a2a)
+    parts = g_ref.shape[2] // BLK
+    group = BLK * m
+
+    def part_copy(t, peer, sender, target):
+        return pltpu.make_async_remote_copy(
+            src_ref=g_ref.at[peer, :, pl.ds(t * BLK, BLK)],
+            dst_ref=landed.at[:, pl.ds(pl.multiple_of(t * group + sender * BLK, BLK), BLK)],
+            send_sem=a2a_sems.at[0, t, peer],
+            recv_sem=a2a_sems.at[1, t, sender],
+            device_id={"seq": target},
+            device_id_type=MESH,
+        )
+
+    width = a_ref.shape[2]
+
+    def att_copy(peer, sender, target):
+        return pltpu.make_async_remote_copy(
+            src_ref=a_ref.at[peer],
+            dst_ref=att_landed.at[:, pl.ds(pl.multiple_of(sender * width, width), width)],
+            send_sem=a2a_sems.at[0, parts, peer],
+            recv_sem=a2a_sems.at[1, parts, sender],
+            device_id={"seq": target},
+            device_id_type=MESH,
+        )
+
+    a2a_started = []
+    for k in range(1, m):
+        peer = lax.rem(here + k, m)
+        copy = att_copy(peer, here, peer)
+        copy.start()
+        a2a_started.append(copy)
+    for k in range(1, m):
+        peer = lax.rem(here + k, m)
+        for t in range(parts):
+            copy = part_copy(t, peer, here, peer)
+            copy.start()
+            a2a_started.append(copy)
     rs = (lambda peer: x_ref.at[peer], recv, sems.at[0], sems.at[1], "dp", me, n)
     finish_all(start_all(*rs), *rs)
     total = x_ref[me]
@@ -245,36 +282,55 @@
     ag = (lambda peer: gath.at[me], gath, sems.at[2], sems.at[3], "dp", me, n)
     finish_all(start_all(*ag), *ag)
     o_ref[...] = gath[...]
-    landed[here] = g_ref[here]
-    finish_all(a2a_started, *a2a)
+    own = g_ref[here]
+    for t in range(parts):
+        landed[:, pl.ds(pl.multiple_of(t * group + here * BLK, BLK), BLK)] = own[
+            :, t * BLK : (t + 1) * BLK
+        ]
+    att_landed[:, pl.ds(pl.multiple_of(here * width, width), width)] = a_ref[here]
+    for k in range(1, m):
+        source = lax.rem(here + m - k, m)
+        att_copy(source, source, source).wait_recv()
+        for t in range(parts):
+            part_copy(t, source, source, source).wait_recv()
+    for copy in a2a_started:
+        copy.wait_send()
     moved_ref[...] = landed[...]
-
-
-def sum_and_exchange(term, grads):
+    att_ref[...] = att_landed[...]
+
+
+def sum_and_exchange(term, grads, attended_heads):
     n = lax.axis_size("dp")
     m = lax.axis_size("seq")
     rows, cols = term.shape
     chunked = term.reshape(n, rows // n, cols)
     pieces = grads.reshape(m, grads.shape[0] // m, grads.shape[1])
-    out, moved = pl.pallas_call(
+    att_pieces = attended_heads.reshape(m, attended_heads.shape[0] // m, attended_heads.shape[1])
+    parts = grads.shape[1] // BLK
+    final = (pieces.shape[1], parts * m * BLK)
+    att_final = (att_pieces.shape[1], m * att_pieces.shape[2])
+    out, moved, attended = pl.pallas_call(
         functools.partial(exchange_kernel, n, m),
         out_shape=(
             jax.ShapeDtypeStruct(chunked.shape, jnp.bfloat16),
-            jax.ShapeDtypeStruct(pieces.shape, pieces.dtype),
+            jax.ShapeDtypeStruct(final, pieces.dtype),
+            jax.ShapeDtypeStruct(att_final, att_pieces.dtype),
         ),
-        in_specs=[vmem_spec(), vmem_spec()],
-        out_specs=(vmem_spec(), vmem_spec()),
+        in_specs=[vmem_spec(), vmem_spec(), vmem_spec()],
+        out_specs=(vmem_spec(), vmem_spec(), vmem_spec()),
         scratch_shapes=[
             pltpu.VMEM(chunked.shape, jnp.float32),
             pltpu.VMEM(chunked.shape, jnp.bfloat16),
-            pltpu.VMEM(pieces.shape, pieces.dtype),
-            pltpu.SemaphoreType.DMA((6, max(n, m))),
+            pltpu.VMEM(final, pieces.dtype),
+            pltpu.VMEM(att_final, att_pieces.dtype),
+            pltpu.SemaphoreType.DMA((4, n)),
+            pltpu.SemaphoreType.DMA((2, parts + 1, m)),
         ],
         compiler_params=pltpu.CompilerParams(
             collective_id=0, has_side_effects=True, vmem_limit_bytes=VMEM_LIMIT
         ),
-    )(chunked, pieces)
-    return out.reshape(rows, cols), jnp.concatenate(list(moved), axis=1)
+    )(chunked, pieces, att_pieces)
+    return out.reshape(rows, cols), moved, attended
 
 
 def body(feats, gain, w_qkv, w_out, block_cols, block_counts, cotan):
@@ -301,10 +357,6 @@
     cols = block_cols[0].reshape(-1)
     counts = block_counts[0]
     attended_heads, lse = attention_forward(query_heads, key_heads, value_heads, cols, counts)
-    attended = lax.all_to_all(attended_heads, "seq", split_axis=0, concat_axis=1, tiled=True)
-    result = (
-        feats.astype(jnp.float32) + jnp.dot(attended, w_out, preferred_element_type=jnp.float32)
-    ).astype(jnp.bfloat16)
     w_out_rows = lax.dynamic_slice_in_dim(w_out, seq_at * group_width, group_width, 0)
     grad_heads = lax.dot_general(
         cotan_all, w_out_rows, (((1,), (1,)), ((), ())), preferred_element_type=jnp.float32
@@ -316,11 +368,15 @@
     term_qkv = contract_rows(normed_all, grad_heads_mixed)
     term_out = contract_rows(attended_heads, cotan_all)
     qkv_cols = term_qkv.shape[1]
-    summed, moved_grads = sum_and_exchange(
+    summed, moved_grads, attended = sum_and_exchange(
         jnp.concatenate([term_qkv, term_out.reshape(term_qkv.shape[0], -1)], axis=1),
         grad_heads_mixed,
-    )
-    grad_mixed = regroup_columns(moved_grads, seq_count, group_width)
+        attended_heads,
+    )
+    result = (
+        feats.astype(jnp.float32) + jnp.dot(attended, w_out, preferred_element_type=jnp.float32)
+    ).astype(jnp.bfloat16)
+    grad_mixed = moved_grads
     grad_normed = lax.dot_general(
         grad_mixed, w_qkv, (((1,), (1,)), ((), ())), preferred_element_type=jnp.float32
     )

time: 298 us -> 265 us (0.89)
  local copies, waits for them, and re-layouts: 37.9 us -> 13 us
  starting transfers between devices: 8.99 us -> 4.81 us
  other arithmetic: 10.1 us -> 6.63 us
    another operation x9 -> x0, local copies, waits for them, and re-layouts: 18.2 us -> none  [sum_and_exchange(): return (out.reshape(rows, cols), jnp.concatenate(list(moved), axis=1))]
    all_to_all x1 -> x0, starting transfers between devices: 4.69 us -> none  [body(): lax.all_to_all(attended_heads, 'seq', split_axis=0, concat_axis=1, tiled=...]
    unnamed x43 -> x36, local copies, waits for them, and re-layouts: 8.97 us -> 5.63 us
  transfers between devices with their start and end apart: 4 -> 3, of which waited for: 2 -> 3; matrix products, arithmetic and copies ran while one was open for 16% -> 8% of each run, Pallas kernels for 10% -> 11%
where the time goes in v8:
time: 265 us; the launch traced here: 263 us
  Pallas kernels  122 us (46%)
  waiting for transfers between devices  63.7 us (24%)
  matrix products  38.9 us (15%)
  between operations  14.3 us (5%)
  local copies, waits for them, and re-layouts  13 us (5%)
  other arithmetic  6.63 us (3%)
  starting transfers between devices  4.81 us (2%)
    pallas_call x1, Pallas kernels, sum_and_exchange(): pl.pallas_call(functools.partial(exchange_kernel, n, m), out_shape=(jax.S...  55.7 us
    all_gather x1, waiting for transfers between devices, body(): normed_all = lax.all_gather(normed, 'seq', axis=0, tiled=True)  50.4 us
    pallas_call x1, Pallas kernels, attention_backward(): pl.pallas_call(attn_bwd_kernel, out_shape=tuple((jax.ShapeDtypeStruct((n,...  37.8 us
    pallas_call x1, Pallas kernels, attention_forward(): pl.pallas_call(attn_fwd_kernel, out_shape=(jax.ShapeDtypeStruct((n, width...  28.7 us
    dot_general x2, matrix products, contract_rows(): lax.dot_general(left_cols, right_cols, (((0,), (0,)), ((), ())), preferre...  13.8 us
    all_gather x1, waiting for transfers between devices, body(): cotan_all = lax.all_gather(cotan, 'seq', axis=0, tiled=True)  11.1 us
    dot_general x1, matrix products, body(): jnp.dot(normed_all, w_heads, preferred_element_type=jnp.float32)  8.27 us
    dot_general x1, matrix products, body(): lax.dot_general(grad_mixed, w_qkv, (((1,), (1,)), ((), ())), preferred_el...  7.75 us
  transfers between devices with their start and end apart: 3, of which 3 were waited for; matrix products, arithmetic and copies ran while one was open for 8% of the time, Pallas kernels for 11%

profile of v8, /device:TPU:0, one launch (start us, length us, event | category | flops | bytes accessed | tf_op | source)
XLA Modules:
  0.0 263.5 jit_solution(3527519983643824759)
XLA Ops:
  7.2 1.6 convert_reduce_fusion
  8.8 1.6 fusion.12
  10.5 1.4 fusion.6
  11.9 0.7 all-gather.5.cloned.1.call-update
  12.8 1.2 constant_dynamic-slice_fusion.2
  14.0 50.4 %all-gather.3.cloned.1.call-done = bf16[4096,1024]{1,0:T(8,128)(2,1)} async-done(((bf16[512,1024]{1,0:T(8,128)(2,1)}), bf16[4096,1024]{1,0:T(8,128)(2,1)}) %all-gather.3.cloned.1.call-update) | async-done | bytes 8388624 | tf_op jit(solution)/shard_map/all_gather | solution.py:342
  64.5 8.3 %convolution_convert_fusion = bf16[4096,384]{1,0:T(8,128)(2,1)S(1)} fusion(bf16[4096,1024]{1,0:T(8,128)(2,1)} %all-gather.3.cloned.1.call-done, bf16[1024,128]{1,0:T(8,128)(2,1)S(1)} %get-tuple-element.24, bf16[1024,128]{1,0:T(8,128)(2,1)S(1)} %get-tuple-element.23, bf16[1024,128]{1,0:T(8,128)(2,1)S(1)} %get-tuple-element.22), kind=kOutput, calls=%fused_computation | convolution fusion | flops 3225157632 | bytes 12320768 | tf_op jit(solution)/shard_map/dot_general | solution.py:351
  72.7 0.5 fusion.22
  73.4 28.7 %shard_map.102 = (bf16[4096,128]{1,0:T(8,128)(2,1)S(1)}, f32[8192,128]{1,0:T(8,128)}) custom-call(s32[256]{0:T(256)S(1)} %reshape_squeeze.3.cols_ref, s32[32]{0:T(128)S(1)} %bitcast.30, bf16[4096,128]{1,0:T(8,128)(2,1)S(1)} %get-tuple-element.27.q_ref, bf16[4096,128]{1,0:T(8,128)(2,1)S(1)} %get-tuple-element.26.k_ref, ...), custom_call_target="tpu_custom_call" | custom-call | tf_op jit(solution)/shard_map/pallas_call | solution.py:157
  102.1 1.0 copy-done.3
  103.1 1.0 copy-done.4
  104.1 1.0 copy-done.6
  105.0 11.1 %all-gather.5.cloned.1.call-done = bf16[4096,1024]{1,0:T(8,128)(2,1)} async-done(((bf16[512,1024]{1,0:T(8,128)(2,1)}), bf16[4096,1024]{1,0:T(8,128)(2,1)}) %all-gather.5.cloned.1.call-update) | async-done | bytes 8388624 | tf_op jit(solution)/shard_map/all_gather | solution.py:343
  116.2 5.5 %fusion.24 = f32[128,1024]{1,0:T(8,128)} fusion(bf16[4096,128]{1,0:T(8,128)(2,1)S(1)} %get-tuple-element.12.o_ref, bf16[4096,1024]{1,0:T(8,128)(2,1)} %all-gather.5.cloned.1.call-done), kind=kOutput, calls=%fused_computation.42 | convolution fusion | flops 1073741824 | bytes 9961472 | tf_op jit(solution)/shard_map/dot_general | solution.py:28
  121.7 1.9 concatenate.17
  123.6 6.9 %fusion.do_ref = bf16[4096,128]{1,0:T(8,128)(2,1)} fusion(bf16[4096,1024]{1,0:T(8,128)(2,1)} %all-gather.5.cloned.1.call-done, bf16[1024,1024]{1,0:T(8,128)(2,1)S(1)} %copy-done, s32[]{:T(128)S(6)} %select_n.15), kind=kOutput, calls=%fused_computation.2 | convolution fusion | flops 1074266112 | bytes 9699332 | tf_op jit(solution)/shard_map/dot_general | solution.py:361
  130.5 37.8 %shard_map.103 = (bf16[4096,128]{1,0:T(8,128)(2,1)S(1)}, bf16[4096,128]{1,0:T(8,128)(2,1)S(1)}, bf16[4096,128]{1,0:T(8,128)(2,1)S(1)}) custom-call(s32[256]{0:T(256)S(1)} %reshape_squeeze.3.cols_ref, s32[32]{0:T(128)S(1)} %bitcast.31, bf16[4096,128]{1,0:T(8,128)(2,1)S(1)} %copy-done.7, bf16[4096,128]{1,0:T(8,128)(2,1)S(1)} %copy-done.5, ...), custom_call_target="tpu_custom_call" | custom-call | tf_op jit(solution)/shard_map/pallas_call | solution.py:171
  168.5 0.2 constant_dynamic-update-slice_fusion.1
  168.7 0.2 constant_dynamic-update-slice_fusion
  169.0 8.3 %fusion.23 = f32[1024,384]{1,0:T(8,128)S(1)} fusion(bf16[4096,1024]{1,0:T(8,128)(2,1)} %all-gather.3.cloned.1.call-done, bf16[4096,384]{1,0:T(8,128)(2,1)S(1)} %constant_dynamic-update-slice_fusion), kind=kOutput, calls=%fused_computation.41 | convolution fusion | flops 3221225472 | bytes 13107200 | tf_op jit(solution)/shard_map/dot_general | solution.py:28
  177.3 0.2 pad_maximum_fusion.x_ref
  177.5 1.0 copy-done.2
  178.5 55.7 %shard_map.104 = (bf16[16,64,512]{2,1,0:T(8,128)(2,1)S(1)}, bf16[512,3072]{1,0:T(8,128)(2,1)}, bf16[512,1024]{1,0:T(8,128)(2,1)S(1)}) custom-call(f32[16,64,512]{2,1,0:T(8,128)S(1)} %pad_maximum_fusion.x_ref, bf16[8,512,384]{2,1,0:T(8,128)(2,1)} %bitcast.32, bf16[8,512,128]{2,1,0:T(8,128)(2,1)S(1)} %bitcast.27), custom_call_target="tpu_custom_call" | custom-call | tf_op jit(solution)/shard_map/pallas_call | solution.py:312
  234.2 1.0 slice.23
  235.2 0.8 reshape.61
  236.0 4.7 %all-to-all-start = ((bf16[8,128,384]{2,1,0:T(8,128)(2,1)}), bf16[8,128,384]{2,1,0:T(8,128)(2,1)}, u32[]{:S(2)}, u32[]{:S(2)}) async-start(bf16[8,128,384]{2,1,0:T(8,128)(2,1)} %bitcast.34), calls=%async_computation | async-start | bytes 1572864 | tf_op jit(solution)/shard_map/all_to_all | solution.py:392
  240.8 7.7 %multiply_reduce_fusion = (f32[512]{0:T(512)S(1)}, f32[512]{0:T(512)S(1)}, f32[512,1024]{1,0:T(8,128)S(1)}) fusion(f32[1024]{0:T(1024)S(1)} %copy-done.14, f32[512]{0:T(512)S(1)} %add_rsqrt_fusion, f32[512]{0:T(512)S(1)} %broadcast_multiply_fusion.2, bf16[512,1024]{1,0:T(8,128)(2,1)} %param.7, bf16[512,3072]{1,0:T(8,128)(2,1)} %get-tuple-element.18, ...), kind=kOutput, calls=%fused_computation.20 | convolution fusion | flops 3224894464 | bytes 12595200 | tf_op jit(solution)/shard_map/dot_general | solution.py:380
  248.5 1.8 fusion.11
  250.4 2.2 fusion.13
  252.6 1.4 all-to-all-done
  254.0 1.6 copy.16
  255.6 1.0 copy.20
  (38 shorter events, 0.7 us)
Async XLA Ops:
  7.2 116.4 %copy-start = (bf16[1024,1024]{1,0:T(8,128)(2,1)S(1)}, bf16[1024,1024]{1,0:T(8,128)(2,1)}, u32[]{:S(2)}) copy-start(bf16[1024,1024]{1,0:T(8,128)(2,1)} %param.10) | copy-start | bytes 6291460
  7.2 3.3 %copy-start.10 = (bf16[512,1024]{1,0:T(8,128)(2,1)S(1)}, bf16[512,1024]{1,0:T(8,128)(2,1)}, u32[]{:S(2)}) copy-start(bf16[512,1024]{1,0:T(8,128)(2,1)} %param.7) | copy-start | bytes 3145732
  7.2 3.3 %copy-start.14 = (f32[1024]{0:T(1024)S(1)}, f32[1024]{0:T(1024)}, u32[]{:S(2)}) copy-start(f32[1024]{0:T(1024)} %param.8) | copy-start | bytes 12292
  7.2 57.3 %all-gather.3.cloned.1.call-start = ((), (), s32[]{:S(2)}) async-start(), calls=%async_computation.1 | async-start | bytes 9437184 | tf_op jit(solution)/shard_map/all_gather | solution.py:342
  10.5 2.1 copy-start.15
  11.9 104.3 %all-gather.5.cloned.1.call-start = ((), (), s32[]{:S(2)}) async-start(), calls=%async_computation.2 | async-start | bytes 9437184 | tf_op jit(solution)/shard_map/all_gather | solution.py:343
  72.7 0.7 copy-start.8
  102.1 1.0 copy-start.3
  103.1 1.0 copy-start.4
  104.1 1.0 copy-start.6
  105.0 16.6 %copy-start.1 = (bf16[4096,128]{1,0:T(8,128)(2,1)}, bf16[4096,128]{1,0:T(8,128)(2,1)S(1)}, u32[]{:S(2)}) copy-start(bf16[4096,128]{1,0:T(8,128)(2,1)S(1)} %get-tuple-element.12.o_ref) | copy-start | bytes 3145732
  123.6 6.9 %copy-start.5 = (bf16[4096,128]{1,0:T(8,128)(2,1)S(1)}, bf16[4096,128]{1,0:T(8,128)(2,1)}, u32[]{:S(2)}) copy-start(bf16[4096,128]{1,0:T(8,128)(2,1)} %copy-done.4) | copy-start | bytes 3145732
  123.6 6.9 %copy-start.7 = (bf16[4096,128]{1,0:T(8,128)(2,1)S(1)}, bf16[4096,128]{1,0:T(8,128)(2,1)}, u32[]{:S(2)}) copy-start(bf16[4096,128]{1,0:T(8,128)(2,1)} %copy-done.6) | copy-start | bytes 3145732
  169.0 8.3 %copy-start.9 = (bf16[4096,384]{1,0:T(8,128)(2,1)}, bf16[4096,384]{1,0:T(8,128)(2,1)S(1)}, u32[]{:S(2)}) copy-start(bf16[4096,384]{1,0:T(8,128)(2,1)S(1)} %constant_dynamic-update-slice_fusion) | copy-start | bytes 9437188
  169.0 8.3 %copy-start.13 = (f32[16,64,128]{2,1,0:T(8,128)S(1)}, f32[16,64,128]{2,1,0:T(8,128)}, u32[]{:S(2)}) copy-start(f32[16,64,128]{2,1,0:T(8,128)} %concatenate.17) | copy-start | bytes 1572868
  177.3 1.2 copy-start.2
  236.0 18.0 %all-to-all-start = ((bf16[8,128,384]{2,1,0:T(8,128)(2,1)}), bf16[8,128,384]{2,1,0:T(8,128)(2,1)}, u32[]{:S(2)}, u32[]{:S(2)}) async-start(bf16[8,128,384]{2,1,0:T(8,128)(2,1)} %bitcast.34), calls=%async_computation | async-start | bytes 1572864 | tf_op jit(solution)/shard_map/all_to_all | solution.py:392
  240.7 7.8 %copy-start.11 = (bf16[512,1024]{1,0:T(8,128)(2,1)S(1)}, bf16[512,1024]{1,0:T(8,128)(2,1)}, u32[]{:S(2)}) copy-start(bf16[512,1024]{1,0:T(8,128)(2,1)} %param.7) | copy-start | bytes 3145732
  240.8 7.8 %copy-start.12 = (bf16[512,1024]{1,0:T(8,128)(2,1)S(1)}, bf16[512,1024]{1,0:T(8,128)(2,1)}, u32[]{:S(2)}) copy-start(bf16[512,1024]{1,0:T(8,128)(2,1)} %param.13) | copy-start | bytes 3145732
Sparse Core Ops, SparseCore 0:
  12.0 52.3 all-gather.2
  66.2 49.9 all-gather.4

commit v9 on v8

--- a/solution.py
+++ b/solution.py
@@ -54,18 +54,28 @@
     return lax.dot_general(a, b, (((0,), (0,)), ((), ())), preferred_element_type=jnp.float32)
 
 
-def gather_blocks(ref, cols_ref, r):
+SLOT_TIERS = (2, 4, MAXB)
+
+
+def gather_blocks(ref, cols_ref, r, slots):
     return jnp.concatenate(
         [
             ref[pl.ds(pl.multiple_of(cols_ref[r * MAXB + s] * BLK, BLK), BLK), :]
-            for s in range(MAXB)
+            for s in range(slots)
         ],
         axis=0,
     )
 
 
-def live_lanes(cnt):
-    return lax.broadcasted_iota(jnp.int32, (1, MAXB * BLK), 1) < cnt * BLK
+def live_lanes(cnt, slots):
+    return lax.broadcasted_iota(jnp.int32, (1, slots * BLK), 1) < cnt * BLK
+
+
+def by_tier(cnt, body):
+    low = 0
+    for slots in SLOT_TIERS:
+        pl.when((cnt > low) & (cnt <= slots))(functools.partial(body, slots))
+        low = slots
 
 
 def attn_fwd_kernel(cols_ref, counts_ref, q_ref, k_ref, v_ref, o_ref, lse_ref):
@@ -76,18 +86,25 @@
 
     def row_body(r, carry):
         row0 = pl.multiple_of(r * BLK, BLK)
-        live = live_lanes(counts_ref[r])
-        q2 = stack_heads(q_ref[pl.ds(row0, BLK), :], masks)
-        sc = jnp.where(live, nt_dot(q2, gather_blocks(k_ref, cols_ref, r)) * SCALE, NEG)
-        m = jnp.max(sc, axis=1, keepdims=True)
-        e = jnp.where(live, jnp.exp(sc - m), 0.0)
-        l = jnp.sum(e, axis=1, keepdims=True)
-        p = (e * (1.0 / l)).astype(jnp.bfloat16)
-        acc = jnp.dot(p, gather_blocks(v_ref, cols_ref, r), preferred_element_type=jnp.float32)
-        o_ref[pl.ds(row0, BLK), :] = unstack_heads(acc, masks).astype(o_ref.dtype)
-        lse_ref[pl.ds(pl.multiple_of(r * rows, rows), rows), :] = jnp.broadcast_to(
-            m + jnp.log(l), (rows, lse_ref.shape[1])
-        )
+        cnt = counts_ref[r]
+
+        def tier(slots):
+            live = live_lanes(cnt, slots)
+            q2 = stack_heads(q_ref[pl.ds(row0, BLK), :], masks)
+            kc = gather_blocks(k_ref, cols_ref, r, slots)
+            sc = jnp.where(live, nt_dot(q2, kc) * SCALE, NEG)
+            m = jnp.max(sc, axis=1, keepdims=True)
+            e = jnp.where(live, jnp.exp(sc - m), 0.0)
+            l = jnp.sum(e, axis=1, keepdims=True)
+            p = (e * (1.0 / l)).astype(jnp.bfloat16)
+            vc = gather_blocks(v_ref, cols_ref, r, slots)
+            acc = jnp.dot(p, vc, preferred_element_type=jnp.float32)
+            o_ref[pl.ds(row0, BLK), :] = unstack_heads(acc, masks).astype(o_ref.dtype)
+            lse_ref[pl.ds(pl.multiple_of(r * rows, rows), rows), :] = jnp.broadcast_to(
+                m + jnp.log(l), (rows, lse_ref.shape[1])
+            )
+
+        by_tier(cnt, tier)
         return carry
 
     lax.fori_loop(0, nblk, row_body, 0)
@@ -106,33 +123,36 @@
     def row_body(r, carry):
         row0 = pl.multiple_of(r * BLK, BLK)
         cnt = counts_ref[r]
-        live = live_lanes(cnt)
-        q2 = stack_heads(q_ref[pl.ds(row0, BLK), :], masks)
-        do_blk = do_ref[pl.ds(row0, BLK), :]
-        do2 = stack_heads(do_blk, masks)
-        prod = o_ref[pl.ds(row0, BLK), :].astype(jnp.float32) * do_blk.astype(jnp.float32)
-        delta = jnp.concatenate(
-            [jnp.sum(jnp.where(m, prod, 0.0), axis=1, keepdims=True) for m in masks], axis=0
-        )
-        lse = lse_ref[pl.ds(pl.multiple_of(r * rows, rows), rows), :][:, 0:1]
-        kc = gather_blocks(k_ref, cols_ref, r)
-        vc = gather_blocks(v_ref, cols_ref, r)
-        sc = nt_dot(q2, kc) * SCALE
-        p = jnp.where(live, jnp.exp(sc - lse), 0.0).astype(jnp.bfloat16)
-        dp = nt_dot(do2, vc)
-        ds = (p.astype(jnp.float32) * (dp - delta) * SCALE).astype(jnp.bfloat16)
-        dq = jnp.dot(ds, kc, preferred_element_type=jnp.float32)
-        dq_ref[pl.ds(row0, BLK), :] = unstack_heads(dq, masks).astype(dq_ref.dtype)
-        dkc = tn_dot(ds, q2)
-        dvc = tn_dot(p, do2)
-        for s in range(MAXB):
-
-            @pl.when(s < cnt)
-            def _():
-                col0 = pl.multiple_of(cols_ref[r * MAXB + s] * BLK, BLK)
-                dk_acc[pl.ds(col0, BLK), :] += dkc[s * BLK : (s + 1) * BLK]
-                dv_acc[pl.ds(col0, BLK), :] += dvc[s * BLK : (s + 1) * BLK]
-
+
+        def tier(slots):
+            live = live_lanes(cnt, slots)
+            q2 = stack_heads(q_ref[pl.ds(row0, BLK), :], masks)
+            do_blk = do_ref[pl.ds(row0, BLK), :]
+            do2 = stack_heads(do_blk, masks)
+            prod = o_ref[pl.ds(row0, BLK), :].astype(jnp.float32) * do_blk.astype(jnp.float32)
+            delta = jnp.concatenate(
+                [jnp.sum(jnp.where(m, prod, 0.0), axis=1, keepdims=True) for m in masks], axis=0
+            )
+            lse = lse_ref[pl.ds(pl.multiple_of(r * rows, rows), rows), :][:, 0:1]
+            kc = gather_blocks(k_ref, cols_ref, r, slots)
+            vc = gather_blocks(v_ref, cols_ref, r, slots)
+            sc = nt_dot(q2, kc) * SCALE
+            p = jnp.where(live, jnp.exp(sc - lse), 0.0).astype(jnp.bfloat16)
+            dp = nt_dot(do2, vc)
+            ds = (p.astype(jnp.float32) * (dp - delta) * SCALE).astype(jnp.bfloat16)
+            dq = jnp.dot(ds, kc, preferred_element_type=jnp.float32)
+            dq_ref[pl.ds(row0, BLK), :] = unstack_heads(dq, masks).astype(dq_ref.dtype)
+            dkc = tn_dot(ds, q2)
+            dvc = tn_dot(p, do2)
+            for s in range(slots):
+
+                @pl.when(s < cnt)
+                def _():
+                    col0 = pl.multiple_of(cols_ref[r * MAXB + s] * BLK, BLK)
+                    dk_acc[pl.ds(col0, BLK), :] += dkc[s * BLK : (s + 1) * BLK]
+                    dv_acc[pl.ds(col0, BLK), :] += dvc[s * BLK : (s + 1) * BLK]
+
+        by_tier(cnt, tier)
         return carry
 
     lax.fori_loop(0, nblk, row_body, 0)

time: 265 us -> 258 us (0.974)
  Pallas kernels: 122 us -> 110 us
  waiting for transfers between devices: 63.7 us -> 68.6 us
    pallas_call x1, Pallas kernels: 37.8 us -> 30.6 us  [attention_backward(): pl.pallas_call(attn_bwd_kernel, out_shape=tuple((jax.ShapeDtypeStruct((n,...]
    all_gather x1, waiting for transfers between devices: 11.1 us -> 16 us  [body(): cotan_all = lax.all_gather(cotan, 'seq', axis=0, tiled=True)]
    pallas_call x1, Pallas kernels: 28.7 us -> 24 us  [attention_forward(): pl.pallas_call(attn_fwd_kernel, out_shape=(jax.ShapeDtypeStruct((n, width...]
  transfers between devices with their start and end apart: 3 -> 3, of which waited for: 3 -> 3; matrix products, arithmetic and copies ran while one was open for 8% -> 9% of each run, Pallas kernels for 11% -> 9%
where the time goes in v9:
time: 258 us; the launch traced here: 256 us
  Pallas kernels  110 us (43%)
  waiting for transfers between devices  68.6 us (27%)
  matrix products  38.8 us (15%)
  between operations  14.3 us (6%)
  local copies, waits for them, and re-layouts  13 us (5%)
  other arithmetic  6.63 us (3%)
  starting transfers between devices  4.81 us (2%)
    pallas_call x1, Pallas kernels, sum_and_exchange(): pl.pallas_call(functools.partial(exchange_kernel, n, m), out_shape=(jax.S...  55.7 us
    all_gather x1, waiting for transfers between devices, body(): normed_all = lax.all_gather(normed, 'seq', axis=0, tiled=True)  50.4 us
    pallas_call x1, Pallas kernels, attention_backward(): pl.pallas_call(attn_bwd_kernel, out_shape=tuple((jax.ShapeDtypeStruct((n,...  30.6 us
    pallas_call x1, Pallas kernels, attention_forward(): pl.pallas_call(attn_fwd_kernel, out_shape=(jax.ShapeDtypeStruct((n, width...  24 us
    all_gather x1, waiting for transfers between devices, body(): cotan_all = lax.all_gather(cotan, 'seq', axis=0, tiled=True)  16 us
    dot_general x2, matrix products, contract_rows(): lax.dot_general(left_cols, right_cols, (((0,), (0,)), ((), ())), preferre...  13.7 us
    dot_general x1, matrix products, body(): jnp.dot(normed_all, w_heads, preferred_element_type=jnp.float32)  8.27 us
    dot_general x1, matrix products, body(): lax.dot_general(grad_mixed, w_qkv, (((1,), (1,)), ((), ())), preferred_el...  7.74 us
  transfers between devices with their start and end apart: 3, of which 3 were waited for; matrix products, arithmetic and copies ran while one was open for 9% of the time, Pallas kernels for 9%

profile of v9, /device:TPU:0, one launch (start us, length us, event | category | flops | bytes accessed | tf_op | source)
XLA Modules:
  0.0 256.4 jit_solution(15292211011834809230)
XLA Ops:
  7.2 1.6 convert_reduce_fusion
  8.8 1.6 fusion.12
  10.5 1.4 fusion.6
  11.9 0.7 all-gather.5.cloned.1.call-update
  12.8 1.2 constant_dynamic-slice_fusion.2
  14.0 50.4 %all-gather.3.cloned.1.call-done = bf16[4096,1024]{1,0:T(8,128)(2,1)} async-done(((bf16[512,1024]{1,0:T(8,128)(2,1)}), bf16[4096,1024]{1,0:T(8,128)(2,1)}) %all-gather.3.cloned.1.call-update) | async-done | bytes 8388624 | tf_op jit(solution)/shard_map/all_gather | solution.py:362
  64.5 8.3 %convolution_convert_fusion = bf16[4096,384]{1,0:T(8,128)(2,1)S(1)} fusion(bf16[4096,1024]{1,0:T(8,128)(2,1)} %all-gather.3.cloned.1.call-done, bf16[1024,128]{1,0:T(8,128)(2,1)S(1)} %get-tuple-element.24, bf16[1024,128]{1,0:T(8,128)(2,1)S(1)} %get-tuple-element.23, bf16[1024,128]{1,0:T(8,128)(2,1)S(1)} %get-tuple-element.22), kind=kOutput, calls=%fused_computation | convolution fusion | flops 3225157632 | bytes 12320768 | tf_op jit(solution)/shard_map/dot_general | solution.py:371
  72.7 0.5 fusion.22
  73.4 24.0 %shard_map.102 = (bf16[4096,128]{1,0:T(8,128)(2,1)S(1)}, f32[8192,128]{1,0:T(8,128)}) custom-call(s32[256]{0:T(256)S(1)} %reshape_squeeze.3.cols_ref, s32[32]{0:T(128)S(1)} %bitcast.30, bf16[4096,128]{1,0:T(8,128)(2,1)S(1)} %get-tuple-element.27.q_ref, bf16[4096,128]{1,0:T(8,128)(2,1)S(1)} %get-tuple-element.26.k_ref, ...), custom_call_target="tpu_custom_call" | custom-call | tf_op jit(solution)/shard_map/pallas_call | solution.py:177
  97.4 1.0 copy-done.3
  98.4 1.0 copy-done.4
  99.4 1.0 copy-done.6
  100.3 16.0 %all-gather.5.cloned.1.call-done = bf16[4096,1024]{1,0:T(8,128)(2,1)} async-done(((bf16[512,1024]{1,0:T(8,128)(2,1)}), bf16[4096,1024]{1,0:T(8,128)(2,1)}) %all-gather.5.cloned.1.call-update) | async-done | bytes 8388624 | tf_op jit(solution)/shard_map/all_gather | solution.py:363
  116.4 5.5 %fusion.24 = f32[128,1024]{1,0:T(8,128)} fusion(bf16[4096,128]{1,0:T(8,128)(2,1)S(1)} %get-tuple-element.12.o_ref, bf16[4096,1024]{1,0:T(8,128)(2,1)} %all-gather.5.cloned.1.call-done), kind=kOutput, calls=%fused_computation.42 | convolution fusion | flops 1073741824 | bytes 9961472 | tf_op jit(solution)/shard_map/dot_general | solution.py:28
  121.9 1.9 concatenate.17
  123.8 6.9 %fusion.do_ref = bf16[4096,128]{1,0:T(8,128)(2,1)} fusion(bf16[4096,1024]{1,0:T(8,128)(2,1)} %all-gather.5.cloned.1.call-done, bf16[1024,1024]{1,0:T(8,128)(2,1)S(1)} %copy-done, s32[]{:T(128)S(6)} %select_n.15), kind=kOutput, calls=%fused_computation.2 | convolution fusion | flops 1074266112 | bytes 9699332 | tf_op jit(solution)/shard_map/dot_general | solution.py:381
  130.7 30.6 %shard_map.103 = (bf16[4096,128]{1,0:T(8,128)(2,1)S(1)}, bf16[4096,128]{1,0:T(8,128)(2,1)S(1)}, bf16[4096,128]{1,0:T(8,128)(2,1)S(1)}) custom-call(s32[256]{0:T(256)S(1)} %reshape_squeeze.3.cols_ref, s32[32]{0:T(128)S(1)} %bitcast.31, bf16[4096,128]{1,0:T(8,128)(2,1)S(1)} %copy-done.7, bf16[4096,128]{1,0:T(8,128)(2,1)S(1)} %copy-done.5, ...), custom_call_target="tpu_custom_call" | custom-call | tf_op jit(solution)/shard_map/pallas_call | solution.py:191
  161.5 0.2 constant_dynamic-update-slice_fusion.1
  161.7 0.2 constant_dynamic-update-slice_fusion
  162.0 8.2 %fusion.23 = f32[1024,384]{1,0:T(8,128)S(1)} fusion(bf16[4096,1024]{1,0:T(8,128)(2,1)} %all-gather.3.cloned.1.call-done, bf16[4096,384]{1,0:T(8,128)(2,1)S(1)} %constant_dynamic-update-slice_fusion), kind=kOutput, calls=%fused_computation.41 | convolution fusion | flops 3221225472 | bytes 13107200 | tf_op jit(solution)/shard_map/dot_general | solution.py:28
  170.2 0.2 pad_maximum_fusion.x_ref
  170.5 1.0 copy-done.2
  171.5 55.7 %shard_map.104 = (bf16[16,64,512]{2,1,0:T(8,128)(2,1)S(1)}, bf16[512,3072]{1,0:T(8,128)(2,1)}, bf16[512,1024]{1,0:T(8,128)(2,1)S(1)}) custom-call(f32[16,64,512]{2,1,0:T(8,128)S(1)} %pad_maximum_fusion.x_ref, bf16[8,512,384]{2,1,0:T(8,128)(2,1)} %bitcast.32, bf16[8,512,128]{2,1,0:T(8,128)(2,1)S(1)} %bitcast.27), custom_call_target="tpu_custom_call" | custom-call | tf_op jit(solution)/shard_map/pallas_call | solution.py:332
  227.2 1.0 slice.23
  228.1 0.8 reshape.61
  228.9 4.7 %all-to-all-start = ((bf16[8,128,384]{2,1,0:T(8,128)(2,1)}), bf16[8,128,384]{2,1,0:T(8,128)(2,1)}, u32[]{:S(2)}, u32[]{:S(2)}) async-start(bf16[8,128,384]{2,1,0:T(8,128)(2,1)} %bitcast.34), calls=%async_computation | async-start | bytes 1572864 | tf_op jit(solution)/shard_map/all_to_all | solution.py:412
  233.7 7.7 %multiply_reduce_fusion = (f32[512]{0:T(512)S(1)}, f32[512]{0:T(512)S(1)}, f32[512,1024]{1,0:T(8,128)S(1)}) fusion(f32[1024]{0:T(1024)S(1)} %copy-done.14, f32[512]{0:T(512)S(1)} %add_rsqrt_fusion, f32[512]{0:T(512)S(1)} %broadcast_multiply_fusion.2, bf16[512,1024]{1,0:T(8,128)(2,1)} %param.7, bf16[512,3072]{1,0:T(8,128)(2,1)} %get-tuple-element.18, ...), kind=kOutput, calls=%fused_computation.20 | convolution fusion | flops 3224894464 | bytes 12595200 | tf_op jit(solution)/shard_map/dot_general | solution.py:400
  241.5 1.8 fusion.11
  243.3 2.2 fusion.13
  245.5 1.4 all-to-all-done
  246.9 1.6 copy.16
  248.5 1.0 copy.20
  (38 shorter events, 0.7 us)
Async XLA Ops:
  7.2 116.6 %copy-start = (bf16[1024,1024]{1,0:T(8,128)(2,1)S(1)}, bf16[1024,1024]{1,0:T(8,128)(2,1)}, u32[]{:S(2)}) copy-start(bf16[1024,1024]{1,0:T(8,128)(2,1)} %param.10) | copy-start | bytes 6291460
  7.2 3.3 %copy-start.10 = (bf16[512,1024]{1,0:T(8,128)(2,1)S(1)}, bf16[512,1024]{1,0:T(8,128)(2,1)}, u32[]{:S(2)}) copy-start(bf16[512,1024]{1,0:T(8,128)(2,1)} %param.7) | copy-start | bytes 3145732
  7.2 3.3 %copy-start.14 = (f32[1024]{0:T(1024)S(1)}, f32[1024]{0:T(1024)}, u32[]{:S(2)}) copy-start(f32[1024]{0:T(1024)} %param.8) | copy-start | bytes 12292
  7.2 57.3 %all-gather.3.cloned.1.call-start = ((), (), s32[]{:S(2)}) async-start(), calls=%async_computation.1 | async-start | bytes 9437184 | tf_op jit(solution)/shard_map/all_gather | solution.py:362
  10.5 2.1 copy-start.15
  11.9 104.5 %all-gather.5.cloned.1.call-start = ((), (), s32[]{:S(2)}) async-start(), calls=%async_computation.2 | async-start | bytes 9437184 | tf_op jit(solution)/shard_map/all_gather | solution.py:363
  72.7 0.7 copy-start.8
  97.4 1.0 copy-start.3
  98.4 1.0 copy-start.4
  99.4 1.0 copy-start.6
  100.3 21.5 %copy-start.1 = (bf16[4096,128]{1,0:T(8,128)(2,1)}, bf16[4096,128]{1,0:T(8,128)(2,1)S(1)}, u32[]{:S(2)}) copy-start(bf16[4096,128]{1,0:T(8,128)(2,1)S(1)} %get-tuple-element.12.o_ref) | copy-start | bytes 3145732
  123.8 6.9 %copy-start.5 = (bf16[4096,128]{1,0:T(8,128)(2,1)S(1)}, bf16[4096,128]{1,0:T(8,128)(2,1)}, u32[]{:S(2)}) copy-start(bf16[4096,128]{1,0:T(8,128)(2,1)} %copy-done.4) | copy-start | bytes 3145732
  123.8 6.9 %copy-start.7 = (bf16[4096,128]{1,0:T(8,128)(2,1)S(1)}, bf16[4096,128]{1,0:T(8,128)(2,1)}, u32[]{:S(2)}) copy-start(bf16[4096,128]{1,0:T(8,128)(2,1)} %copy-done.6) | copy-start | bytes 3145732
  162.0 8.2 %copy-start.9 = (bf16[4096,384]{1,0:T(8,128)(2,1)}, bf16[4096,384]{1,0:T(8,128)(2,1)S(1)}, u32[]{:S(2)}) copy-start(bf16[4096,384]{1,0:T(8,128)(2,1)S(1)} %constant_dynamic-update-slice_fusion) | copy-start | bytes 9437188
  162.0 8.2 %copy-start.13 = (f32[16,64,128]{2,1,0:T(8,128)S(1)}, f32[16,64,128]{2,1,0:T(8,128)}, u32[]{:S(2)}) copy-start(f32[16,64,128]{2,1,0:T(8,128)} %concatenate.17) | copy-start | bytes 1572868
  170.2 1.2 copy-start.2
  228.9 18.0 %all-to-all-start = ((bf16[8,128,384]{2,1,0:T(8,128)(2,1)}), bf16[8,128,384]{2,1,0:T(8,128)(2,1)}, u32[]{:S(2)}, u32[]{:S(2)}) async-start(bf16[8,128,384]{2,1,0:T(8,128)(2,1)} %bitcast.34), calls=%async_computation | async-start | bytes 1572864 | tf_op jit(solution)/shard_map/all_to_all | solution.py:412
  233.7 7.8 %copy-start.11 = (bf16[512,1024]{1,0:T(8,128)(2,1)S(1)}, bf16[512,1024]{1,0:T(8,128)(2,1)}, u32[]{:S(2)}) copy-start(bf16[512,1024]{1,0:T(8,128)(2,1)} %param.7) | copy-start | bytes 3145732
  233.7 7.8 %copy-start.12 = (bf16[512,1024]{1,0:T(8,128)(2,1)S(1)}, bf16[512,1024]{1,0:T(8,128)(2,1)}, u32[]{:S(2)}) copy-start(bf16[512,1024]{1,0:T(8,128)(2,1)} %param.13) | copy-start | bytes 3145732
Sparse Core Ops, SparseCore 0:
  12.0 52.3 all-gather.2
  66.2 50.1 all-gather.4

commit v10 on v9

--- a/solution.py
+++ b/solution.py
@@ -111,7 +111,20 @@
 
 
 def attn_bwd_kernel(
-    cols_ref, counts_ref, q_ref, k_ref, v_ref, o_ref, do_ref, lse_ref, dq_ref, dk_ref, dv_ref, dk_acc, dv_acc
+    cols_ref,
+    counts_ref,
+    q_ref,
+    k_ref,
+    v_ref,
+    o_ref,
+    cotan_ref,
+    w_ref,
+    lse_ref,
+    dq_ref,
+    dk_ref,
+    dv_ref,
+    dk_acc,
+    dv_acc,
 ):
     width = q_ref.shape[1]
     nblk = q_ref.shape[0] // BLK
@@ -123,11 +136,11 @@
     def row_body(r, carry):
         row0 = pl.multiple_of(r * BLK, BLK)
         cnt = counts_ref[r]
+        do_blk = nt_dot(cotan_ref[pl.ds(row0, BLK), :], w_ref[...]).astype(jnp.bfloat16)
 
         def tier(slots):
             live = live_lanes(cnt, slots)
             q2 = stack_heads(q_ref[pl.ds(row0, BLK), :], masks)
-            do_blk = do_ref[pl.ds(row0, BLK), :]
             do2 = stack_heads(do_blk, masks)
             prod = o_ref[pl.ds(row0, BLK), :].astype(jnp.float32) * do_blk.astype(jnp.float32)
             delta = jnp.concatenate(
@@ -186,16 +199,16 @@
     )(cols, counts, q, k, v)
 
 
-def attention_backward(q, k, v, o, do, lse, cols, counts):
+def attention_backward(q, k, v, o, cotan_all, w_out_rows, lse, cols, counts):
     n, width = q.shape
     return pl.pallas_call(
         attn_bwd_kernel,
         out_shape=tuple(jax.ShapeDtypeStruct((n, width), jnp.bfloat16) for _ in range(3)),
-        in_specs=[smem_spec(), smem_spec()] + [vmem_spec()] * 6,
+        in_specs=[smem_spec(), smem_spec()] + [vmem_spec()] * 7,
         out_specs=(vmem_spec(), vmem_spec(), vmem_spec()),
         scratch_shapes=[pltpu.VMEM((n, width), jnp.float32), pltpu.VMEM((n, width), jnp.float32)],
         compiler_params=pltpu.CompilerParams(vmem_limit_bytes=VMEM_LIMIT),
-    )(cols, counts, q, k, v, o, do, lse)
+    )(cols, counts, q, k, v, o, cotan_all, w_out_rows, lse)
 
 
 def regroup_columns(moved, seq_count, group_width):
@@ -378,11 +391,8 @@
     counts = block_counts[0]
     attended_heads, lse = attention_forward(query_heads, key_heads, value_heads, cols, counts)
     w_out_rows = lax.dynamic_slice_in_dim(w_out, seq_at * group_width, group_width, 0)
-    grad_heads = lax.dot_general(
-        cotan_all, w_out_rows, (((1,), (1,)), ((), ())), preferred_element_type=jnp.float32
-    ).astype(jnp.bfloat16)
     query_grad, key_grad, value_grad = attention_backward(
-        query_heads, key_heads, value_heads, attended_heads, grad_heads, lse, cols, counts
+        query_heads, key_heads, value_heads, attended_heads, cotan_all, w_out_rows, lse, cols, counts
     )
     grad_heads_mixed = jnp.concatenate([query_grad, key_grad, value_grad], axis=1)
     term_qkv = contract_rows(normed_all, grad_heads_mixed)

time: 258 us -> 263 us (1.019)
  Pallas kernels: 110 us -> 120 us
  matrix products: 38.8 us -> 32 us
    pallas_call x1, Pallas kernels: 30.6 us -> 39.5 us  [attention_backward(): pl.pallas_call(attn_bwd_kernel, out_shape=tuple((jax.ShapeDtypeStruct((n,...]
    dot_general x1 -> x0, matrix products: 6.86 us -> none  [body(): lax.dot_general(cotan_all, w_out_rows, (((1,), (1,)), ((), ())), preferre...]
  transfers between devices with their start and end apart: 3 -> 3, of which waited for: 3 -> 3; matrix products, arithmetic and copies ran while one was open for 9% -> 8% of each run, Pallas kernels for 9% -> 9%
where the time goes in v10:
time: 263 us; the launch traced here: 261 us
  Pallas kernels  120 us (46%)
  waiting for transfers between devices  68.2 us (26%)
  matrix products  32 us (12%)
  local copies, waits for them, and re-layouts  15.5 us (6%)
  between operations  14.3 us (5%)
  other arithmetic  6.63 us (3%)
  starting transfers between devices  4.81 us (2%)
    pallas_call x1, Pallas kernels, sum_and_exchange(): pl.pallas_call(functools.partial(exchange_kernel, n, m), out_shape=(jax.S...  55.9 us
    all_gather x1, waiting for transfers between devices, body(): normed_all = lax.all_gather(normed, 'seq', axis=0, tiled=True)  50.4 us
    pallas_call x1, Pallas kernels, attention_backward(): pl.pallas_call(attn_bwd_kernel, out_shape=tuple((jax.ShapeDtypeStruct((n,...  39.5 us
    pallas_call x1, Pallas kernels, attention_forward(): pl.pallas_call(attn_fwd_kernel, out_shape=(jax.ShapeDtypeStruct((n, width...  24.2 us
    all_gather x1, waiting for transfers between devices, body(): cotan_all = lax.all_gather(cotan, 'seq', axis=0, tiled=True)  15.6 us
    dot_general x2, matrix products, contract_rows(): lax.dot_general(left_cols, right_cols, (((0,), (0,)), ((), ())), preferre...  13.8 us
    dot_general x1, matrix products, body(): jnp.dot(normed_all, w_heads, preferred_element_type=jnp.float32)  8.26 us
    unnamed x36, local copies, waits for them, and re-layouts  8.07 us
  transfers between devices with their start and end apart: 3, of which 3 were waited for; matrix products, arithmetic and copies ran while one was open for 8% of the time, Pallas kernels for 9%

profile of v10, /device:TPU:0, one launch (start us, length us, event | category | flops | bytes accessed | tf_op | source)
XLA Modules:
  0.0 261.0 jit_solution(8420131122356282252)
XLA Ops:
  7.2 1.6 convert_reduce_fusion
  8.8 1.6 fusion.11
  10.5 1.3 fusion.5
  11.9 0.7 all-gather.5.cloned.1.call-update
  12.9 1.2 constant_dynamic-slice_fusion.3
  14.1 50.4 %all-gather.3.cloned.1.call-done = bf16[4096,1024]{1,0:T(8,128)(2,1)} async-done(((bf16[512,1024]{1,0:T(8,128)(2,1)}), bf16[4096,1024]{1,0:T(8,128)(2,1)}) %all-gather.3.cloned.1.call-update) | async-done | bytes 8388624 | tf_op jit(solution)/shard_map/all_gather | solution.py:375
  64.5 8.3 %convolution_convert_fusion = bf16[4096,384]{1,0:T(8,128)(2,1)S(1)} fusion(bf16[4096,1024]{1,0:T(8,128)(2,1)} %all-gather.3.cloned.1.call-done, bf16[1024,128]{1,0:T(8,128)(2,1)S(1)} %get-tuple-element.24, bf16[1024,128]{1,0:T(8,128)(2,1)S(1)} %get-tuple-element.23, bf16[1024,128]{1,0:T(8,128)(2,1)S(1)} %get-tuple-element.22), kind=kOutput, calls=%fused_computation | convolution fusion | flops 3225157632 | bytes 12320768 | tf_op jit(solution)/shard_map/dot_general | solution.py:384
  72.7 0.5 fusion.19
  73.4 24.2 %shard_map.102 = (bf16[4096,128]{1,0:T(8,128)(2,1)S(1)}, f32[8192,128]{1,0:T(8,128)}) custom-call(s32[256]{0:T(256)S(1)} %reshape_squeeze.3.cols_ref, s32[32]{0:T(128)S(1)} %bitcast.27, bf16[4096,128]{1,0:T(8,128)(2,1)S(1)} %get-tuple-element.27.q_ref, bf16[4096,128]{1,0:T(8,128)(2,1)S(1)} %get-tuple-element.26.k_ref, ...), custom_call_target="tpu_custom_call" | custom-call | tf_op jit(solution)/shard_map/pallas_call | solution.py:190
  97.6 1.0 copy-done.3
  98.6 1.0 copy-done.4
  99.6 1.0 copy-done.6
  100.5 15.6 %all-gather.5.cloned.1.call-done.cotan_ref = bf16[4096,1024]{1,0:T(8,128)(2,1)} async-done(((bf16[512,1024]{1,0:T(8,128)(2,1)}), bf16[4096,1024]{1,0:T(8,128)(2,1)}) %all-gather.5.cloned.1.call-update) | async-done | bytes 8388624 | tf_op jit(solution)/shard_map/all_gather | solution.py:376
  116.2 5.5 %fusion.21 = f32[128,1024]{1,0:T(8,128)} fusion(bf16[4096,128]{1,0:T(8,128)(2,1)S(1)} %get-tuple-element.12.o_ref, bf16[4096,1024]{1,0:T(8,128)(2,1)} %all-gather.5.cloned.1.call-done.cotan_ref), kind=kOutput, calls=%fused_computation.39 | convolution fusion | flops 1073741824 | bytes 9961472 | tf_op jit(solution)/shard_map/dot_general | solution.py:28
  121.7 1.9 concatenate.17
  123.6 1.2 copy-done.5
  124.8 1.2 copy-done.7
  126.0 39.5 %shard_map.103 = (bf16[4096,128]{1,0:T(8,128)(2,1)S(1)}, bf16[4096,128]{1,0:T(8,128)(2,1)S(1)}, bf16[4096,128]{1,0:T(8,128)(2,1)S(1)}) custom-call(s32[256]{0:T(256)S(1)} %reshape_squeeze.3.cols_ref, s32[32]{0:T(128)S(1)} %bitcast.28, bf16[4096,128]{1,0:T(8,128)(2,1)S(1)} %copy-done.7, bf16[4096,128]{1,0:T(8,128)(2,1)S(1)} %copy-done.5, ...), custom_call_target="tpu_custom_call" | custom-call | tf_op jit(solution)/shard_map/pallas_call | solution.py:204
  165.7 0.2 constant_dynamic-update-slice_fusion.1
  166.0 0.2 constant_dynamic-update-slice_fusion
  166.3 8.3 %fusion.20 = f32[1024,384]{1,0:T(8,128)S(1)} fusion(bf16[4096,1024]{1,0:T(8,128)(2,1)} %all-gather.3.cloned.1.call-done, bf16[4096,384]{1,0:T(8,128)(2,1)S(1)} %constant_dynamic-update-slice_fusion), kind=kOutput, calls=%fused_computation.38 | convolution fusion | flops 3221225472 | bytes 13107200 | tf_op jit(solution)/shard_map/dot_general | solution.py:28
  174.8 1.0 copy-done.2
  175.8 55.9 %shard_map.104 = (bf16[16,64,512]{2,1,0:T(8,128)(2,1)S(1)}, bf16[512,3072]{1,0:T(8,128)(2,1)}, bf16[512,1024]{1,0:T(8,128)(2,1)S(1)}) custom-call(f32[16,64,512]{2,1,0:T(8,128)S(1)} %pad_maximum_fusion.x_ref, bf16[8,512,384]{2,1,0:T(8,128)(2,1)} %bitcast.29, bf16[8,512,128]{2,1,0:T(8,128)(2,1)S(1)} %bitcast.24), custom_call_target="tpu_custom_call" | custom-call | tf_op jit(solution)/shard_map/pallas_call | solution.py:345
  231.7 1.0 slice.23
  232.7 0.8 reshape.61
  233.5 4.7 %all-to-all-start = ((bf16[8,128,384]{2,1,0:T(8,128)(2,1)}), bf16[8,128,384]{2,1,0:T(8,128)(2,1)}, u32[]{:S(2)}, u32[]{:S(2)}) async-start(bf16[8,128,384]{2,1,0:T(8,128)(2,1)} %bitcast.31), calls=%async_computation | async-start | bytes 1572864 | tf_op jit(solution)/shard_map/all_to_all | solution.py:422
  238.3 7.7 %multiply_reduce_fusion = (f32[512]{0:T(512)S(1)}, f32[512]{0:T(512)S(1)}, f32[512,1024]{1,0:T(8,128)S(1)}) fusion(f32[1024]{0:T(1024)S(1)} %copy-done.14, f32[512]{0:T(512)S(1)} %add_rsqrt_fusion, f32[512]{0:T(512)S(1)} %broadcast_multiply_fusion.2, bf16[512,1024]{1,0:T(8,128)(2,1)} %param.7, bf16[512,3072]{1,0:T(8,128)(2,1)} %get-tuple-element.18, ...), kind=kOutput, calls=%fused_computation.18 | convolution fusion | flops 3224894464 | bytes 12595200 | tf_op jit(solution)/shard_map/dot_general | solution.py:410
  246.1 1.8 fusion.10
  247.9 2.2 fusion.12
  250.1 1.4 all-to-all-done
  251.5 1.6 copy.13
  253.1 1.0 copy.16
  (38 shorter events, 0.9 us)
Async XLA Ops:
  7.2 5.7 %copy-start = (bf16[1024,1024]{1,0:T(8,128)(2,1)S(1)}, bf16[1024,1024]{1,0:T(8,128)(2,1)}, u32[]{:S(2)}) copy-start(bf16[1024,1024]{1,0:T(8,128)(2,1)} %param.10) | copy-start | bytes 6291460
  7.2 3.3 %copy-start.10 = (bf16[512,1024]{1,0:T(8,128)(2,1)S(1)}, bf16[512,1024]{1,0:T(8,128)(2,1)}, u32[]{:S(2)}) copy-start(bf16[512,1024]{1,0:T(8,128)(2,1)} %param.7) | copy-start | bytes 3145732
  7.2 3.3 %copy-start.14 = (f32[1024]{0:T(1024)S(1)}, f32[1024]{0:T(1024)}, u32[]{:S(2)}) copy-start(f32[1024]{0:T(1024)} %param.8) | copy-start | bytes 12292
  7.2 57.2 %all-gather.3.cloned.1.call-start = ((), (), s32[]{:S(2)}) async-start(), calls=%async_computation.1 | async-start | bytes 9437184 | tf_op jit(solution)/shard_map/all_gather | solution.py:375
  10.5 2.1 copy-start.15
  11.9 104.3 %all-gather.5.cloned.1.call-start = ((), (), s32[]{:S(2)}) async-start(), calls=%async_computation.2 | async-start | bytes 9437184 | tf_op jit(solution)/shard_map/all_gather | solution.py:376
  72.7 0.7 copy-start.8
  97.6 1.0 copy-start.3
  98.6 1.0 copy-start.4
  99.5 1.0 copy-start.6
  100.5 21.2 %copy-start.1 = (bf16[4096,128]{1,0:T(8,128)(2,1)}, bf16[4096,128]{1,0:T(8,128)(2,1)S(1)}, u32[]{:S(2)}) copy-start(bf16[4096,128]{1,0:T(8,128)(2,1)S(1)} %get-tuple-element.12.o_ref) | copy-start | bytes 3145732
  123.6 1.2 copy-start.5
  124.8 1.2 copy-start.7
  166.2 8.3 %copy-start.9 = (bf16[4096,384]{1,0:T(8,128)(2,1)}, bf16[4096,384]{1,0:T(8,128)(2,1)S(1)}, u32[]{:S(2)}) copy-start(bf16[4096,384]{1,0:T(8,128)(2,1)S(1)} %constant_dynamic-update-slice_fusion) | copy-start | bytes 9437188
  166.3 8.3 %copy-start.13 = (f32[16,64,128]{2,1,0:T(8,128)S(1)}, f32[16,64,128]{2,1,0:T(8,128)}, u32[]{:S(2)}) copy-start(f32[16,64,128]{2,1,0:T(8,128)} %concatenate.17) | copy-start | bytes 1572868
  174.6 1.2 copy-start.2
  233.5 18.0 %all-to-all-start = ((bf16[8,128,384]{2,1,0:T(8,128)(2,1)}), bf16[8,128,384]{2,1,0:T(8,128)(2,1)}, u32[]{:S(2)}, u32[]{:S(2)}) async-start(bf16[8,128,384]{2,1,0:T(8,128)(2,1)} %bitcast.31), calls=%async_computation | async-start | bytes 1572864 | tf_op jit(solution)/shard_map/all_to_all | solution.py:422
  238.3 7.8 %copy-start.11 = (bf16[512,1024]{1,0:T(8,128)(2,1)S(1)}, bf16[512,1024]{1,0:T(8,128)(2,1)}, u32[]{:S(2)}) copy-start(bf16[512,1024]{1,0:T(8,128)(2,1)} %param.7) | copy-start | bytes 3145732
  238.3 7.8 %copy-start.12 = (bf16[512,1024]{1,0:T(8,128)(2,1)S(1)}, bf16[512,1024]{1,0:T(8,128)(2,1)}, u32[]{:S(2)}) copy-start(bf16[512,1024]{1,0:T(8,128)(2,1)} %param.13) | copy-start | bytes 3145732
Sparse Core Ops, SparseCore 0:
  12.0 52.3 all-gather.2
  66.2 49.9 all-gather.4

commit v11 on v9

--- a/solution.py
+++ b/solution.py
@@ -211,7 +211,24 @@
 
 
 def exchange_kernel(
-    n, m, x_ref, g_ref, a_ref, o_ref, moved_ref, att_ref, recv, gath, landed, att_landed, sems, a2a_sems
+    n,
+    m,
+    qkv_cols,
+    x_ref,
+    g_ref,
+    a_ref,
+    o_ref,
+    moved_ref,
+    att_ref,
+    qkv_ref,
+    recv,
+    gath,
+    landed,
+    att_landed,
+    qkv_landed,
+    sems,
+    a2a_sems,
+    qkv_sems,
 ):
     me = lax.axis_index("dp")
     here = lax.axis_index("seq")
@@ -302,6 +319,36 @@
     ag = (lambda peer: gath.at[me], gath, sems.at[2], sems.at[3], "dp", me, n)
     finish_all(start_all(*ag), *ag)
     o_ref[...] = gath[...]
+    halves = n // m
+    half_rows = gath.shape[1]
+
+    def qkv_copy(t, h, peer, sender, target):
+        return pltpu.make_async_remote_copy(
+            src_ref=gath.at[peer * halves + h, :, pl.ds(t * BLK, BLK)],
+            dst_ref=qkv_landed.at[
+                pl.ds(h * half_rows, half_rows),
+                pl.ds(pl.multiple_of(t * group + sender * BLK, BLK), BLK),
+            ],
+            send_sem=qkv_sems.at[0, t * halves + h, peer],
+            recv_sem=qkv_sems.at[1, t * halves + h, sender],
+            device_id={"seq": target},
+            device_id_type=MESH,
+        )
+
+    qkv_started = []
+    for k in range(1, m):
+        peer = lax.rem(here + k, m)
+        for t in range(qkv_cols // BLK):
+            for h in range(halves):
+                copy = qkv_copy(t, h, peer, here, peer)
+                copy.start()
+                qkv_started.append(copy)
+    for t in range(qkv_cols // BLK):
+        for h in range(halves):
+            qkv_landed[
+                pl.ds(h * half_rows, half_rows),
+                pl.ds(pl.multiple_of(t * group + here * BLK, BLK), BLK),
+            ] = gath[here * halves + h, :, t * BLK : (t + 1) * BLK]
     own = g_ref[here]
     for t in range(parts):
         landed[:, pl.ds(pl.multiple_of(t * group + here * BLK, BLK), BLK)] = own[
@@ -317,9 +364,17 @@
         copy.wait_send()
     moved_ref[...] = landed[...]
     att_ref[...] = att_landed[...]
-
-
-def sum_and_exchange(term, grads, attended_heads):
+    for k in range(1, m):
+        source = lax.rem(here + m - k, m)
+        for t in range(qkv_cols // BLK):
+            for h in range(halves):
+                qkv_copy(t, h, source, source, source).wait_recv()
+    for copy in qkv_started:
+        copy.wait_send()
+    qkv_ref[...] = qkv_landed[...]
+
+
+def sum_and_exchange(term, grads, attended_heads, qkv_cols):
     n = lax.axis_size("dp")
     m = lax.axis_size("seq")
     rows, cols = term.shape
@@ -329,28 +384,33 @@
     parts = grads.shape[1] // BLK
     final = (pieces.shape[1], parts * m * BLK)
     att_final = (att_pieces.shape[1], m * att_pieces.shape[2])
-    out, moved, attended = pl.pallas_call(
-        functools.partial(exchange_kernel, n, m),
+    qkv_final = (rows // m, (qkv_cols // BLK) * m * BLK)
+    halves = n // m
+    out, moved, attended, grad_qkv = pl.pallas_call(
+        functools.partial(exchange_kernel, n, m, qkv_cols),
         out_shape=(
             jax.ShapeDtypeStruct(chunked.shape, jnp.bfloat16),
             jax.ShapeDtypeStruct(final, pieces.dtype),
             jax.ShapeDtypeStruct(att_final, att_pieces.dtype),
+            jax.ShapeDtypeStruct(qkv_final, jnp.bfloat16),
         ),
         in_specs=[vmem_spec(), vmem_spec(), vmem_spec()],
-        out_specs=(vmem_spec(), vmem_spec(), vmem_spec()),
+        out_specs=(vmem_spec(), vmem_spec(), vmem_spec(), vmem_spec()),
         scratch_shapes=[
             pltpu.VMEM(chunked.shape, jnp.float32),
             pltpu.VMEM(chunked.shape, jnp.bfloat16),
             pltpu.VMEM(final, pieces.dtype),
             pltpu.VMEM(att_final, att_pieces.dtype),
+            pltpu.VMEM(qkv_final, jnp.bfloat16),
             pltpu.SemaphoreType.DMA((4, n)),
             pltpu.SemaphoreType.DMA((2, parts + 1, m)),
+            pltpu.SemaphoreType.DMA((2, (qkv_cols // BLK) * halves, m)),
         ],
         compiler_params=pltpu.CompilerParams(
             collective_id=0, has_side_effects=True, vmem_limit_bytes=VMEM_LIMIT
         ),
     )(chunked, pieces, att_pieces)
-    return out.reshape(rows, cols), moved, attended
+    return out.reshape(rows, cols), moved, attended, grad_qkv
 
 
 def body(feats, gain, w_qkv, w_out, block_cols, block_counts, cotan):
@@ -388,10 +448,11 @@
     term_qkv = contract_rows(normed_all, grad_heads_mixed)
     term_out = contract_rows(attended_heads, cotan_all)
     qkv_cols = term_qkv.shape[1]
-    summed, moved_grads, attended = sum_and_exchange(
+    summed, moved_grads, attended, grad_qkv = sum_and_exchange(
         jnp.concatenate([term_qkv, term_out.reshape(term_qkv.shape[0], -1)], axis=1),
         grad_heads_mixed,
         attended_heads,
+        qkv_cols,
     )
     result = (
         feats.astype(jnp.float32) + jnp.dot(attended, w_out, preferred_element_type=jnp.float32)
@@ -406,14 +467,7 @@
     grad_feats = (
         cotan.astype(jnp.float32) + inverse * (gained - mean_one - scaled * mean_two)
     ).astype(jnp.bfloat16)
-    term_qkv = summed[:, :qkv_cols]
-    term_out = summed[:, qkv_cols:].reshape(term_out.shape)
-    grad_qkv = regroup_columns(
-        lax.all_to_all(term_qkv, "seq", split_axis=0, concat_axis=1, tiled=True),
-        seq_count,
-        group_width,
-    )
-    grad_out = term_out
+    grad_out = summed[:, qkv_cols:].reshape(term_out.shape)
     return (result, grad_feats, grad_qkv, grad_out)
 
 

time: 258 us -> 260 us (level)
  Pallas kernels: 110 us -> 120 us
  starting transfers between devices: 4.81 us -> 0.08 us
  local copies, waits for them, and re-layouts: 13 us -> 10.3 us
    pallas_call x1, Pallas kernels: 55.7 us -> 65.1 us  [sum_and_exchange(): pl.pallas_call(functools.partial(exchange_kernel, n, m, qkv_cols), out_sh...]
    all_to_all x1 -> x0, starting transfers between devices: 4.73 us -> none  [body(): lax.all_to_all(term_qkv, 'seq', split_axis=0, concat_axis=1, tiled=True)]
    unnamed x36 -> x38, local copies, waits for them, and re-layouts: 5.63 us -> 5.49 us
  transfers between devices with their start and end apart: 3 -> 2, of which waited for: 3 -> 2; matrix products, arithmetic and copies ran while one was open for 9% -> 4% of each run, Pallas kernels for 9% -> 9%
where the time goes in v11:
time: 260 us; the launch traced here: 257 us
  Pallas kernels  120 us (46%)
  waiting for transfers between devices  66.8 us (26%)
  matrix products  38.8 us (15%)
  between operations  14.3 us (6%)
  local copies, waits for them, and re-layouts  10.3 us (4%)
  other arithmetic  6.63 us (3%)
    pallas_call x1, Pallas kernels, sum_and_exchange(): pl.pallas_call(functools.partial(exchange_kernel, n, m, qkv_cols), out_sh...  65.1 us
    all_gather x1, waiting for transfers between devices, body(): normed_all = lax.all_gather(normed, 'seq', axis=0, tiled=True)  50.4 us
    pallas_call x1, Pallas kernels, attention_backward(): pl.pallas_call(attn_bwd_kernel, out_shape=tuple((jax.ShapeDtypeStruct((n,...  31.1 us
    pallas_call x1, Pallas kernels, attention_forward(): pl.pallas_call(attn_fwd_kernel, out_shape=(jax.ShapeDtypeStruct((n, width...  24.3 us
    all_gather x1, waiting for transfers between devices, body(): cotan_all = lax.all_gather(cotan, 'seq', axis=0, tiled=True)  15.7 us
    dot_general x2, matrix products, contract_rows(): lax.dot_general(left_cols, right_cols, (((0,), (0,)), ((), ())), preferre...  13.7 us
    dot_general x1, matrix products, body(): jnp.dot(normed_all, w_heads, preferred_element_type=jnp.float32)  8.26 us
    dot_general x1, matrix products, body(): lax.dot_general(grad_mixed, w_qkv, (((1,), (1,)), ((), ())), preferred_el...  7.75 us
  transfers between devices with their start and end apart: 2, of which 2 were waited for; matrix products, arithmetic and copies ran while one was open for 4% of the time, Pallas kernels for 9%

profile of v11, /device:TPU:0, one launch (start us, length us, event | category | flops | bytes accessed | tf_op | source)
XLA Modules:
  0.0 257.4 jit_solution(4074640397424323934)
XLA Ops:
  7.2 1.6 convert_reduce_fusion
  8.8 1.6 fusion.12
  10.5 1.3 fusion.6
  11.9 0.7 all-gather.5.cloned.1.call-update
  12.7 0.1 copy.12
  12.7 0.1 reshape_squeeze.3.cols_ref
  12.8 1.2 constant_dynamic-slice_fusion.2
  14.0 50.4 %all-gather.3.cloned.1.call-done = bf16[4096,1024]{1,0:T(8,128)(2,1)} async-done(((bf16[512,1024]{1,0:T(8,128)(2,1)}), bf16[4096,1024]{1,0:T(8,128)(2,1)}) %all-gather.3.cloned.1.call-update) | async-done | bytes 8388624 | tf_op jit(solution)/shard_map/all_gather | solution.py:422
  64.5 8.3 %convolution_convert_fusion = bf16[4096,384]{1,0:T(8,128)(2,1)S(1)} fusion(bf16[4096,1024]{1,0:T(8,128)(2,1)} %all-gather.3.cloned.1.call-done, bf16[1024,128]{1,0:T(8,128)(2,1)S(1)} %get-tuple-element.26, bf16[1024,128]{1,0:T(8,128)(2,1)S(1)} %get-tuple-element.25, bf16[1024,128]{1,0:T(8,128)(2,1)S(1)} %get-tuple-element.24), kind=kOutput, calls=%fused_computation | convolution fusion | flops 3225157632 | bytes 12320768 | tf_op jit(solution)/shard_map/dot_general | solution.py:431
  72.7 0.5 fusion.22
  73.3 0.1 copy-done.8
  73.4 24.3 %shard_map.102 = (bf16[4096,128]{1,0:T(8,128)(2,1)S(1)}, f32[8192,128]{1,0:T(8,128)}) custom-call(s32[256]{0:T(256)S(1)} %reshape_squeeze.3.cols_ref, s32[32]{0:T(128)S(1)} %bitcast.19, bf16[4096,128]{1,0:T(8,128)(2,1)S(1)} %get-tuple-element.29.q_ref, bf16[4096,128]{1,0:T(8,128)(2,1)S(1)} %get-tuple-element.28.k_ref, ...), custom_call_target="tpu_custom_call" | custom-call | tf_op jit(solution)/shard_map/pallas_call | solution.py:177
  97.7 1.0 copy-done.3
  98.7 1.0 copy-done.4
  99.7 1.0 copy-done.6
  100.6 15.7 %all-gather.5.cloned.1.call-done = bf16[4096,1024]{1,0:T(8,128)(2,1)} async-done(((bf16[512,1024]{1,0:T(8,128)(2,1)}), bf16[4096,1024]{1,0:T(8,128)(2,1)}) %all-gather.5.cloned.1.call-update) | async-done | bytes 8388624 | tf_op jit(solution)/shard_map/all_gather | solution.py:423
  116.3 5.5 %fusion.24 = f32[128,1024]{1,0:T(8,128)} fusion(bf16[4096,128]{1,0:T(8,128)(2,1)S(1)} %get-tuple-element.13.o_ref, bf16[4096,1024]{1,0:T(8,128)(2,1)} %all-gather.5.cloned.1.call-done), kind=kOutput, calls=%fused_computation.41 | convolution fusion | flops 1073741824 | bytes 9961472 | tf_op jit(solution)/shard_map/dot_general | solution.py:28
  121.8 1.9 concatenate.17
  123.8 6.9 %fusion.do_ref = bf16[4096,128]{1,0:T(8,128)(2,1)} fusion(bf16[4096,1024]{1,0:T(8,128)(2,1)} %all-gather.5.cloned.1.call-done, bf16[1024,1024]{1,0:T(8,128)(2,1)S(1)} %copy-done, s32[]{:T(128)S(6)} %select_n.15), kind=kOutput, calls=%fused_computation.2 | convolution fusion | flops 1074266112 | bytes 9699332 | tf_op jit(solution)/shard_map/dot_general | solution.py:441
  130.7 31.1 %shard_map.103 = (bf16[4096,128]{1,0:T(8,128)(2,1)S(1)}, bf16[4096,128]{1,0:T(8,128)(2,1)S(1)}, bf16[4096,128]{1,0:T(8,128)(2,1)S(1)}) custom-call(s32[256]{0:T(256)S(1)} %reshape_squeeze.3.cols_ref, s32[32]{0:T(128)S(1)} %bitcast.20, bf16[4096,128]{1,0:T(8,128)(2,1)S(1)} %copy-done.7, bf16[4096,128]{1,0:T(8,128)(2,1)S(1)} %copy-done.5, ...), custom_call_target="tpu_custom_call" | custom-call | tf_op jit(solution)/shard_map/pallas_call | solution.py:191
  161.7 0.2 constant_dynamic-update-slice_fusion.2
  161.9 0.2 constant_dynamic-update-slice_fusion.1
  162.2 0.2 constant_dynamic-update-slice_fusion
  162.5 8.2 %fusion.23 = f32[1024,384]{1,0:T(8,128)S(1)} fusion(bf16[4096,1024]{1,0:T(8,128)(2,1)} %all-gather.3.cloned.1.call-done, bf16[4096,384]{1,0:T(8,128)(2,1)S(1)} %constant_dynamic-update-slice_fusion), kind=kOutput, calls=%fused_computation.40 | convolution fusion | flops 3221225472 | bytes 13107200 | tf_op jit(solution)/shard_map/dot_general | solution.py:28
  170.7 0.2 pad_maximum_fusion.x_ref
  170.9 1.0 copy-done.2
  171.9 65.1 %shard_map.104 = (bf16[16,64,512]{2,1,0:T(8,128)(2,1)S(1)}, bf16[512,3072]{1,0:T(8,128)(2,1)}, bf16[512,1024]{1,0:T(8,128)(2,1)S(1)}, bf16[128,3072]{1,0:T(8,128)(2,1)S(1)}) custom-call(f32[16,64,512]{2,1,0:T(8,128)S(1)} %pad_maximum_fusion.x_ref, bf16[8,512,384]{2,1,0:T(8,128)(2,1)} %bitcast.21, bf16[8,512,128]{2,1,0:T(8,128)(2,1)S(1)} %bitcast.17), custom_call_target="tpu_custom_call" | custom-call | tf_op jit(solution)/shard_map/pallas_call | solution.py:389
  237.0 2.2 fusion.13
  239.3 0.8 reshape.49
  240.1 7.7 %multiply_reduce_fusion = (f32[512]{0:T(512)S(1)}, f32[512]{0:T(512)S(1)}, f32[512,1024]{1,0:T(8,128)S(1)}) fusion(f32[1024]{0:T(1024)S(1)} %copy-done.15, f32[512]{0:T(512)S(1)} %add_rsqrt_fusion, f32[512]{0:T(512)S(1)} %broadcast_multiply_fusion.2, bf16[512,1024]{1,0:T(8,128)(2,1)} %param.7, bf16[512,3072]{1,0:T(8,128)(2,1)} %get-tuple-element.19, ...), kind=kOutput, calls=%fused_computation.20 | convolution fusion | flops 3224894464 | bytes 12595200 | tf_op jit(solution)/shard_map/dot_general | solution.py:461
  247.9 1.8 fusion.11
  249.7 0.9 copy.18
  (36 shorter events, 0.2 us)
Async XLA Ops:
  7.2 116.6 %copy-start = (bf16[1024,1024]{1,0:T(8,128)(2,1)S(1)}, bf16[1024,1024]{1,0:T(8,128)(2,1)}, u32[]{:S(2)}) copy-start(bf16[1024,1024]{1,0:T(8,128)(2,1)} %param.10) | copy-start | bytes 6291460
  7.2 3.3 %copy-start.10 = (bf16[512,1024]{1,0:T(8,128)(2,1)S(1)}, bf16[512,1024]{1,0:T(8,128)(2,1)}, u32[]{:S(2)}) copy-start(bf16[512,1024]{1,0:T(8,128)(2,1)} %param.7) | copy-start | bytes 3145732
  7.2 3.3 %copy-start.15 = (f32[1024]{0:T(1024)S(1)}, f32[1024]{0:T(1024)}, u32[]{:S(2)}) copy-start(f32[1024]{0:T(1024)} %param.8) | copy-start | bytes 12292
  7.2 57.2 %all-gather.3.cloned.1.call-start = ((), (), s32[]{:S(2)}) async-start(), calls=%async_computation | async-start | bytes 9437184 | tf_op jit(solution)/shard_map/all_gather | solution.py:422
  10.5 2.1 copy-start.16
  11.9 104.4 %all-gather.5.cloned.1.call-start = ((), (), s32[]{:S(2)}) async-start(), calls=%async_computation.1 | async-start | bytes 9437184 | tf_op jit(solution)/shard_map/all_gather | solution.py:423
  72.7 0.7 copy-start.8
  97.7 1.0 copy-start.3
  98.7 1.0 copy-start.4
  99.7 1.0 copy-start.6
  100.6 21.2 %copy-start.1 = (bf16[4096,128]{1,0:T(8,128)(2,1)}, bf16[4096,128]{1,0:T(8,128)(2,1)S(1)}, u32[]{:S(2)}) copy-start(bf16[4096,128]{1,0:T(8,128)(2,1)S(1)} %get-tuple-element.13.o_ref) | copy-start | bytes 3145732
  123.8 6.9 %copy-start.5 = (bf16[4096,128]{1,0:T(8,128)(2,1)S(1)}, bf16[4096,128]{1,0:T(8,128)(2,1)}, u32[]{:S(2)}) copy-start(bf16[4096,128]{1,0:T(8,128)(2,1)} %copy-done.4) | copy-start | bytes 3145732
  123.8 6.9 %copy-start.7 = (bf16[4096,128]{1,0:T(8,128)(2,1)S(1)}, bf16[4096,128]{1,0:T(8,128)(2,1)}, u32[]{:S(2)}) copy-start(bf16[4096,128]{1,0:T(8,128)(2,1)} %copy-done.6) | copy-start | bytes 3145732
  162.4 8.2 %copy-start.9 = (bf16[4096,384]{1,0:T(8,128)(2,1)}, bf16[4096,384]{1,0:T(8,128)(2,1)S(1)}, u32[]{:S(2)}) copy-start(bf16[4096,384]{1,0:T(8,128)(2,1)S(1)} %constant_dynamic-update-slice_fusion) | copy-start | bytes 9437188
  162.5 8.2 %copy-start.14 = (f32[16,64,128]{2,1,0:T(8,128)S(1)}, f32[16,64,128]{2,1,0:T(8,128)}, u32[]{:S(2)}) copy-start(f32[16,64,128]{2,1,0:T(8,128)} %concatenate.17) | copy-start | bytes 1572868
  170.7 1.2 copy-start.2
  171.9 65.1 %copy-start.11 = (bf16[512,1024]{1,0:T(8,128)(2,1)S(1)}, bf16[512,1024]{1,0:T(8,128)(2,1)}, u32[]{:S(2)}) copy-start(bf16[512,1024]{1,0:T(8,128)(2,1)} %param.7) | copy-start | bytes 3145732
  240.1 7.8 %copy-start.12 = (bf16[512,1024]{1,0:T(8,128)(2,1)S(1)}, bf16[512,1024]{1,0:T(8,128)(2,1)}, u32[]{:S(2)}) copy-start(bf16[512,1024]{1,0:T(8,128)(2,1)} %param.7) | copy-start | bytes 3145732
  240.1 7.8 %copy-start.13 = (bf16[512,1024]{1,0:T(8,128)(2,1)S(1)}, bf16[512,1024]{1,0:T(8,128)(2,1)}, u32[]{:S(2)}) copy-start(bf16[512,1024]{1,0:T(8,128)(2,1)} %param.13) | copy-start | bytes 3145732
Sparse Core Ops, SparseCore 0:
  12.0 52.3 all-gather.2
  66.2 50.1 all-gather.4

commit v12 on v11

--- a/solution.py
+++ b/solution.py
@@ -233,15 +233,13 @@
     me = lax.axis_index("dp")
     here = lax.axis_index("seq")
     barrier = pltpu.get_barrier_semaphore()
-    for k in range(1, n):
+    flat = me * m + here
+    for k in range(1, n * m):
+        other = lax.rem(flat + k, n * m)
         pl.semaphore_signal(
-            barrier, inc=1, device_id={"dp": lax.rem(me + k, n)}, device_id_type=MESH
+            barrier, inc=1, device_id=(other // m, lax.rem(other, m)), device_id_type=MESH
         )
-    for k in range(1, m):
-        pl.semaphore_signal(
-            barrier, inc=1, device_id={"seq": lax.rem(here + k, m)}, device_id_type=MESH
-        )
-    pl.semaphore_wait(barrier, n - 1 + m - 1)
+    pl.semaphore_wait(barrier, n * m - 1)
 
     def start_all(src_of, dst, send, arrive, axis, at, size):
         started = []
@@ -316,39 +314,48 @@
     for k in range(1, n):
         total = total + recv[lax.rem(me + k, n)]
     gath[me] = total.astype(gath.dtype)
+    halves = n // m
+    half_rows = gath.shape[1]
+    owner = me // halves
+    lower = lax.rem(me, halves)
+    qkv_parts = qkv_cols // BLK
+
+    def qkv_copy(t, target_dp, src_dp, row_half, sender_seq, target_seq):
+        return pltpu.make_async_remote_copy(
+            src_ref=gath.at[src_dp, :, pl.ds(t * BLK, BLK)],
+            dst_ref=qkv_landed.at[
+                pl.ds(pl.multiple_of(row_half * half_rows, half_rows), half_rows),
+                pl.ds(pl.multiple_of(t * group + sender_seq * BLK, BLK), BLK),
+            ],
+            send_sem=qkv_sems.at[0, t, target_dp],
+            recv_sem=qkv_sems.at[1, t * halves + row_half, sender_seq],
+            device_id=(target_dp, target_seq),
+            device_id_type=MESH,
+        )
+
+    not_self = owner != here
+    qkv_started = []
+    for k in range(n):
+        target_dp = lax.rem(me + k, n)
+        for t in range(qkv_parts):
+            copy = qkv_copy(t, target_dp, me, lower, here, owner)
+            if k == 0:
+                pl.when(not_self)(copy.start)
+            else:
+                copy.start()
+            qkv_started.append((k, copy))
+
+    @pl.when(owner == here)
+    def _():
+        for t in range(qkv_parts):
+            qkv_landed[
+                pl.ds(pl.multiple_of(lower * half_rows, half_rows), half_rows),
+                pl.ds(pl.multiple_of(t * group + here * BLK, BLK), BLK),
+            ] = gath[me, :, t * BLK : (t + 1) * BLK]
+
     ag = (lambda peer: gath.at[me], gath, sems.at[2], sems.at[3], "dp", me, n)
     finish_all(start_all(*ag), *ag)
     o_ref[...] = gath[...]
-    halves = n // m
-    half_rows = gath.shape[1]
-
-    def qkv_copy(t, h, peer, sender, target):
-        return pltpu.make_async_remote_copy(
-            src_ref=gath.at[peer * halves + h, :, pl.ds(t * BLK, BLK)],
-            dst_ref=qkv_landed.at[
-                pl.ds(h * half_rows, half_rows),
-                pl.ds(pl.multiple_of(t * group + sender * BLK, BLK), BLK),
-            ],
-            send_sem=qkv_sems.at[0, t * halves + h, peer],
-            recv_sem=qkv_sems.at[1, t * halves + h, sender],
-            device_id={"seq": target},
-            device_id_type=MESH,
-        )
-
-    qkv_started = []
-    for k in range(1, m):
-        peer = lax.rem(here + k, m)
-        for t in range(qkv_cols // BLK):
-            for h in range(halves):
-                copy = qkv_copy(t, h, peer, here, peer)
-                copy.start()
-                qkv_started.append(copy)
-    for t in range(qkv_cols // BLK):
-        for h in range(halves):
-            qkv_landed[
-                pl.ds(h * half_rows, half_rows),
-                pl.ds(pl.multiple_of(t * group + here * BLK, BLK), BLK),
-            ] = gath[here * halves + h, :, t * BLK : (t + 1) * BLK]
     own = g_ref[here]
     for t in range(parts):
         landed[:, pl.ds(pl.multiple_of(t * group + here * BLK, BLK), BLK)] = own[
@@ -364,13 +371,21 @@
         copy.wait_send()
     moved_ref[...] = landed[...]
     att_ref[...] = att_landed[...]
-    for k in range(1, m):
-        source = lax.rem(here + m - k, m)
-        for t in range(qkv_cols // BLK):
-            for h in range(halves):
-                qkv_copy(t, h, source, source, source).wait_recv()
-    for copy in qkv_started:
-        copy.wait_send()
+    for h in range(halves):
+        source_dp = here * halves + h
+        for k in range(m):
+            source_seq = lax.rem(here + k, m)
+            for t in range(qkv_parts):
+                copy = qkv_copy(t, me, source_dp, h, source_seq, here)
+                if k == 0:
+                    pl.when(source_dp != me)(copy.wait_recv)
+                else:
+                    copy.wait_recv()
+    for k, copy in qkv_started:
+        if k == 0:
+            pl.when(not_self)(copy.wait_send)
+        else:
+            copy.wait_send()
     qkv_ref[...] = qkv_landed[...]
 
 
@@ -404,7 +419,7 @@
             pltpu.VMEM(qkv_final, jnp.bfloat16),
             pltpu.SemaphoreType.DMA((4, n)),
             pltpu.SemaphoreType.DMA((2, parts + 1, m)),
-            pltpu.SemaphoreType.DMA((2, (qkv_cols // BLK) * halves, m)),
+            pltpu.SemaphoreType.DMA((2, (qkv_cols // BLK) * halves, max(n, m))),
         ],
         compiler_params=pltpu.CompilerParams(
             collective_id=0, has_side_effects=True, vmem_limit_bytes=VMEM_LIMIT

time: 260 us -> 265 us (1.019)
  Pallas kernels: 120 us -> 126 us
    pallas_call x1, Pallas kernels: 65.1 us -> 72.8 us  [sum_and_exchange(): pl.pallas_call(functools.partial(exchange_kernel, n, m, qkv_cols), out_sh...]
where the time goes in v12:
time: 265 us; the launch traced here: 264 us
  Pallas kernels  126 us (48%)
  waiting for transfers between devices  67.4 us (25%)
  matrix products  38.8 us (15%)
  between operations  14.3 us (5%)
  local copies, waits for them, and re-layouts  10.3 us (4%)
  other arithmetic  6.63 us (3%)
    pallas_call x1, Pallas kernels, sum_and_exchange(): pl.pallas_call(functools.partial(exchange_kernel, n, m, qkv_cols), out_sh...  72.8 us
    all_gather x1, waiting for transfers between devices, body(): normed_all = lax.all_gather(normed, 'seq', axis=0, tiled=True)  50.4 us
    pallas_call x1, Pallas kernels, attention_backward(): pl.pallas_call(attn_bwd_kernel, out_shape=tuple((jax.ShapeDtypeStruct((n,...  30 us
    pallas_call x1, Pallas kernels, attention_forward(): pl.pallas_call(attn_fwd_kernel, out_shape=(jax.ShapeDtypeStruct((n, width...  23.5 us
    all_gather x1, waiting for transfers between devices, body(): cotan_all = lax.all_gather(cotan, 'seq', axis=0, tiled=True)  16.3 us
    dot_general x2, matrix products, contract_rows(): lax.dot_general(left_cols, right_cols, (((0,), (0,)), ((), ())), preferre...  13.7 us
    dot_general x1, matrix products, body(): jnp.dot(normed_all, w_heads, preferred_element_type=jnp.float32)  8.26 us
    dot_general x1, matrix products, body(): lax.dot_general(grad_mixed, w_qkv, (((1,), (1,)), ((), ())), preferred_el...  7.74 us
  transfers between devices with their start and end apart: 2, of which 2 were waited for; matrix products, arithmetic and copies ran while one was open for 4% of the time, Pallas kernels for 9%

profile of v12, /device:TPU:0, one launch (start us, length us, event | category | flops | bytes accessed | tf_op | source)
XLA Modules:
  0.0 263.9 jit_solution(2120406984042236698)
XLA Ops:
  7.2 1.6 convert_reduce_fusion
  8.8 1.6 fusion.12
  10.5 1.3 fusion.6
  11.9 0.7 all-gather.5.cloned.1.call-update
  12.7 0.1 copy.12
  12.7 0.1 reshape_squeeze.3.cols_ref
  12.8 1.2 constant_dynamic-slice_fusion.2
  14.0 50.4 %all-gather.3.cloned.1.call-done = bf16[4096,1024]{1,0:T(8,128)(2,1)} async-done(((bf16[512,1024]{1,0:T(8,128)(2,1)}), bf16[4096,1024]{1,0:T(8,128)(2,1)}) %all-gather.3.cloned.1.call-update) | async-done | bytes 8388624 | tf_op jit(solution)/shard_map/all_gather | solution.py:437
  64.5 8.3 %convolution_convert_fusion = bf16[4096,384]{1,0:T(8,128)(2,1)S(1)} fusion(bf16[4096,1024]{1,0:T(8,128)(2,1)} %all-gather.3.cloned.1.call-done, bf16[1024,128]{1,0:T(8,128)(2,1)S(1)} %get-tuple-element.26, bf16[1024,128]{1,0:T(8,128)(2,1)S(1)} %get-tuple-element.25, bf16[1024,128]{1,0:T(8,128)(2,1)S(1)} %get-tuple-element.24), kind=kOutput, calls=%fused_computation | convolution fusion | flops 3225157632 | bytes 12320768 | tf_op jit(solution)/shard_map/dot_general | solution.py:446
  72.7 0.5 fusion.22
  73.3 0.1 copy-done.8
  73.4 23.5 %shard_map.102 = (bf16[4096,128]{1,0:T(8,128)(2,1)S(1)}, f32[8192,128]{1,0:T(8,128)}) custom-call(s32[256]{0:T(256)S(1)} %reshape_squeeze.3.cols_ref, s32[32]{0:T(128)S(1)} %bitcast.19, bf16[4096,128]{1,0:T(8,128)(2,1)S(1)} %get-tuple-element.29.q_ref, bf16[4096,128]{1,0:T(8,128)(2,1)S(1)} %get-tuple-element.28.k_ref, ...), custom_call_target="tpu_custom_call" | custom-call | tf_op jit(solution)/shard_map/pallas_call | solution.py:177
  96.9 1.0 copy-done.3
  97.9 1.0 copy-done.4
  98.9 1.0 copy-done.6
  99.9 16.3 %all-gather.5.cloned.1.call-done = bf16[4096,1024]{1,0:T(8,128)(2,1)} async-done(((bf16[512,1024]{1,0:T(8,128)(2,1)}), bf16[4096,1024]{1,0:T(8,128)(2,1)}) %all-gather.5.cloned.1.call-update) | async-done | bytes 8388624 | tf_op jit(solution)/shard_map/all_gather | solution.py:438
  116.2 5.5 %fusion.24 = f32[128,1024]{1,0:T(8,128)} fusion(bf16[4096,128]{1,0:T(8,128)(2,1)S(1)} %get-tuple-element.13.o_ref, bf16[4096,1024]{1,0:T(8,128)(2,1)} %all-gather.5.cloned.1.call-done), kind=kOutput, calls=%fused_computation.41 | convolution fusion | flops 1073741824 | bytes 9961472 | tf_op jit(solution)/shard_map/dot_general | solution.py:28
  121.7 1.9 concatenate.17
  123.6 6.9 %fusion.do_ref = bf16[4096,128]{1,0:T(8,128)(2,1)} fusion(bf16[4096,1024]{1,0:T(8,128)(2,1)} %all-gather.5.cloned.1.call-done, bf16[1024,1024]{1,0:T(8,128)(2,1)S(1)} %copy-done, s32[]{:T(128)S(6)} %select_n.15), kind=kOutput, calls=%fused_computation.2 | convolution fusion | flops 1074266112 | bytes 9699332 | tf_op jit(solution)/shard_map/dot_general | solution.py:456
  130.5 30.0 %shard_map.103 = (bf16[4096,128]{1,0:T(8,128)(2,1)S(1)}, bf16[4096,128]{1,0:T(8,128)(2,1)S(1)}, bf16[4096,128]{1,0:T(8,128)(2,1)S(1)}) custom-call(s32[256]{0:T(256)S(1)} %reshape_squeeze.3.cols_ref, s32[32]{0:T(128)S(1)} %bitcast.20, bf16[4096,128]{1,0:T(8,128)(2,1)S(1)} %copy-done.7, bf16[4096,128]{1,0:T(8,128)(2,1)S(1)} %copy-done.5, ...), custom_call_target="tpu_custom_call" | custom-call | tf_op jit(solution)/shard_map/pallas_call | solution.py:191
  160.5 0.2 constant_dynamic-update-slice_fusion.2
  160.7 0.2 constant_dynamic-update-slice_fusion.1
  160.9 0.2 constant_dynamic-update-slice_fusion
  161.2 8.2 %fusion.23 = f32[1024,384]{1,0:T(8,128)S(1)} fusion(bf16[4096,1024]{1,0:T(8,128)(2,1)} %all-gather.3.cloned.1.call-done, bf16[4096,384]{1,0:T(8,128)(2,1)S(1)} %constant_dynamic-update-slice_fusion), kind=kOutput, calls=%fused_computation.40 | convolution fusion | flops 3221225472 | bytes 13107200 | tf_op jit(solution)/shard_map/dot_general | solution.py:28
  169.5 0.2 pad_maximum_fusion.x_ref
  169.7 1.0 copy-done.2
  170.7 72.8 %shard_map.104 = (bf16[16,64,512]{2,1,0:T(8,128)(2,1)S(1)}, bf16[512,3072]{1,0:T(8,128)(2,1)}, bf16[512,1024]{1,0:T(8,128)(2,1)S(1)}, bf16[128,3072]{1,0:T(8,128)(2,1)S(1)}) custom-call(f32[16,64,512]{2,1,0:T(8,128)S(1)} %pad_maximum_fusion.x_ref, bf16[8,512,384]{2,1,0:T(8,128)(2,1)} %bitcast.21, bf16[8,512,128]{2,1,0:T(8,128)(2,1)S(1)} %bitcast.17), custom_call_target="tpu_custom_call" | custom-call | tf_op jit(solution)/shard_map/pallas_call | solution.py:404
  243.5 2.2 fusion.13
  245.8 0.8 reshape.49
  246.6 7.7 %multiply_reduce_fusion = (f32[512]{0:T(512)S(1)}, f32[512]{0:T(512)S(1)}, f32[512,1024]{1,0:T(8,128)S(1)}) fusion(f32[1024]{0:T(1024)S(1)} %copy-done.15, f32[512]{0:T(512)S(1)} %add_rsqrt_fusion, f32[512]{0:T(512)S(1)} %broadcast_multiply_fusion.2, bf16[512,1024]{1,0:T(8,128)(2,1)} %param.7, bf16[512,3072]{1,0:T(8,128)(2,1)} %get-tuple-element.19, ...), kind=kOutput, calls=%fused_computation.20 | convolution fusion | flops 3224894464 | bytes 12595200 | tf_op jit(solution)/shard_map/dot_general | solution.py:476
  254.4 1.8 fusion.11
  256.2 0.9 copy.18
  (36 shorter events, 0.2 us)
Async XLA Ops:
  7.2 116.4 %copy-start = (bf16[1024,1024]{1,0:T(8,128)(2,1)S(1)}, bf16[1024,1024]{1,0:T(8,128)(2,1)}, u32[]{:S(2)}) copy-start(bf16[1024,1024]{1,0:T(8,128)(2,1)} %param.10) | copy-start | bytes 6291460
  7.2 3.3 %copy-start.10 = (bf16[512,1024]{1,0:T(8,128)(2,1)S(1)}, bf16[512,1024]{1,0:T(8,128)(2,1)}, u32[]{:S(2)}) copy-start(bf16[512,1024]{1,0:T(8,128)(2,1)} %param.7) | copy-start | bytes 3145732
  7.2 3.3 %copy-start.15 = (f32[1024]{0:T(1024)S(1)}, f32[1024]{0:T(1024)}, u32[]{:S(2)}) copy-start(f32[1024]{0:T(1024)} %param.8) | copy-start | bytes 12292
  7.2 57.2 %all-gather.3.cloned.1.call-start = ((), (), s32[]{:S(2)}) async-start(), calls=%async_computation | async-start | bytes 9437184 | tf_op jit(solution)/shard_map/all_gather | solution.py:437
  10.5 2.1 copy-start.16
  11.9 104.3 %all-gather.5.cloned.1.call-start = ((), (), s32[]{:S(2)}) async-start(), calls=%async_computation.1 | async-start | bytes 9437184 | tf_op jit(solution)/shard_map/all_gather | solution.py:438
  72.7 0.7 copy-start.8
  96.9 1.0 copy-start.3
  97.9 1.0 copy-start.4
  98.9 1.0 copy-start.6
  99.9 21.8 %copy-start.1 = (bf16[4096,128]{1,0:T(8,128)(2,1)}, bf16[4096,128]{1,0:T(8,128)(2,1)S(1)}, u32[]{:S(2)}) copy-start(bf16[4096,128]{1,0:T(8,128)(2,1)S(1)} %get-tuple-element.13.o_ref) | copy-start | bytes 3145732
  123.6 6.9 %copy-start.5 = (bf16[4096,128]{1,0:T(8,128)(2,1)S(1)}, bf16[4096,128]{1,0:T(8,128)(2,1)}, u32[]{:S(2)}) copy-start(bf16[4096,128]{1,0:T(8,128)(2,1)} %copy-done.4) | copy-start | bytes 3145732
  123.6 6.9 %copy-start.7 = (bf16[4096,128]{1,0:T(8,128)(2,1)S(1)}, bf16[4096,128]{1,0:T(8,128)(2,1)}, u32[]{:S(2)}) copy-start(bf16[4096,128]{1,0:T(8,128)(2,1)} %copy-done.6) | copy-start | bytes 3145732
  161.2 8.2 %copy-start.9 = (bf16[4096,384]{1,0:T(8,128)(2,1)}, bf16[4096,384]{1,0:T(8,128)(2,1)S(1)}, u32[]{:S(2)}) copy-start(bf16[4096,384]{1,0:T(8,128)(2,1)S(1)} %constant_dynamic-update-slice_fusion) | copy-start | bytes 9437188
  161.2 8.2 %copy-start.14 = (f32[16,64,128]{2,1,0:T(8,128)S(1)}, f32[16,64,128]{2,1,0:T(8,128)}, u32[]{:S(2)}) copy-start(f32[16,64,128]{2,1,0:T(8,128)} %concatenate.17) | copy-start | bytes 1572868
  169.5 1.2 copy-start.2
  170.7 72.8 %copy-start.11 = (bf16[512,1024]{1,0:T(8,128)(2,1)S(1)}, bf16[512,1024]{1,0:T(8,128)(2,1)}, u32[]{:S(2)}) copy-start(bf16[512,1024]{1,0:T(8,128)(2,1)} %param.7) | copy-start | bytes 3145732
  246.6 7.8 %copy-start.12 = (bf16[512,1024]{1,0:T(8,128)(2,1)S(1)}, bf16[512,1024]{1,0:T(8,128)(2,1)}, u32[]{:S(2)}) copy-start(bf16[512,1024]{1,0:T(8,128)(2,1)} %param.7) | copy-start | bytes 3145732
  246.6 7.8 %copy-start.13 = (bf16[512,1024]{1,0:T(8,128)(2,1)S(1)}, bf16[512,1024]{1,0:T(8,128)(2,1)}, u32[]{:S(2)}) copy-start(bf16[512,1024]{1,0:T(8,128)(2,1)} %param.13) | copy-start | bytes 3145732
Sparse Core Ops, SparseCore 0:
  12.0 52.3 all-gather.2
  66.2 49.9 all-gather.4

commit v13 on v9

--- a/solution.py
+++ b/solution.py
@@ -133,17 +133,19 @@
             delta = jnp.concatenate(
                 [jnp.sum(jnp.where(m, prod, 0.0), axis=1, keepdims=True) for m in masks], axis=0
             )
-            lse = lse_ref[pl.ds(pl.multiple_of(r * rows, rows), rows), :][:, 0:1]
+            lse_t = jnp.transpose(lse_ref[pl.ds(pl.multiple_of(r * rows, rows), rows), :])[0:1, :]
+            delta_t = jnp.transpose(jnp.broadcast_to(delta, (rows, BLK)))[0:1, :]
+            live_t = lax.broadcasted_iota(jnp.int32, (slots * BLK, 1), 0) < cnt * BLK
             kc = gather_blocks(k_ref, cols_ref, r, slots)
             vc = gather_blocks(v_ref, cols_ref, r, slots)
-            sc = nt_dot(q2, kc) * SCALE
-            p = jnp.where(live, jnp.exp(sc - lse), 0.0).astype(jnp.bfloat16)
-            dp = nt_dot(do2, vc)
-            ds = (p.astype(jnp.float32) * (dp - delta) * SCALE).astype(jnp.bfloat16)
-            dq = jnp.dot(ds, kc, preferred_element_type=jnp.float32)
+            sc_t = nt_dot(kc, q2) * SCALE
+            p_t = jnp.where(live_t, jnp.exp(sc_t - lse_t), 0.0).astype(jnp.bfloat16)
+            dp_t = nt_dot(vc, do2)
+            ds_t = (p_t.astype(jnp.float32) * (dp_t - delta_t) * SCALE).astype(jnp.bfloat16)
+            dq = tn_dot(ds_t, kc)
             dq_ref[pl.ds(row0, BLK), :] = unstack_heads(dq, masks).astype(dq_ref.dtype)
-            dkc = tn_dot(ds, q2)
-            dvc = tn_dot(p, do2)
+            dkc = jnp.dot(ds_t, q2, preferred_element_type=jnp.float32)
+            dvc = jnp.dot(p_t, do2, preferred_element_type=jnp.float32)
             for s in range(slots):
 
                 @pl.when(s < cnt)

time: 258 us -> 263 us (1.019)
  Pallas kernels: 110 us -> 115 us
    pallas_call x1, Pallas kernels: 30.6 us -> 35 us  [attention_backward(): pl.pallas_call(attn_bwd_kernel, out_shape=tuple((jax.ShapeDtypeStruct((n,...]
  transfers between devices with their start and end apart: 3 -> 3, of which waited for: 3 -> 3; matrix products, arithmetic and copies ran while one was open for 9% -> 8% of each run, Pallas kernels for 9% -> 9%
where the time goes in v13:
time: 263 us; the launch traced here: 262 us
  Pallas kernels  115 us (44%)
  waiting for transfers between devices  68.9 us (26%)
  matrix products  38.8 us (15%)
  between operations  14.3 us (5%)
  local copies, waits for them, and re-layouts  13 us (5%)
  other arithmetic  6.63 us (3%)
  starting transfers between devices  4.81 us (2%)
    pallas_call x1, Pallas kernels, sum_and_exchange(): pl.pallas_call(functools.partial(exchange_kernel, n, m), out_shape=(jax.S...  56.7 us
    all_gather x1, waiting for transfers between devices, body(): normed_all = lax.all_gather(normed, 'seq', axis=0, tiled=True)  50.4 us
    pallas_call x1, Pallas kernels, attention_backward(): pl.pallas_call(attn_bwd_kernel, out_shape=tuple((jax.ShapeDtypeStruct((n,...  35 us
    pallas_call x1, Pallas kernels, attention_forward(): pl.pallas_call(attn_fwd_kernel, out_shape=(jax.ShapeDtypeStruct((n, width...  23.5 us
    all_gather x1, waiting for transfers between devices, body(): cotan_all = lax.all_gather(cotan, 'seq', axis=0, tiled=True)  16.3 us
    dot_general x2, matrix products, contract_rows(): lax.dot_general(left_cols, right_cols, (((0,), (0,)), ((), ())), preferre...  13.7 us
    dot_general x1, matrix products, body(): jnp.dot(normed_all, w_heads, preferred_element_type=jnp.float32)  8.27 us
    dot_general x1, matrix products, body(): lax.dot_general(grad_mixed, w_qkv, (((1,), (1,)), ((), ())), preferred_el...  7.74 us
  transfers between devices with their start and end apart: 3, of which 3 were waited for; matrix products, arithmetic and copies ran while one was open for 8% of the time, Pallas kernels for 9%

profile of v13, /device:TPU:0, one launch (start us, length us, event | category | flops | bytes accessed | tf_op | source)
XLA Modules:
  0.0 261.7 jit_solution(6349580607664171543)
XLA Ops:
  7.2 1.6 convert_reduce_fusion
  8.8 1.6 fusion.12
  10.5 1.4 fusion.6
  11.9 0.7 all-gather.5.cloned.1.call-update
  12.8 1.2 constant_dynamic-slice_fusion.2
  14.0 50.4 %all-gather.3.cloned.1.call-done = bf16[4096,1024]{1,0:T(8,128)(2,1)} async-done(((bf16[512,1024]{1,0:T(8,128)(2,1)}), bf16[4096,1024]{1,0:T(8,128)(2,1)}) %all-gather.3.cloned.1.call-update) | async-done | bytes 8388624 | tf_op jit(solution)/shard_map/all_gather | solution.py:364
  64.5 8.3 %convolution_convert_fusion = bf16[4096,384]{1,0:T(8,128)(2,1)S(1)} fusion(bf16[4096,1024]{1,0:T(8,128)(2,1)} %all-gather.3.cloned.1.call-done, bf16[1024,128]{1,0:T(8,128)(2,1)S(1)} %get-tuple-element.24, bf16[1024,128]{1,0:T(8,128)(2,1)S(1)} %get-tuple-element.23, bf16[1024,128]{1,0:T(8,128)(2,1)S(1)} %get-tuple-element.22), kind=kOutput, calls=%fused_computation | convolution fusion | flops 3225157632 | bytes 12320768 | tf_op jit(solution)/shard_map/dot_general | solution.py:373
  72.7 0.5 fusion.22
  73.4 23.5 %shard_map.102 = (bf16[4096,128]{1,0:T(8,128)(2,1)S(1)}, f32[8192,128]{1,0:T(8,128)}) custom-call(s32[256]{0:T(256)S(1)} %reshape_squeeze.3.cols_ref, s32[32]{0:T(128)S(1)} %bitcast.30, bf16[4096,128]{1,0:T(8,128)(2,1)S(1)} %get-tuple-element.27.q_ref, bf16[4096,128]{1,0:T(8,128)(2,1)S(1)} %get-tuple-element.26.k_ref, ...), custom_call_target="tpu_custom_call" | custom-call | tf_op jit(solution)/shard_map/pallas_call | solution.py:179
  96.9 1.0 copy-done.3
  97.9 1.0 copy-done.4
  98.9 1.0 copy-done.6
  99.8 16.3 %all-gather.5.cloned.1.call-done = bf16[4096,1024]{1,0:T(8,128)(2,1)} async-done(((bf16[512,1024]{1,0:T(8,128)(2,1)}), bf16[4096,1024]{1,0:T(8,128)(2,1)}) %all-gather.5.cloned.1.call-update) | async-done | bytes 8388624 | tf_op jit(solution)/shard_map/all_gather | solution.py:365
  116.2 5.5 %fusion.24 = f32[128,1024]{1,0:T(8,128)} fusion(bf16[4096,128]{1,0:T(8,128)(2,1)S(1)} %get-tuple-element.12.o_ref, bf16[4096,1024]{1,0:T(8,128)(2,1)} %all-gather.5.cloned.1.call-done), kind=kOutput, calls=%fused_computation.42 | convolution fusion | flops 1073741824 | bytes 9961472 | tf_op jit(solution)/shard_map/dot_general | solution.py:28
  121.7 1.9 concatenate.17
  123.6 6.9 %fusion.do_ref = bf16[4096,128]{1,0:T(8,128)(2,1)} fusion(bf16[4096,1024]{1,0:T(8,128)(2,1)} %all-gather.5.cloned.1.call-done, bf16[1024,1024]{1,0:T(8,128)(2,1)S(1)} %copy-done, s32[]{:T(128)S(6)} %select_n.15), kind=kOutput, calls=%fused_computation.2 | convolution fusion | flops 1074266112 | bytes 9699332 | tf_op jit(solution)/shard_map/dot_general | solution.py:383
  130.5 35.0 %shard_map.103 = (bf16[4096,128]{1,0:T(8,128)(2,1)S(1)}, bf16[4096,128]{1,0:T(8,128)(2,1)S(1)}, bf16[4096,128]{1,0:T(8,128)(2,1)S(1)}) custom-call(s32[256]{0:T(256)S(1)} %reshape_squeeze.3.cols_ref, s32[32]{0:T(128)S(1)} %bitcast.31, bf16[4096,128]{1,0:T(8,128)(2,1)S(1)} %copy-done.7, bf16[4096,128]{1,0:T(8,128)(2,1)S(1)} %copy-done.5, ...), custom_call_target="tpu_custom_call" | custom-call | tf_op jit(solution)/shard_map/pallas_call | solution.py:193
  165.7 0.2 constant_dynamic-update-slice_fusion.1
  165.9 0.2 constant_dynamic-update-slice_fusion
  166.2 8.2 %fusion.23 = f32[1024,384]{1,0:T(8,128)S(1)} fusion(bf16[4096,1024]{1,0:T(8,128)(2,1)} %all-gather.3.cloned.1.call-done, bf16[4096,384]{1,0:T(8,128)(2,1)S(1)} %constant_dynamic-update-slice_fusion), kind=kOutput, calls=%fused_computation.41 | convolution fusion | flops 3221225472 | bytes 13107200 | tf_op jit(solution)/shard_map/dot_general | solution.py:28
  174.5 0.2 pad_maximum_fusion.x_ref
  174.7 1.0 copy-done.2
  175.7 56.7 %shard_map.104 = (bf16[16,64,512]{2,1,0:T(8,128)(2,1)S(1)}, bf16[512,3072]{1,0:T(8,128)(2,1)}, bf16[512,1024]{1,0:T(8,128)(2,1)S(1)}) custom-call(f32[16,64,512]{2,1,0:T(8,128)S(1)} %pad_maximum_fusion.x_ref, bf16[8,512,384]{2,1,0:T(8,128)(2,1)} %bitcast.32, bf16[8,512,128]{2,1,0:T(8,128)(2,1)S(1)} %bitcast.27), custom_call_target="tpu_custom_call" | custom-call | tf_op jit(solution)/shard_map/pallas_call | solution.py:334
  232.5 1.0 slice.23
  233.4 0.8 reshape.61
  234.2 4.7 %all-to-all-start = ((bf16[8,128,384]{2,1,0:T(8,128)(2,1)}), bf16[8,128,384]{2,1,0:T(8,128)(2,1)}, u32[]{:S(2)}, u32[]{:S(2)}) async-start(bf16[8,128,384]{2,1,0:T(8,128)(2,1)} %bitcast.34), calls=%async_computation | async-start | bytes 1572864 | tf_op jit(solution)/shard_map/all_to_all | solution.py:414
  239.0 7.7 %multiply_reduce_fusion = (f32[512]{0:T(512)S(1)}, f32[512]{0:T(512)S(1)}, f32[512,1024]{1,0:T(8,128)S(1)}) fusion(f32[1024]{0:T(1024)S(1)} %copy-done.14, f32[512]{0:T(512)S(1)} %add_rsqrt_fusion, f32[512]{0:T(512)S(1)} %broadcast_multiply_fusion.2, bf16[512,1024]{1,0:T(8,128)(2,1)} %param.7, bf16[512,3072]{1,0:T(8,128)(2,1)} %get-tuple-element.18, ...), kind=kOutput, calls=%fused_computation.20 | convolution fusion | flops 3224894464 | bytes 12595200 | tf_op jit(solution)/shard_map/dot_general | solution.py:402
  246.8 1.8 fusion.11
  248.6 2.2 fusion.13
  250.8 1.4 all-to-all-done
  252.2 1.6 copy.16
  253.8 1.0 copy.20
  (38 shorter events, 0.7 us)
Async XLA Ops:
  7.2 116.4 %copy-start = (bf16[1024,1024]{1,0:T(8,128)(2,1)S(1)}, bf16[1024,1024]{1,0:T(8,128)(2,1)}, u32[]{:S(2)}) copy-start(bf16[1024,1024]{1,0:T(8,128)(2,1)} %param.10) | copy-start | bytes 6291460
  7.2 3.3 %copy-start.10 = (bf16[512,1024]{1,0:T(8,128)(2,1)S(1)}, bf16[512,1024]{1,0:T(8,128)(2,1)}, u32[]{:S(2)}) copy-start(bf16[512,1024]{1,0:T(8,128)(2,1)} %param.7) | copy-start | bytes 3145732
  7.2 3.3 %copy-start.14 = (f32[1024]{0:T(1024)S(1)}, f32[1024]{0:T(1024)}, u32[]{:S(2)}) copy-start(f32[1024]{0:T(1024)} %param.8) | copy-start | bytes 12292
  7.2 57.3 %all-gather.3.cloned.1.call-start = ((), (), s32[]{:S(2)}) async-start(), calls=%async_computation.1 | async-start | bytes 9437184 | tf_op jit(solution)/shard_map/all_gather | solution.py:364
  10.5 2.1 copy-start.15
  11.9 104.3 %all-gather.5.cloned.1.call-start = ((), (), s32[]{:S(2)}) async-start(), calls=%async_computation.2 | async-start | bytes 9437184 | tf_op jit(solution)/shard_map/all_gather | solution.py:365
  72.7 0.7 copy-start.8
  96.9 1.0 copy-start.3
  97.9 1.0 copy-start.4
  98.9 1.0 copy-start.6
  99.8 21.8 %copy-start.1 = (bf16[4096,128]{1,0:T(8,128)(2,1)}, bf16[4096,128]{1,0:T(8,128)(2,1)S(1)}, u32[]{:S(2)}) copy-start(bf16[4096,128]{1,0:T(8,128)(2,1)S(1)} %get-tuple-element.12.o_ref) | copy-start | bytes 3145732
  123.6 6.9 %copy-start.5 = (bf16[4096,128]{1,0:T(8,128)(2,1)S(1)}, bf16[4096,128]{1,0:T(8,128)(2,1)}, u32[]{:S(2)}) copy-start(bf16[4096,128]{1,0:T(8,128)(2,1)} %copy-done.4) | copy-start | bytes 3145732
  123.6 6.9 %copy-start.7 = (bf16[4096,128]{1,0:T(8,128)(2,1)S(1)}, bf16[4096,128]{1,0:T(8,128)(2,1)}, u32[]{:S(2)}) copy-start(bf16[4096,128]{1,0:T(8,128)(2,1)} %copy-done.6) | copy-start | bytes 3145732
  166.2 8.2 %copy-start.9 = (bf16[4096,384]{1,0:T(8,128)(2,1)}, bf16[4096,384]{1,0:T(8,128)(2,1)S(1)}, u32[]{:S(2)}) copy-start(bf16[4096,384]{1,0:T(8,128)(2,1)S(1)} %constant_dynamic-update-slice_fusion) | copy-start | bytes 9437188
  166.2 8.2 %copy-start.13 = (f32[16,64,128]{2,1,0:T(8,128)S(1)}, f32[16,64,128]{2,1,0:T(8,128)}, u32[]{:S(2)}) copy-start(f32[16,64,128]{2,1,0:T(8,128)} %concatenate.17) | copy-start | bytes 1572868
  174.5 1.2 copy-start.2
  234.2 18.0 %all-to-all-start = ((bf16[8,128,384]{2,1,0:T(8,128)(2,1)}), bf16[8,128,384]{2,1,0:T(8,128)(2,1)}, u32[]{:S(2)}, u32[]{:S(2)}) async-start(bf16[8,128,384]{2,1,0:T(8,128)(2,1)} %bitcast.34), calls=%async_computation | async-start | bytes 1572864 | tf_op jit(solution)/shard_map/all_to_all | solution.py:414
  239.0 7.8 %copy-start.11 = (bf16[512,1024]{1,0:T(8,128)(2,1)S(1)}, bf16[512,1024]{1,0:T(8,128)(2,1)}, u32[]{:S(2)}) copy-start(bf16[512,1024]{1,0:T(8,128)(2,1)} %param.7) | copy-start | bytes 3145732
  239.0 7.8 %copy-start.12 = (bf16[512,1024]{1,0:T(8,128)(2,1)S(1)}, bf16[512,1024]{1,0:T(8,128)(2,1)}, u32[]{:S(2)}) copy-start(bf16[512,1024]{1,0:T(8,128)(2,1)} %param.13) | copy-start | bytes 3145732
Sparse Core Ops, SparseCore 0:
  12.0 52.3 all-gather.2
  66.2 49.9 all-gather.4

commit v14 on v9

--- a/solution.py
+++ b/solution.py
@@ -71,9 +71,12 @@
     return lax.broadcasted_iota(jnp.int32, (1, slots * BLK), 1) < cnt * BLK
 
 
-def by_tier(cnt, body):
+FINE_TIERS = (1, 2, 3, 4, 6, MAXB)
+
+
+def by_tier(cnt, body, tiers=SLOT_TIERS):
     low = 0
-    for slots in SLOT_TIERS:
+    for slots in tiers:
         pl.when((cnt > low) & (cnt <= slots))(functools.partial(body, slots))
         low = slots
 
@@ -152,7 +155,7 @@
                     dk_acc[pl.ds(col0, BLK), :] += dkc[s * BLK : (s + 1) * BLK]
                     dv_acc[pl.ds(col0, BLK), :] += dvc[s * BLK : (s + 1) * BLK]
 
-        by_tier(cnt, tier)
+        by_tier(cnt, tier, FINE_TIERS)
         return carry
 
     lax.fori_loop(0, nblk, row_body, 0)

time: 258 us -> 257 us (level)
  no operation moved by 1% of the time
where the time goes in v14:
time: 257 us; the launch traced here: 255 us
  Pallas kernels  109 us (42%)
  waiting for transfers between devices  68.4 us (27%)
  matrix products  38.7 us (15%)
  between operations  14.3 us (6%)
  local copies, waits for them, and re-layouts  13 us (5%)
  other arithmetic  6.63 us (3%)
  starting transfers between devices  4.81 us (2%)
    pallas_call x1, Pallas kernels, sum_and_exchange(): pl.pallas_call(functools.partial(exchange_kernel, n, m), out_shape=(jax.S...  55.9 us
    all_gather x1, waiting for transfers between devices, body(): normed_all = lax.all_gather(normed, 'seq', axis=0, tiled=True)  50.4 us
    pallas_call x1, Pallas kernels, attention_backward(): pl.pallas_call(attn_bwd_kernel, out_shape=tuple((jax.ShapeDtypeStruct((n,...  29.5 us
    pallas_call x1, Pallas kernels, attention_forward(): pl.pallas_call(attn_fwd_kernel, out_shape=(jax.ShapeDtypeStruct((n, width...  24 us
    all_gather x1, waiting for transfers between devices, body(): cotan_all = lax.all_gather(cotan, 'seq', axis=0, tiled=True)  15.8 us
    dot_general x2, matrix products, contract_rows(): lax.dot_general(left_cols, right_cols, (((0,), (0,)), ((), ())), preferre...  13.6 us
    dot_general x1, matrix products, body(): jnp.dot(normed_all, w_heads, preferred_element_type=jnp.float32)  8.27 us
    dot_general x1, matrix products, body(): lax.dot_general(grad_mixed, w_qkv, (((1,), (1,)), ((), ())), preferred_el...  7.75 us
  transfers between devices with their start and end apart: 3, of which 3 were waited for; matrix products, arithmetic and copies ran while one was open for 9% of the time, Pallas kernels for 9%

profile of v14, /device:TPU:0, one launch (start us, length us, event | category | flops | bytes accessed | tf_op | source)
XLA Modules:
  0.0 255.2 jit_solution(12685774662801212859)
XLA Ops:
  7.2 1.6 convert_reduce_fusion
  8.8 1.6 fusion.12
  10.5 1.4 fusion.6
  11.9 0.7 all-gather.5.cloned.1.call-update
  12.8 1.2 constant_dynamic-slice_fusion.2
  14.0 50.4 %all-gather.3.cloned.1.call-done = bf16[4096,1024]{1,0:T(8,128)(2,1)} async-done(((bf16[512,1024]{1,0:T(8,128)(2,1)}), bf16[4096,1024]{1,0:T(8,128)(2,1)}) %all-gather.3.cloned.1.call-update) | async-done | bytes 8388624 | tf_op jit(solution)/shard_map/all_gather | solution.py:365
  64.5 8.3 %convolution_convert_fusion = bf16[4096,384]{1,0:T(8,128)(2,1)S(1)} fusion(bf16[4096,1024]{1,0:T(8,128)(2,1)} %all-gather.3.cloned.1.call-done, bf16[1024,128]{1,0:T(8,128)(2,1)S(1)} %get-tuple-element.24, bf16[1024,128]{1,0:T(8,128)(2,1)S(1)} %get-tuple-element.23, bf16[1024,128]{1,0:T(8,128)(2,1)S(1)} %get-tuple-element.22), kind=kOutput, calls=%fused_computation | convolution fusion | flops 3225157632 | bytes 12320768 | tf_op jit(solution)/shard_map/dot_general | solution.py:374
  72.7 0.5 fusion.22
  73.4 24.0 %shard_map.102 = (bf16[4096,128]{1,0:T(8,128)(2,1)S(1)}, f32[8192,128]{1,0:T(8,128)}) custom-call(s32[256]{0:T(256)S(1)} %reshape_squeeze.3.cols_ref, s32[32]{0:T(128)S(1)} %bitcast.30, bf16[4096,128]{1,0:T(8,128)(2,1)S(1)} %get-tuple-element.27.q_ref, bf16[4096,128]{1,0:T(8,128)(2,1)S(1)} %get-tuple-element.26.k_ref, ...), custom_call_target="tpu_custom_call" | custom-call | tf_op jit(solution)/shard_map/pallas_call | solution.py:180
  97.4 1.0 copy-done.3
  98.4 1.0 copy-done.4
  99.4 1.0 copy-done.6
  100.3 15.8 %all-gather.5.cloned.1.call-done = bf16[4096,1024]{1,0:T(8,128)(2,1)} async-done(((bf16[512,1024]{1,0:T(8,128)(2,1)}), bf16[4096,1024]{1,0:T(8,128)(2,1)}) %all-gather.5.cloned.1.call-update) | async-done | bytes 8388624 | tf_op jit(solution)/shard_map/all_gather | solution.py:366
  116.2 5.5 %fusion.24 = f32[128,1024]{1,0:T(8,128)} fusion(bf16[4096,128]{1,0:T(8,128)(2,1)S(1)} %get-tuple-element.12.o_ref, bf16[4096,1024]{1,0:T(8,128)(2,1)} %all-gather.5.cloned.1.call-done), kind=kOutput, calls=%fused_computation.42 | convolution fusion | flops 1073741824 | bytes 9961472 | tf_op jit(solution)/shard_map/dot_general | solution.py:28
  121.7 1.9 concatenate.17
  123.6 6.9 %fusion.do_ref = bf16[4096,128]{1,0:T(8,128)(2,1)} fusion(bf16[4096,1024]{1,0:T(8,128)(2,1)} %all-gather.5.cloned.1.call-done, bf16[1024,1024]{1,0:T(8,128)(2,1)S(1)} %copy-done, s32[]{:T(128)S(6)} %select_n.15), kind=kOutput, calls=%fused_computation.2 | convolution fusion | flops 1074266112 | bytes 9699332 | tf_op jit(solution)/shard_map/dot_general | solution.py:384
  130.5 29.5 %shard_map.103 = (bf16[4096,128]{1,0:T(8,128)(2,1)S(1)}, bf16[4096,128]{1,0:T(8,128)(2,1)S(1)}, bf16[4096,128]{1,0:T(8,128)(2,1)S(1)}) custom-call(s32[256]{0:T(256)S(1)} %reshape_squeeze.3.cols_ref, s32[32]{0:T(128)S(1)} %bitcast.31, bf16[4096,128]{1,0:T(8,128)(2,1)S(1)} %copy-done.7, bf16[4096,128]{1,0:T(8,128)(2,1)S(1)} %copy-done.5, ...), custom_call_target="tpu_custom_call" | custom-call | tf_op jit(solution)/shard_map/pallas_call | solution.py:194
  160.2 0.2 constant_dynamic-update-slice_fusion.1
  160.4 0.2 constant_dynamic-update-slice_fusion
  160.7 8.1 %fusion.23 = f32[1024,384]{1,0:T(8,128)S(1)} fusion(bf16[4096,1024]{1,0:T(8,128)(2,1)} %all-gather.3.cloned.1.call-done, bf16[4096,384]{1,0:T(8,128)(2,1)S(1)} %constant_dynamic-update-slice_fusion), kind=kOutput, calls=%fused_computation.41 | convolution fusion | flops 3221225472 | bytes 13107200 | tf_op jit(solution)/shard_map/dot_general | solution.py:28
  168.8 0.2 pad_maximum_fusion.x_ref
  169.0 1.0 copy-done.2
  170.0 55.9 %shard_map.104 = (bf16[16,64,512]{2,1,0:T(8,128)(2,1)S(1)}, bf16[512,3072]{1,0:T(8,128)(2,1)}, bf16[512,1024]{1,0:T(8,128)(2,1)S(1)}) custom-call(f32[16,64,512]{2,1,0:T(8,128)S(1)} %pad_maximum_fusion.x_ref, bf16[8,512,384]{2,1,0:T(8,128)(2,1)} %bitcast.32, bf16[8,512,128]{2,1,0:T(8,128)(2,1)S(1)} %bitcast.27), custom_call_target="tpu_custom_call" | custom-call | tf_op jit(solution)/shard_map/pallas_call | solution.py:335
  226.0 1.0 slice.23
  227.0 0.8 reshape.61
  227.8 4.7 %all-to-all-start = ((bf16[8,128,384]{2,1,0:T(8,128)(2,1)}), bf16[8,128,384]{2,1,0:T(8,128)(2,1)}, u32[]{:S(2)}, u32[]{:S(2)}) async-start(bf16[8,128,384]{2,1,0:T(8,128)(2,1)} %bitcast.34), calls=%async_computation | async-start | bytes 1572864 | tf_op jit(solution)/shard_map/all_to_all | solution.py:415
  232.5 7.7 %multiply_reduce_fusion = (f32[512]{0:T(512)S(1)}, f32[512]{0:T(512)S(1)}, f32[512,1024]{1,0:T(8,128)S(1)}) fusion(f32[1024]{0:T(1024)S(1)} %copy-done.14, f32[512]{0:T(512)S(1)} %add_rsqrt_fusion, f32[512]{0:T(512)S(1)} %broadcast_multiply_fusion.2, bf16[512,1024]{1,0:T(8,128)(2,1)} %param.7, bf16[512,3072]{1,0:T(8,128)(2,1)} %get-tuple-element.18, ...), kind=kOutput, calls=%fused_computation.20 | convolution fusion | flops 3224894464 | bytes 12595200 | tf_op jit(solution)/shard_map/dot_general | solution.py:403
  240.3 1.8 fusion.11
  242.1 2.2 fusion.13
  244.4 1.4 all-to-all-done
  245.8 1.6 copy.16
  247.4 1.0 copy.20
  (38 shorter events, 0.7 us)
Async XLA Ops:
  7.2 116.4 %copy-start = (bf16[1024,1024]{1,0:T(8,128)(2,1)S(1)}, bf16[1024,1024]{1,0:T(8,128)(2,1)}, u32[]{:S(2)}) copy-start(bf16[1024,1024]{1,0:T(8,128)(2,1)} %param.10) | copy-start | bytes 6291460
  7.2 3.3 %copy-start.10 = (bf16[512,1024]{1,0:T(8,128)(2,1)S(1)}, bf16[512,1024]{1,0:T(8,128)(2,1)}, u32[]{:S(2)}) copy-start(bf16[512,1024]{1,0:T(8,128)(2,1)} %param.7) | copy-start | bytes 3145732
  7.2 3.3 %copy-start.14 = (f32[1024]{0:T(1024)S(1)}, f32[1024]{0:T(1024)}, u32[]{:S(2)}) copy-start(f32[1024]{0:T(1024)} %param.8) | copy-start | bytes 12292
  7.2 57.3 %all-gather.3.cloned.1.call-start = ((), (), s32[]{:S(2)}) async-start(), calls=%async_computation.1 | async-start | bytes 9437184 | tf_op jit(solution)/shard_map/all_gather | solution.py:365
  10.5 2.1 copy-start.15
  11.9 104.3 %all-gather.5.cloned.1.call-start = ((), (), s32[]{:S(2)}) async-start(), calls=%async_computation.2 | async-start | bytes 9437184 | tf_op jit(solution)/shard_map/all_gather | solution.py:366
  72.7 0.7 copy-start.8
  97.4 1.0 copy-start.3
  98.4 1.0 copy-start.4
  99.4 1.0 copy-start.6
  100.3 21.4 %copy-start.1 = (bf16[4096,128]{1,0:T(8,128)(2,1)}, bf16[4096,128]{1,0:T(8,128)(2,1)S(1)}, u32[]{:S(2)}) copy-start(bf16[4096,128]{1,0:T(8,128)(2,1)S(1)} %get-tuple-element.12.o_ref) | copy-start | bytes 3145732
  123.6 6.9 %copy-start.5 = (bf16[4096,128]{1,0:T(8,128)(2,1)S(1)}, bf16[4096,128]{1,0:T(8,128)(2,1)}, u32[]{:S(2)}) copy-start(bf16[4096,128]{1,0:T(8,128)(2,1)} %copy-done.4) | copy-start | bytes 3145732
  123.6 6.9 %copy-start.7 = (bf16[4096,128]{1,0:T(8,128)(2,1)S(1)}, bf16[4096,128]{1,0:T(8,128)(2,1)}, u32[]{:S(2)}) copy-start(bf16[4096,128]{1,0:T(8,128)(2,1)} %copy-done.6) | copy-start | bytes 3145732
  160.7 8.1 %copy-start.9 = (bf16[4096,384]{1,0:T(8,128)(2,1)}, bf16[4096,384]{1,0:T(8,128)(2,1)S(1)}, u32[]{:S(2)}) copy-start(bf16[4096,384]{1,0:T(8,128)(2,1)S(1)} %constant_dynamic-update-slice_fusion) | copy-start | bytes 9437188
  160.7 8.1 %copy-start.13 = (f32[16,64,128]{2,1,0:T(8,128)S(1)}, f32[16,64,128]{2,1,0:T(8,128)}, u32[]{:S(2)}) copy-start(f32[16,64,128]{2,1,0:T(8,128)} %concatenate.17) | copy-start | bytes 1572868
  168.8 1.2 copy-start.2
  227.8 18.0 %all-to-all-start = ((bf16[8,128,384]{2,1,0:T(8,128)(2,1)}), bf16[8,128,384]{2,1,0:T(8,128)(2,1)}, u32[]{:S(2)}, u32[]{:S(2)}) async-start(bf16[8,128,384]{2,1,0:T(8,128)(2,1)} %bitcast.34), calls=%async_computation | async-start | bytes 1572864 | tf_op jit(solution)/shard_map/all_to_all | solution.py:415
  232.5 7.8 %copy-start.11 = (bf16[512,1024]{1,0:T(8,128)(2,1)S(1)}, bf16[512,1024]{1,0:T(8,128)(2,1)}, u32[]{:S(2)}) copy-start(bf16[512,1024]{1,0:T(8,128)(2,1)} %param.7) | copy-start | bytes 3145732
  232.5 7.8 %copy-start.12 = (bf16[512,1024]{1,0:T(8,128)(2,1)S(1)}, bf16[512,1024]{1,0:T(8,128)(2,1)}, u32[]{:S(2)}) copy-start(bf16[512,1024]{1,0:T(8,128)(2,1)} %param.13) | copy-start | bytes 3145732
Sparse Core Ops, SparseCore 0:
  12.0 52.3 all-gather.2
  66.2 49.9 all-gather.4

commit v15 on v14

--- a/solution.py
+++ b/solution.py
@@ -284,6 +284,8 @@
             device_id_type=MESH,
         )
 
+    rs = (lambda peer: x_ref.at[peer], recv, sems.at[0], sems.at[1], "dp", me, n)
+    rs_started = start_all(*rs)
     a2a_started = []
     for k in range(1, m):
         peer = lax.rem(here + k, m)
@@ -296,8 +298,7 @@
             copy = part_copy(t, peer, here, peer)
             copy.start()
             a2a_started.append(copy)
-    rs = (lambda peer: x_ref.at[peer], recv, sems.at[0], sems.at[1], "dp", me, n)
-    finish_all(start_all(*rs), *rs)
+    finish_all(rs_started, *rs)
     total = x_ref[me]
     for k in range(1, n):
         total = total + recv[lax.rem(me + k, n)]

time: 257 us -> 257 us (level)
  no operation moved by 1% of the time
where the time goes in v15:
time: 257 us; the launch traced here: 255 us
  Pallas kernels  109 us (42%)
  waiting for transfers between devices  68.7 us (27%)
  matrix products  38.7 us (15%)
  between operations  14.3 us (6%)
  local copies, waits for them, and re-layouts  13 us (5%)
  other arithmetic  6.63 us (3%)
  starting transfers between devices  4.81 us (2%)
    pallas_call x1, Pallas kernels, sum_and_exchange(): pl.pallas_call(functools.partial(exchange_kernel, n, m), out_shape=(jax.S...  55.7 us
    all_gather x1, waiting for transfers between devices, body(): normed_all = lax.all_gather(normed, 'seq', axis=0, tiled=True)  50.4 us
    pallas_call x1, Pallas kernels, attention_backward(): pl.pallas_call(attn_bwd_kernel, out_shape=tuple((jax.ShapeDtypeStruct((n,...  29.3 us
    pallas_call x1, Pallas kernels, attention_forward(): pl.pallas_call(attn_fwd_kernel, out_shape=(jax.ShapeDtypeStruct((n, width...  23.9 us
    all_gather x1, waiting for transfers between devices, body(): cotan_all = lax.all_gather(cotan, 'seq', axis=0, tiled=True)  16.1 us
    dot_general x2, matrix products, contract_rows(): lax.dot_general(left_cols, right_cols, (((0,), (0,)), ((), ())), preferre...  13.6 us
    dot_general x1, matrix products, body(): jnp.dot(normed_all, w_heads, preferred_element_type=jnp.float32)  8.27 us
    dot_general x1, matrix products, body(): lax.dot_general(grad_mixed, w_qkv, (((1,), (1,)), ((), ())), preferred_el...  7.75 us
  transfers between devices with their start and end apart: 3, of which 3 were waited for; matrix products, arithmetic and copies ran while one was open for 9% of the time, Pallas kernels for 9%

profile of v15, /device:TPU:0, one launch (start us, length us, event | category | flops | bytes accessed | tf_op | source)
XLA Modules:
  0.0 254.9 jit_solution(10031471154448941012)
XLA Ops:
  7.2 1.6 convert_reduce_fusion
  8.8 1.6 fusion.12
  10.5 1.4 fusion.6
  11.9 0.7 all-gather.5.cloned.1.call-update
  12.8 1.2 constant_dynamic-slice_fusion.2
  14.0 50.4 %all-gather.3.cloned.1.call-done = bf16[4096,1024]{1,0:T(8,128)(2,1)} async-done(((bf16[512,1024]{1,0:T(8,128)(2,1)}), bf16[4096,1024]{1,0:T(8,128)(2,1)}) %all-gather.3.cloned.1.call-update) | async-done | bytes 8388624 | tf_op jit(solution)/shard_map/all_gather | solution.py:366
  64.5 8.3 %convolution_convert_fusion = bf16[4096,384]{1,0:T(8,128)(2,1)S(1)} fusion(bf16[4096,1024]{1,0:T(8,128)(2,1)} %all-gather.3.cloned.1.call-done, bf16[1024,128]{1,0:T(8,128)(2,1)S(1)} %get-tuple-element.24, bf16[1024,128]{1,0:T(8,128)(2,1)S(1)} %get-tuple-element.23, bf16[1024,128]{1,0:T(8,128)(2,1)S(1)} %get-tuple-element.22), kind=kOutput, calls=%fused_computation | convolution fusion | flops 3225157632 | bytes 12320768 | tf_op jit(solution)/shard_map/dot_general | solution.py:375
  72.7 0.5 fusion.22
  73.4 23.9 %shard_map.102 = (bf16[4096,128]{1,0:T(8,128)(2,1)S(1)}, f32[8192,128]{1,0:T(8,128)}) custom-call(s32[256]{0:T(256)S(1)} %reshape_squeeze.3.cols_ref, s32[32]{0:T(128)S(1)} %bitcast.30, bf16[4096,128]{1,0:T(8,128)(2,1)S(1)} %get-tuple-element.27.q_ref, bf16[4096,128]{1,0:T(8,128)(2,1)S(1)} %get-tuple-element.26.k_ref, ...), custom_call_target="tpu_custom_call" | custom-call | tf_op jit(solution)/shard_map/pallas_call | solution.py:180
  97.2 1.0 copy-done.3
  98.3 1.0 copy-done.4
  99.2 1.0 copy-done.6
  100.2 16.1 %all-gather.5.cloned.1.call-done = bf16[4096,1024]{1,0:T(8,128)(2,1)} async-done(((bf16[512,1024]{1,0:T(8,128)(2,1)}), bf16[4096,1024]{1,0:T(8,128)(2,1)}) %all-gather.5.cloned.1.call-update) | async-done | bytes 8388624 | tf_op jit(solution)/shard_map/all_gather | solution.py:367
  116.3 5.5 %fusion.24 = f32[128,1024]{1,0:T(8,128)} fusion(bf16[4096,128]{1,0:T(8,128)(2,1)S(1)} %get-tuple-element.12.o_ref, bf16[4096,1024]{1,0:T(8,128)(2,1)} %all-gather.5.cloned.1.call-done), kind=kOutput, calls=%fused_computation.42 | convolution fusion | flops 1073741824 | bytes 9961472 | tf_op jit(solution)/shard_map/dot_general | solution.py:28
  121.8 1.9 concatenate.17
  123.7 6.9 %fusion.do_ref = bf16[4096,128]{1,0:T(8,128)(2,1)} fusion(bf16[4096,1024]{1,0:T(8,128)(2,1)} %all-gather.5.cloned.1.call-done, bf16[1024,1024]{1,0:T(8,128)(2,1)S(1)} %copy-done, s32[]{:T(128)S(6)} %select_n.15), kind=kOutput, calls=%fused_computation.2 | convolution fusion | flops 1074266112 | bytes 9699332 | tf_op jit(solution)/shard_map/dot_general | solution.py:385
  130.6 29.3 %shard_map.103 = (bf16[4096,128]{1,0:T(8,128)(2,1)S(1)}, bf16[4096,128]{1,0:T(8,128)(2,1)S(1)}, bf16[4096,128]{1,0:T(8,128)(2,1)S(1)}) custom-call(s32[256]{0:T(256)S(1)} %reshape_squeeze.3.cols_ref, s32[32]{0:T(128)S(1)} %bitcast.31, bf16[4096,128]{1,0:T(8,128)(2,1)S(1)} %copy-done.7, bf16[4096,128]{1,0:T(8,128)(2,1)S(1)} %copy-done.5, ...), custom_call_target="tpu_custom_call" | custom-call | tf_op jit(solution)/shard_map/pallas_call | solution.py:194
  160.1 0.2 constant_dynamic-update-slice_fusion.1
  160.3 0.2 constant_dynamic-update-slice_fusion
  160.6 8.1 %fusion.23 = f32[1024,384]{1,0:T(8,128)S(1)} fusion(bf16[4096,1024]{1,0:T(8,128)(2,1)} %all-gather.3.cloned.1.call-done, bf16[4096,384]{1,0:T(8,128)(2,1)S(1)} %constant_dynamic-update-slice_fusion), kind=kOutput, calls=%fused_computation.41 | convolution fusion | flops 3221225472 | bytes 13107200 | tf_op jit(solution)/shard_map/dot_general | solution.py:28
  168.7 0.2 pad_maximum_fusion.x_ref
  169.0 1.0 copy-done.2
  169.9 55.7 %shard_map.104 = (bf16[16,64,512]{2,1,0:T(8,128)(2,1)S(1)}, bf16[512,3072]{1,0:T(8,128)(2,1)}, bf16[512,1024]{1,0:T(8,128)(2,1)S(1)}) custom-call(f32[16,64,512]{2,1,0:T(8,128)S(1)} %pad_maximum_fusion.x_ref, bf16[8,512,384]{2,1,0:T(8,128)(2,1)} %bitcast.32, bf16[8,512,128]{2,1,0:T(8,128)(2,1)S(1)} %bitcast.27), custom_call_target="tpu_custom_call" | custom-call | tf_op jit(solution)/shard_map/pallas_call | solution.py:336
  225.7 1.0 slice.23
  226.7 0.8 reshape.61
  227.5 4.7 %all-to-all-start = ((bf16[8,128,384]{2,1,0:T(8,128)(2,1)}), bf16[8,128,384]{2,1,0:T(8,128)(2,1)}, u32[]{:S(2)}, u32[]{:S(2)}) async-start(bf16[8,128,384]{2,1,0:T(8,128)(2,1)} %bitcast.34), calls=%async_computation | async-start | bytes 1572864 | tf_op jit(solution)/shard_map/all_to_all | solution.py:416
  232.2 7.7 %multiply_reduce_fusion = (f32[512]{0:T(512)S(1)}, f32[512]{0:T(512)S(1)}, f32[512,1024]{1,0:T(8,128)S(1)}) fusion(f32[1024]{0:T(1024)S(1)} %copy-done.14, f32[512]{0:T(512)S(1)} %add_rsqrt_fusion, f32[512]{0:T(512)S(1)} %broadcast_multiply_fusion.2, bf16[512,1024]{1,0:T(8,128)(2,1)} %param.7, bf16[512,3072]{1,0:T(8,128)(2,1)} %get-tuple-element.18, ...), kind=kOutput, calls=%fused_computation.20 | convolution fusion | flops 3224894464 | bytes 12595200 | tf_op jit(solution)/shard_map/dot_general | solution.py:404
  240.0 1.8 fusion.11
  241.8 2.2 fusion.13
  244.1 1.4 all-to-all-done
  245.5 1.6 copy.16
  247.1 1.0 copy.20
  (38 shorter events, 0.7 us)
Async XLA Ops:
  7.2 116.6 %copy-start = (bf16[1024,1024]{1,0:T(8,128)(2,1)S(1)}, bf16[1024,1024]{1,0:T(8,128)(2,1)}, u32[]{:S(2)}) copy-start(bf16[1024,1024]{1,0:T(8,128)(2,1)} %param.10) | copy-start | bytes 6291460
  7.2 3.3 %copy-start.10 = (bf16[512,1024]{1,0:T(8,128)(2,1)S(1)}, bf16[512,1024]{1,0:T(8,128)(2,1)}, u32[]{:S(2)}) copy-start(bf16[512,1024]{1,0:T(8,128)(2,1)} %param.7) | copy-start | bytes 3145732
  7.2 3.3 %copy-start.14 = (f32[1024]{0:T(1024)S(1)}, f32[1024]{0:T(1024)}, u32[]{:S(2)}) copy-start(f32[1024]{0:T(1024)} %param.8) | copy-start | bytes 12292
  7.2 57.3 %all-gather.3.cloned.1.call-start = ((), (), s32[]{:S(2)}) async-start(), calls=%async_computation.1 | async-start | bytes 9437184 | tf_op jit(solution)/shard_map/all_gather | solution.py:366
  10.5 2.1 copy-start.15
  11.9 104.4 %all-gather.5.cloned.1.call-start = ((), (), s32[]{:S(2)}) async-start(), calls=%async_computation.2 | async-start | bytes 9437184 | tf_op jit(solution)/shard_map/all_gather | solution.py:367
  72.7 0.7 copy-start.8
  97.2 1.0 copy-start.3
  98.2 1.0 copy-start.4
  99.2 1.0 copy-start.6
  100.2 21.6 %copy-start.1 = (bf16[4096,128]{1,0:T(8,128)(2,1)}, bf16[4096,128]{1,0:T(8,128)(2,1)S(1)}, u32[]{:S(2)}) copy-start(bf16[4096,128]{1,0:T(8,128)(2,1)S(1)} %get-tuple-element.12.o_ref) | copy-start | bytes 3145732
  123.7 6.9 %copy-start.5 = (bf16[4096,128]{1,0:T(8,128)(2,1)S(1)}, bf16[4096,128]{1,0:T(8,128)(2,1)}, u32[]{:S(2)}) copy-start(bf16[4096,128]{1,0:T(8,128)(2,1)} %copy-done.4) | copy-start | bytes 3145732
  123.7 6.9 %copy-start.7 = (bf16[4096,128]{1,0:T(8,128)(2,1)S(1)}, bf16[4096,128]{1,0:T(8,128)(2,1)}, u32[]{:S(2)}) copy-start(bf16[4096,128]{1,0:T(8,128)(2,1)} %copy-done.6) | copy-start | bytes 3145732
  160.6 8.1 %copy-start.9 = (bf16[4096,384]{1,0:T(8,128)(2,1)}, bf16[4096,384]{1,0:T(8,128)(2,1)S(1)}, u32[]{:S(2)}) copy-start(bf16[4096,384]{1,0:T(8,128)(2,1)S(1)} %constant_dynamic-update-slice_fusion) | copy-start | bytes 9437188
  160.6 8.1 %copy-start.13 = (f32[16,64,128]{2,1,0:T(8,128)S(1)}, f32[16,64,128]{2,1,0:T(8,128)}, u32[]{:S(2)}) copy-start(f32[16,64,128]{2,1,0:T(8,128)} %concatenate.17) | copy-start | bytes 1572868
  168.7 1.2 copy-start.2
  227.5 18.0 %all-to-all-start = ((bf16[8,128,384]{2,1,0:T(8,128)(2,1)}), bf16[8,128,384]{2,1,0:T(8,128)(2,1)}, u32[]{:S(2)}, u32[]{:S(2)}) async-start(bf16[8,128,384]{2,1,0:T(8,128)(2,1)} %bitcast.34), calls=%async_computation | async-start | bytes 1572864 | tf_op jit(solution)/shard_map/all_to_all | solution.py:416
  232.2 7.8 %copy-start.11 = (bf16[512,1024]{1,0:T(8,128)(2,1)S(1)}, bf16[512,1024]{1,0:T(8,128)(2,1)}, u32[]{:S(2)}) copy-start(bf16[512,1024]{1,0:T(8,128)(2,1)} %param.7) | copy-start | bytes 3145732
  232.2 7.8 %copy-start.12 = (bf16[512,1024]{1,0:T(8,128)(2,1)S(1)}, bf16[512,1024]{1,0:T(8,128)(2,1)}, u32[]{:S(2)}) copy-start(bf16[512,1024]{1,0:T(8,128)(2,1)} %param.13) | copy-start | bytes 3145732
Sparse Core Ops, SparseCore 0:
  12.0 52.3 all-gather.2
  66.2 50.0 all-gather.4

commit v16 on v14

--- a/solution.py
+++ b/solution.py
@@ -214,7 +214,22 @@
 
 
 def exchange_kernel(
-    n, m, x_ref, g_ref, a_ref, o_ref, moved_ref, att_ref, recv, gath, landed, att_landed, sems, a2a_sems
+    n,
+    m,
+    na_ref,
+    xo_ref,
+    g_ref,
+    a_ref,
+    o_ref,
+    moved_ref,
+    att_ref,
+    x_ref,
+    recv,
+    gath,
+    landed,
+    att_landed,
+    sems,
+    a2a_sems,
 ):
     me = lax.axis_index("dp")
     here = lax.axis_index("seq")
@@ -296,6 +311,13 @@
             copy = part_copy(t, peer, here, peer)
             copy.start()
             a2a_started.append(copy)
+    share = g_ref.shape[1]
+    qkv = tn_dot(na_ref[0:share, :], g_ref[0])
+    for c in range(1, m):
+        qkv = qkv + tn_dot(na_ref[c * share : (c + 1) * share, :], g_ref[c])
+    qkv_cols = g_ref.shape[2]
+    x_ref[:, :, 0:qkv_cols] = qkv.reshape(n, x_ref.shape[1], qkv_cols)
+    x_ref[:, :, qkv_cols:] = xo_ref[...]
     rs = (lambda peer: x_ref.at[peer], recv, sems.at[0], sems.at[1], "dp", me, n)
     finish_all(start_all(*rs), *rs)
     total = x_ref[me]
@@ -322,11 +344,15 @@
     att_ref[...] = att_landed[...]
 
 
-def sum_and_exchange(term, grads, attended_heads):
+def sum_and_exchange(normed_all, term_out, grads, attended_heads):
     n = lax.axis_size("dp")
     m = lax.axis_size("seq")
-    rows, cols = term.shape
-    chunked = term.reshape(n, rows // n, cols)
+    rows = normed_all.shape[1]
+    qkv_cols = grads.shape[1]
+    extra = term_out.size // rows
+    cols = qkv_cols + extra
+    chunk_shape = (n, rows // n, cols)
+    term_part = term_out.reshape(n, rows // n, extra)
     pieces = grads.reshape(m, grads.shape[0] // m, grads.shape[1])
     att_pieces = attended_heads.reshape(m, attended_heads.shape[0] // m, attended_heads.shape[1])
     parts = grads.shape[1] // BLK
@@ -335,15 +361,16 @@
     out, moved, attended = pl.pallas_call(
         functools.partial(exchange_kernel, n, m),
         out_shape=(
-            jax.ShapeDtypeStruct(chunked.shape, jnp.bfloat16),
+            jax.ShapeDtypeStruct(chunk_shape, jnp.bfloat16),
             jax.ShapeDtypeStruct(final, pieces.dtype),
             jax.ShapeDtypeStruct(att_final, att_pieces.dtype),
         ),
-        in_specs=[vmem_spec(), vmem_spec(), vmem_spec()],
+        in_specs=[vmem_spec(), vmem_spec(), vmem_spec(), vmem_spec()],
         out_specs=(vmem_spec(), vmem_spec(), vmem_spec()),
         scratch_shapes=[
-            pltpu.VMEM(chunked.shape, jnp.float32),
-            pltpu.VMEM(chunked.shape, jnp.bfloat16),
+            pltpu.VMEM(chunk_shape, jnp.float32),
+            pltpu.VMEM(chunk_shape, jnp.float32),
+            pltpu.VMEM(chunk_shape, jnp.bfloat16),
             pltpu.VMEM(final, pieces.dtype),
             pltpu.VMEM(att_final, att_pieces.dtype),
             pltpu.SemaphoreType.DMA((4, n)),
@@ -352,7 +379,7 @@
         compiler_params=pltpu.CompilerParams(
             collective_id=0, has_side_effects=True, vmem_limit_bytes=VMEM_LIMIT
         ),
-    )(chunked, pieces, att_pieces)
+    )(normed_all, term_part, pieces, att_pieces)
     return out.reshape(rows, cols), moved, attended
 
 
@@ -388,13 +415,10 @@
         query_heads, key_heads, value_heads, attended_heads, grad_heads, lse, cols, counts
     )
     grad_heads_mixed = jnp.concatenate([query_grad, key_grad, value_grad], axis=1)
-    term_qkv = contract_rows(normed_all, grad_heads_mixed)
     term_out = contract_rows(attended_heads, cotan_all)
-    qkv_cols = term_qkv.shape[1]
+    qkv_cols = grad_heads_mixed.shape[1]
     summed, moved_grads, attended = sum_and_exchange(
-        jnp.concatenate([term_qkv, term_out.reshape(term_qkv.shape[0], -1)], axis=1),
-        grad_heads_mixed,
-        attended_heads,
+        normed_all, term_out, grad_heads_mixed, attended_heads
     )
     result = (
         feats.astype(jnp.float32) + jnp.dot(attended, w_out, preferred_element_type=jnp.float32)

time: 257 us -> 254 us (0.988)
  matrix products: 38.7 us -> 30.6 us
  Pallas kernels: 109 us -> 115 us
    dot_general x2 -> x1, matrix products: 13.6 us -> 5.51 us  [contract_rows(): lax.dot_general(left_cols, right_cols, (((0,), (0,)), ((), ())), preferre...]
    pallas_call x1, Pallas kernels: 55.9 us -> 62 us  [sum_and_exchange(): pl.pallas_call(functools.partial(exchange_kernel, n, m), out_shape=(jax.S...]
    unnamed x36 -> x32, local copies, waits for them, and re-layouts: 5.63 us -> 4.21 us
where the time goes in v16:
time: 254 us; the launch traced here: 253 us
  Pallas kernels  115 us (45%)
  waiting for transfers between devices  68.3 us (27%)
  matrix products  30.6 us (12%)
  between operations  14.2 us (6%)
  local copies, waits for them, and re-layouts  11.4 us (4%)
  other arithmetic  8.54 us (3%)
  starting transfers between devices  4.3 us (2%)
    pallas_call x1, Pallas kernels, sum_and_exchange(): pl.pallas_call(functools.partial(exchange_kernel, n, m), out_shape=(jax.S...  62 us
    all_gather x1, waiting for transfers between devices, body(): normed_all = lax.all_gather(normed, 'seq', axis=0, tiled=True)  50.4 us
    pallas_call x1, Pallas kernels, attention_backward(): pl.pallas_call(attn_bwd_kernel, out_shape=tuple((jax.ShapeDtypeStruct((n,...  29.5 us
    pallas_call x1, Pallas kernels, attention_forward(): pl.pallas_call(attn_fwd_kernel, out_shape=(jax.ShapeDtypeStruct((n, width...  24 us
    all_gather x1, waiting for transfers between devices, body(): cotan_all = lax.all_gather(cotan, 'seq', axis=0, tiled=True)  15.9 us
    dot_general x1, matrix products, body(): jnp.dot(normed_all, w_heads, preferred_element_type=jnp.float32)  8.27 us
    dot_general x1, matrix products, body(): lax.dot_general(grad_mixed, w_qkv, (((1,), (1,)), ((), ())), preferred_el...  7.74 us
    dot_general x1, matrix products, body(): lax.dot_general(cotan_all, w_out_rows, (((1,), (1,)), ((), ())), preferre...  6.87 us
  transfers between devices with their start and end apart: 3, of which 3 were waited for; matrix products, arithmetic and copies ran while one was open for 9% of the time, Pallas kernels for 9%

profile of v16, /device:TPU:0, one launch (start us, length us, event | category | flops | bytes accessed | tf_op | source)
XLA Modules:
  0.0 252.8 jit_solution(9810529755342016376)
XLA Ops:
  7.2 1.6 convert_reduce_fusion
  8.8 1.6 fusion.12
  10.5 1.4 fusion.6
  11.9 0.0 all-gather.5.cloned.1.call-start
  11.9 0.7 all-gather.5.cloned.1.call-update
  12.7 0.1 copy.14
  12.7 0.1 reshape_squeeze.3.cols_ref
  12.8 1.2 constant_dynamic-slice_fusion.2
  14.0 50.4 %all-gather.3.cloned.1.call-done.na_ref = bf16[4096,1024]{1,0:T(8,128)(2,1)} async-done(((bf16[512,1024]{1,0:T(8,128)(2,1)}), bf16[4096,1024]{1,0:T(8,128)(2,1)}) %all-gather.3.cloned.1.call-update) | async-done | bytes 8388624 | tf_op jit(solution)/shard_map/all_gather | solution.py:392
  64.5 8.3 %convolution_convert_fusion = bf16[4096,384]{1,0:T(8,128)(2,1)S(1)} fusion(bf16[4096,1024]{1,0:T(8,128)(2,1)} %all-gather.3.cloned.1.call-done.na_ref, bf16[1024,128]{1,0:T(8,128)(2,1)S(1)} %get-tuple-element.24, bf16[1024,128]{1,0:T(8,128)(2,1)S(1)} %get-tuple-element.23, bf16[1024,128]{1,0:T(8,128)(2,1)S(1)} %get-tuple-element.22), kind=kOutput, calls=%fused_computation | convolution fusion | flops 3225157632 | bytes 12320768 | tf_op jit(solution)/shard_map/dot_general | solution.py:401
  72.7 0.5 fusion.22
  73.3 0.1 copy-done.9
  73.4 24.0 %shard_map.102 = (bf16[4096,128]{1,0:T(8,128)(2,1)S(1)}, f32[8192,128]{1,0:T(8,128)}) custom-call(s32[256]{0:T(256)S(1)} %reshape_squeeze.3.cols_ref, s32[32]{0:T(128)S(1)} %bitcast.27, bf16[4096,128]{1,0:T(8,128)(2,1)S(1)} %get-tuple-element.27.q_ref, bf16[4096,128]{1,0:T(8,128)(2,1)S(1)} %get-tuple-element.26.k_ref, ...), custom_call_target="tpu_custom_call" | custom-call | tf_op jit(solution)/shard_map/pallas_call | solution.py:180
  97.4 1.0 copy-done.3
  98.4 1.0 copy-done.4
  99.3 1.0 copy-done.6
  100.3 15.9 %all-gather.5.cloned.1.call-done = bf16[4096,1024]{1,0:T(8,128)(2,1)} async-done(((bf16[512,1024]{1,0:T(8,128)(2,1)}), bf16[4096,1024]{1,0:T(8,128)(2,1)}) %all-gather.5.cloned.1.call-update) | async-done | bytes 8388624 | tf_op jit(solution)/shard_map/all_gather | solution.py:393
  116.2 5.5 %fusion.23 = f32[128,1024]{1,0:T(8,128)} fusion(bf16[4096,128]{1,0:T(8,128)(2,1)S(1)} %get-tuple-element.12.o_ref, bf16[4096,1024]{1,0:T(8,128)(2,1)} %all-gather.5.cloned.1.call-done), kind=kOutput, calls=%fused_computation.38 | convolution fusion | flops 1073741824 | bytes 9961472 | tf_op jit(solution)/shard_map/dot_general | solution.py:28
  121.7 1.9 reshape.54.xo_ref
  123.6 6.9 %fusion.do_ref = bf16[4096,128]{1,0:T(8,128)(2,1)} fusion(bf16[4096,1024]{1,0:T(8,128)(2,1)} %all-gather.5.cloned.1.call-done, bf16[1024,1024]{1,0:T(8,128)(2,1)S(1)} %copy-done, s32[]{:T(128)S(6)} %select_n.15), kind=kOutput, calls=%fused_computation.2 | convolution fusion | flops 1074266112 | bytes 9699332 | tf_op jit(solution)/shard_map/dot_general | solution.py:411
  130.5 29.5 %shard_map.103 = (bf16[4096,128]{1,0:T(8,128)(2,1)S(1)}, bf16[4096,128]{1,0:T(8,128)(2,1)S(1)}, bf16[4096,128]{1,0:T(8,128)(2,1)S(1)}) custom-call(s32[256]{0:T(256)S(1)} %reshape_squeeze.3.cols_ref, s32[32]{0:T(128)S(1)} %bitcast.28, bf16[4096,128]{1,0:T(8,128)(2,1)S(1)} %copy-done.7, bf16[4096,128]{1,0:T(8,128)(2,1)S(1)} %copy-done.5, ...), custom_call_target="tpu_custom_call" | custom-call | tf_op jit(solution)/shard_map/pallas_call | solution.py:194
  160.1 2.1 pad_maximum_fusion
  162.2 62.0 %shard_map.104 = (bf16[16,64,512]{2,1,0:T(8,128)(2,1)S(1)}, bf16[512,3072]{1,0:T(8,128)(2,1)}, bf16[512,1024]{1,0:T(8,128)(2,1)S(1)}) custom-call(bf16[4096,1024]{1,0:T(8,128)(2,1)} %all-gather.3.cloned.1.call-done.na_ref, f32[16,64,128]{2,1,0:T(8,128)S(1)} %copy-done.8, bf16[8,512,384]{2,1,0:T(8,128)(2,1)} %bitcast.29, bf16[8,512,128]{2,1,0:T(8,128)(2,1)S(1)} %bitcast.24), custom_call_target="tpu_custom_call" | custom-call | tf_op jit(solution)/shard_map/pallas_call | solution.py:361
  224.2 1.0 slice.23
  225.2 0.8 reshape.60
  226.0 4.2 %all-to-all-start = ((bf16[8,128,384]{2,1,0:T(8,128)(2,1)}), bf16[8,128,384]{2,1,0:T(8,128)(2,1)}, u32[]{:S(2)}, u32[]{:S(2)}) async-start(bf16[8,128,384]{2,1,0:T(8,128)(2,1)} %bitcast.30), calls=%async_computation | async-start | bytes 1572864 | tf_op jit(solution)/shard_map/all_to_all | solution.py:439
  230.2 7.7 %multiply_reduce_fusion = (f32[512]{0:T(512)S(1)}, f32[512]{0:T(512)S(1)}, f32[512,1024]{1,0:T(8,128)S(1)}) fusion(f32[1024]{0:T(1024)S(1)} %copy-done.13, f32[512]{0:T(512)S(1)} %add_rsqrt_fusion, f32[512]{0:T(512)S(1)} %broadcast_multiply_fusion.2, bf16[512,1024]{1,0:T(8,128)(2,1)} %param.7, bf16[512,3072]{1,0:T(8,128)(2,1)} %get-tuple-element.18, ...), kind=kOutput, calls=%fused_computation.20 | convolution fusion | flops 3224894464 | bytes 12595200 | tf_op jit(solution)/shard_map/dot_general | solution.py:427
  238.0 1.8 fusion.11
  239.8 2.2 fusion.13
  242.1 1.3 all-to-all-done
  243.4 1.6 copy.16
  245.0 1.0 copy.20
  (32 shorter events, 0.2 us)
Async XLA Ops:
  7.2 116.4 %copy-start = (bf16[1024,1024]{1,0:T(8,128)(2,1)S(1)}, bf16[1024,1024]{1,0:T(8,128)(2,1)}, u32[]{:S(2)}) copy-start(bf16[1024,1024]{1,0:T(8,128)(2,1)} %param.10) | copy-start | bytes 6291460
  7.2 3.3 %copy-start.10 = (bf16[512,1024]{1,0:T(8,128)(2,1)S(1)}, bf16[512,1024]{1,0:T(8,128)(2,1)}, u32[]{:S(2)}) copy-start(bf16[512,1024]{1,0:T(8,128)(2,1)} %param.7) | copy-start | bytes 3145732
  7.2 3.3 %copy-start.13 = (f32[1024]{0:T(1024)S(1)}, f32[1024]{0:T(1024)}, u32[]{:S(2)}) copy-start(f32[1024]{0:T(1024)} %param.8) | copy-start | bytes 12292
  7.2 57.3 %all-gather.3.cloned.1.call-start = ((), (), s32[]{:S(2)}) async-start(), calls=%async_computation.1 | async-start | bytes 9437184 | tf_op jit(solution)/shard_map/all_gather | solution.py:392
  10.5 2.1 copy-start.14
  11.9 104.3 %all-gather.5.cloned.1.call-start = ((), (), s32[]{:S(2)}) async-start(), calls=%async_computation.2 | async-start | bytes 9437184 | tf_op jit(solution)/shard_map/all_gather | solution.py:393
  72.7 0.7 copy-start.9
  97.3 1.0 copy-start.3
  98.4 1.0 copy-start.4
  99.3 1.0 copy-start.6
  100.3 21.4 %copy-start.1 = (bf16[4096,128]{1,0:T(8,128)(2,1)}, bf16[4096,128]{1,0:T(8,128)(2,1)S(1)}, u32[]{:S(2)}) copy-start(bf16[4096,128]{1,0:T(8,128)(2,1)S(1)} %get-tuple-element.12.o_ref) | copy-start | bytes 3145732
  123.6 6.9 %copy-start.5 = (bf16[4096,128]{1,0:T(8,128)(2,1)S(1)}, bf16[4096,128]{1,0:T(8,128)(2,1)}, u32[]{:S(2)}) copy-start(bf16[4096,128]{1,0:T(8,128)(2,1)} %copy-done.4) | copy-start | bytes 3145732
  123.6 6.9 %copy-start.7 = (bf16[4096,128]{1,0:T(8,128)(2,1)S(1)}, bf16[4096,128]{1,0:T(8,128)(2,1)}, u32[]{:S(2)}) copy-start(bf16[4096,128]{1,0:T(8,128)(2,1)} %copy-done.6) | copy-start | bytes 3145732
  160.0 2.1 copy-start.2
  160.0 2.1 copy-start.8
  226.0 17.4 %all-to-all-start = ((bf16[8,128,384]{2,1,0:T(8,128)(2,1)}), bf16[8,128,384]{2,1,0:T(8,128)(2,1)}, u32[]{:S(2)}, u32[]{:S(2)}) async-start(bf16[8,128,384]{2,1,0:T(8,128)(2,1)} %bitcast.30), calls=%async_computation | async-start | bytes 1572864 | tf_op jit(solution)/shard_map/all_to_all | solution.py:439
  230.2 7.8 %copy-start.11 = (bf16[512,1024]{1,0:T(8,128)(2,1)S(1)}, bf16[512,1024]{1,0:T(8,128)(2,1)}, u32[]{:S(2)}) copy-start(bf16[512,1024]{1,0:T(8,128)(2,1)} %param.7) | copy-start | bytes 3145732
  230.2 7.8 %copy-start.12 = (bf16[512,1024]{1,0:T(8,128)(2,1)S(1)}, bf16[512,1024]{1,0:T(8,128)(2,1)}, u32[]{:S(2)}) copy-start(bf16[512,1024]{1,0:T(8,128)(2,1)} %param.13) | copy-start | bytes 3145732
Sparse Core Ops, SparseCore 0:
  12.0 52.3 all-gather.2
  66.2 49.9 all-gather.4

commit v17 on v16

--- a/solution.py
+++ b/solution.py
@@ -217,15 +217,19 @@
     n,
     m,
     na_ref,
-    xo_ref,
+    co_ref,
     g_ref,
     a_ref,
     o_ref,
+    oo_ref,
     moved_ref,
     att_ref,
     x_ref,
     recv,
     gath,
+    xo_ref,
+    recv_o,
+    gath_o,
     landed,
     att_landed,
     sems,
@@ -315,18 +319,33 @@
     qkv = tn_dot(na_ref[0:share, :], g_ref[0])
     for c in range(1, m):
         qkv = qkv + tn_dot(na_ref[c * share : (c + 1) * share, :], g_ref[c])
-    qkv_cols = g_ref.shape[2]
-    x_ref[:, :, 0:qkv_cols] = qkv.reshape(n, x_ref.shape[1], qkv_cols)
-    x_ref[:, :, qkv_cols:] = xo_ref[...]
+    x_ref[...] = qkv.reshape(x_ref.shape)
+    cshare = a_ref.shape[1]
+    term_out = tn_dot(a_ref[0], co_ref[0:cshare, :])
+    for c in range(1, m):
+        term_out = term_out + tn_dot(a_ref[c], co_ref[c * cshare : (c + 1) * cshare, :])
+    xo_ref[...] = term_out.reshape(xo_ref.shape)
     rs = (lambda peer: x_ref.at[peer], recv, sems.at[0], sems.at[1], "dp", me, n)
-    finish_all(start_all(*rs), *rs)
+    rs_o = (lambda peer: xo_ref.at[peer], recv_o, sems.at[4], sems.at[5], "dp", me, n)
+    rs_started = start_all(*rs)
+    rs_o_started = start_all(*rs_o)
+    finish_all(rs_started, *rs)
+    finish_all(rs_o_started, *rs_o)
     total = x_ref[me]
+    total_o = xo_ref[me]
     for k in range(1, n):
         total = total + recv[lax.rem(me + k, n)]
+        total_o = total_o + recv_o[lax.rem(me + k, n)]
     gath[me] = total.astype(gath.dtype)
+    gath_o[me] = total_o.astype(gath_o.dtype)
     ag = (lambda peer: gath.at[me], gath, sems.at[2], sems.at[3], "dp", me, n)
-    finish_all(start_all(*ag), *ag)
+    ag_o = (lambda peer: gath_o.at[me], gath_o, sems.at[6], sems.at[7], "dp", me, n)
+    ag_started = start_all(*ag)
+    ag_o_started = start_all(*ag_o)
+    finish_all(ag_started, *ag)
+    finish_all(ag_o_started, *ag_o)
     o_ref[...] = gath[...]
+    oo_ref[...] = gath_o[...]
     own = g_ref[here]
     for t in range(parts):
         landed[:, pl.ds(pl.multiple_of(t * group + here * BLK, BLK), BLK)] = own[
@@ -344,43 +363,46 @@
     att_ref[...] = att_landed[...]
 
 
-def sum_and_exchange(normed_all, term_out, grads, attended_heads):
+def sum_and_exchange(normed_all, cotan_all, grads, attended_heads):
     n = lax.axis_size("dp")
     m = lax.axis_size("seq")
     rows = normed_all.shape[1]
     qkv_cols = grads.shape[1]
-    extra = term_out.size // rows
-    cols = qkv_cols + extra
-    chunk_shape = (n, rows // n, cols)
-    term_part = term_out.reshape(n, rows // n, extra)
+    out_rows, out_cols = attended_heads.shape[1], cotan_all.shape[1]
+    chunk_shape = (n, rows // n, qkv_cols)
+    out_chunks = (n, out_rows // n, out_cols)
     pieces = grads.reshape(m, grads.shape[0] // m, grads.shape[1])
     att_pieces = attended_heads.reshape(m, attended_heads.shape[0] // m, attended_heads.shape[1])
     parts = grads.shape[1] // BLK
     final = (pieces.shape[1], parts * m * BLK)
     att_final = (att_pieces.shape[1], m * att_pieces.shape[2])
-    out, moved, attended = pl.pallas_call(
+    out, out_o, moved, attended = pl.pallas_call(
         functools.partial(exchange_kernel, n, m),
         out_shape=(
             jax.ShapeDtypeStruct(chunk_shape, jnp.bfloat16),
+            jax.ShapeDtypeStruct(out_chunks, jnp.bfloat16),
             jax.ShapeDtypeStruct(final, pieces.dtype),
             jax.ShapeDtypeStruct(att_final, att_pieces.dtype),
         ),
         in_specs=[vmem_spec(), vmem_spec(), vmem_spec(), vmem_spec()],
-        out_specs=(vmem_spec(), vmem_spec(), vmem_spec()),
+        out_specs=(vmem_spec(), vmem_spec(), vmem_spec(), vmem_spec()),
         scratch_shapes=[
             pltpu.VMEM(chunk_shape, jnp.float32),
             pltpu.VMEM(chunk_shape, jnp.float32),
             pltpu.VMEM(chunk_shape, jnp.bfloat16),
+            pltpu.VMEM(out_chunks, jnp.float32),
+            pltpu.VMEM(out_chunks, jnp.float32),
+            pltpu.VMEM(out_chunks, jnp.bfloat16),
             pltpu.VMEM(final, pieces.dtype),
             pltpu.VMEM(att_final, att_pieces.dtype),
-            pltpu.SemaphoreType.DMA((4, n)),
+            pltpu.SemaphoreType.DMA((8, n)),
             pltpu.SemaphoreType.DMA((2, parts + 1, m)),
         ],
         compiler_params=pltpu.CompilerParams(
             collective_id=0, has_side_effects=True, vmem_limit_bytes=VMEM_LIMIT
         ),
-    )(normed_all, term_part, pieces, att_pieces)
-    return out.reshape(rows, cols), moved, attended
+    )(normed_all, cotan_all, pieces, att_pieces)
+    return out.reshape(rows, qkv_cols), out_o.reshape(out_rows, out_cols), moved, attended
 
 
 def body(feats, gain, w_qkv, w_out, block_cols, block_counts, cotan):
@@ -415,10 +437,8 @@
         query_heads, key_heads, value_heads, attended_heads, grad_heads, lse, cols, counts
     )
     grad_heads_mixed = jnp.concatenate([query_grad, key_grad, value_grad], axis=1)
-    term_out = contract_rows(attended_heads, cotan_all)
-    qkv_cols = grad_heads_mixed.shape[1]
-    summed, moved_grads, attended = sum_and_exchange(
-        normed_all, term_out, grad_heads_mixed, attended_heads
+    term_qkv, grad_out, moved_grads, attended = sum_and_exchange(
+        normed_all, cotan_all, grad_heads_mixed, attended_heads
     )
     result = (
         feats.astype(jnp.float32) + jnp.dot(attended, w_out, preferred_element_type=jnp.float32)
@@ -433,14 +453,11 @@
     grad_feats = (
         cotan.astype(jnp.float32) + inverse * (gained - mean_one - scaled * mean_two)
     ).astype(jnp.bfloat16)
-    term_qkv = summed[:, :qkv_cols]
-    term_out = summed[:, qkv_cols:].reshape(term_out.shape)
     grad_qkv = regroup_columns(
         lax.all_to_all(term_qkv, "seq", split_axis=0, concat_axis=1, tiled=True),
         seq_count,
         group_width,
     )
-    grad_out = term_out
     return (result, grad_feats, grad_qkv, grad_out)
 
 

time: 254 us -> 247 us (0.972)
  matrix products: 30.6 us -> 25.1 us
  local copies, waits for them, and re-layouts: 11.4 us -> 8.28 us
    dot_general x1 -> x0, matrix products: 5.51 us -> none  [contract_rows(): lax.dot_general(left_cols, right_cols, (((0,), (0,)), ((), ())), preferre...]
    reshape x2 -> x0, local copies, waits for them, and re-layouts: 2.75 us -> none  [the longest x1 1.93 us: sum_and_exchange(): term_part = term_out.reshape(n, rows // n, extra)]
    pallas_call x1, Pallas kernels: 62 us -> 64.7 us  [sum_and_exchange(): pl.pallas_call(functools.partial(exchange_kernel, n, m), out_shape=(jax.S...]
  transfers between devices with their start and end apart: 3 -> 3, of which waited for: 3 -> 3; matrix products, arithmetic and copies ran while one was open for 9% -> 9% of each run, Pallas kernels for 9% -> 10%
where the time goes in v17:
time: 247 us
  Pallas kernels  117 us (47%)
  waiting for transfers between devices  68.5 us (28%)
  matrix products  25.1 us (10%)
  between operations  14.2 us (6%)
  other arithmetic  8.47 us (3%)
  local copies, waits for them, and re-layouts  8.28 us (3%)
  starting transfers between devices  4.54 us (2%)
    pallas_call x1, Pallas kernels, sum_and_exchange(): pl.pallas_call(functools.partial(exchange_kernel, n, m), out_shape=(jax.S...  64.7 us
    all_gather x1, waiting for transfers between devices, body(): normed_all = lax.all_gather(normed, 'seq', axis=0, tiled=True)  50.4 us
    pallas_call x1, Pallas kernels, attention_backward(): pl.pallas_call(attn_bwd_kernel, out_shape=tuple((jax.ShapeDtypeStruct((n,...  29.3 us
    pallas_call x1, Pallas kernels, attention_forward(): pl.pallas_call(attn_fwd_kernel, out_shape=(jax.ShapeDtypeStruct((n, width...  23.5 us
    all_gather x1, waiting for transfers between devices, body(): cotan_all = lax.all_gather(cotan, 'seq', axis=0, tiled=True)  16.3 us
    dot_general x1, matrix products, body(): jnp.dot(normed_all, w_heads, preferred_element_type=jnp.float32)  8.27 us
    dot_general x1, matrix products, body(): lax.dot_general(grad_mixed, w_qkv, (((1,), (1,)), ((), ())), preferred_el...  7.74 us
    dot_general x1, matrix products, body(): lax.dot_general(cotan_all, w_out_rows, (((1,), (1,)), ((), ())), preferre...  6.88 us
  transfers between devices with their start and end apart: 3, of which 3 were waited for; matrix products, arithmetic and copies ran while one was open for 9% of the time, Pallas kernels for 10%

profile of v17, /device:TPU:0, one launch (start us, length us, event | category | flops | bytes accessed | tf_op | source)
XLA Modules:
  0.0 246.6 jit_solution(12548166846827918813)
XLA Ops:
  7.2 0.0 copy-start
  7.2 0.0 all-gather.3.cloned.1.call-start
  7.2 1.6 convert_reduce_fusion
  8.8 1.6 fusion.12
  10.5 1.4 fusion.6
  11.9 0.0 all-gather.3.cloned.1.call-update
  11.9 0.0 all-gather.5.cloned.1.call-start
  11.9 0.7 all-gather.5.cloned.1.call-update
  12.7 0.1 copy.16
  12.7 0.1 reshape_squeeze.3.cols_ref
  12.8 1.2 constant_dynamic-slice_fusion.2
  14.0 50.4 %all-gather.3.cloned.1.call-done.na_ref = bf16[4096,1024]{1,0:T(8,128)(2,1)} async-done(((bf16[512,1024]{1,0:T(8,128)(2,1)}), bf16[4096,1024]{1,0:T(8,128)(2,1)}) %all-gather.3.cloned.1.call-update) | async-done | bytes 8388624 | tf_op jit(solution)/shard_map/all_gather | solution.py:414
  64.5 8.3 %convolution_convert_fusion = bf16[4096,384]{1,0:T(8,128)(2,1)S(1)} fusion(bf16[4096,1024]{1,0:T(8,128)(2,1)} %all-gather.3.cloned.1.call-done.na_ref, bf16[1024,128]{1,0:T(8,128)(2,1)S(1)} %get-tuple-element.26, bf16[1024,128]{1,0:T(8,128)(2,1)S(1)} %get-tuple-element.25, bf16[1024,128]{1,0:T(8,128)(2,1)S(1)} %get-tuple-element.24), kind=kOutput, calls=%fused_computation | convolution fusion | flops 3225157632 | bytes 12320768 | tf_op jit(solution)/shard_map/dot_general | solution.py:423
  72.7 0.5 fusion.22
  73.3 0.1 copy-done.8
  73.4 23.5 %shard_map.102 = (bf16[4096,128]{1,0:T(8,128)(2,1)S(1)}, f32[8192,128]{1,0:T(8,128)}) custom-call(s32[256]{0:T(256)S(1)} %reshape_squeeze.3.cols_ref, s32[32]{0:T(128)S(1)} %bitcast.25, bf16[4096,128]{1,0:T(8,128)(2,1)S(1)} %get-tuple-element.29.q_ref, bf16[4096,128]{1,0:T(8,128)(2,1)S(1)} %get-tuple-element.28.k_ref, ...), custom_call_target="tpu_custom_call" | custom-call | tf_op jit(solution)/shard_map/pallas_call | solution.py:180
  96.9 1.0 copy-done.2
  97.9 1.0 copy-done.4
  98.9 1.0 copy-done.6
  99.9 16.3 %all-gather.5.cloned.1.call-done.co_ref = bf16[4096,1024]{1,0:T(8,128)(2,1)} async-done(((bf16[512,1024]{1,0:T(8,128)(2,1)}), bf16[4096,1024]{1,0:T(8,128)(2,1)}) %all-gather.5.cloned.1.call-update) | async-done | bytes 8388624 | tf_op jit(solution)/shard_map/all_gather | solution.py:415
  116.2 6.9 %fusion.do_ref = bf16[4096,128]{1,0:T(8,128)(2,1)} fusion(bf16[4096,1024]{1,0:T(8,128)(2,1)} %all-gather.5.cloned.1.call-done.co_ref, bf16[1024,1024]{1,0:T(8,128)(2,1)S(1)} %copy-done, s32[]{:T(128)S(6)} %select_n.15), kind=kOutput, calls=%fused_computation.2 | convolution fusion | flops 1074266112 | bytes 9699332 | tf_op jit(solution)/shard_map/dot_general | solution.py:433
  123.1 29.3 %shard_map.103 = (bf16[4096,128]{1,0:T(8,128)(2,1)S(1)}, bf16[4096,128]{1,0:T(8,128)(2,1)S(1)}, bf16[4096,128]{1,0:T(8,128)(2,1)S(1)}) custom-call(s32[256]{0:T(256)S(1)} %reshape_squeeze.3.cols_ref, s32[32]{0:T(128)S(1)} %bitcast.26, bf16[4096,128]{1,0:T(8,128)(2,1)S(1)} %copy-done.5, bf16[4096,128]{1,0:T(8,128)(2,1)S(1)} %copy-done.3, ...), custom_call_target="tpu_custom_call" | custom-call | tf_op jit(solution)/shard_map/pallas_call | solution.py:194
  152.3 2.1 pad_maximum_fusion
  154.4 64.7 %shard_map.104 = (bf16[16,64,384]{2,1,0:T(8,128)(2,1)}, bf16[16,8,1024]{2,1,0:T(8,128)(2,1)S(1)}, bf16[512,3072]{1,0:T(8,128)(2,1)}, bf16[512,1024]{1,0:T(8,128)(2,1)S(1)}) custom-call(bf16[4096,1024]{1,0:T(8,128)(2,1)} %all-gather.3.cloned.1.call-done.na_ref, bf16[4096,1024]{1,0:T(8,128)(2,1)} %all-gather.5.cloned.1.call-done.co_ref, ...), custom_call_target="tpu_custom_call" | custom-call | tf_op jit(solution)/shard_map/pallas_call | solution.py:379
  219.1 4.5 %all-to-all-start = ((bf16[8,128,384]{2,1,0:T(8,128)(2,1)}), bf16[8,128,384]{2,1,0:T(8,128)(2,1)}, u32[]{:S(2)}, u32[]{:S(2)}) async-start(bf16[8,128,384]{2,1,0:T(8,128)(2,1)} %bitcast.4), calls=%async_computation | async-start | bytes 1572864 | tf_op jit(solution)/shard_map/all_to_all | solution.py:457
  223.5 7.7 %multiply_reduce_fusion = (f32[512]{0:T(512)S(1)}, f32[512]{0:T(512)S(1)}, f32[512,1024]{1,0:T(8,128)S(1)}) fusion(f32[1024]{0:T(1024)S(1)} %copy-done.12, f32[512]{0:T(512)S(1)} %add_rsqrt_fusion, f32[512]{0:T(512)S(1)} %broadcast_multiply_fusion.2, bf16[512,1024]{1,0:T(8,128)(2,1)} %param.7, bf16[512,3072]{1,0:T(8,128)(2,1)} %get-tuple-element.19, ...), kind=kOutput, calls=%fused_computation.20 | convolution fusion | flops 3224894464 | bytes 12595200 | tf_op jit(solution)/shard_map/dot_general | solution.py:447
  231.3 1.8 fusion.11
  233.1 2.2 fusion.13
  235.4 1.1 all-to-all-done
  236.5 1.6 copy.18
  238.0 1.0 copy.22
  239.1 0.7 copy.24
  (26 shorter events, 0.1 us)
Async XLA Ops:
  7.2 109.0 %copy-start = (bf16[1024,1024]{1,0:T(8,128)(2,1)S(1)}, bf16[1024,1024]{1,0:T(8,128)(2,1)}, u32[]{:S(2)}) copy-start(bf16[1024,1024]{1,0:T(8,128)(2,1)} %param.10) | copy-start | bytes 6291460
  7.2 3.3 %copy-start.9 = (bf16[512,1024]{1,0:T(8,128)(2,1)S(1)}, bf16[512,1024]{1,0:T(8,128)(2,1)}, u32[]{:S(2)}) copy-start(bf16[512,1024]{1,0:T(8,128)(2,1)} %param.7) | copy-start | bytes 3145732
  7.2 3.3 %copy-start.12 = (f32[1024]{0:T(1024)S(1)}, f32[1024]{0:T(1024)}, u32[]{:S(2)}) copy-start(f32[1024]{0:T(1024)} %param.8) | copy-start | bytes 12292
  7.2 57.3 %all-gather.3.cloned.1.call-start = ((), (), s32[]{:S(2)}) async-start(), calls=%async_computation.1 | async-start | bytes 9437184 | tf_op jit(solution)/shard_map/all_gather | solution.py:414
  10.5 2.1 copy-start.13
  11.9 104.3 %all-gather.5.cloned.1.call-start = ((), (), s32[]{:S(2)}) async-start(), calls=%async_computation.2 | async-start | bytes 9437184 | tf_op jit(solution)/shard_map/all_gather | solution.py:415
  72.7 0.7 copy-start.8
  73.3 49.8 %copy-start.1 = (bf16[4096,128]{1,0:T(8,128)(2,1)}, bf16[4096,128]{1,0:T(8,128)(2,1)S(1)}, u32[]{:S(2)}) copy-start(bf16[4096,128]{1,0:T(8,128)(2,1)S(1)} %get-tuple-element.27.v_ref) | copy-start | bytes 3145732
  96.9 1.0 copy-start.2
  97.9 1.0 copy-start.4
  98.9 1.0 copy-start.6
  116.2 6.9 %copy-start.3 = (bf16[4096,128]{1,0:T(8,128)(2,1)S(1)}, bf16[4096,128]{1,0:T(8,128)(2,1)}, u32[]{:S(2)}) copy-start(bf16[4096,128]{1,0:T(8,128)(2,1)} %copy-done.2) | copy-start | bytes 3145732
  116.2 6.9 %copy-start.5 = (bf16[4096,128]{1,0:T(8,128)(2,1)S(1)}, bf16[4096,128]{1,0:T(8,128)(2,1)}, u32[]{:S(2)}) copy-start(bf16[4096,128]{1,0:T(8,128)(2,1)} %copy-done.4) | copy-start | bytes 3145732
  152.3 2.1 copy-start.7
  219.1 17.4 %all-to-all-start = ((bf16[8,128,384]{2,1,0:T(8,128)(2,1)}), bf16[8,128,384]{2,1,0:T(8,128)(2,1)}, u32[]{:S(2)}, u32[]{:S(2)}) async-start(bf16[8,128,384]{2,1,0:T(8,128)(2,1)} %bitcast.4), calls=%async_computation | async-start | bytes 1572864 | tf_op jit(solution)/shard_map/all_to_all | solution.py:457
  223.5 7.8 %copy-start.10 = (bf16[512,1024]{1,0:T(8,128)(2,1)S(1)}, bf16[512,1024]{1,0:T(8,128)(2,1)}, u32[]{:S(2)}) copy-start(bf16[512,1024]{1,0:T(8,128)(2,1)} %param.7) | copy-start | bytes 3145732
  223.5 7.8 %copy-start.11 = (bf16[512,1024]{1,0:T(8,128)(2,1)S(1)}, bf16[512,1024]{1,0:T(8,128)(2,1)}, u32[]{:S(2)}) copy-start(bf16[512,1024]{1,0:T(8,128)(2,1)} %param.13) | copy-start | bytes 3145732
Sparse Core Ops, SparseCore 0:
  12.0 52.3 all-gather.2
  66.2 49.9 all-gather.4

commit v18 on v17

--- a/solution.py
+++ b/solution.py
@@ -71,7 +71,7 @@
     return lax.broadcasted_iota(jnp.int32, (1, slots * BLK), 1) < cnt * BLK
 
 
-FINE_TIERS = (1, 2, 3, 4, 6, MAXB)
+FINE_TIERS = tuple(range(1, MAXB + 1))
 
 
 def by_tier(cnt, body, tiers=SLOT_TIERS):
@@ -181,7 +181,7 @@
         attn_fwd_kernel,
         out_shape=(
             jax.ShapeDtypeStruct((n, width), jnp.bfloat16),
-            jax.ShapeDtypeStruct(((n // BLK) * rows, 128), jnp.float32),
+            jax.ShapeDtypeStruct(((n // BLK) * rows, 8), jnp.float32),
         ),
         in_specs=[smem_spec(), smem_spec(), vmem_spec(), vmem_spec(), vmem_spec()],
         out_specs=(vmem_spec(), vmem_spec()),

time: 247 us -> 247 us (level)
  no operation moved by 1% of the time
where the time goes in v18:
time: 247 us
  Pallas kernels  118 us (48%)
  waiting for transfers between devices  67.6 us (27%)
  matrix products  25.1 us (10%)
  between operations  14.2 us (6%)
  other arithmetic  8.47 us (3%)
  local copies, waits for them, and re-layouts  8.28 us (3%)
  starting transfers between devices  4.58 us (2%)
    pallas_call x1, Pallas kernels, sum_and_exchange(): pl.pallas_call(functools.partial(exchange_kernel, n, m), out_shape=(jax.S...  64.6 us
    all_gather x1, waiting for transfers between devices, body(): normed_all = lax.all_gather(normed, 'seq', axis=0, tiled=True)  50.4 us
    pallas_call x1, Pallas kernels, attention_backward(): pl.pallas_call(attn_bwd_kernel, out_shape=tuple((jax.ShapeDtypeStruct((n,...  29.3 us
    pallas_call x1, Pallas kernels, attention_forward(): pl.pallas_call(attn_fwd_kernel, out_shape=(jax.ShapeDtypeStruct((n, width...  24.4 us
    all_gather x1, waiting for transfers between devices, body(): cotan_all = lax.all_gather(cotan, 'seq', axis=0, tiled=True)  15.4 us
    dot_general x1, matrix products, body(): jnp.dot(normed_all, w_heads, preferred_element_type=jnp.float32)  8.27 us
    dot_general x1, matrix products, body(): lax.dot_general(grad_mixed, w_qkv, (((1,), (1,)), ((), ())), preferred_el...  7.75 us
    dot_general x1, matrix products, body(): lax.dot_general(cotan_all, w_out_rows, (((1,), (1,)), ((), ())), preferre...  6.88 us
  transfers between devices with their start and end apart: 3, of which 3 were waited for; matrix products, arithmetic and copies ran while one was open for 9% of the time, Pallas kernels for 10%

profile of v18, /device:TPU:0, one launch (start us, length us, event | category | flops | bytes accessed | tf_op | source)
XLA Modules:
  0.0 246.6 jit_solution(9683602100807163309)
XLA Ops:
  7.2 0.0 copy-start
  7.2 0.0 all-gather.3.cloned.1.call-start
  7.2 1.6 convert_reduce_fusion
  8.8 1.6 fusion.12
  10.5 1.4 fusion.6
  11.9 0.0 all-gather.3.cloned.1.call-update
  11.9 0.0 all-gather.5.cloned.1.call-start
  11.9 0.7 all-gather.5.cloned.1.call-update
  12.7 0.1 copy.16
  12.7 0.1 reshape_squeeze.3.cols_ref
  12.8 1.2 constant_dynamic-slice_fusion.2
  14.0 50.4 %all-gather.3.cloned.1.call-done.na_ref = bf16[4096,1024]{1,0:T(8,128)(2,1)} async-done(((bf16[512,1024]{1,0:T(8,128)(2,1)}), bf16[4096,1024]{1,0:T(8,128)(2,1)}) %all-gather.3.cloned.1.call-update) | async-done | bytes 8388624 | tf_op jit(solution)/shard_map/all_gather | solution.py:414
  64.5 8.3 %convolution_convert_fusion = bf16[4096,384]{1,0:T(8,128)(2,1)S(1)} fusion(bf16[4096,1024]{1,0:T(8,128)(2,1)} %all-gather.3.cloned.1.call-done.na_ref, bf16[1024,128]{1,0:T(8,128)(2,1)S(1)} %get-tuple-element.26, bf16[1024,128]{1,0:T(8,128)(2,1)S(1)} %get-tuple-element.25, bf16[1024,128]{1,0:T(8,128)(2,1)S(1)} %get-tuple-element.24), kind=kOutput, calls=%fused_computation | convolution fusion | flops 3225157632 | bytes 12320768 | tf_op jit(solution)/shard_map/dot_general | solution.py:423
  72.7 0.5 fusion.22
  73.3 0.1 copy-done.8
  73.4 24.4 %shard_map.102 = (bf16[4096,128]{1,0:T(8,128)(2,1)S(1)}, f32[8192,8]{1,0:T(8,128)}) custom-call(s32[256]{0:T(256)S(1)} %reshape_squeeze.3.cols_ref, s32[32]{0:T(128)S(1)} %bitcast.25, bf16[4096,128]{1,0:T(8,128)(2,1)S(1)} %get-tuple-element.29.q_ref, bf16[4096,128]{1,0:T(8,128)(2,1)S(1)} %get-tuple-element.28.k_ref, ...), custom_call_target="tpu_custom_call" | custom-call | tf_op jit(solution)/shard_map/pallas_call | solution.py:180
  97.8 1.0 copy-done.2
  98.8 1.0 copy-done.4
  99.8 1.0 copy-done.6
  100.8 15.4 %all-gather.5.cloned.1.call-done.co_ref = bf16[4096,1024]{1,0:T(8,128)(2,1)} async-done(((bf16[512,1024]{1,0:T(8,128)(2,1)}), bf16[4096,1024]{1,0:T(8,128)(2,1)}) %all-gather.5.cloned.1.call-update) | async-done | bytes 8388624 | tf_op jit(solution)/shard_map/all_gather | solution.py:415
  116.2 6.9 %fusion.do_ref = bf16[4096,128]{1,0:T(8,128)(2,1)} fusion(bf16[4096,1024]{1,0:T(8,128)(2,1)} %all-gather.5.cloned.1.call-done.co_ref, bf16[1024,1024]{1,0:T(8,128)(2,1)S(1)} %copy-done, s32[]{:T(128)S(6)} %select_n.15), kind=kOutput, calls=%fused_computation.2 | convolution fusion | flops 1074266112 | bytes 9699332 | tf_op jit(solution)/shard_map/dot_general | solution.py:433
  123.1 29.3 %shard_map.103 = (bf16[4096,128]{1,0:T(8,128)(2,1)S(1)}, bf16[4096,128]{1,0:T(8,128)(2,1)S(1)}, bf16[4096,128]{1,0:T(8,128)(2,1)S(1)}) custom-call(s32[256]{0:T(256)S(1)} %reshape_squeeze.3.cols_ref, s32[32]{0:T(128)S(1)} %bitcast.26, bf16[4096,128]{1,0:T(8,128)(2,1)S(1)} %copy-done.5, bf16[4096,128]{1,0:T(8,128)(2,1)S(1)} %copy-done.3, ...), custom_call_target="tpu_custom_call" | custom-call | tf_op jit(solution)/shard_map/pallas_call | solution.py:194
  152.3 2.1 pad_maximum_fusion
  154.4 64.6 %shard_map.104 = (bf16[16,64,384]{2,1,0:T(8,128)(2,1)}, bf16[16,8,1024]{2,1,0:T(8,128)(2,1)S(1)}, bf16[512,3072]{1,0:T(8,128)(2,1)}, bf16[512,1024]{1,0:T(8,128)(2,1)S(1)}) custom-call(bf16[4096,1024]{1,0:T(8,128)(2,1)} %all-gather.3.cloned.1.call-done.na_ref, bf16[4096,1024]{1,0:T(8,128)(2,1)} %all-gather.5.cloned.1.call-done.co_ref, ...), custom_call_target="tpu_custom_call" | custom-call | tf_op jit(solution)/shard_map/pallas_call | solution.py:379
  219.0 4.5 %all-to-all-start = ((bf16[8,128,384]{2,1,0:T(8,128)(2,1)}), bf16[8,128,384]{2,1,0:T(8,128)(2,1)}, u32[]{:S(2)}, u32[]{:S(2)}) async-start(bf16[8,128,384]{2,1,0:T(8,128)(2,1)} %bitcast.4), calls=%async_computation | async-start | bytes 1572864 | tf_op jit(solution)/shard_map/all_to_all | solution.py:457
  223.6 7.8 %multiply_reduce_fusion = (f32[512]{0:T(512)S(1)}, f32[512]{0:T(512)S(1)}, f32[512,1024]{1,0:T(8,128)S(1)}) fusion(f32[1024]{0:T(1024)S(1)} %copy-done.12, f32[512]{0:T(512)S(1)} %add_rsqrt_fusion, f32[512]{0:T(512)S(1)} %broadcast_multiply_fusion.2, bf16[512,1024]{1,0:T(8,128)(2,1)} %param.7, bf16[512,3072]{1,0:T(8,128)(2,1)} %get-tuple-element.19, ...), kind=kOutput, calls=%fused_computation.20 | convolution fusion | flops 3224894464 | bytes 12595200 | tf_op jit(solution)/shard_map/dot_general | solution.py:447
  231.4 1.8 fusion.11
  233.2 2.2 fusion.13
  235.4 1.0 all-to-all-done
  236.4 1.6 copy.18
  238.0 1.0 copy.22
  239.1 0.7 copy.24
  (26 shorter events, 0.1 us)
Async XLA Ops:
  7.2 109.0 %copy-start = (bf16[1024,1024]{1,0:T(8,128)(2,1)S(1)}, bf16[1024,1024]{1,0:T(8,128)(2,1)}, u32[]{:S(2)}) copy-start(bf16[1024,1024]{1,0:T(8,128)(2,1)} %param.10) | copy-start | bytes 6291460
  7.2 3.3 %copy-start.9 = (bf16[512,1024]{1,0:T(8,128)(2,1)S(1)}, bf16[512,1024]{1,0:T(8,128)(2,1)}, u32[]{:S(2)}) copy-start(bf16[512,1024]{1,0:T(8,128)(2,1)} %param.7) | copy-start | bytes 3145732
  7.2 3.3 %copy-start.12 = (f32[1024]{0:T(1024)S(1)}, f32[1024]{0:T(1024)}, u32[]{:S(2)}) copy-start(f32[1024]{0:T(1024)} %param.8) | copy-start | bytes 12292
  7.2 57.3 %all-gather.3.cloned.1.call-start = ((), (), s32[]{:S(2)}) async-start(), calls=%async_computation.1 | async-start | bytes 9437184 | tf_op jit(solution)/shard_map/all_gather | solution.py:414
  10.5 2.1 copy-start.13
  11.9 104.3 %all-gather.5.cloned.1.call-start = ((), (), s32[]{:S(2)}) async-start(), calls=%async_computation.2 | async-start | bytes 9437184 | tf_op jit(solution)/shard_map/all_gather | solution.py:415
  72.7 0.7 copy-start.8
  73.3 49.8 %copy-start.1 = (bf16[4096,128]{1,0:T(8,128)(2,1)}, bf16[4096,128]{1,0:T(8,128)(2,1)S(1)}, u32[]{:S(2)}) copy-start(bf16[4096,128]{1,0:T(8,128)(2,1)S(1)} %get-tuple-element.27.v_ref) | copy-start | bytes 3145732
  97.8 1.0 copy-start.2
  98.8 1.0 copy-start.4
  99.8 1.0 copy-start.6
  116.2 6.9 %copy-start.3 = (bf16[4096,128]{1,0:T(8,128)(2,1)S(1)}, bf16[4096,128]{1,0:T(8,128)(2,1)}, u32[]{:S(2)}) copy-start(bf16[4096,128]{1,0:T(8,128)(2,1)} %copy-done.2) | copy-start | bytes 3145732
  116.2 6.9 %copy-start.5 = (bf16[4096,128]{1,0:T(8,128)(2,1)S(1)}, bf16[4096,128]{1,0:T(8,128)(2,1)}, u32[]{:S(2)}) copy-start(bf16[4096,128]{1,0:T(8,128)(2,1)} %copy-done.4) | copy-start | bytes 3145732
  152.3 2.1 copy-start.7
  219.0 17.4 %all-to-all-start = ((bf16[8,128,384]{2,1,0:T(8,128)(2,1)}), bf16[8,128,384]{2,1,0:T(8,128)(2,1)}, u32[]{:S(2)}, u32[]{:S(2)}) async-start(bf16[8,128,384]{2,1,0:T(8,128)(2,1)} %bitcast.4), calls=%async_computation | async-start | bytes 1572864 | tf_op jit(solution)/shard_map/all_to_all | solution.py:457
  223.6 7.8 %copy-start.10 = (bf16[512,1024]{1,0:T(8,128)(2,1)S(1)}, bf16[512,1024]{1,0:T(8,128)(2,1)}, u32[]{:S(2)}) copy-start(bf16[512,1024]{1,0:T(8,128)(2,1)} %param.7) | copy-start | bytes 3145732
  223.6 7.8 %copy-start.11 = (bf16[512,1024]{1,0:T(8,128)(2,1)S(1)}, bf16[512,1024]{1,0:T(8,128)(2,1)}, u32[]{:S(2)}) copy-start(bf16[512,1024]{1,0:T(8,128)(2,1)} %param.13) | copy-start | bytes 3145732
Sparse Core Ops, SparseCore 0:
  12.0 52.3 all-gather.2
  66.2 49.9 all-gather.4

commit v19 on v17

--- a/solution.py
+++ b/solution.py
@@ -315,20 +315,20 @@
             copy = part_copy(t, peer, here, peer)
             copy.start()
             a2a_started.append(copy)
+    cshare = a_ref.shape[1]
+    term_out = tn_dot(a_ref[0], co_ref[0:cshare, :])
+    for c in range(1, m):
+        term_out = term_out + tn_dot(a_ref[c], co_ref[c * cshare : (c + 1) * cshare, :])
+    xo_ref[...] = term_out.reshape(xo_ref.shape)
+    rs_o = (lambda peer: xo_ref.at[peer], recv_o, sems.at[4], sems.at[5], "dp", me, n)
+    rs_o_started = start_all(*rs_o)
     share = g_ref.shape[1]
     qkv = tn_dot(na_ref[0:share, :], g_ref[0])
     for c in range(1, m):
         qkv = qkv + tn_dot(na_ref[c * share : (c + 1) * share, :], g_ref[c])
     x_ref[...] = qkv.reshape(x_ref.shape)
-    cshare = a_ref.shape[1]
-    term_out = tn_dot(a_ref[0], co_ref[0:cshare, :])
-    for c in range(1, m):
-        term_out = term_out + tn_dot(a_ref[c], co_ref[c * cshare : (c + 1) * cshare, :])
-    xo_ref[...] = term_out.reshape(xo_ref.shape)
     rs = (lambda peer: x_ref.at[peer], recv, sems.at[0], sems.at[1], "dp", me, n)
-    rs_o = (lambda peer: xo_ref.at[peer], recv_o, sems.at[4], sems.at[5], "dp", me, n)
     rs_started = start_all(*rs)
-    rs_o_started = start_all(*rs_o)
     finish_all(rs_started, *rs)
     finish_all(rs_o_started, *rs_o)
     total = x_ref[me]

time: 247 us -> 246 us (level)
    pallas_call x1, Pallas kernels: 64.7 us -> 61.2 us  [sum_and_exchange(): pl.pallas_call(functools.partial(exchange_kernel, n, m), out_shape=(jax.S...]
where the time goes in v19:
time: 246 us; the launch traced here: 244 us
  Pallas kernels  115 us (47%)
  waiting for transfers between devices  68.2 us (28%)
  matrix products  25.1 us (10%)
  between operations  14.2 us (6%)
  other arithmetic  8.47 us (3%)
  local copies, waits for them, and re-layouts  8.28 us (3%)
  starting transfers between devices  4.83 us (2%)
    pallas_call x1, Pallas kernels, sum_and_exchange(): pl.pallas_call(functools.partial(exchange_kernel, n, m), out_shape=(jax.S...  61.2 us
    all_gather x1, waiting for transfers between devices, body(): normed_all = lax.all_gather(normed, 'seq', axis=0, tiled=True)  50.4 us
    pallas_call x1, Pallas kernels, attention_backward(): pl.pallas_call(attn_bwd_kernel, out_shape=tuple((jax.ShapeDtypeStruct((n,...  29.4 us
    pallas_call x1, Pallas kernels, attention_forward(): pl.pallas_call(attn_fwd_kernel, out_shape=(jax.ShapeDtypeStruct((n, width...  24.2 us
    all_gather x1, waiting for transfers between devices, body(): cotan_all = lax.all_gather(cotan, 'seq', axis=0, tiled=True)  15.7 us
    dot_general x1, matrix products, body(): jnp.dot(normed_all, w_heads, preferred_element_type=jnp.float32)  8.27 us
    dot_general x1, matrix products, body(): lax.dot_general(grad_mixed, w_qkv, (((1,), (1,)), ((), ())), preferred_el...  7.75 us
    dot_general x1, matrix products, body(): lax.dot_general(cotan_all, w_out_rows, (((1,), (1,)), ((), ())), preferre...  6.88 us
  transfers between devices with their start and end apart: 3, of which 3 were waited for; matrix products, arithmetic and copies ran while one was open for 9% of the time, Pallas kernels for 10%

profile of v19, /device:TPU:0, one launch (start us, length us, event | category | flops | bytes accessed | tf_op | source)
XLA Modules:
  0.0 243.9 jit_solution(4428587606079680760)
XLA Ops:
  7.2 0.0 copy-start
  7.2 0.0 all-gather.3.cloned.1.call-start
  7.2 1.6 convert_reduce_fusion
  8.8 1.6 fusion.12
  10.5 1.4 fusion.6
  11.9 0.0 all-gather.3.cloned.1.call-update
  11.9 0.0 all-gather.5.cloned.1.call-start
  11.9 0.7 all-gather.5.cloned.1.call-update
  12.7 0.1 copy.16
  12.7 0.1 reshape_squeeze.3.cols_ref
  12.8 1.2 constant_dynamic-slice_fusion.2
  14.0 50.4 %all-gather.3.cloned.1.call-done.na_ref = bf16[4096,1024]{1,0:T(8,128)(2,1)} async-done(((bf16[512,1024]{1,0:T(8,128)(2,1)}), bf16[4096,1024]{1,0:T(8,128)(2,1)}) %all-gather.3.cloned.1.call-update) | async-done | bytes 8388624 | tf_op jit(solution)/shard_map/all_gather | solution.py:414
  64.5 8.3 %convolution_convert_fusion = bf16[4096,384]{1,0:T(8,128)(2,1)S(1)} fusion(bf16[4096,1024]{1,0:T(8,128)(2,1)} %all-gather.3.cloned.1.call-done.na_ref, bf16[1024,128]{1,0:T(8,128)(2,1)S(1)} %get-tuple-element.26, bf16[1024,128]{1,0:T(8,128)(2,1)S(1)} %get-tuple-element.25, bf16[1024,128]{1,0:T(8,128)(2,1)S(1)} %get-tuple-element.24), kind=kOutput, calls=%fused_computation | convolution fusion | flops 3225157632 | bytes 12320768 | tf_op jit(solution)/shard_map/dot_general | solution.py:423
  72.7 0.5 fusion.22
  73.3 0.1 copy-done.8
  73.4 24.2 %shard_map.102 = (bf16[4096,128]{1,0:T(8,128)(2,1)S(1)}, f32[8192,128]{1,0:T(8,128)}) custom-call(s32[256]{0:T(256)S(1)} %reshape_squeeze.3.cols_ref, s32[32]{0:T(128)S(1)} %bitcast.25, bf16[4096,128]{1,0:T(8,128)(2,1)S(1)} %get-tuple-element.29.q_ref, bf16[4096,128]{1,0:T(8,128)(2,1)S(1)} %get-tuple-element.28.k_ref, ...), custom_call_target="tpu_custom_call" | custom-call | tf_op jit(solution)/shard_map/pallas_call | solution.py:180
  97.6 1.0 copy-done.2
  98.5 1.0 copy-done.4
  99.5 1.0 copy-done.6
  100.5 15.7 %all-gather.5.cloned.1.call-done.co_ref = bf16[4096,1024]{1,0:T(8,128)(2,1)} async-done(((bf16[512,1024]{1,0:T(8,128)(2,1)}), bf16[4096,1024]{1,0:T(8,128)(2,1)}) %all-gather.5.cloned.1.call-update) | async-done | bytes 8388624 | tf_op jit(solution)/shard_map/all_gather | solution.py:415
  116.2 6.9 %fusion.do_ref = bf16[4096,128]{1,0:T(8,128)(2,1)} fusion(bf16[4096,1024]{1,0:T(8,128)(2,1)} %all-gather.5.cloned.1.call-done.co_ref, bf16[1024,1024]{1,0:T(8,128)(2,1)S(1)} %copy-done, s32[]{:T(128)S(6)} %select_n.15), kind=kOutput, calls=%fused_computation.2 | convolution fusion | flops 1074266112 | bytes 9699332 | tf_op jit(solution)/shard_map/dot_general | solution.py:433
  123.1 29.4 %shard_map.103 = (bf16[4096,128]{1,0:T(8,128)(2,1)S(1)}, bf16[4096,128]{1,0:T(8,128)(2,1)S(1)}, bf16[4096,128]{1,0:T(8,128)(2,1)S(1)}) custom-call(s32[256]{0:T(256)S(1)} %reshape_squeeze.3.cols_ref, s32[32]{0:T(128)S(1)} %bitcast.26, bf16[4096,128]{1,0:T(8,128)(2,1)S(1)} %copy-done.5, bf16[4096,128]{1,0:T(8,128)(2,1)S(1)} %copy-done.3, ...), custom_call_target="tpu_custom_call" | custom-call | tf_op jit(solution)/shard_map/pallas_call | solution.py:194
  152.5 2.1 pad_maximum_fusion
  154.6 61.2 %shard_map.104 = (bf16[16,64,384]{2,1,0:T(8,128)(2,1)}, bf16[16,8,1024]{2,1,0:T(8,128)(2,1)S(1)}, bf16[512,3072]{1,0:T(8,128)(2,1)}, bf16[512,1024]{1,0:T(8,128)(2,1)S(1)}) custom-call(bf16[4096,1024]{1,0:T(8,128)(2,1)} %all-gather.3.cloned.1.call-done.na_ref, bf16[4096,1024]{1,0:T(8,128)(2,1)} %all-gather.5.cloned.1.call-done.co_ref, ...), custom_call_target="tpu_custom_call" | custom-call | tf_op jit(solution)/shard_map/pallas_call | solution.py:379
  215.8 4.7 %all-to-all-start = ((bf16[8,128,384]{2,1,0:T(8,128)(2,1)}), bf16[8,128,384]{2,1,0:T(8,128)(2,1)}, u32[]{:S(2)}, u32[]{:S(2)}) async-start(bf16[8,128,384]{2,1,0:T(8,128)(2,1)} %bitcast.4), calls=%async_computation | async-start | bytes 1572864 | tf_op jit(solution)/shard_map/all_to_all | solution.py:457
  220.5 7.8 %multiply_reduce_fusion = (f32[512]{0:T(512)S(1)}, f32[512]{0:T(512)S(1)}, f32[512,1024]{1,0:T(8,128)S(1)}) fusion(f32[1024]{0:T(1024)S(1)} %copy-done.12, f32[512]{0:T(512)S(1)} %add_rsqrt_fusion, f32[512]{0:T(512)S(1)} %broadcast_multiply_fusion.2, bf16[512,1024]{1,0:T(8,128)(2,1)} %param.7, bf16[512,3072]{1,0:T(8,128)(2,1)} %get-tuple-element.19, ...), kind=kOutput, calls=%fused_computation.20 | convolution fusion | flops 3224894464 | bytes 12595200 | tf_op jit(solution)/shard_map/dot_general | solution.py:447
  228.3 1.8 fusion.11
  230.1 2.2 fusion.13
  232.4 1.4 all-to-all-done
  233.8 1.6 copy.18
  235.4 1.0 copy.22
  236.4 0.7 copy.24
  (26 shorter events, 0.1 us)
Async XLA Ops:
  7.2 109.0 %copy-start = (bf16[1024,1024]{1,0:T(8,128)(2,1)S(1)}, bf16[1024,1024]{1,0:T(8,128)(2,1)}, u32[]{:S(2)}) copy-start(bf16[1024,1024]{1,0:T(8,128)(2,1)} %param.10) | copy-start | bytes 6291460
  7.2 3.3 %copy-start.9 = (bf16[512,1024]{1,0:T(8,128)(2,1)S(1)}, bf16[512,1024]{1,0:T(8,128)(2,1)}, u32[]{:S(2)}) copy-start(bf16[512,1024]{1,0:T(8,128)(2,1)} %param.7) | copy-start | bytes 3145732
  7.2 3.3 %copy-start.12 = (f32[1024]{0:T(1024)S(1)}, f32[1024]{0:T(1024)}, u32[]{:S(2)}) copy-start(f32[1024]{0:T(1024)} %param.8) | copy-start | bytes 12292
  7.2 57.3 %all-gather.3.cloned.1.call-start = ((), (), s32[]{:S(2)}) async-start(), calls=%async_computation.1 | async-start | bytes 9437184 | tf_op jit(solution)/shard_map/all_gather | solution.py:414
  10.5 2.1 copy-start.13
  11.9 104.3 %all-gather.5.cloned.1.call-start = ((), (), s32[]{:S(2)}) async-start(), calls=%async_computation.2 | async-start | bytes 9437184 | tf_op jit(solution)/shard_map/all_gather | solution.py:415
  72.7 0.7 copy-start.8
  73.3 49.8 %copy-start.1 = (bf16[4096,128]{1,0:T(8,128)(2,1)}, bf16[4096,128]{1,0:T(8,128)(2,1)S(1)}, u32[]{:S(2)}) copy-start(bf16[4096,128]{1,0:T(8,128)(2,1)S(1)} %get-tuple-element.27.v_ref) | copy-start | bytes 3145732
  97.6 1.0 copy-start.2
  98.5 1.0 copy-start.4
  99.5 1.0 copy-start.6
  116.2 6.9 %copy-start.3 = (bf16[4096,128]{1,0:T(8,128)(2,1)S(1)}, bf16[4096,128]{1,0:T(8,128)(2,1)}, u32[]{:S(2)}) copy-start(bf16[4096,128]{1,0:T(8,128)(2,1)} %copy-done.2) | copy-start | bytes 3145732
  116.2 6.9 %copy-start.5 = (bf16[4096,128]{1,0:T(8,128)(2,1)S(1)}, bf16[4096,128]{1,0:T(8,128)(2,1)}, u32[]{:S(2)}) copy-start(bf16[4096,128]{1,0:T(8,128)(2,1)} %copy-done.4) | copy-start | bytes 3145732
  152.5 2.1 copy-start.7
  215.8 18.0 %all-to-all-start = ((bf16[8,128,384]{2,1,0:T(8,128)(2,1)}), bf16[8,128,384]{2,1,0:T(8,128)(2,1)}, u32[]{:S(2)}, u32[]{:S(2)}) async-start(bf16[8,128,384]{2,1,0:T(8,128)(2,1)} %bitcast.4), calls=%async_computation | async-start | bytes 1572864 | tf_op jit(solution)/shard_map/all_to_all | solution.py:457
  220.5 7.8 %copy-start.10 = (bf16[512,1024]{1,0:T(8,128)(2,1)S(1)}, bf16[512,1024]{1,0:T(8,128)(2,1)}, u32[]{:S(2)}) copy-start(bf16[512,1024]{1,0:T(8,128)(2,1)} %param.7) | copy-start | bytes 3145732
  220.5 7.8 %copy-start.11 = (bf16[512,1024]{1,0:T(8,128)(2,1)S(1)}, bf16[512,1024]{1,0:T(8,128)(2,1)}, u32[]{:S(2)}) copy-start(bf16[512,1024]{1,0:T(8,128)(2,1)} %param.13) | copy-start | bytes 3145732
Sparse Core Ops, SparseCore 0:
  12.0 52.3 all-gather.2
  66.2 49.9 all-gather.4

commit v20 on v19

--- a/solution.py
+++ b/solution.py
@@ -329,21 +329,22 @@
     x_ref[...] = qkv.reshape(x_ref.shape)
     rs = (lambda peer: x_ref.at[peer], recv, sems.at[0], sems.at[1], "dp", me, n)
     rs_started = start_all(*rs)
-    finish_all(rs_started, *rs)
     finish_all(rs_o_started, *rs_o)
-    total = x_ref[me]
     total_o = xo_ref[me]
     for k in range(1, n):
+        total_o = total_o + recv_o[lax.rem(me + k, n)]
+    gath_o[me] = total_o.astype(gath_o.dtype)
+    ag_o = (lambda peer: gath_o.at[me], gath_o, sems.at[6], sems.at[7], "dp", me, n)
+    ag_o_started = start_all(*ag_o)
+    finish_all(rs_started, *rs)
+    total = x_ref[me]
+    for k in range(1, n):
         total = total + recv[lax.rem(me + k, n)]
-        total_o = total_o + recv_o[lax.rem(me + k, n)]
     gath[me] = total.astype(gath.dtype)
-    gath_o[me] = total_o.astype(gath_o.dtype)
     ag = (lambda peer: gath.at[me], gath, sems.at[2], sems.at[3], "dp", me, n)
-    ag_o = (lambda peer: gath_o.at[me], gath_o, sems.at[6], sems.at[7], "dp", me, n)
     ag_started = start_all(*ag)
-    ag_o_started = start_all(*ag_o)
+    finish_all(ag_o_started, *ag_o)
     finish_all(ag_started, *ag)
-    finish_all(ag_o_started, *ag_o)
     o_ref[...] = gath[...]
     oo_ref[...] = gath_o[...]
     own = g_ref[here]

time: 246 us -> 246 us (level)
  no operation moved by 1% of the time
where the time goes in v20:
time: 246 us; the launch traced here: 244 us
  Pallas kernels  115 us (47%)
  waiting for transfers between devices  68.3 us (28%)
  matrix products  25.1 us (10%)
  between operations  14.2 us (6%)
  other arithmetic  8.47 us (3%)
  local copies, waits for them, and re-layouts  8.28 us (3%)
  starting transfers between devices  4.83 us (2%)
    pallas_call x1, Pallas kernels, sum_and_exchange(): pl.pallas_call(functools.partial(exchange_kernel, n, m), out_shape=(jax.S...  61.3 us
    all_gather x1, waiting for transfers between devices, body(): normed_all = lax.all_gather(normed, 'seq', axis=0, tiled=True)  50.4 us
    pallas_call x1, Pallas kernels, attention_backward(): pl.pallas_call(attn_bwd_kernel, out_shape=tuple((jax.ShapeDtypeStruct((n,...  29.3 us
    pallas_call x1, Pallas kernels, attention_forward(): pl.pallas_call(attn_fwd_kernel, out_shape=(jax.ShapeDtypeStruct((n, width...  24.1 us
    all_gather x1, waiting for transfers between devices, body(): cotan_all = lax.all_gather(cotan, 'seq', axis=0, tiled=True)  15.8 us
    dot_general x1, matrix products, body(): jnp.dot(normed_all, w_heads, preferred_element_type=jnp.float32)  8.27 us
    dot_general x1, matrix products, body(): lax.dot_general(grad_mixed, w_qkv, (((1,), (1,)), ((), ())), preferred_el...  7.75 us
    dot_general x1, matrix products, body(): lax.dot_general(cotan_all, w_out_rows, (((1,), (1,)), ((), ())), preferre...  6.88 us
  transfers between devices with their start and end apart: 3, of which 3 were waited for; matrix products, arithmetic and copies ran while one was open for 9% of the time, Pallas kernels for 10%

profile of v20, /device:TPU:0, one launch (start us, length us, event | category | flops | bytes accessed | tf_op | source)
XLA Modules:
  0.0 243.9 jit_solution(1906567315638704887)
XLA Ops:
  7.2 0.0 copy-start
  7.2 0.0 all-gather.3.cloned.1.call-start
  7.2 1.6 convert_reduce_fusion
  8.8 1.6 fusion.12
  10.5 1.4 fusion.6
  11.9 0.0 all-gather.3.cloned.1.call-update
  11.9 0.0 all-gather.5.cloned.1.call-start
  11.9 0.7 all-gather.5.cloned.1.call-update
  12.7 0.1 copy.16
  12.7 0.1 reshape_squeeze.3.cols_ref
  12.8 1.2 constant_dynamic-slice_fusion.2
  14.0 50.4 %all-gather.3.cloned.1.call-done.na_ref = bf16[4096,1024]{1,0:T(8,128)(2,1)} async-done(((bf16[512,1024]{1,0:T(8,128)(2,1)}), bf16[4096,1024]{1,0:T(8,128)(2,1)}) %all-gather.3.cloned.1.call-update) | async-done | bytes 8388624 | tf_op jit(solution)/shard_map/all_gather | solution.py:415
  64.5 8.3 %convolution_convert_fusion = bf16[4096,384]{1,0:T(8,128)(2,1)S(1)} fusion(bf16[4096,1024]{1,0:T(8,128)(2,1)} %all-gather.3.cloned.1.call-done.na_ref, bf16[1024,128]{1,0:T(8,128)(2,1)S(1)} %get-tuple-element.26, bf16[1024,128]{1,0:T(8,128)(2,1)S(1)} %get-tuple-element.25, bf16[1024,128]{1,0:T(8,128)(2,1)S(1)} %get-tuple-element.24), kind=kOutput, calls=%fused_computation | convolution fusion | flops 3225157632 | bytes 12320768 | tf_op jit(solution)/shard_map/dot_general | solution.py:424
  72.7 0.5 fusion.22
  73.3 0.1 copy-done.8
  73.4 24.1 %shard_map.102 = (bf16[4096,128]{1,0:T(8,128)(2,1)S(1)}, f32[8192,128]{1,0:T(8,128)}) custom-call(s32[256]{0:T(256)S(1)} %reshape_squeeze.3.cols_ref, s32[32]{0:T(128)S(1)} %bitcast.25, bf16[4096,128]{1,0:T(8,128)(2,1)S(1)} %get-tuple-element.29.q_ref, bf16[4096,128]{1,0:T(8,128)(2,1)S(1)} %get-tuple-element.28.k_ref, ...), custom_call_target="tpu_custom_call" | custom-call | tf_op jit(solution)/shard_map/pallas_call | solution.py:180
  97.5 1.0 copy-done.2
  98.4 1.0 copy-done.4
  99.4 1.0 copy-done.6
  100.4 15.8 %all-gather.5.cloned.1.call-done.co_ref = bf16[4096,1024]{1,0:T(8,128)(2,1)} async-done(((bf16[512,1024]{1,0:T(8,128)(2,1)}), bf16[4096,1024]{1,0:T(8,128)(2,1)}) %all-gather.5.cloned.1.call-update) | async-done | bytes 8388624 | tf_op jit(solution)/shard_map/all_gather | solution.py:416
  116.2 6.9 %fusion.do_ref = bf16[4096,128]{1,0:T(8,128)(2,1)} fusion(bf16[4096,1024]{1,0:T(8,128)(2,1)} %all-gather.5.cloned.1.call-done.co_ref, bf16[1024,1024]{1,0:T(8,128)(2,1)S(1)} %copy-done, s32[]{:T(128)S(6)} %select_n.15), kind=kOutput, calls=%fused_computation.2 | convolution fusion | flops 1074266112 | bytes 9699332 | tf_op jit(solution)/shard_map/dot_general | solution.py:434
  123.1 29.3 %shard_map.103 = (bf16[4096,128]{1,0:T(8,128)(2,1)S(1)}, bf16[4096,128]{1,0:T(8,128)(2,1)S(1)}, bf16[4096,128]{1,0:T(8,128)(2,1)S(1)}) custom-call(s32[256]{0:T(256)S(1)} %reshape_squeeze.3.cols_ref, s32[32]{0:T(128)S(1)} %bitcast.26, bf16[4096,128]{1,0:T(8,128)(2,1)S(1)} %copy-done.5, bf16[4096,128]{1,0:T(8,128)(2,1)S(1)} %copy-done.3, ...), custom_call_target="tpu_custom_call" | custom-call | tf_op jit(solution)/shard_map/pallas_call | solution.py:194
  152.4 2.1 pad_maximum_fusion
  154.5 61.3 %shard_map.104 = (bf16[16,64,384]{2,1,0:T(8,128)(2,1)}, bf16[16,8,1024]{2,1,0:T(8,128)(2,1)S(1)}, bf16[512,3072]{1,0:T(8,128)(2,1)}, bf16[512,1024]{1,0:T(8,128)(2,1)S(1)}) custom-call(bf16[4096,1024]{1,0:T(8,128)(2,1)} %all-gather.3.cloned.1.call-done.na_ref, bf16[4096,1024]{1,0:T(8,128)(2,1)} %all-gather.5.cloned.1.call-done.co_ref, ...), custom_call_target="tpu_custom_call" | custom-call | tf_op jit(solution)/shard_map/pallas_call | solution.py:380
  215.8 4.7 %all-to-all-start = ((bf16[8,128,384]{2,1,0:T(8,128)(2,1)}), bf16[8,128,384]{2,1,0:T(8,128)(2,1)}, u32[]{:S(2)}, u32[]{:S(2)}) async-start(bf16[8,128,384]{2,1,0:T(8,128)(2,1)} %bitcast.4), calls=%async_computation | async-start | bytes 1572864 | tf_op jit(solution)/shard_map/all_to_all | solution.py:458
  220.5 7.7 %multiply_reduce_fusion = (f32[512]{0:T(512)S(1)}, f32[512]{0:T(512)S(1)}, f32[512,1024]{1,0:T(8,128)S(1)}) fusion(f32[1024]{0:T(1024)S(1)} %copy-done.12, f32[512]{0:T(512)S(1)} %add_rsqrt_fusion, f32[512]{0:T(512)S(1)} %broadcast_multiply_fusion.2, bf16[512,1024]{1,0:T(8,128)(2,1)} %param.7, bf16[512,3072]{1,0:T(8,128)(2,1)} %get-tuple-element.19, ...), kind=kOutput, calls=%fused_computation.20 | convolution fusion | flops 3224894464 | bytes 12595200 | tf_op jit(solution)/shard_map/dot_general | solution.py:448
  228.3 1.8 fusion.11
  230.1 2.2 fusion.13
  232.3 1.4 all-to-all-done
  233.8 1.6 copy.18
  235.4 1.0 copy.22
  236.4 0.7 copy.24
  (26 shorter events, 0.1 us)
Async XLA Ops:
  7.2 109.0 %copy-start = (bf16[1024,1024]{1,0:T(8,128)(2,1)S(1)}, bf16[1024,1024]{1,0:T(8,128)(2,1)}, u32[]{:S(2)}) copy-start(bf16[1024,1024]{1,0:T(8,128)(2,1)} %param.10) | copy-start | bytes 6291460
  7.2 3.3 %copy-start.9 = (bf16[512,1024]{1,0:T(8,128)(2,1)S(1)}, bf16[512,1024]{1,0:T(8,128)(2,1)}, u32[]{:S(2)}) copy-start(bf16[512,1024]{1,0:T(8,128)(2,1)} %param.7) | copy-start | bytes 3145732
  7.2 3.3 %copy-start.12 = (f32[1024]{0:T(1024)S(1)}, f32[1024]{0:T(1024)}, u32[]{:S(2)}) copy-start(f32[1024]{0:T(1024)} %param.8) | copy-start | bytes 12292
  7.2 57.3 %all-gather.3.cloned.1.call-start = ((), (), s32[]{:S(2)}) async-start(), calls=%async_computation.1 | async-start | bytes 9437184 | tf_op jit(solution)/shard_map/all_gather | solution.py:415
  10.5 2.1 copy-start.13
  11.9 104.3 %all-gather.5.cloned.1.call-start = ((), (), s32[]{:S(2)}) async-start(), calls=%async_computation.2 | async-start | bytes 9437184 | tf_op jit(solution)/shard_map/all_gather | solution.py:416
  72.7 0.7 copy-start.8
  73.3 49.8 %copy-start.1 = (bf16[4096,128]{1,0:T(8,128)(2,1)}, bf16[4096,128]{1,0:T(8,128)(2,1)S(1)}, u32[]{:S(2)}) copy-start(bf16[4096,128]{1,0:T(8,128)(2,1)S(1)} %get-tuple-element.27.v_ref) | copy-start | bytes 3145732
  97.5 1.0 copy-start.2
  98.4 1.0 copy-start.4
  99.4 1.0 copy-start.6
  116.2 6.9 %copy-start.3 = (bf16[4096,128]{1,0:T(8,128)(2,1)S(1)}, bf16[4096,128]{1,0:T(8,128)(2,1)}, u32[]{:S(2)}) copy-start(bf16[4096,128]{1,0:T(8,128)(2,1)} %copy-done.2) | copy-start | bytes 3145732
  116.2 6.9 %copy-start.5 = (bf16[4096,128]{1,0:T(8,128)(2,1)S(1)}, bf16[4096,128]{1,0:T(8,128)(2,1)}, u32[]{:S(2)}) copy-start(bf16[4096,128]{1,0:T(8,128)(2,1)} %copy-done.4) | copy-start | bytes 3145732
  152.4 2.1 copy-start.7
  215.8 18.0 %all-to-all-start = ((bf16[8,128,384]{2,1,0:T(8,128)(2,1)}), bf16[8,128,384]{2,1,0:T(8,128)(2,1)}, u32[]{:S(2)}, u32[]{:S(2)}) async-start(bf16[8,128,384]{2,1,0:T(8,128)(2,1)} %bitcast.4), calls=%async_computation | async-start | bytes 1572864 | tf_op jit(solution)/shard_map/all_to_all | solution.py:458
  220.5 7.8 %copy-start.10 = (bf16[512,1024]{1,0:T(8,128)(2,1)S(1)}, bf16[512,1024]{1,0:T(8,128)(2,1)}, u32[]{:S(2)}) copy-start(bf16[512,1024]{1,0:T(8,128)(2,1)} %param.7) | copy-start | bytes 3145732
  220.5 7.8 %copy-start.11 = (bf16[512,1024]{1,0:T(8,128)(2,1)S(1)}, bf16[512,1024]{1,0:T(8,128)(2,1)}, u32[]{:S(2)}) copy-start(bf16[512,1024]{1,0:T(8,128)(2,1)} %param.13) | copy-start | bytes 3145732
Sparse Core Ops, SparseCore 0:
  12.0 52.3 all-gather.2
  66.2 49.9 all-gather.4
